TPU v7x, 32 devices: a whole 2x2x4 slice. The times are simulated.
32 devices in a mesh: ctx: 8 (over z, x), fsdp: 4 (over y, core).
Axes of the slice: x: 2, y: 2, z: 4, core: 2. Of those that a mesh axis runs over, the one named last changes fastest.
Arguments:
- tokens: bfloat16 [4, 2048, 768], P('fsdp', 'ctx'), may hold values from -6 to 6
- lengths: int32 [4, 4], P('fsdp'), may hold values from 1 to 1024, 2048 in all within a row
- span_order: int32 [4, 16], P('fsdp'), may hold values from 0 to 15, each once within a row
- w_query: bfloat16 [768, 768], P('fsdp'), may hold values from -0.109375 to 0.109375
- w_key: bfloat16 [768, 768], P('fsdp'), may hold values from -0.109375 to 0.109375
- w_value: bfloat16 [768, 768], P('fsdp'), may hold values from -0.21875 to 0.21875
- w_out: bfloat16 [768, 768], P('fsdp'), may hold values from -1.25 to 1.25
- w_in: bfloat16 [768, 3072], P('fsdp'), may hold values from -0.21875 to 0.21875
- w_ffn_out: bfloat16 [3072, 768], P('fsdp'), may hold values from -0.109375 to 0.109375
- gain_attn: bfloat16 [768], P('fsdp'), may hold values from 0.099609375 to 1.8984375
- gain_ffn: bfloat16 [768], P('fsdp'), may hold values from 0.099609375 to 1.8984375
- rel_table: bfloat16 [32, 12], P('fsdp'), may hold values from -4 to 4
- cotangent: bfloat16 [4, 2048, 768], P('fsdp', 'ctx'), may hold values from -6 to 6
Outputs:
- output: bfloat16 [4, 2048, 768], P('fsdp', 'ctx')
- grad_tokens: bfloat16 [4, 2048, 768], P('fsdp', 'ctx')
- grad_query: float32 [768, 768], P('fsdp')
- grad_key: float32 [768, 768], P('fsdp')
- grad_value: float32 [768, 768], P('fsdp')
- grad_out: float32 [768, 768], P('fsdp')
- grad_in: float32 [768, 3072], P('fsdp')
- grad_ffn_out: float32 [3072, 768], P('fsdp')
- grad_gain_attn: float32 [768], P('fsdp')
- grad_gain_ffn: float32 [768], P('fsdp')
- grad_table: float32 [32, 12], P('fsdp')
Inputs may be any that keep to these rules, and one draw needn't show every extreme that they name: Each group's 4 lengths sum to 2048, and the longest is exactly 1024. `span_order`: each row is a permutation of the group's span numbers; slot s lies on ctx device s // 2.
All inputs are finite; a program needn't handle non-finite values.
Results may differ from a plain program's by a relative error of at most 0.02.
Values may be sent and summed in bfloat16 or wider, within the bound.
No kernel may reach another device: no remote copies, remote signals or barrier semaphores. Data moves between devices by JAX's collectives and lax.ppermute only.
A program may use at most 192 MiB of HBM per device.

v0:
```python
import jax
import jax.numpy as jnp
from jax import lax
from jax.sharding import PartitionSpec as P

D = 768
H = 12
DH = 64
NB = 32
SPAN = 128


norm_eps = 1e-06
masked_score = -1e30


def rms_norm(values, gain_vec):
    inv_rms = lax.rsqrt(jnp.mean(values * values, axis=-1, keepdims=True) + norm_eps)
    return values * inv_rms * gain_vec


def gelu_tanh(values):
    return (
        0.5
        * values
        * (1.0 + jnp.tanh(0.7978845608028654 * (values + 0.044715 * values * values * values)))
    )


def bucket_of(relative):
    distance = jnp.abs(relative)
    far_steps = jnp.zeros_like(distance)
    for exponent in range(1, 8):
        far_steps = far_steps + (distance * distance >= 64 * 2**exponent).astype(jnp.int32)
    magnitude = jnp.where(distance < 8, distance, 8 + far_steps)
    return magnitude + jnp.where(relative > 0, 16, 0).astype(jnp.int32)


def block_score_matrix(
    query_heads, key_block, query_pos, key_pos, query_segment_ids, key_seg, bucket_bias_matrix
):
    raw_scores = jnp.einsum(
        "qhd,khd->hqk", query_heads, key_block, preferred_element_type=jnp.float32
    )
    buckets = bucket_of(key_pos[None, :] - query_pos[:, None])
    bucket_indicator = (buckets[None] == jnp.arange(NB, dtype=jnp.int32)[:, None, None]).astype(
        jnp.bfloat16
    )
    position_bias_values = jnp.einsum(
        "umx,uv->vmx", bucket_indicator, bucket_bias_matrix, preferred_element_type=jnp.float32
    )
    inside = (query_segment_ids[:, None] == key_seg[None, :])[None]
    return (jnp.where(inside, raw_scores + position_bias_values, masked_score), bucket_indicator)


def on_device(
    tokens,
    lengths,
    span_order,
    w_query,
    w_key,
    w_value,
    w_out,
    w_in,
    w_ffn_out,
    gain_attn,
    gain_ffn,
    rel_table,
    cotangent,
):
    gathered = (
        lax.all_gather(w_query, "fsdp", axis=0, tiled=True),
        lax.all_gather(w_key, "fsdp", axis=0, tiled=True),
        lax.all_gather(w_value, "fsdp", axis=0, tiled=True),
        lax.all_gather(w_out, "fsdp", axis=0, tiled=True),
        lax.all_gather(w_in, "fsdp", axis=0, tiled=True),
        lax.all_gather(w_ffn_out, "fsdp", axis=0, tiled=True),
        lax.all_gather(gain_attn, "fsdp", axis=0, tiled=True),
        lax.all_gather(gain_ffn, "fsdp", axis=0, tiled=True),
        lax.all_gather(rel_table, "fsdp", axis=0, tiled=True),
    )
    query_w, key_w, value_w, out_w, in_w, ffn_w, attn_gain, ffn_gain, bucket_bias_matrix = gathered
    ctx_count = lax.axis_size("ctx")
    local_rows = tokens.shape[1]
    group_rows = local_rows * ctx_count
    block_len = min(512, group_rows)
    block_count = group_rows // block_len
    row_index = jnp.arange(group_rows, dtype=jnp.int32)
    key_pos = jnp.repeat(span_order[0], SPAN) * SPAN + row_index % SPAN
    bounds = jnp.cumsum(lengths[0])
    key_seg = jnp.sum((key_pos[:, None] >= bounds[None, :-1]).astype(jnp.int32), axis=1)
    row_start = lax.axis_index("ctx") * local_rows
    query_pos = lax.dynamic_slice_in_dim(key_pos, row_start, local_rows)
    query_segment_ids = lax.dynamic_slice_in_dim(key_seg, row_start, local_rows)
    inputs_f = tokens[0].astype(jnp.float32)
    normed, norm_attn_back = jax.vjp(rms_norm, inputs_f, attn_gain.astype(jnp.float32))
    normed_b = normed.astype(jnp.bfloat16)
    query_b = jnp.dot(normed_b, query_w, preferred_element_type=jnp.float32).astype(jnp.bfloat16)
    key_b = jnp.dot(normed_b, key_w, preferred_element_type=jnp.float32).astype(jnp.bfloat16)
    value_b = jnp.dot(normed_b, value_w, preferred_element_type=jnp.float32).astype(jnp.bfloat16)
    all_keys, all_values = (
        lax.all_gather(key_b, "ctx", axis=0, tiled=True),
        lax.all_gather(value_b, "ctx", axis=0, tiled=True),
    )
    query_heads = query_b.reshape(local_rows, H, DH)
    block_inputs = (
        all_keys.reshape(block_count, block_len, H, DH),
        all_values.reshape(block_count, block_len, H, DH),
        key_pos.reshape(block_count, block_len),
        key_seg.reshape(block_count, block_len),
    )

    def max_step(running, inputs):
        run_max, run_sum = running
        key_block, value_block, pos_block, seg_block = inputs
        scores, bucket_indicator = block_score_matrix(
            query_heads,
            key_block,
            query_pos,
            pos_block,
            query_segment_ids,
            seg_block,
            bucket_bias_matrix,
        )
        new_max = jnp.maximum(run_max, jnp.max(scores, axis=2))
        run_sum = run_sum * jnp.exp(run_max - new_max) + jnp.sum(
            jnp.exp(scores - new_max[:, :, None]), axis=2
        )
        return ((new_max, run_sum), None)

    start_max = jnp.full((H, local_rows), masked_score, jnp.float32)
    (row_max, row_sum), unused = lax.scan(
        max_step, (start_max, jnp.zeros((H, local_rows), jnp.float32)), block_inputs
    )
    log_total = row_max + jnp.log(row_sum)

    def out_step(accumulated, inputs):
        key_block, value_block, pos_block, seg_block = inputs
        scores, bucket_indicator = block_score_matrix(
            query_heads,
            key_block,
            query_pos,
            pos_block,
            query_segment_ids,
            seg_block,
            bucket_bias_matrix,
        )
        probabilities = jnp.exp(scores - log_total[:, :, None]).astype(jnp.bfloat16)
        return (
            accumulated
            + jnp.einsum(
                "hqk,khd->qhd", probabilities, value_block, preferred_element_type=jnp.float32
            ),
            None,
        )

    attended, unused = lax.scan(out_step, jnp.zeros((local_rows, H, DH), jnp.float32), block_inputs)
    attended_b = attended.reshape(local_rows, D).astype(jnp.bfloat16)
    residual = inputs_f + jnp.dot(attended_b, out_w, preferred_element_type=jnp.float32)
    normed_ffn, norm_ffn_back = jax.vjp(rms_norm, residual, ffn_gain.astype(jnp.float32))
    feedforward_normed_block = normed_ffn.astype(jnp.bfloat16)
    up_rows = jnp.dot(feedforward_normed_block, in_w, preferred_element_type=jnp.float32)
    activated, gelu_back = jax.vjp(gelu_tanh, up_rows)
    activated_b = activated.astype(jnp.bfloat16)
    result = residual + jnp.dot(activated_b, ffn_w, preferred_element_type=jnp.float32)
    back_weights = (
        lax.all_gather(w_query, "fsdp", axis=0, tiled=True),
        lax.all_gather(w_key, "fsdp", axis=0, tiled=True),
        lax.all_gather(w_value, "fsdp", axis=0, tiled=True),
        lax.all_gather(w_out, "fsdp", axis=0, tiled=True),
        lax.all_gather(w_in, "fsdp", axis=0, tiled=True),
        lax.all_gather(w_ffn_out, "fsdp", axis=0, tiled=True),
        lax.all_gather(gain_attn, "fsdp", axis=0, tiled=True),
        lax.all_gather(gain_ffn, "fsdp", axis=0, tiled=True),
        lax.all_gather(rel_table, "fsdp", axis=0, tiled=True),
    )
    query_w, key_w, value_w, out_w, in_w, ffn_w, attn_gain, ffn_gain, bucket_bias_matrix = (
        back_weights
    )
    grad_b = cotangent[0]
    grad_ffn = jnp.einsum("tf,td->fd", activated_b, grad_b, preferred_element_type=jnp.float32)
    grad_act = jnp.einsum("td,fd->tf", grad_b, ffn_w, preferred_element_type=jnp.float32)
    (grad_up,) = gelu_back(grad_act)
    grad_up_b = grad_up.astype(jnp.bfloat16)
    grad_inw = jnp.einsum(
        "td,tf->df", feedforward_normed_block, grad_up_b, preferred_element_type=jnp.float32
    )
    grad_normed_ffn = jnp.einsum("tf,df->td", grad_up_b, in_w, preferred_element_type=jnp.float32)
    grad_resid_norm, grad_ffn_gain = norm_ffn_back(grad_normed_ffn)
    grad_resid = grad_b.astype(jnp.float32) + grad_resid_norm
    grad_resid_b = grad_resid.astype(jnp.bfloat16)
    grad_outw = jnp.einsum(
        "tc,td->cd", attended_b, grad_resid_b, preferred_element_type=jnp.float32
    )
    grad_att_b = jnp.einsum(
        "td,cd->tc", grad_resid_b, out_w, preferred_element_type=jnp.float32
    ).astype(jnp.bfloat16)
    grad_heads = grad_att_b.reshape(local_rows, H, DH)
    row_delta = jnp.einsum("qhd,qhd->hq", grad_heads.astype(jnp.float32), attended)

    def back_step(running, inputs):
        grad_query, grad_table = running
        key_block, value_block, pos_block, seg_block = inputs
        scores, bucket_indicator = block_score_matrix(
            query_heads,
            key_block,
            query_pos,
            pos_block,
            query_segment_ids,
            seg_block,
            bucket_bias_matrix,
        )
        probabilities = jnp.exp(scores - log_total[:, :, None])
        grad_prob = jnp.einsum(
            "qhd,khd->hqk", grad_heads, value_block, preferred_element_type=jnp.float32
        )
        score_gradient_matrix = (probabilities * (grad_prob - row_delta[:, :, None])).astype(
            jnp.bfloat16
        )
        grad_query = grad_query + jnp.einsum(
            "hqk,khd->qhd", score_gradient_matrix, key_block, preferred_element_type=jnp.float32
        )
        grad_table = grad_table + jnp.einsum(
            "fry,wry->fw",
            bucket_indicator,
            score_gradient_matrix,
            preferred_element_type=jnp.float32,
        )
        grad_key = jnp.einsum(
            "hqk,qhd->khd", score_gradient_matrix, query_heads, preferred_element_type=jnp.float32
        )
        grad_value = jnp.einsum(
            "hqk,qhd->khd",
            probabilities.astype(jnp.bfloat16),
            grad_heads,
            preferred_element_type=jnp.float32,
        )
        return ((grad_query, grad_table), (grad_key, grad_value))

    start_grads = (jnp.zeros((local_rows, H, DH), jnp.float32), jnp.zeros((NB, H), jnp.float32))
    (grad_query, grad_table), (grad_keys, grad_values) = lax.scan(
        back_step, start_grads, block_inputs
    )
    own_keys, own_values = (
        lax.psum_scatter(
            grad_keys.reshape(group_rows, D).astype(jnp.bfloat16),
            "ctx",
            scatter_dimension=0,
            tiled=True,
        ).astype(jnp.float32),
        lax.psum_scatter(
            grad_values.reshape(group_rows, D).astype(jnp.bfloat16),
            "ctx",
            scatter_dimension=0,
            tiled=True,
        ).astype(jnp.float32),
    )
    grad_q_b = grad_query.reshape(local_rows, D).astype(jnp.bfloat16)
    grad_k_b = own_keys.astype(jnp.bfloat16)
    grad_v_b = own_values.astype(jnp.bfloat16)
    query_weight_gradient = jnp.einsum(
        "tc,td->cd", normed_b, grad_q_b, preferred_element_type=jnp.float32
    )
    grad_kw = jnp.einsum("tc,td->cd", normed_b, grad_k_b, preferred_element_type=jnp.float32)
    grad_vw = jnp.einsum("tc,td->cd", normed_b, grad_v_b, preferred_element_type=jnp.float32)
    grad_normed = jnp.einsum("td,cd->tc", grad_q_b, query_w, preferred_element_type=jnp.float32)
    grad_normed = grad_normed + jnp.einsum(
        "td,cd->tc", grad_k_b, key_w, preferred_element_type=jnp.float32
    )
    grad_normed = grad_normed + jnp.einsum(
        "td,cd->tc", grad_v_b, value_w, preferred_element_type=jnp.float32
    )
    grad_input_norm, grad_attn_gain = norm_attn_back(grad_normed)
    grad_input = (grad_resid + grad_input_norm).astype(jnp.bfloat16)
    pieces = (
        lax.psum_scatter(
            query_weight_gradient.astype(jnp.bfloat16), "fsdp", scatter_dimension=0, tiled=True
        ).astype(jnp.float32),
        lax.psum_scatter(
            grad_kw.astype(jnp.bfloat16), "fsdp", scatter_dimension=0, tiled=True
        ).astype(jnp.float32),
        lax.psum_scatter(
            grad_vw.astype(jnp.bfloat16), "fsdp", scatter_dimension=0, tiled=True
        ).astype(jnp.float32),
        lax.psum_scatter(
            grad_outw.astype(jnp.bfloat16), "fsdp", scatter_dimension=0, tiled=True
        ).astype(jnp.float32),
        lax.psum_scatter(
            grad_inw.astype(jnp.bfloat16), "fsdp", scatter_dimension=0, tiled=True
        ).astype(jnp.float32),
        lax.psum_scatter(
            grad_ffn.astype(jnp.bfloat16), "fsdp", scatter_dimension=0, tiled=True
        ).astype(jnp.float32),
        lax.psum_scatter(
            grad_attn_gain.astype(jnp.bfloat16), "fsdp", scatter_dimension=0, tiled=True
        ).astype(jnp.float32),
        lax.psum_scatter(
            grad_ffn_gain.astype(jnp.bfloat16), "fsdp", scatter_dimension=0, tiled=True
        ).astype(jnp.float32),
        lax.psum_scatter(
            grad_table.astype(jnp.bfloat16), "fsdp", scatter_dimension=0, tiled=True
        ).astype(jnp.float32),
    )
    final_grads = (
        lax.psum(pieces[0].astype(jnp.bfloat16), "ctx").astype(jnp.float32),
        lax.psum(pieces[1].astype(jnp.bfloat16), "ctx").astype(jnp.float32),
        lax.psum(pieces[2].astype(jnp.bfloat16), "ctx").astype(jnp.float32),
        lax.psum(pieces[3].astype(jnp.bfloat16), "ctx").astype(jnp.float32),
        lax.psum(pieces[4].astype(jnp.bfloat16), "ctx").astype(jnp.float32),
        lax.psum(pieces[5].astype(jnp.bfloat16), "ctx").astype(jnp.float32),
        lax.psum(pieces[6].astype(jnp.bfloat16), "ctx").astype(jnp.float32),
        lax.psum(pieces[7].astype(jnp.bfloat16), "ctx").astype(jnp.float32),
        lax.psum(pieces[8].astype(jnp.bfloat16), "ctx").astype(jnp.float32),
    )
    return (
        result.astype(jnp.bfloat16)[None],
        grad_input[None],
        final_grads[0],
        final_grads[1],
        final_grads[2],
        final_grads[3],
        final_grads[4],
        final_grads[5],
        final_grads[6],
        final_grads[7],
        final_grads[8],
    )


def solution(mesh):
    in_specs = (
        P("fsdp", "ctx", None),
        P("fsdp", None),
        P("fsdp", None),
        P("fsdp", None),
        P("fsdp", None),
        P("fsdp", None),
        P("fsdp", None),
        P("fsdp", None),
        P("fsdp", None),
        P("fsdp"),
        P("fsdp"),
        P("fsdp", None),
        P("fsdp", "ctx", None),
    )
    out_specs = (
        P("fsdp", "ctx", None),
        P("fsdp", "ctx", None),
        P("fsdp", None),
        P("fsdp", None),
        P("fsdp", None),
        P("fsdp", None),
        P("fsdp", None),
        P("fsdp", None),
        P("fsdp"),
        P("fsdp"),
        P("fsdp", None),
    )
    return jax.shard_map(
        on_device, mesh=mesh, in_specs=in_specs, out_specs=out_specs, check_vma=False
    )
```

profile of v0, /device:TPU:0, one launch (start us, length us, event | category | flops | bytes accessed | tf_op | source)
XLA Modules:
  0.0 1097.1 jit_solution(17188709474122920209)
XLA Ops:
  13.1 8.3 all-reduce.8
  22.7 7.1 all-gather.13.cloned.1.call-done
  32.5 16.3 %all-gather.9.cloned.1.call-done = bf16[768,768]{1,0:T(8,128)(2,1)} async-done(((bf16[192,768]{1,0:T(8,128)(2,1)}), bf16[768,768]{1,0:T(8,128)(2,1)}) %all-gather.9.cloned.1.call-update) | async-done | bytes 1179664 | tf_op jit(solution)/shard_map/all_gather | solution.py:74
  69.9 61.1 %all-gather.15.cloned.1.call-done = bf16[2048,768]{1,0:T(8,128)(2,1)} async-done(((bf16[256,768]{1,0:T(8,128)(2,1)}), bf16[2048,768]{1,0:T(8,128)(2,1)}) %all-gather.15.cloned.1.call-update) | async-done | bytes 3145744 | tf_op jit(solution)/shard_map/all_gather | solution.py:102
  141.0 99.2 %while.41 = (s32[]{:T(128)}, f32[12,256]{1,0:T(8,128)S(1)}, f32[12,256]{1,0:T(8,128)}, s32[256]{0:T(256)}, s32[4,512]{1,0:T(4,128)}, /*index=5*/bf16[4,512,12,64...) while((s32[]{:T(128)}, f32[12,256]{1,0:T(8,128)S(1)}, ...), condition=%wide.region_6.7_spmd.clone, body=%wide.region_3.6_spmd.clone.sunk | while | flops 317996032 | bytes 40512452 | solution.py:132
  144.5 6.5 fusion.203
  151.0 9.1 copy.149
  169.5 6.5 fusion.203
  176.1 9.1 copy.149
  194.2 6.5 fusion.203
  200.7 9.1 copy.149
  218.9 6.5 fusion.203
  225.4 9.2 copy.149
  244.8 6.2 reshape.395
  256.1 101.8 %while.42 = (s32[]{:T(128)}, f32[256,12,64]{0,2,1:T(8,128)}, bf16[4,512,12,64]{1,3,2,0:T(8,128)(2,1)}, s32[256]{0:T(256)}, s32[4,512]{1,0:T(4,128)}, /*index=5*/...) while((s32[]{:T(128)}, f32[256,12,64]{0,2,1:T(8,128)}, ...), condition=%wide.region_8.9_spmd.clone, body=%wide.region_7.8_spmd.clone.sunk | while | flops 518127616 | bytes 30097836 | solution.py:157
  260.0 6.5 fusion.212
  266.5 9.1 copy.150
  275.7 6.0 fusion.213
  285.2 6.5 fusion.212
  291.7 9.1 copy.150
  300.8 6.2 fusion.213
  310.5 6.5 fusion.212
  317.1 9.1 copy.150
  326.2 6.2 fusion.213
  335.9 6.5 fusion.212
  342.5 9.1 copy.150
  351.6 6.2 fusion.213
  368.5 6.8 fusion.87
  384.6 176.5 %while.43 = (s32[]{:T(128)}, f32[256,12,64]{0,2,1:T(8,128)}, f32[32,12]{0,1:T(8,128)}, bf16[4,512,12,64]{1,3,2,0:T(8,128)(2,1)}, bf16[4,512,12,64]{1,3,2,0:T(8,1...) while((s32[]{:T(128)}, f32[256,12,64]{0,2,1:T(8,128)}, ...), condition=%wide.region_12.13_spmd.clone, body=%wide.region_11.12_spmd.clone.sunk | while | flops 1231684352 | bytes 127494288 | solution.py:241
  393.7 9.1 copy.151
  437.5 9.1 copy.151
  475.8 5.9 fusion.227
  481.6 9.1 copy.151
  519.9 5.9 fusion.227
  525.7 9.1 copy.151
  581.0 61.1 %reduce-scatter.11.cloned.1.call-done = bf16[256,768]{0,1:T(8,128)(2,1)} async-done(((bf16[2048,768]{0,1:T(8,128)(2,1)}), bf16[256,768]{0,1:T(8,128)(2,1)}) %reduce-scatter.11.cloned.1.call-update) | async-done | bytes 393232 | tf_op jit(solution)/shard_map/reduce_scatter | solution.py:251
  644.8 75.1 %reduce-scatter.9.cloned.1.call-done = bf16[256,768]{0,1:T(8,128)(2,1)} async-done(((bf16[2048,768]{0,1:T(8,128)(2,1)}), bf16[256,768]{0,1:T(8,128)(2,1)}) %reduce-scatter.9.cloned.1.call-update) | async-done | bytes 393232 | tf_op jit(solution)/shard_map/reduce_scatter | solution.py:245
  722.5 6.3 convolution_convert_fusion
  735.2 12.1 %reduce-scatter.19.cloned.1.call-done = bf16[192,768]{1,0:T(8,128)(2,1)} async-done(((bf16[768,768]{1,0:T(8,128)(2,1)}), bf16[192,768]{1,0:T(8,128)(2,1)}) %reduce-scatter.19.cloned.1.call-update) | async-done | bytes 294928 | tf_op jit(solution)/shard_map/reduce_scatter | solution.py:285
  747.2 28.9 %reduce-scatter.13.cloned.1.call-done = bf16[192,768]{1,0:T(8,128)(2,1)} async-done(((bf16[768,768]{1,0:T(8,128)(2,1)}), bf16[192,768]{1,0:T(8,128)(2,1)}) %reduce-scatter.13.cloned.1.call-update) | async-done | bytes 294928 | tf_op jit(solution)/shard_map/reduce_scatter | solution.py:276
  776.2 28.3 %reduce-scatter.17.cloned.1.call-done = bf16[192,768]{1,0:T(8,128)(2,1)} async-done(((bf16[768,768]{1,0:T(8,128)(2,1)}), bf16[192,768]{1,0:T(8,128)(2,1)}) %reduce-scatter.17.cloned.1.call-update) | async-done | bytes 294928 | tf_op jit(solution)/shard_map/reduce_scatter | solution.py:282
  804.5 28.3 %reduce-scatter.15.cloned.1.call-done = bf16[192,768]{1,0:T(8,128)(2,1)} async-done(((bf16[768,768]{1,0:T(8,128)(2,1)}), bf16[192,768]{1,0:T(8,128)(2,1)}) %reduce-scatter.15.cloned.1.call-update) | async-done | bytes 294928 | tf_op jit(solution)/shard_map/reduce_scatter | solution.py:279
  832.8 50.2 %reduce-scatter.23.cloned.1.call-done = bf16[768,768]{1,0:T(8,128)(2,1)} async-done(((bf16[3072,768]{1,0:T(8,128)(2,1)}), bf16[768,768]{1,0:T(8,128)(2,1)}) %reduce-scatter.23.cloned.1.call-update) | async-done | bytes 1179664 | tf_op jit(solution)/shard_map/reduce_scatter | solution.py:291
  883.0 50.4 %reduce-scatter.21.cloned.1.call-done = bf16[192,3072]{1,0:T(8,128)(2,1)} async-done(((bf16[768,3072]{1,0:T(8,128)(2,1)}), bf16[192,3072]{1,0:T(8,128)(2,1)}) %reduce-scatter.21.cloned.1.call-update) | async-done | bytes 1179664 | tf_op jit(solution)/shard_map/reduce_scatter | solution.py:288
  936.6 6.1 fusion.91
  945.2 10.9 all-reduce.7
  956.3 22.7 %all-reduce.5 = (bf16[192]{0:T(256)(128)(2,1)S(1)}, bf16[192]{0:T(256)(128)(2,1)S(1)}, bf16[8,12]{1,0:T(8,128)(2,1)S(1)}) all-reduce(bf16[192]{0:T(256)(128)(2,1)S(1)} %dynamic-slice.3, bf16[192]{0:T(256)(128)(2,1)S(1)} %dynamic-slice.5, bf16[8,12]{1,0:T(8,128)(2,1)S(1)} %constant_dynamic-slice_fusion.6), channel_id=1, replica_groups=mesh['ctx'=8,'fsdp'=4] {'ctx'}, use_global_device_ids=true, to_apply=%region_30.31 | all-reduce | flops 480 | bytes 1920 | tf_op jit(solution)/shard_map/psum | solution.py:311
  981.7 97.7 %all-reduce.11.cloned.1.call-done = (bf16[192,768]{1,0:T(8,128)(2,1)}, bf16[192,768]{1,0:T(8,128)(2,1)}, bf16[192,768]{1,0:T(8,128)(2,1)}, bf16[192,768]{1,0:T(8...) async-done(((bf16[192,768]{1,0:T(8,128)(2,1)}, bf16[192,768]{1,0:T(8,128)(2,1)}, bf16[192,768]{1,0:T(8,128)(2,1)}, bf16[192,768]{1,0:T(8,128)(2,1)}, ...) | async-done | bytes 3538960 | tf_op jit(solution)/shard_map/psum | solution.py:305
  (357 shorter events, 296.6 us)
Async XLA Ops:
  7.2 41.7 %copy-start.6 = (bf16[1,256,768]{2,1,0:T(8,128)(2,1)S(1)}, bf16[1,256,768]{2,1,0:T(8,128)(2,1)}, u32[]{:S(2)}) copy-start(bf16[1,256,768]{2,1,0:T(8,128)(2,1)} %param.19) | copy-start | bytes 1179652
  7.2 22.6 %all-gather.13.cloned.1.call-start = ((), (), s32[]{:S(2)}) async-start(), calls=%async_computation.10 | async-start | bytes 1474560 | tf_op jit(solution)/shard_map/all_gather | solution.py:73
  7.9 40.9 %all-gather.9.cloned.1.call-start = ((), (), s32[]{:S(2)}) async-start(), calls=%async_computation.8 | async-start | bytes 1474560 | tf_op jit(solution)/shard_map/all_gather | solution.py:74
  8.7 59.3 %all-gather.17.cloned.1.call-start = ((), (), s32[]{:S(2)}) async-start(), calls=%async_computation.12 | async-start | bytes 1474560 | tf_op jit(solution)/shard_map/all_gather | solution.py:72
  9.4 121.6 %all-gather.15.cloned.1.call-start = ((), (), s32[]{:S(2)}) async-start(), calls=%async_computation.11 | async-start | bytes 3538944 | tf_op jit(solution)/shard_map/all_gather | solution.py:102
  21.5 46.4 %copy-start.34 = (f32[768]{0:T(1024)}, f32[768]{0:T(1024)S(1)}, u32[]{:S(2)}) copy-start(f32[768]{0:T(1024)S(1)} %convert_element_type.322) | copy-start | bytes 9220
  22.6 30.1 %copy-start.41 = (f32[256]{0:T(256)}, f32[256]{0:T(256)S(1)}, u32[]{:S(2)}) copy-start(f32[256]{0:T(256)S(1)} %fusion.100) | copy-start | bytes 3076
  22.7 45.3 %copy-start.36 = (f32[256]{0:T(256)}, f32[256]{0:T(256)S(1)}, u32[]{:S(2)}) copy-start(f32[256]{0:T(256)S(1)} %fusion.126) | copy-start | bytes 3076
  32.4 21.1 %copy-start.45 = (s32[1,4]{1,0:T(1,128)S(1)}, s32[1,4]{1,0:T(1,128)}, u32[]{:S(2)}) copy-start(s32[1,4]{1,0:T(1,128)} %param.20) | copy-start | bytes 52
  32.4 21.3 %copy-start.46 = (s32[1,16]{1,0:T(1,128)S(1)}, s32[1,16]{1,0:T(1,128)}, u32[]{:S(2)}) copy-start(s32[1,16]{1,0:T(1,128)} %param.21) | copy-start | bytes 196
  32.4 24.7 %copy-start.43 = (bf16[8,12]{1,0:T(8,128)(2,1)S(1)}, bf16[8,12]{1,0:T(8,128)(2,1)}, u32[]{:S(2)}) copy-start(bf16[8,12]{1,0:T(8,128)(2,1)} %param.30) | copy-start | bytes 580
  32.5 207.7 %all-gather.11.cloned.1.call-start = ((), (), s32[]{:S(2)}) async-start(), calls=%async_computation.9 | async-start | bytes 3538944 | tf_op jit(solution)/shard_map/all_gather | solution.py:103
  51.4 308.4 %all-gather.19.cloned.1.call-start = ((), (), s32[]{:S(2)}) async-start(), calls=%async_computation.13 | async-start | bytes 1474560 | tf_op jit(solution)/shard_map/all_gather | solution.py:75
  52.0 310.7 %all-gather.21.cloned.1.call-start = ((), (), s32[]{:S(2)}) async-start(), calls=%async_computation.14 | async-start | bytes 5898240 | tf_op jit(solution)/shard_map/all_gather | solution.py:76
  52.7 315.8 %all-gather.23.cloned.1.call-start = ((), (), s32[]{:S(2)}) async-start(), calls=%async_computation.15 | async-start | bytes 5898240 | tf_op jit(solution)/shard_map/all_gather | solution.py:77
  53.5 588.6 %reduce-scatter.11.cloned.1.call-start = ((), (), s32[]{:S(2)}) async-start(), calls=%async_computation.17 | async-start | bytes 3538944 | tf_op jit(solution)/shard_map/reduce_scatter | solution.py:251
  266.5 9.2 copy-start.25
  291.7 9.1 copy-start.25
  317.1 9.1 copy-start.25
  342.5 9.1 copy-start.25
  362.7 12.7 %copy-start.38 = (f32[256]{0:T(256)}, f32[256]{0:T(256)S(1)}, u32[]{:S(2)}) copy-start(f32[256]{0:T(256)S(1)} %fusion.127) | copy-start | bytes 3076
  368.5 6.8 copy-start.4
  368.5 6.9 copy-start.8
  377.5 7.1 copy-start.23
  377.5 7.0 copy-start.32
  377.6 7.0 copy-start.33
  384.8 18.1 %copy-start = (bf16[4,512,12,64]{1,3,2,0:T(8,128)(2,1)}, bf16[4,512,12,64]{1,3,2,0:T(8,128)(2,1)S(1)}, u32[]{:S(2)}) copy-start(bf16[4,512,12,64]{1,3,2,0:T(8,128)(2,1)S(1)} %get-tuple-element.983) | copy-start | bytes 9437188 | tf_op jit(solution)/shard_map/while
  428.6 18.1 %copy-start = (bf16[4,512,12,64]{1,3,2,0:T(8,128)(2,1)}, bf16[4,512,12,64]{1,3,2,0:T(8,128)(2,1)S(1)}, u32[]{:S(2)}) copy-start(bf16[4,512,12,64]{1,3,2,0:T(8,128)(2,1)S(1)} %get-tuple-element.983) | copy-start | bytes 9437188 | tf_op jit(solution)/shard_map/while
  466.9 5.8 copy-start.1
  472.7 18.1 %copy-start = (bf16[4,512,12,64]{1,3,2,0:T(8,128)(2,1)}, bf16[4,512,12,64]{1,3,2,0:T(8,128)(2,1)S(1)}, u32[]{:S(2)}) copy-start(bf16[4,512,12,64]{1,3,2,0:T(8,128)(2,1)S(1)} %get-tuple-element.983) | copy-start | bytes 9437188 | tf_op jit(solution)/shard_map/while
  511.0 5.8 copy-start.1
  516.8 18.1 %copy-start = (bf16[4,512,12,64]{1,3,2,0:T(8,128)(2,1)}, bf16[4,512,12,64]{1,3,2,0:T(8,128)(2,1)S(1)}, u32[]{:S(2)}) copy-start(bf16[4,512,12,64]{1,3,2,0:T(8,128)(2,1)S(1)} %get-tuple-element.983) | copy-start | bytes 9437188 | tf_op jit(solution)/shard_map/while
  555.1 5.8 copy-start.1
  568.2 151.6 %reduce-scatter.9.cloned.1.call-start = ((), (), s32[]{:S(2)}) async-start(), calls=%async_computation.16 | async-start | bytes 3538944 | tf_op jit(solution)/shard_map/reduce_scatter | solution.py:245
  575.3 171.9 %reduce-scatter.19.cloned.1.call-start = ((), (), s32[]{:S(2)}) async-start(), calls=%async_computation.21 | async-start | bytes 1474560 | tf_op jit(solution)/shard_map/reduce_scatter | solution.py:285
  578.0 198.1 %reduce-scatter.13.cloned.1.call-start = ((), (), s32[]{:S(2)}) async-start(), calls=%async_computation.18 | async-start | bytes 1474560 | tf_op jit(solution)/shard_map/reduce_scatter | solution.py:276
  580.9 141.6 %copy-start.31 = (bf16[1,256,768]{2,1,0:T(8,128)(2,1)S(1)}, bf16[1,256,768]{2,1,0:T(8,128)(2,1)}, u32[]{:S(2)}) copy-start(bf16[1,256,768]{2,1,0:T(8,128)(2,1)} %param.31) | copy-start | bytes 1179652
  581.0 223.5 %reduce-scatter.17.cloned.1.call-start = ((), (), s32[]{:S(2)}) async-start(), calls=%async_computation.20 | async-start | bytes 1474560 | tf_op jit(solution)/shard_map/reduce_scatter | solution.py:282
  644.7 188.1 %reduce-scatter.15.cloned.1.call-start = ((), (), s32[]{:S(2)}) async-start(), calls=%async_computation.19 | async-start | bytes 1474560 | tf_op jit(solution)/shard_map/reduce_scatter | solution.py:279
  722.5 160.6 %reduce-scatter.23.cloned.1.call-start = ((), (), s32[]{:S(2)}) async-start(), calls=%async_computation.23 | async-start | bytes 5898240 | tf_op jit(solution)/shard_map/reduce_scatter | solution.py:291
  728.8 204.7 %reduce-scatter.21.cloned.1.call-start = ((), (), s32[]{:S(2)}) async-start(), calls=%async_computation.22 | async-start | bytes 5898240 | tf_op jit(solution)/shard_map/reduce_scatter | solution.py:288
  735.1 200.9 %copy-start.22 = (bf16[768,768]{1,0:T(8,128)(2,1)S(1)}, bf16[768,768]{1,0:T(8,128)(2,1)}, u32[]{:S(2)}) copy-start(bf16[768,768]{1,0:T(8,128)(2,1)} %all-gather.17.cloned.1.call-done) | copy-start | bytes 3538948
  735.1 344.3 %all-reduce.11.cloned.1.call-start = ((), (), s32[]{:S(2)}) async-start(), calls=%async_computation.24 | async-start | bytes 7077888 | tf_op jit(solution)/shard_map/psum | solution.py:305
  936.5 6.1 copy-start.17
  936.5 6.1 copy-start.18
  942.7 38.0 %copy-start.42 = (f32[256]{0:T(256)S(1)}, f32[256]{0:T(256)}, u32[]{:S(2)}) copy-start(f32[256]{0:T(256)} %copy-done.41) | copy-start | bytes 3076
  1079.4 7.5 copy-start.21
  1081.4 7.2 copy-start.20
  (46 other events, 107.7 us)
Sparse Core Ops, SparseCore 0:
  9.6 20.1 all-gather.12
  31.3 17.4 all-gather.8
  50.4 17.4 all-gather.16
  70.5 60.4 all-gather.14
  133.6 59.0 all-gather.10
  194.2 16.0 all-gather.18
  211.8 37.4 all-gather.20
  250.9 37.4 all-gather.22
  568.3 73.7 reduce-scatter.10
  645.5 74.2 reduce-scatter.8
  722.4 24.8 reduce-scatter.18
  750.4 25.7 reduce-scatter.12
  778.7 25.7 reduce-scatter.16
  807.1 25.7 reduce-scatter.14
  835.2 47.8 reduce-scatter.22
  885.6 47.8 reduce-scatter.20
  937.7 141.7 all-reduce.10
where the time goes:
time: 1110 us; the launch traced here: 1100 us
  waiting for transfers between devices  526 us (47%)
  matrix products  244 us (22%)
  local copies, waits for them, and re-layouts  206 us (19%)
  other arithmetic  55 us (5%)
  blocking collectives  47.1 us (4%)
  between operations  16.6 us (1%)
    dot_general x12, local copies, waits for them, and re-layouts, block_score_matrix(): jnp.einsum('umx,uv->vmx', bucket_indicator, bucket_bias_matrix, preferred...  110 us
    psum x1, waiting for transfers between devices, on_device(): lax.psum(pieces[0].astype(jnp.bfloat16), 'ctx').astype(jnp.float32)  97.7 us
    dot_general x12, matrix products, block_score_matrix(): jnp.einsum('umx,uv->vmx', bucket_indicator, bucket_bias_matrix, preferred...  75.7 us
    reduce_scatter x1, waiting for transfers between devices, on_device(): lax.psum_scatter(grad_keys.reshape(group_rows, D).astype(jnp.bfloat16), '...  75.1 us
    all_gather x1, waiting for transfers between devices, on_device(): lax.all_gather(key_b, 'ctx', axis=0, tiled=True)  61.1 us
    reduce_scatter x1, waiting for transfers between devices, on_device(): lax.psum_scatter(grad_values.reshape(group_rows, D).astype(jnp.bfloat16),...  61.1 us
    reduce_scatter x1, waiting for transfers between devices, on_device(): lax.psum_scatter(grad_inw.astype(jnp.bfloat16), 'fsdp', scatter_dimension...  50.4 us
    reduce_scatter x1, waiting for transfers between devices, on_device(): lax.psum_scatter(grad_ffn.astype(jnp.bfloat16), 'fsdp', scatter_dimension...  50.2 us
  transfers between devices with their start and end apart: 17, of which 13 were waited for; matrix products, arithmetic and copies ran while one was open for 26% of the time, Pallas kernels for 0%

commit v1 on v0

v1 whole, which is shorter than its diff:
```python
import jax
import jax.numpy as jnp
from jax import lax
from jax.experimental import pallas as pl
from jax.experimental.pallas import tpu as pltpu
from jax.sharding import PartitionSpec as P

D = 768
H = 12
DH = 64
NB = 32
SPAN = 128
PAIRS = H // 2
BIG = 1e30
VMEM_LIMIT = 58 * 2**20
norm_eps = 1e-06


def bucket_of(relative):
    distance = jnp.abs(relative)
    far_steps = jnp.zeros_like(distance)
    for exponent in range(1, 8):
        far_steps = far_steps + (distance * distance >= 64 * 2**exponent).astype(jnp.int32)
    magnitude = jnp.where(distance < 8, distance, 8 + far_steps)
    return magnitude + jnp.where(relative > 0, 16, 0).astype(jnp.int32)


def dot(a, b, ca=1, cb=0):
    return lax.dot_general(a, b, (((ca,), (cb,)), ((), ())), preferred_element_type=jnp.float32)


def diagonal_onehot(offset):
    lane = lax.broadcasted_iota(jnp.int32, (128, 256), 1)
    row = lax.broadcasted_iota(jnp.int32, (128, 256), 0)
    return (bucket_of(offset * SPAN + 127 - lane) == row).astype(jnp.bfloat16)


def fill_inverse(order_ref, inv_ref, spans):
    def put(i, carry):
        inv_ref[order_ref[0, i]] = i
        return carry

    lax.fori_loop(0, spans, put, 0)


def fill_near_bias(table_t, near_ref):
    for index in range(3):
        rows = dot(table_t, diagonal_onehot(index - 1))
        for head in range(H):
            wide = jnp.broadcast_to(rows[head : head + 1, :], (128, 256))
            tile = pltpu.roll(wide, 129, 1, stride=1, stride_axis=0)[:, :128]
            near_ref[index, head // 2, :, (head % 2) * 128 : (head % 2) * 128 + 128] = tile
    near_ref[3] = jnp.zeros_like(near_ref[3])


def key_range(span, b1, b2, b3, total):
    first, last = span * SPAN, span * SPAN + SPAN - 1
    start = jnp.where(first >= b3, b3, jnp.where(first >= b2, b2, jnp.where(first >= b1, b1, 0)))
    end = jnp.where(last < b1, b1, jnp.where(last < b2, b2, jnp.where(last < b3, b3, total)))
    return start // 256, (end + 255) // 256


def key_features(chunk, span, b1, b2, b3):
    lane = lax.broadcasted_iota(jnp.int32, (256, 128), 1)
    pos = lax.broadcasted_iota(jnp.int32, (256, 128), 0) + chunk * 256
    seg = (pos >= b1).astype(jnp.int32) + (pos >= b2).astype(jnp.int32) + (pos >= b3).astype(jnp.int32)
    code = jnp.where(pos < (span - 1) * SPAN, 4, jnp.where(pos >= (span + 2) * SPAN, 5, seg))
    hot = (lane == seg) | (lane == code) | ((lane >= 6) & (lane < 9))
    return jnp.where(hot, 1.0, 0.0).astype(jnp.bfloat16)


def query_features(span, pair, tab_ref, b1, b2, b3, extra=None):
    row = lax.broadcasted_iota(jnp.int32, (128, 256), 0)
    lane = lax.broadcasted_iota(jnp.int32, (128, 256), 1)
    pos = (lane % SPAN) + span * SPAN
    seg = (pos >= b1).astype(jnp.int32) + (pos >= b2).astype(jnp.int32) + (pos >= b3).astype(jnp.int32)
    first = lane < 128
    below = jnp.where(first, tab_ref[NB // 2 - 1, 2 * pair], tab_ref[NB // 2 - 1, 2 * pair + 1])
    above = jnp.where(first, tab_ref[NB - 1, 2 * pair], tab_ref[NB - 1, 2 * pair + 1])
    feat = jnp.where((row < 4) & (row != seg), -BIG, 0.0)
    feat = jnp.where(row == 4, below, jnp.where(row == 5, above, feat))
    if extra is not None:
        high = extra.astype(jnp.bfloat16).astype(jnp.float32)
        rest = extra - high
        mid = rest.astype(jnp.bfloat16).astype(jnp.float32)
        low = rest - mid
        feat = jnp.where(row == 6, high, jnp.where(row == 7, mid, jnp.where(row == 8, low, feat)))
    return feat.astype(jnp.bfloat16)


def block_diagonal(x_t):
    row = lax.broadcasted_iota(jnp.int32, (128, 128), 0)
    zero = jnp.zeros_like(x_t)
    return jnp.concatenate([jnp.where(row < DH, x_t, zero), jnp.where(row >= DH, x_t, zero)], axis=1)


def stacked_heads(x):
    lane = lax.broadcasted_iota(jnp.int32, (128, 128), 1)
    zero = jnp.zeros_like(x)
    return jnp.concatenate([jnp.where(lane < DH, x, zero), jnp.where(lane >= DH, x, zero)], axis=0)


def near_index(delta):
    return jnp.where((delta >= -1) & (delta <= 1), delta + 1, 3)


def fwd_kernel(
    place_ref, order_ref, len_ref, tab_ref, table_t_ref, q_ref, k_ref, v_ref,
    o_ref, ot_ref, lse_ref,
    inv_ref, rhs_ref, near_ref, m_ref, l_ref, acc_ref,
):
    spans, own = k_ref.shape[0], q_ref.shape[0]
    b1 = len_ref[0, 0]
    b2 = b1 + len_ref[0, 1]
    b3 = b2 + len_ref[0, 2]
    fill_inverse(order_ref, inv_ref, spans)
    fill_near_bias(table_t_ref[...], near_ref)

    def one_span(i, carry):
        span = order_ref[0, place_ref[0] * own + i]
        low, high = key_range(span, b1, b2, b3, spans * SPAN)
        for p in range(PAIRS):
            q_t = q_ref[i, :, p * 128 : p * 128 + 128].T
            rhs_ref[p, 0:128, :] = block_diagonal(q_t)
            rhs_ref[p, 128:256, :] = query_features(span, p, tab_ref, b1, b2, b3)
        m_ref[...] = jnp.full_like(m_ref, -BIG)
        l_ref[...] = jnp.zeros_like(l_ref)
        acc_ref[...] = jnp.zeros_like(acc_ref)

        def chunk_body(t, near):
            s0, s1 = inv_ref[2 * t], inv_ref[2 * t + 1]
            feat = key_features(t, span, b1, b2, b3)
            for p in range(PAIRS):
                cols = slice(p * 128, p * 128 + 128)
                kp = jnp.concatenate([k_ref[s0, :, cols], k_ref[s1, :, cols]], axis=0)
                s = dot(jnp.concatenate([kp, feat], axis=1), rhs_ref[p])
                if near:
                    n0, n1 = near_index(2 * t - span), near_index(2 * t + 1 - span)
                    s = s + jnp.concatenate([near_ref[n0, p], near_ref[n1, p]], axis=0)
                old = m_ref[p]
                new = jnp.maximum(old, jnp.max(s, axis=0, keepdims=True))
                scale = jnp.exp(old - new)
                e = jnp.exp(s - new)
                m_ref[p] = new
                l_ref[p] = l_ref[p] * scale + jnp.sum(e, axis=0, keepdims=True)
                vp = jnp.concatenate([v_ref[s0, :, cols], v_ref[s1, :, cols]], axis=0)
                o = dot(vp, e.astype(jnp.bfloat16), 0, 0)
                acc_ref[p, 0:64, :] = acc_ref[p, 0:64, :] * scale[:, 0:128] + o[0:64, 0:128]
                acc_ref[p, 64:128, :] = acc_ref[p, 64:128, :] * scale[:, 128:256] + o[64:128, 128:256]

        def step(t, carry):
            near = (2 * t + 2 >= span) & (2 * t <= span + 1)
            pl.when(near)(lambda: chunk_body(t, True))
            pl.when(jnp.logical_not(near))(lambda: chunk_body(t, False))
            return carry

        lax.fori_loop(low, high, step, 0)
        for p in range(PAIRS):
            total = l_ref[p]
            lse_ref[i, p] = m_ref[p] + jnp.log(total)
            inv = 1.0 / total
            out = jnp.concatenate(
                [acc_ref[p, 0:64, :] * inv[:, 0:128], acc_ref[p, 64:128, :] * inv[:, 128:256]], axis=0
            )
            ot_ref[i, p] = out
            o_ref[i, :, p * 128 : p * 128 + 128] = out.T.astype(jnp.bfloat16)
        return carry

    lax.fori_loop(0, own, one_span, 0)


def bwd_kernel(
    place_ref, order_ref, len_ref, tab_ref, table_t_ref, q_ref, k_ref, v_ref, do_ref, ot_ref, lse_ref,
    dq_ref, dk_ref, dv_ref, dtab_ref,
    inv_ref, rhs_ref, dorhs_ref, qbd_ref, dobd_ref, near_ref, nacc_ref, acc_ref, far_ref,
):
    spans, own = k_ref.shape[0], q_ref.shape[0]
    b1 = len_ref[0, 0]
    b2 = b1 + len_ref[0, 1]
    b3 = b2 + len_ref[0, 2]
    fill_inverse(order_ref, inv_ref, spans)
    fill_near_bias(table_t_ref[...], near_ref)
    nacc_ref[...] = jnp.zeros_like(nacc_ref)
    far_ref[...] = jnp.zeros_like(far_ref)

    def clear(i, carry):
        dk_ref[i] = jnp.zeros_like(dk_ref[i])
        dv_ref[i] = jnp.zeros_like(dv_ref[i])
        return carry

    lax.fori_loop(0, spans, clear, 0)

    def one_span(i, carry):
        span = order_ref[0, place_ref[0] * own + i]
        low, high = key_range(span, b1, b2, b3, spans * SPAN)
        for p in range(PAIRS):
            cols = slice(p * 128, p * 128 + 128)
            qp, dop = q_ref[i, :, cols], do_ref[i, :, cols]
            do_t = dop.T
            prod = do_t.astype(jnp.float32) * ot_ref[i, p]
            delta = jnp.concatenate(
                [jnp.sum(prod[0:64], axis=0, keepdims=True), jnp.sum(prod[64:128], axis=0, keepdims=True)], axis=1
            )
            rhs_ref[p, 0:128, :] = block_diagonal(qp.T)
            rhs_ref[p, 128:256, :] = query_features(span, p, tab_ref, b1, b2, b3, -lse_ref[i, p])
            row = lax.broadcasted_iota(jnp.int32, (128, 256), 0)
            neg = -delta
            h1 = neg.astype(jnp.bfloat16).astype(jnp.float32)
            h2 = (neg - h1).astype(jnp.bfloat16).astype(jnp.float32)
            h3 = neg - h1 - h2
            dfeat = jnp.where(row == 6, h1, jnp.where(row == 7, h2, jnp.where(row == 8, h3, 0.0)))
            dorhs_ref[p, 0:128, :] = block_diagonal(do_t)
            dorhs_ref[p, 128:256, :] = dfeat.astype(jnp.bfloat16)
            qbd_ref[p] = stacked_heads(qp)
            dobd_ref[p] = stacked_heads(dop)
        acc_ref[...] = jnp.zeros_like(acc_ref)

        def chunk_body(t, near):
            s0, s1 = inv_ref[2 * t], inv_ref[2 * t + 1]
            feat = key_features(t, span, b1, b2, b3)
            far_sum = jnp.zeros((8, 256), jnp.float32)
            for p in range(PAIRS):
                cols = slice(p * 128, p * 128 + 128)
                kp = jnp.concatenate([k_ref[s0, :, cols], k_ref[s1, :, cols]], axis=0)
                vp = jnp.concatenate([v_ref[s0, :, cols], v_ref[s1, :, cols]], axis=0)
                kf = jnp.concatenate([kp, feat], axis=1)
                s = dot(kf, rhs_ref[p])
                if near:
                    n0, n1 = near_index(2 * t - span), near_index(2 * t + 1 - span)
                    s = s + jnp.concatenate([near_ref[n0, p], near_ref[n1, p]], axis=0)
                prob = jnp.exp(s)
                dp = dot(jnp.concatenate([vp, feat], axis=1), dorhs_ref[p])
                ds = prob * dp
                if near:
                    nacc_ref[n0, p] += ds[0:128]
                    nacc_ref[n1, p] += ds[128:256]
                dsb = ds.astype(jnp.bfloat16)
                dv = dot(prob.astype(jnp.bfloat16), dobd_ref[p])
                dk = dot(dsb, qbd_ref[p])
                dv_ref[s0, :, cols] += dv[0:128]
                dv_ref[s1, :, cols] += dv[128:256]
                dk_ref[s0, :, cols] += dk[0:128]
                dk_ref[s1, :, cols] += dk[128:256]
                dq = dot(kf, dsb, 0, 0)
                acc_ref[p, 0:64, :] += dq[0:64, 0:128]
                acc_ref[p, 64:128, :] += dq[64:128, 128:256]
                far_ref[p] += dq[128:136, :]

        def step(t, carry):
            near = (2 * t + 2 >= span) & (2 * t <= span + 1)
            pl.when(near)(lambda: chunk_body(t, True))
            pl.when(jnp.logical_not(near))(lambda: chunk_body(t, False))
            return carry

        lax.fori_loop(low, high, step, 0)
        for p in range(PAIRS):
            dq_ref[i, :, p * 128 : p * 128 + 128] = acc_ref[p].T.astype(jnp.bfloat16)
        return carry

    lax.fori_loop(0, own, one_span, 0)

    row16 = lax.broadcasted_iota(jnp.int32, (16, 128), 0)
    lane16 = lax.broadcasted_iota(jnp.int32, (16, 128), 1)
    grad = jnp.zeros((16, 128), jnp.float32)
    for head in range(H):
        half = slice((head % 2) * 128, (head % 2) * 128 + 128)
        sums = jnp.sum(far_ref[head // 2, 4:6, half], axis=1, keepdims=True)
        grad = grad + jnp.where((row16 == head) & (lane16 == NB // 2 - 1), sums[0:1], 0.0)
        grad = grad + jnp.where((row16 == head) & (lane16 == NB - 1), sums[1:2], 0.0)
    rowd = lax.broadcasted_iota(jnp.int32, (16, 256), 0)
    flip_row = lax.broadcasted_iota(jnp.int32, (128, 128), 0)
    flip_lane = lax.broadcasted_iota(jnp.int32, (128, 128), 1)
    flip = (flip_row + flip_lane == 127).astype(jnp.bfloat16)
    for index in range(3):
        sums = jnp.zeros((16, 256), jnp.float32)
        for p in range(PAIRS):
            both = nacc_ref[index, p]
            high = both.astype(jnp.bfloat16)
            rest = (both - high.astype(jnp.float32)).astype(jnp.bfloat16)
            turned = dot(flip, high) + dot(flip, rest)
            for side in range(2):
                tile = turned[:, side * 128 : side * 128 + 128]
                wide = jnp.concatenate([tile, jnp.zeros_like(tile)], axis=1)
                shifted = pltpu.roll(wide, 0, 1, stride=1, stride_axis=0)
                sums = sums + jnp.where(rowd == 2 * p + side, jnp.sum(shifted, axis=0, keepdims=True), 0.0)
        hot = diagonal_onehot(index - 1).astype(jnp.float32)
        grad = grad + lax.dot_general(
            sums, hot, (((1,), (1,)), ((), ())), preferred_element_type=jnp.float32, precision=lax.Precision.HIGHEST
        )
    dtab_ref[...] = grad


def smem():
    return pl.BlockSpec(memory_space=pltpu.SMEM)


def vmem():
    return pl.BlockSpec(memory_space=pltpu.VMEM)


def attend(place, order, lengths, table, table_t, q, k, v):
    own, spans = q.shape[0], k.shape[0]
    return pl.pallas_call(
        fwd_kernel,
        name="attend",
        out_shape=(
            jax.ShapeDtypeStruct((own, SPAN, D), jnp.bfloat16),
            jax.ShapeDtypeStruct((own, PAIRS, 128, 128), jnp.float32),
            jax.ShapeDtypeStruct((own, PAIRS, 1, 256), jnp.float32),
        ),
        in_specs=[smem()] * 4 + [vmem()] * 4,
        out_specs=(vmem(),) * 3,
        scratch_shapes=[
            pltpu.SMEM((spans,), jnp.int32),
            pltpu.VMEM((PAIRS, 256, 256), jnp.bfloat16),
            pltpu.VMEM((4, PAIRS, 128, 256), jnp.float32),
            pltpu.VMEM((PAIRS, 1, 256), jnp.float32),
            pltpu.VMEM((PAIRS, 1, 256), jnp.float32),
            pltpu.VMEM((PAIRS, 128, 128), jnp.float32),
        ],
        compiler_params=pltpu.CompilerParams(vmem_limit_bytes=VMEM_LIMIT),
    )(place, order, lengths, table, table_t, q, k, v)


def attend_back(place, order, lengths, table, table_t, q, k, v, d_out, out_t, lse):
    own, spans = q.shape[0], k.shape[0]
    return pl.pallas_call(
        bwd_kernel,
        name="attend_back",
        out_shape=(
            jax.ShapeDtypeStruct((own, SPAN, D), jnp.bfloat16),
            jax.ShapeDtypeStruct((spans, SPAN, D), jnp.float32),
            jax.ShapeDtypeStruct((spans, SPAN, D), jnp.float32),
            jax.ShapeDtypeStruct((16, 128), jnp.float32),
        ),
        in_specs=[smem()] * 4 + [vmem()] * 7,
        out_specs=(vmem(),) * 4,
        scratch_shapes=[
            pltpu.SMEM((spans,), jnp.int32),
            pltpu.VMEM((PAIRS, 256, 256), jnp.bfloat16),
            pltpu.VMEM((PAIRS, 256, 256), jnp.bfloat16),
            pltpu.VMEM((PAIRS, 256, 128), jnp.bfloat16),
            pltpu.VMEM((PAIRS, 256, 128), jnp.bfloat16),
            pltpu.VMEM((4, PAIRS, 128, 256), jnp.float32),
            pltpu.VMEM((4, PAIRS, 128, 256), jnp.float32),
            pltpu.VMEM((PAIRS, 128, 128), jnp.float32),
            pltpu.VMEM((PAIRS, 8, 256), jnp.float32),
        ],
        compiler_params=pltpu.CompilerParams(vmem_limit_bytes=VMEM_LIMIT),
    )(place, order, lengths, table, table_t, q, k, v, d_out, out_t, lse)


def rms_norm(values, gain_vec):
    inv_rms = lax.rsqrt(jnp.mean(values * values, axis=-1, keepdims=True) + norm_eps)
    return values * inv_rms * gain_vec


def gelu_tanh(values):
    return (
        0.5
        * values
        * (1.0 + jnp.tanh(0.7978845608028654 * (values + 0.044715 * values * values * values)))
    )


def on_device(
    tokens,
    lengths,
    span_order,
    w_query,
    w_key,
    w_value,
    w_out,
    w_in,
    w_ffn_out,
    gain_attn,
    gain_ffn,
    rel_table,
    cotangent,
):
    gathered = (
        lax.all_gather(w_query, "fsdp", axis=0, tiled=True),
        lax.all_gather(w_key, "fsdp", axis=0, tiled=True),
        lax.all_gather(w_value, "fsdp", axis=0, tiled=True),
        lax.all_gather(w_out, "fsdp", axis=0, tiled=True),
        lax.all_gather(w_in, "fsdp", axis=0, tiled=True),
        lax.all_gather(w_ffn_out, "fsdp", axis=0, tiled=True),
        lax.all_gather(gain_attn, "fsdp", axis=0, tiled=True),
        lax.all_gather(gain_ffn, "fsdp", axis=0, tiled=True),
        lax.all_gather(rel_table, "fsdp", axis=0, tiled=True),
    )
    query_w, key_w, value_w, out_w, in_w, ffn_w, attn_gain, ffn_gain, bucket_bias_matrix = gathered
    ctx_count = lax.axis_size("ctx")
    local_rows = tokens.shape[1]
    group_rows = local_rows * ctx_count
    own = local_rows // SPAN
    spans = group_rows // SPAN
    place = lax.axis_index("ctx").astype(jnp.int32).reshape(1)
    table = bucket_bias_matrix.astype(jnp.float32)
    table_t = jnp.pad(bucket_bias_matrix.T, ((0, 16 - H), (0, 128 - NB)))
    inputs_f = tokens[0].astype(jnp.float32)
    normed, norm_attn_back = jax.vjp(rms_norm, inputs_f, attn_gain.astype(jnp.float32))
    normed_b = normed.astype(jnp.bfloat16)
    query_b = jnp.dot(normed_b, query_w, preferred_element_type=jnp.float32).astype(jnp.bfloat16)
    key_b = jnp.dot(normed_b, key_w, preferred_element_type=jnp.float32).astype(jnp.bfloat16)
    value_b = jnp.dot(normed_b, value_w, preferred_element_type=jnp.float32).astype(jnp.bfloat16)
    all_keys, all_values = (
        lax.all_gather(key_b, "ctx", axis=0, tiled=True),
        lax.all_gather(value_b, "ctx", axis=0, tiled=True),
    )
    query_s = query_b.reshape(own, SPAN, D)
    keys_s = all_keys.reshape(spans, SPAN, D)
    values_s = all_values.reshape(spans, SPAN, D)
    attended_s, attended_t, lse = attend(
        place, span_order, lengths, table, table_t, query_s, keys_s, values_s
    )
    attended_b = attended_s.reshape(local_rows, D)
    residual = inputs_f + jnp.dot(attended_b, out_w, preferred_element_type=jnp.float32)
    normed_ffn, norm_ffn_back = jax.vjp(rms_norm, residual, ffn_gain.astype(jnp.float32))
    feedforward_normed_block = normed_ffn.astype(jnp.bfloat16)
    up_rows = jnp.dot(feedforward_normed_block, in_w, preferred_element_type=jnp.float32)
    activated, gelu_back = jax.vjp(gelu_tanh, up_rows)
    activated_b = activated.astype(jnp.bfloat16)
    result = residual + jnp.dot(activated_b, ffn_w, preferred_element_type=jnp.float32)
    grad_b = cotangent[0]
    grad_ffn = jnp.einsum("tf,td->fd", activated_b, grad_b, preferred_element_type=jnp.float32)
    grad_act = jnp.einsum("td,fd->tf", grad_b, ffn_w, preferred_element_type=jnp.float32)
    (grad_up,) = gelu_back(grad_act)
    grad_up_b = grad_up.astype(jnp.bfloat16)
    grad_inw = jnp.einsum(
        "td,tf->df", feedforward_normed_block, grad_up_b, preferred_element_type=jnp.float32
    )
    grad_normed_ffn = jnp.einsum("tf,df->td", grad_up_b, in_w, preferred_element_type=jnp.float32)
    grad_resid_norm, grad_ffn_gain = norm_ffn_back(grad_normed_ffn)
    grad_resid = grad_b.astype(jnp.float32) + grad_resid_norm
    grad_resid_b = grad_resid.astype(jnp.bfloat16)
    grad_outw = jnp.einsum(
        "tc,td->cd", attended_b, grad_resid_b, preferred_element_type=jnp.float32
    )
    grad_att_b = jnp.einsum(
        "td,cd->tc", grad_resid_b, out_w, preferred_element_type=jnp.float32
    ).astype(jnp.bfloat16)
    grad_query, grad_keys, grad_values, grad_table_t = attend_back(
        place,
        span_order,
        lengths,
        table,
        table_t,
        query_s,
        keys_s,
        values_s,
        grad_att_b.reshape(own, SPAN, D),
        attended_t,
        lse,
    )
    grad_table = grad_table_t[:H, :NB].T
    own_keys, own_values = (
        lax.psum_scatter(
            grad_keys.reshape(group_rows, D).astype(jnp.bfloat16),
            "ctx",
            scatter_dimension=0,
            tiled=True,
        ).astype(jnp.float32),
        lax.psum_scatter(
            grad_values.reshape(group_rows, D).astype(jnp.bfloat16),
            "ctx",
            scatter_dimension=0,
            tiled=True,
        ).astype(jnp.float32),
    )
    grad_q_b = grad_query.reshape(local_rows, D).astype(jnp.bfloat16)
    grad_k_b = own_keys.astype(jnp.bfloat16)
    grad_v_b = own_values.astype(jnp.bfloat16)
    query_weight_gradient = jnp.einsum(
        "tc,td->cd", normed_b, grad_q_b, preferred_element_type=jnp.float32
    )
    grad_kw = jnp.einsum("tc,td->cd", normed_b, grad_k_b, preferred_element_type=jnp.float32)
    grad_vw = jnp.einsum("tc,td->cd", normed_b, grad_v_b, preferred_element_type=jnp.float32)
    grad_normed = jnp.einsum("td,cd->tc", grad_q_b, query_w, preferred_element_type=jnp.float32)
    grad_normed = grad_normed + jnp.einsum(
        "td,cd->tc", grad_k_b, key_w, preferred_element_type=jnp.float32
    )
    grad_normed = grad_normed + jnp.einsum(
        "td,cd->tc", grad_v_b, value_w, preferred_element_type=jnp.float32
    )
    grad_input_norm, grad_attn_gain = norm_attn_back(grad_normed)
    grad_input = (grad_resid + grad_input_norm).astype(jnp.bfloat16)
    pieces = (
        lax.psum_scatter(
            query_weight_gradient.astype(jnp.bfloat16), "fsdp", scatter_dimension=0, tiled=True
        ).astype(jnp.float32),
        lax.psum_scatter(
            grad_kw.astype(jnp.bfloat16), "fsdp", scatter_dimension=0, tiled=True
        ).astype(jnp.float32),
        lax.psum_scatter(
            grad_vw.astype(jnp.bfloat16), "fsdp", scatter_dimension=0, tiled=True
        ).astype(jnp.float32),
        lax.psum_scatter(
            grad_outw.astype(jnp.bfloat16), "fsdp", scatter_dimension=0, tiled=True
        ).astype(jnp.float32),
        lax.psum_scatter(
            grad_inw.astype(jnp.bfloat16), "fsdp", scatter_dimension=0, tiled=True
        ).astype(jnp.float32),
        lax.psum_scatter(
            grad_ffn.astype(jnp.bfloat16), "fsdp", scatter_dimension=0, tiled=True
        ).astype(jnp.float32),
        lax.psum_scatter(
            grad_attn_gain.astype(jnp.bfloat16), "fsdp", scatter_dimension=0, tiled=True
        ).astype(jnp.float32),
        lax.psum_scatter(
            grad_ffn_gain.astype(jnp.bfloat16), "fsdp", scatter_dimension=0, tiled=True
        ).astype(jnp.float32),
        lax.psum_scatter(
            grad_table.astype(jnp.bfloat16), "fsdp", scatter_dimension=0, tiled=True
        ).astype(jnp.float32),
    )
    final_grads = (
        lax.psum(pieces[0].astype(jnp.bfloat16), "ctx").astype(jnp.float32),
        lax.psum(pieces[1].astype(jnp.bfloat16), "ctx").astype(jnp.float32),
        lax.psum(pieces[2].astype(jnp.bfloat16), "ctx").astype(jnp.float32),
        lax.psum(pieces[3].astype(jnp.bfloat16), "ctx").astype(jnp.float32),
        lax.psum(pieces[4].astype(jnp.bfloat16), "ctx").astype(jnp.float32),
        lax.psum(pieces[5].astype(jnp.bfloat16), "ctx").astype(jnp.float32),
        lax.psum(pieces[6].astype(jnp.bfloat16), "ctx").astype(jnp.float32),
        lax.psum(pieces[7].astype(jnp.bfloat16), "ctx").astype(jnp.float32),
        lax.psum(pieces[8].astype(jnp.bfloat16), "ctx").astype(jnp.float32),
    )
    return (
        result.astype(jnp.bfloat16)[None],
        grad_input[None],
        final_grads[0],
        final_grads[1],
        final_grads[2],
        final_grads[3],
        final_grads[4],
        final_grads[5],
        final_grads[6],
        final_grads[7],
        final_grads[8],
    )


def solution(mesh):
    in_specs = (
        P("fsdp", "ctx", None),
        P("fsdp", None),
        P("fsdp", None),
        P("fsdp", None),
        P("fsdp", None),
        P("fsdp", None),
        P("fsdp", None),
        P("fsdp", None),
        P("fsdp", None),
        P("fsdp"),
        P("fsdp"),
        P("fsdp", None),
        P("fsdp", "ctx", None),
    )
    out_specs = (
        P("fsdp", "ctx", None),
        P("fsdp", "ctx", None),
        P("fsdp", None),
        P("fsdp", None),
        P("fsdp", None),
        P("fsdp", None),
        P("fsdp", None),
        P("fsdp", None),
        P("fsdp"),
        P("fsdp"),
        P("fsdp", None),
    )
    return jax.shard_map(
        on_device, mesh=mesh, in_specs=in_specs, out_specs=out_specs, check_vma=False
    )
```

time: 1110 us -> 867 us (0.78)
  local copies, waits for them, and re-layouts: 206 us -> 8.05 us
  matrix products: 244 us -> 54.4 us
  waiting for transfers between devices: 526 us -> 664 us
  Pallas kernels: 0 us -> 53.2 us
  other arithmetic: 55 us -> 24.6 us
    dot_general x44 -> x0, matrix products: 191 us -> none  [the longest x12 75.7 us: block_score_matrix(): jnp.einsum('umx,uv->vmx', bucket_indicator, bucket_bias_matrix, preferred...]
    dot_general x12 -> x0, local copies, waits for them, and re-layouts: 110 us -> none  [block_score_matrix(): jnp.einsum('umx,uv->vmx', bucket_indicator, bucket_bias_matrix, preferred...]
    all_gather x1, waiting for transfers between devices: 0.01 us -> 61.7 us  [on_device(): lax.all_gather(value_b, 'ctx', axis=0, tiled=True)]
    pallas_call x0 -> x2, Pallas kernels: none -> 53.2 us  [the longest x1 28.9 us: attend_back(): pl.pallas_call(bwd_kernel, name='attend_back', out_shape=(jax.ShapeDtypeS...]
    all_gather x1, waiting for transfers between devices: 0.01 us -> 33.6 us  [on_device(): lax.all_gather(w_ffn_out, 'fsdp', axis=0, tiled=True)]
    convert_element_type x8 -> x0, local copies, waits for them, and re-layouts: 33.6 us -> none  [the longest x4 22.8 us: back_step(): (probabilities * (grad_prob - row_delta[:, :, None])).astype(jnp.bfloat16)]
    all_gather x1, waiting for transfers between devices: 0.02 us -> 30.2 us  [on_device(): lax.all_gather(w_in, 'fsdp', axis=0, tiled=True)]
    eq x12 -> x0, other arithmetic: 15.5 us -> none  [block_score_matrix(): inside = (query_segment_ids[:, None] == key_seg[None, :])[None]]
  transfers between devices with their start and end apart: 17 -> 17, of which waited for: 13 -> 16; matrix products, arithmetic and copies ran while one was open for 26% -> 7% of each run, Pallas kernels for 0% -> 3%
where the time goes in v1:
time: 867 us; the launch traced here: 864 us
  waiting for transfers between devices  664 us (77%)
  matrix products  54.4 us (6%)
  Pallas kernels  53.2 us (6%)
  blocking collectives  42.7 us (5%)
  other arithmetic  24.6 us (3%)
  between operations  16.1 us (2%)
    psum x1, waiting for transfers between devices, on_device(): lax.psum(pieces[0].astype(jnp.bfloat16), 'ctx').astype(jnp.float32)  103 us
    reduce_scatter x1, waiting for transfers between devices, on_device(): lax.psum_scatter(grad_values.reshape(group_rows, D).astype(jnp.bfloat16),...  74.1 us
    reduce_scatter x1, waiting for transfers between devices, on_device(): lax.psum_scatter(grad_keys.reshape(group_rows, D).astype(jnp.bfloat16), '...  65.1 us
    all_gather x1, waiting for transfers between devices, on_device(): lax.all_gather(value_b, 'ctx', axis=0, tiled=True)  61.7 us
    all_gather x1, waiting for transfers between devices, on_device(): lax.all_gather(key_b, 'ctx', axis=0, tiled=True)  60.6 us
    reduce_scatter x1, waiting for transfers between devices, on_device(): lax.psum_scatter(grad_inw.astype(jnp.bfloat16), 'fsdp', scatter_dimension...  50.4 us
    reduce_scatter x1, waiting for transfers between devices, on_device(): lax.psum_scatter(grad_ffn.astype(jnp.bfloat16), 'fsdp', scatter_dimension...  50.3 us
    all_gather x1, waiting for transfers between devices, on_device(): lax.all_gather(w_ffn_out, 'fsdp', axis=0, tiled=True)  33.6 us
  transfers between devices with their start and end apart: 17, of which 16 were waited for; matrix products, arithmetic and copies ran while one was open for 7% of the time, Pallas kernels for 3%

profile of v1, /device:TPU:0, one launch (start us, length us, event | category | flops | bytes accessed | tf_op | source)
XLA Modules:
  0.0 864.3 jit_solution(17785035411051908552)
XLA Ops:
  9.5 1.3 fusion.44
  13.1 8.3 all-reduce.9
  21.5 1.2 fusion.16
  23.2 6.6 all-gather.11.cloned.1.call-done
  29.8 2.7 convolution_convert_fusion.8
  32.5 16.3 %all-gather.15.cloned.1.call-done = bf16[768,768]{1,0:T(8,128)(2,1)} async-done(((bf16[192,768]{1,0:T(8,128)(2,1)}), bf16[768,768]{1,0:T(8,128)(2,1)}) %all-gather.15.cloned.1.call-update) | async-done | bytes 1179664 | tf_op jit(solution)/shard_map/all_gather | solution.py:384
  48.8 2.5 convolution_convert_fusion.7
  53.5 5.2 all_gather.33
  60.0 7.9 all-gather.9.cloned.1.call-done
  67.9 2.5 convolution_convert_fusion.9
  70.4 60.6 %all-gather.13.cloned.1.call-done = bf16[2048,768]{1,0:T(8,128)(2,1)} async-done(((bf16[256,768]{1,0:T(8,128)(2,1)}), bf16[2048,768]{1,0:T(8,128)(2,1)}) %all-gather.13.cloned.1.call-update) | async-done | bytes 3145744 | tf_op jit(solution)/shard_map/all_gather | solution.py:408
  131.0 61.7 %all-gather.17.cloned.1.call-done = bf16[2048,768]{1,0:T(8,128)(2,1)} async-done(((bf16[256,768]{1,0:T(8,128)(2,1)}), bf16[2048,768]{1,0:T(8,128)(2,1)}) %all-gather.17.cloned.1.call-update) | async-done | bytes 3145744 | tf_op jit(solution)/shard_map/all_gather | solution.py:409
  192.7 24.2 %attend.1 = (bf16[2,128,768]{2,1,0:T(8,128)(2,1)}, f32[2,6,128,128]{3,2,1,0:T(8,128)}, f32[2,6,1,256]{3,2,1,0:T(1,128)}) custom-call(s32[1]{0:T(128)} %bitcast.1.place_ref, s32[1,16]{1,0:T(1,128)} %order_ref.3, s32[1,4]{1,0:T(1,128)} %len_ref.3, f32[32,12]{1,0:T(8,128)} %convert_element_type.152.tab_ref, bf16[16,128]{1,0:T(8,128)(2,1)} %pad.4.table_t_ref, ...), custom_call_target="tpu_custom_call" | custom-call | tf_op jit(solution)/shard_map/attend/pallas_call | solution.py:303
  216.9 2.1 multiply_reduce_fusion.2
  219.0 30.2 %all-gather.21.cloned.1.call-done = bf16[768,3072]{1,0:T(8,128)(2,1)} async-done(((bf16[192,3072]{1,0:T(8,128)(2,1)}), bf16[768,3072]{1,0:T(8,128)(2,1)}) %all-gather.21.cloned.1.call-update) | async-done | bytes 4718608 | tf_op jit(solution)/shard_map/all_gather | solution.py:386
  249.3 5.5 fusion.38
  254.7 33.6 %all-gather.23.cloned.1.call-done = bf16[3072,768]{1,0:T(8,128)(2,1)} async-done(((bf16[768,768]{1,0:T(8,128)(2,1)}), bf16[3072,768]{1,0:T(8,128)(2,1)}) %all-gather.23.cloned.1.call-update) | async-done | bytes 4718608 | tf_op jit(solution)/shard_map/all_gather | solution.py:387
  288.3 7.5 fusion.3
  295.9 2.1 multiply_reduce_fusion
  298.2 1.0 copy-done.2
  299.2 1.3 convolution_convert_fusion.6
  300.5 28.9 %attend_back.1 = (bf16[2,128,768]{2,1,0:T(8,128)(2,1)}, f32[16,128,768]{2,1,0:T(8,128)}, f32[16,128,768]{2,1,0:T(8,128)}, f32[16,128]{1,0:T(8,128)}) custom-call(s32[1]{0:T(128)} %bitcast.1.place_ref, s32[1,16]{1,0:T(1,128)} %order_ref.3, s32[1,4]{1,0:T(1,128)} %len_ref.3, f32[32,12]{1,0:T(8,128)} %convert_element_type.152.tab_ref, ...), custom_call_target="tpu_custom_call" | custom-call | tf_op jit(solution)/shard_map/attend_back/pallas_call | solution.py:327
  329.4 4.8 convert_element_type.166
  334.3 4.9 convert_element_type.168
  339.3 2.5 convolution_convert_fusion.2
  341.9 2.6 convolution_convert_fusion.5
  344.6 65.1 %reduce-scatter.10.cloned.1.call-done = bf16[256,768]{1,0:T(8,128)(2,1)} async-done(((bf16[2048,768]{1,0:T(8,128)(2,1)}), bf16[256,768]{1,0:T(8,128)(2,1)}) %reduce-scatter.10.cloned.1.call-update) | async-done | bytes 393232 | tf_op jit(solution)/shard_map/reduce_scatter | solution.py:458
  409.7 2.6 convolution_convert_fusion.4
  412.4 74.1 %reduce-scatter.12.cloned.1.call-done = bf16[256,768]{1,0:T(8,128)(2,1)} async-done(((bf16[2048,768]{1,0:T(8,128)(2,1)}), bf16[256,768]{1,0:T(8,128)(2,1)}) %reduce-scatter.12.cloned.1.call-update) | async-done | bytes 393232 | tf_op jit(solution)/shard_map/reduce_scatter | solution.py:464
  486.5 2.7 convolution_convert_fusion.3
  489.3 6.3 convolution_convert_fusion
  495.7 3.7 convolution_convert_fusion.1
  499.7 14.2 %reduce-scatter.20.cloned.1.call-done = bf16[192,768]{1,0:T(8,128)(2,1)} async-done(((bf16[768,768]{1,0:T(8,128)(2,1)}), bf16[192,768]{1,0:T(8,128)(2,1)}) %reduce-scatter.20.cloned.1.call-update) | async-done | bytes 294928 | tf_op jit(solution)/shard_map/reduce_scatter | solution.py:498
  513.9 29.0 %reduce-scatter.14.cloned.1.call-done = bf16[192,768]{1,0:T(8,128)(2,1)} async-done(((bf16[768,768]{1,0:T(8,128)(2,1)}), bf16[192,768]{1,0:T(8,128)(2,1)}) %reduce-scatter.14.cloned.1.call-update) | async-done | bytes 294928 | tf_op jit(solution)/shard_map/reduce_scatter | solution.py:489
  542.9 28.9 %reduce-scatter.16.cloned.1.call-done = bf16[192,768]{1,0:T(8,128)(2,1)} async-done(((bf16[768,768]{1,0:T(8,128)(2,1)}), bf16[192,768]{1,0:T(8,128)(2,1)}) %reduce-scatter.16.cloned.1.call-update) | async-done | bytes 294928 | tf_op jit(solution)/shard_map/reduce_scatter | solution.py:492
  571.7 28.4 %reduce-scatter.18.cloned.1.call-done = bf16[192,768]{1,0:T(8,128)(2,1)} async-done(((bf16[768,768]{1,0:T(8,128)(2,1)}), bf16[192,768]{1,0:T(8,128)(2,1)}) %reduce-scatter.18.cloned.1.call-update) | async-done | bytes 294928 | tf_op jit(solution)/shard_map/reduce_scatter | solution.py:495
  600.1 50.3 %reduce-scatter.24.cloned.1.call-done = bf16[768,768]{1,0:T(8,128)(2,1)} async-done(((bf16[3072,768]{1,0:T(8,128)(2,1)}), bf16[768,768]{1,0:T(8,128)(2,1)}) %reduce-scatter.24.cloned.1.call-update) | async-done | bytes 1179664 | tf_op jit(solution)/shard_map/reduce_scatter | solution.py:504
  650.4 50.4 %reduce-scatter.22.cloned.1.call-done = bf16[192,3072]{1,0:T(8,128)(2,1)} async-done(((bf16[768,3072]{1,0:T(8,128)(2,1)}), bf16[192,3072]{1,0:T(8,128)(2,1)}) %reduce-scatter.22.cloned.1.call-update) | async-done | bytes 1179664 | tf_op jit(solution)/shard_map/reduce_scatter | solution.py:501
  703.4 6.1 fusion.7
  711.8 6.2 all-reduce.8
  718.2 23.0 %all-reduce.6 = (bf16[8,12]{0,1:T(8,128)(2,1)S(1)}, bf16[192]{0:T(256)(128)(2,1)S(1)}, bf16[192]{0:T(256)(128)(2,1)S(1)}) all-reduce(bf16[8,12]{0,1:T(8,128)(2,1)S(1)} %constant_dynamic-slice_fusion, bf16[192]{0:T(256)(128)(2,1)S(1)} %dynamic-slice.3, bf16[192]{0:T(256)(128)(2,1)S(1)} %dynamic-slice.5), channel_id=1, replica_groups=mesh['ctx'=8,'fsdp'=4] {'ctx'}, use_global_device_ids=true, to_apply=%region_25.26 | all-reduce | flops 480 | bytes 1920 | tf_op jit(solution)/shard_map/psum | solution.py:526
  744.0 103.0 %all-reduce.12.cloned.1.call-done = (bf16[192,768]{1,0:T(8,128)(2,1)}, bf16[192,768]{1,0:T(8,128)(2,1)}, bf16[192,768]{1,0:T(8,128)(2,1)}, bf16[192,768]{1,0:T(8...) async-done(((bf16[192,768]{1,0:T(8,128)(2,1)}, bf16[192,768]{1,0:T(8,128)(2,1)}, bf16[192,768]{1,0:T(8,128)(2,1)}, bf16[192,768]{1,0:T(8,128)(2,1)}, ...) | async-done | bytes 3538960 | tf_op jit(solution)/shard_map/psum | solution.py:518
  847.1 1.9 convert_element_type.175
  849.0 1.9 convert_element_type.177
  850.9 1.8 convert_element_type.179
  852.7 1.8 convert_element_type.181
  854.5 1.7 convert_element_type.183
  856.2 1.6 convert_element_type.185
  (93 shorter events, 15.5 us)
Async XLA Ops:
  7.2 41.7 %copy-start = (bf16[1,256,768]{2,1,0:T(8,128)(2,1)S(1)}, bf16[1,256,768]{2,1,0:T(8,128)(2,1)}, u32[]{:S(2)}) copy-start(bf16[1,256,768]{2,1,0:T(8,128)(2,1)} %param.13) | copy-start | bytes 1179652
  7.2 22.6 %all-gather.11.cloned.1.call-start = ((), (), s32[]{:S(2)}) async-start(), calls=%async_computation.9 | async-start | bytes 1474560 | tf_op jit(solution)/shard_map/all_gather | solution.py:383
  7.9 40.9 %all-gather.15.cloned.1.call-start = ((), (), s32[]{:S(2)}) async-start(), calls=%async_computation.11 | async-start | bytes 1474560 | tf_op jit(solution)/shard_map/all_gather | solution.py:384
  8.7 59.2 %all-gather.9.cloned.1.call-start = ((), (), s32[]{:S(2)}) async-start(), calls=%async_computation.8 | async-start | bytes 1474560 | tf_op jit(solution)/shard_map/all_gather | solution.py:382
  9.4 121.6 %all-gather.13.cloned.1.call-start = ((), (), s32[]{:S(2)}) async-start(), calls=%async_computation.10 | async-start | bytes 3538944 | tf_op jit(solution)/shard_map/all_gather | solution.py:408
  22.6 0.6 copy-start.13
  32.4 21.1 %copy-start.15 = (bf16[8,12]{1,0:T(8,128)(2,1)S(1)}, bf16[8,12]{1,0:T(8,128)(2,1)}, u32[]{:S(2)}) copy-start(bf16[8,12]{1,0:T(8,128)(2,1)} %param.24) | copy-start | bytes 580
  32.5 160.2 %all-gather.17.cloned.1.call-start = ((), (), s32[]{:S(2)}) async-start(), calls=%async_computation.12 | async-start | bytes 3538944 | tf_op jit(solution)/shard_map/all_gather | solution.py:409
  51.4 165.5 %all-gather.19.cloned.1.call-start = ((), (), s32[]{:S(2)}) async-start(), calls=%async_computation.13 | async-start | bytes 1474560 | tf_op jit(solution)/shard_map/all_gather | solution.py:385
  52.0 197.3 %all-gather.21.cloned.1.call-start = ((), (), s32[]{:S(2)}) async-start(), calls=%async_computation.14 | async-start | bytes 5898240 | tf_op jit(solution)/shard_map/all_gather | solution.py:386
  52.7 235.6 %all-gather.23.cloned.1.call-start = ((), (), s32[]{:S(2)}) async-start(), calls=%async_computation.15 | async-start | bytes 5898240 | tf_op jit(solution)/shard_map/all_gather | solution.py:387
  53.5 356.2 %reduce-scatter.10.cloned.1.call-start = ((), (), s32[]{:S(2)}) async-start(), calls=%async_computation.16 | async-start | bytes 3538944 | tf_op jit(solution)/shard_map/reduce_scatter | solution.py:458
  249.3 39.1 %copy-start.11 = (bf16[1,256,768]{2,1,0:T(8,128)(2,1)S(1)}, bf16[1,256,768]{2,1,0:T(8,128)(2,1)}, u32[]{:S(2)}) copy-start(bf16[1,256,768]{2,1,0:T(8,128)(2,1)} %param.25) | copy-start | bytes 1179652
  288.3 7.5 copy-start.1
  295.8 2.1 copy-start.12
  297.9 1.3 copy-start.2
  334.2 152.2 %reduce-scatter.12.cloned.1.call-start = ((), (), s32[]{:S(2)}) async-start(), calls=%async_computation.17 | async-start | bytes 3538944 | tf_op jit(solution)/shard_map/reduce_scatter | solution.py:464
  339.2 174.7 %reduce-scatter.20.cloned.1.call-start = ((), (), s32[]{:S(2)}) async-start(), calls=%async_computation.21 | async-start | bytes 1474560 | tf_op jit(solution)/shard_map/reduce_scatter | solution.py:498
  341.8 201.0 %reduce-scatter.14.cloned.1.call-start = ((), (), s32[]{:S(2)}) async-start(), calls=%async_computation.18 | async-start | bytes 1474560 | tf_op jit(solution)/shard_map/reduce_scatter | solution.py:489
  344.6 227.2 %reduce-scatter.16.cloned.1.call-start = ((), (), s32[]{:S(2)}) async-start(), calls=%async_computation.19 | async-start | bytes 1474560 | tf_op jit(solution)/shard_map/reduce_scatter | solution.py:492
  412.3 187.8 %reduce-scatter.18.cloned.1.call-start = ((), (), s32[]{:S(2)}) async-start(), calls=%async_computation.20 | async-start | bytes 1474560 | tf_op jit(solution)/shard_map/reduce_scatter | solution.py:495
  489.2 161.2 %reduce-scatter.24.cloned.1.call-start = ((), (), s32[]{:S(2)}) async-start(), calls=%async_computation.23 | async-start | bytes 5898240 | tf_op jit(solution)/shard_map/reduce_scatter | solution.py:504
  495.6 205.2 %reduce-scatter.22.cloned.1.call-start = ((), (), s32[]{:S(2)}) async-start(), calls=%async_computation.22 | async-start | bytes 5898240 | tf_op jit(solution)/shard_map/reduce_scatter | solution.py:501
  499.4 203.4 %copy-start.3 = (bf16[2,128,768]{2,1,0:T(8,128)(2,1)S(1)}, bf16[2,128,768]{2,1,0:T(8,128)(2,1)}, u32[]{:S(2)}) copy-start(bf16[2,128,768]{2,1,0:T(8,128)(2,1)} %get-tuple-element.21) | copy-start | bytes 1179652
  499.4 203.4 %copy-start.10 = (bf16[768,768]{1,0:T(8,128)(2,1)S(1)}, bf16[768,768]{1,0:T(8,128)(2,1)}, u32[]{:S(2)}) copy-start(bf16[768,768]{1,0:T(8,128)(2,1)} %all-gather.9.cloned.1.call-done) | copy-start | bytes 3538948
  499.4 347.6 %all-reduce.12.cloned.1.call-start = ((), (), s32[]{:S(2)}) async-start(), calls=%async_computation.24 | async-start | bytes 7077888 | tf_op jit(solution)/shard_map/psum | solution.py:518
  703.3 6.1 copy-start.4
  703.4 6.1 copy-start.6
  709.5 1.0 copy-start.5
  709.5 1.7 copy-start.7
  709.5 2.3 copy-start.16
  709.5 33.5 %copy-start.14 = (f32[256]{0:T(256)S(1)}, f32[256]{0:T(256)}, u32[]{:S(2)}) copy-start(f32[256]{0:T(256)} %copy-done.13) | copy-start | bytes 3076
  847.1 7.5 copy-start.9
  849.0 7.2 copy-start.8
Sparse Core Ops, SparseCore 0:
  9.6 20.1 all-gather.10
  31.3 17.4 all-gather.14
  50.4 17.4 all-gather.8
  70.5 60.4 all-gather.12
  133.6 59.0 all-gather.16
  194.1 16.0 all-gather.18
  211.8 37.4 all-gather.20
  250.8 37.4 all-gather.22
  334.4 75.2 reduce-scatter.9
  413.1 73.3 reduce-scatter.11
  489.1 24.7 reduce-scatter.19
  517.1 25.7 reduce-scatter.13
  546.0 25.6 reduce-scatter.15
  574.3 25.7 reduce-scatter.17
  602.5 47.8 reduce-scatter.23
  652.9 47.8 reduce-scatter.21
  705.0 142.0 all-reduce.11

commit v2 on v1

v2 whole, which is shorter than its diff:
```python
import jax
import jax.numpy as jnp
from jax import lax
from jax.experimental import pallas as pl
from jax.experimental.pallas import tpu as pltpu
from jax.sharding import PartitionSpec as P

D = 768
H = 12
DH = 64
NB = 32
SPAN = 128
PAIRS = H // 2
BIG = 1e30
VMEM_LIMIT = 56 * 2**20
EPS = 1e-06
GELU_C = 0.7978845608028654
ANY = pl.ANY


def bucket_of(relative):
    distance = jnp.abs(relative)
    far_steps = jnp.zeros_like(distance)
    for exponent in range(1, 8):
        far_steps = far_steps + (distance * distance >= 64 * 2**exponent).astype(jnp.int32)
    magnitude = jnp.where(distance < 8, distance, 8 + far_steps)
    return magnitude + jnp.where(relative > 0, 16, 0).astype(jnp.int32)


def dot(a, b, ca=1, cb=0):
    return lax.dot_general(a, b, (((ca,), (cb,)), ((), ())), preferred_element_type=jnp.float32)


def diagonal_onehot(offset):
    lane = lax.broadcasted_iota(jnp.int32, (128, 256), 1)
    row = lax.broadcasted_iota(jnp.int32, (128, 256), 0)
    return (bucket_of(offset * SPAN + 127 - lane) == row).astype(jnp.bfloat16)


def fill_inverse(order_ref, inv_ref, spans):
    def put(i, carry):
        inv_ref[order_ref[0, i]] = i
        return carry

    lax.fori_loop(0, spans, put, 0)


def fill_near_bias(table_t, near_ref):
    for index in range(3):
        rows = dot(table_t, diagonal_onehot(index - 1))
        for head in range(H):
            wide = jnp.broadcast_to(rows[head : head + 1, :], (128, 256))
            tile = pltpu.roll(wide, 129, 1, stride=1, stride_axis=0)[:, :128]
            near_ref[index, head // 2, :, (head % 2) * 128 : (head % 2) * 128 + 128] = tile
    near_ref[3] = jnp.zeros_like(near_ref[3])


def key_range(span, b1, b2, b3, total):
    first, last = span * SPAN, span * SPAN + SPAN - 1
    start = jnp.where(first >= b3, b3, jnp.where(first >= b2, b2, jnp.where(first >= b1, b1, 0)))
    end = jnp.where(last < b1, b1, jnp.where(last < b2, b2, jnp.where(last < b3, b3, total)))
    return start // 256, (end + 255) // 256


def key_features(chunk, span, b1, b2, b3):
    lane = lax.broadcasted_iota(jnp.int32, (256, 128), 1)
    pos = lax.broadcasted_iota(jnp.int32, (256, 128), 0) + chunk * 256
    seg = (pos >= b1).astype(jnp.int32) + (pos >= b2).astype(jnp.int32) + (pos >= b3).astype(jnp.int32)
    code = jnp.where(pos < (span - 1) * SPAN, 4, jnp.where(pos >= (span + 2) * SPAN, 5, seg))
    hot = (lane == seg) | (lane == code) | ((lane >= 6) & (lane < 9))
    return jnp.where(hot, 1.0, 0.0).astype(jnp.bfloat16)


def query_features(span, pair, tab_ref, b1, b2, b3, extra=None):
    row = lax.broadcasted_iota(jnp.int32, (128, 256), 0)
    lane = lax.broadcasted_iota(jnp.int32, (128, 256), 1)
    pos = (lane % SPAN) + span * SPAN
    seg = (pos >= b1).astype(jnp.int32) + (pos >= b2).astype(jnp.int32) + (pos >= b3).astype(jnp.int32)
    first = lane < 128
    below = jnp.where(first, tab_ref[NB // 2 - 1, 2 * pair], tab_ref[NB // 2 - 1, 2 * pair + 1])
    above = jnp.where(first, tab_ref[NB - 1, 2 * pair], tab_ref[NB - 1, 2 * pair + 1])
    feat = jnp.where((row < 4) & (row != seg), -BIG, 0.0)
    feat = jnp.where(row == 4, below, jnp.where(row == 5, above, feat))
    if extra is not None:
        high = extra.astype(jnp.bfloat16).astype(jnp.float32)
        rest = extra - high
        mid = rest.astype(jnp.bfloat16).astype(jnp.float32)
        low = rest - mid
        feat = jnp.where(row == 6, high, jnp.where(row == 7, mid, jnp.where(row == 8, low, feat)))
    return feat.astype(jnp.bfloat16)


def block_diagonal(x_t):
    row = lax.broadcasted_iota(jnp.int32, (128, 128), 0)
    zero = jnp.zeros_like(x_t)
    return jnp.concatenate([jnp.where(row < DH, x_t, zero), jnp.where(row >= DH, x_t, zero)], axis=1)


def stacked_heads(x):
    lane = lax.broadcasted_iota(jnp.int32, (128, 128), 1)
    zero = jnp.zeros_like(x)
    return jnp.concatenate([jnp.where(lane < DH, x, zero), jnp.where(lane >= DH, x, zero)], axis=0)


def near_index(delta):
    return jnp.where((delta >= -1) & (delta <= 1), delta + 1, 3)


def smem():
    return pl.BlockSpec(memory_space=pltpu.SMEM)


def vmem():
    return pl.BlockSpec(memory_space=pltpu.VMEM)


def once():
    return pl.BlockSpec(memory_space=pltpu.VMEM, pipeline_mode=pl.Buffered(1))


def by_chunk():
    return pl.BlockSpec((256, D), lambda t: (t, 0))


def hbm():
    return pl.BlockSpec(memory_space=ANY)


def load_pieces(pieces, target_ref, flip, sem):
    copies = []
    rows = target_ref.shape[0] // len(pieces)
    for number, (ref, index, place) in enumerate(pieces):
        start = pl.multiple_of(lax.bitwise_xor(jnp.int32(place), flip) * rows, 16)
        source = ref.at[index, pl.ds(0, rows)]
        copies.append(pltpu.make_async_copy(source, target_ref.at[pl.ds(start, rows)], sem.at[number]))
    for copy in copies:
        copy.start()
    return copies


def expand(refs):
    out, place = [], 0
    for ref in refs:
        for index in range(ref.shape[0]):
            out.append((ref, index, place))
            place += 1
    return out


def forward_kernel(counts, *refs):
    n_x, n_w = counts
    ids_ref, order_ref, len_ref, tab_ref, table_t_ref, gain_ref = refs[:6]
    x_refs, w_refs = refs[6 : 6 + n_x], refs[6 + n_x : 6 + n_x + n_w]
    (
        nf_ref, res_ref, o_ref, ot_ref, lse_ref, q_ref, k_ref, v_ref, xn_ref,
        inv_ref, x_ref, w_ref, rhs_ref, near_ref, s_ref, m_ref, l_ref, acc_ref, sem_x, sem_w,
    ) = refs[6 + n_x + n_w :]
    spans, own = order_ref.shape[1], q_ref.shape[0] // SPAN
    b1 = len_ref[0, 0]
    b2 = b1 + len_ref[0, 1]
    b3 = b2 + len_ref[0, 2]
    copies = load_pieces(expand(x_refs), x_ref, jnp.int32(0), sem_x)
    copies += load_pieces(expand(w_refs), w_ref, ids_ref[2], sem_w)
    fill_inverse(order_ref, inv_ref, spans)
    fill_near_bias(table_t_ref[...], near_ref)
    for copy in copies:
        copy.wait()
    own_rows = own * SPAN
    gain = gain_ref[0:1, :]

    def normed(x):
        x = x.astype(jnp.float32)
        return (x * lax.rsqrt(jnp.mean(x * x, axis=1, keepdims=True) + EPS) * gain).astype(jnp.bfloat16)

    my_spans = [order_ref[0, ids_ref[0] * own + i] for i in range(own)]
    my_ranges = [key_range(span, b1, b2, b3, spans * SPAN) for span in my_spans]

    def project(t, carry):
        needed = jnp.bool_(False)
        for low, high in my_ranges:
            needed = needed | ((t >= low) & (t < high))
        rows = pl.ds(pl.multiple_of(t * 256, 256), 256)

        def fill():
            parts = []
            for half in range(2):
                slot = inv_ref[2 * t + half]
                piece = lax.bitwise_xor(slot // own, ids_ref[1])
                start = pl.multiple_of(piece * own_rows + (slot % own) * SPAN, SPAN)
                parts.append(x_ref[pl.ds(start, SPAN), :])
            xn = normed(jnp.concatenate(parts, axis=0))
            xn_ref[rows, :] = xn
            k_ref[rows, :] = dot(xn, w_ref[:, D : 2 * D]).astype(jnp.bfloat16)
            v_ref[rows, :] = dot(xn, w_ref[:, 2 * D : 3 * D]).astype(jnp.bfloat16)

        def skip():
            xn_ref[rows, :] = jnp.zeros((256, D), jnp.bfloat16)

        pl.when(needed)(fill)
        pl.when(jnp.logical_not(needed))(skip)
        return carry

    lax.fori_loop(0, spans // 2, project, 0)
    mine = pl.multiple_of(lax.bitwise_xor(ids_ref[0], ids_ref[1]) * own_rows, SPAN)
    x_own = x_ref[pl.ds(mine, own_rows), :]
    q_ref[...] = dot(normed(x_own), w_ref[:, 0:D]).astype(jnp.bfloat16)

    def one_span(i, carry):
        span = order_ref[0, ids_ref[0] * own + i]
        low, high = key_range(span, b1, b2, b3, spans * SPAN)
        my_rows = pl.ds(pl.multiple_of(i * SPAN, SPAN), SPAN)
        for p in range(PAIRS):
            q_t = q_ref[my_rows, p * 128 : p * 128 + 128].T
            rhs_ref[p, 0:128, :] = block_diagonal(q_t)
            rhs_ref[p, 128:256, :] = query_features(span, p, tab_ref, b1, b2, b3)
        m_ref[...] = jnp.full_like(m_ref, -BIG)
        l_ref[...] = jnp.zeros_like(l_ref)
        acc_ref[...] = jnp.zeros_like(acc_ref)

        def chunk_body(t, near):
            rows = pl.ds(pl.multiple_of(t * 256, 256), 256)
            feat = key_features(t, span, b1, b2, b3)
            scales, tops = [], []
            for p in range(PAIRS):
                kp = k_ref[rows, p * 128 : p * 128 + 128]
                s = dot(jnp.concatenate([kp, feat], axis=1), rhs_ref[p])
                if near:
                    n0, n1 = near_index(2 * t - span), near_index(2 * t + 1 - span)
                    s = s + jnp.concatenate([near_ref[n0, p], near_ref[n1, p]], axis=0)
                s_ref[p] = s
                old = m_ref[p]
                new = jnp.maximum(old, jnp.max(s, axis=0, keepdims=True))
                m_ref[p] = new
                scales.append(jnp.exp(old - new))
                tops.append(new)
            for p in range(PAIRS):
                scale = scales[p]
                e = jnp.exp(s_ref[p] - tops[p])
                l_ref[p] = l_ref[p] * scale + jnp.sum(e, axis=0, keepdims=True)
                vp = v_ref[rows, p * 128 : p * 128 + 128]
                o = dot(vp, e.astype(jnp.bfloat16), 0, 0)
                acc_ref[p, 0:64, :] = acc_ref[p, 0:64, :] * scale[:, 0:128] + o[0:64, 0:128]
                acc_ref[p, 64:128, :] = acc_ref[p, 64:128, :] * scale[:, 128:256] + o[64:128, 128:256]

        def step(t, carry):
            near = (2 * t + 2 >= span) & (2 * t <= span + 1)
            pl.when(near)(lambda: chunk_body(t, True))
            pl.when(jnp.logical_not(near))(lambda: chunk_body(t, False))
            return carry

        lax.fori_loop(low, high, step, 0)
        for p in range(PAIRS):
            total = l_ref[p]
            lse_ref[i, p] = m_ref[p] + jnp.log(total)
            inv = 1.0 / total
            out = jnp.concatenate(
                [acc_ref[p, 0:64, :] * inv[:, 0:128], acc_ref[p, 64:128, :] * inv[:, 128:256]], axis=0
            )
            ot_ref[i, p] = out
            o_ref[my_rows, p * 128 : p * 128 + 128] = out.T.astype(jnp.bfloat16)
        return carry

    lax.fori_loop(0, own, one_span, 0)
    res = x_own.astype(jnp.float32) + dot(o_ref[...], w_ref[:, 3 * D : 4 * D])
    res_ref[...] = res
    inv_rms = lax.rsqrt(jnp.mean(res * res, axis=1, keepdims=True) + EPS)
    nf_ref[...] = (res * inv_rms * gain_ref[1:2, :]).astype(jnp.bfloat16)


def forward(ids, order, lengths, table, table_t, gains, xs, ws, local_rows):
    spans, own = order.shape[1], local_rows // SPAN
    rows = spans * SPAN
    n_x, n_w = sum(x.shape[0] for x in xs), sum(w.shape[0] for w in ws)
    bf, f32 = jnp.bfloat16, jnp.float32
    return pl.pallas_call(
        lambda *refs: forward_kernel((len(xs), len(ws)), *refs),
        name="forward",
        out_shape=(
            jax.ShapeDtypeStruct((local_rows, D), bf),
            jax.ShapeDtypeStruct((local_rows, D), f32),
            jax.ShapeDtypeStruct((local_rows, D), bf),
            jax.ShapeDtypeStruct((own, PAIRS, 128, 128), f32),
            jax.ShapeDtypeStruct((own, PAIRS, 1, 256), f32),
            jax.ShapeDtypeStruct((local_rows, D), bf),
            jax.ShapeDtypeStruct((rows, D), bf),
            jax.ShapeDtypeStruct((rows, D), bf),
            jax.ShapeDtypeStruct((rows, D), bf),
        ),
        in_specs=[smem()] * 4 + [vmem()] * 2 + [hbm()] * (len(xs) + len(ws)),
        out_specs=(vmem(),) * 9,
        scratch_shapes=[
            pltpu.SMEM((spans,), jnp.int32),
            pltpu.VMEM((rows, D), bf),
            pltpu.VMEM((D, 4 * D), bf),
            pltpu.VMEM((PAIRS, 256, 256), bf),
            pltpu.VMEM((4, PAIRS, 128, 256), f32),
            pltpu.VMEM((PAIRS, 256, 256), f32),
            pltpu.VMEM((PAIRS, 1, 256), f32),
            pltpu.VMEM((PAIRS, 1, 256), f32),
            pltpu.VMEM((PAIRS, 128, 128), f32),
            pltpu.SemaphoreType.DMA((n_x,)),
            pltpu.SemaphoreType.DMA((n_w,)),
        ],
        compiler_params=pltpu.CompilerParams(vmem_limit_bytes=VMEM_LIMIT),
    )(ids, order, lengths, table, table_t, gains, *xs, *ws)


def ffn_kernel(counts, *refs):
    n_t, n_w = counts
    ids_ref = refs[0]
    nf_refs, cot_refs = refs[1 : 1 + n_t], refs[1 + n_t : 1 + 2 * n_t]
    win_refs = refs[1 + 2 * n_t : 1 + 2 * n_t + n_w]
    wffn_ref, act_ref, dup_ref, dn_ref, w_ref, sem_w = refs[1 + 2 * n_t + n_w :]
    copies = load_pieces(expand(win_refs), w_ref, ids_ref[2], sem_w)
    for copy in copies:
        copy.wait()
    start = 0
    for nf_ref, cot_ref in zip(nf_refs, cot_refs):
        for piece in range(nf_ref.shape[0]):
            rows = slice(start, start + nf_ref.shape[1])
            up = dot(nf_ref[piece], w_ref[...])
            square = up * up
            th = jnp.tanh(GELU_C * (up + 0.044715 * square * up))
            half = 0.5 * (1.0 + th)
            act_ref[rows, :] = (up * half).astype(jnp.bfloat16)
            slope = half + 0.5 * up * (1.0 - th * th) * (GELU_C * (1.0 + 3 * 0.044715 * square))
            d_up = (dot(cot_ref[piece], wffn_ref[...], 1, 1) * slope).astype(jnp.bfloat16)
            dup_ref[rows, :] = d_up
            dn_ref[rows, :] = dot(d_up, w_ref[...], 1, 1).astype(jnp.bfloat16)
            start += nf_ref.shape[1]


def ffn(ids, nfs, cots, wins, wffn):
    rows = sum(x.shape[0] * x.shape[1] for x in nfs)
    width = wffn.shape[0]
    n_w = sum(w.shape[0] for w in wins)
    bf = jnp.bfloat16
    return pl.pallas_call(
        lambda *refs: ffn_kernel((len(nfs), len(wins)), *refs),
        name="ffn",
        out_shape=(
            jax.ShapeDtypeStruct((rows, width), bf),
            jax.ShapeDtypeStruct((rows, width), bf),
            jax.ShapeDtypeStruct((rows, D), bf),
        ),
        in_specs=[smem()] + [vmem()] * (2 * len(nfs)) + [hbm()] * len(wins) + [vmem()],
        out_specs=(vmem(),) * 3,
        scratch_shapes=[pltpu.VMEM((D, width), bf), pltpu.SemaphoreType.DMA((n_w,))],
        compiler_params=pltpu.CompilerParams(vmem_limit_bytes=VMEM_LIMIT),
    )(ids, *nfs, *cots, *wins, wffn)


def backward_kernel(counts, *refs):
    n_x, n_w = counts
    (
        ids_ref, order_ref, len_ref, tab_ref, table_t_ref, gain_ref,
        dnf_ref, res_ref, cot_ref, o_ref, ot_ref, lse_ref, q_ref, k_ref, v_ref,
    ) = refs[:15]
    x_refs, w_refs = refs[15 : 15 + n_x], refs[15 + n_x : 15 + n_x + n_w]
    (
        dres_ref, dlow_ref, dq_ref, dk_ref, dv_ref, dn_ref, dn_own_ref, dgain_ref, dtab_ref,
        inv_ref, x_ref, w_ref, do_ref, rhs_ref, dorhs_ref, qbd_ref, dobd_ref, near_ref, nacc_ref, acc_ref, far_ref,
        dkacc_ref, dvacc_ref, sem_x, sem_w,
    ) = refs[15 + n_x + n_w :]
    spans, own = order_ref.shape[1], q_ref.shape[0] // SPAN
    own_rows = own * SPAN
    b1 = len_ref[0, 0]
    b2 = b1 + len_ref[0, 1]
    b3 = b2 + len_ref[0, 2]
    t = pl.program_id(0)

    @pl.when(t == 0)
    def begin():
        copies_x = load_pieces(expand(x_refs), x_ref, jnp.int32(0), sem_x)
        copies_w = load_pieces(expand(w_refs), w_ref, ids_ref[2], sem_w)
        fill_inverse(order_ref, inv_ref, spans)
        fill_near_bias(table_t_ref[...], near_ref)
        nacc_ref[...] = jnp.zeros_like(nacc_ref)
        far_ref[...] = jnp.zeros_like(far_ref)

        res, dnf = res_ref[...], dnf_ref[...]
        inv_rms = lax.rsqrt(jnp.mean(res * res, axis=1, keepdims=True) + EPS)
        dgain_ref[...] = jnp.zeros_like(dgain_ref)
        dgain_ref[1:2, :] = jnp.sum(dnf * res * inv_rms, axis=0, keepdims=True)
        scaled = dnf * gain_ref[1:2, :]
        inner = jnp.mean(scaled * res, axis=1, keepdims=True)
        dres = cot_ref[...].astype(jnp.float32) + inv_rms * scaled - res * (inv_rms * inv_rms * inv_rms * inner)
        dres_ref[...] = dres
        dlow = dres.astype(jnp.bfloat16)
        dlow_ref[...] = dlow
        for copy in copies_w:
            copy.wait()
        do_ref[...] = dot(dlow, w_ref[:, 3 * D : 4 * D], 1, 1).astype(jnp.bfloat16)

        def prepare(i, carry):
            span = order_ref[0, ids_ref[0] * own + i]
            my_rows = pl.ds(pl.multiple_of(i * SPAN, SPAN), SPAN)
            for p in range(PAIRS):
                cols = slice(p * 128, p * 128 + 128)
                qp, dop = q_ref[my_rows, cols], do_ref[my_rows, cols]
                do_t = dop.T
                prod = do_t.astype(jnp.float32) * ot_ref[i, p]
                neg = -jnp.concatenate(
                    [jnp.sum(prod[0:64], axis=0, keepdims=True), jnp.sum(prod[64:128], axis=0, keepdims=True)], axis=1
                )
                rhs_ref[i, p, 0:128, :] = block_diagonal(qp.T)
                rhs_ref[i, p, 128:256, :] = query_features(span, p, tab_ref, b1, b2, b3, -lse_ref[i, p])
                row = lax.broadcasted_iota(jnp.int32, (128, 256), 0)
                h1 = neg.astype(jnp.bfloat16).astype(jnp.float32)
                h2 = (neg - h1).astype(jnp.bfloat16).astype(jnp.float32)
                h3 = neg - h1 - h2
                dfeat = jnp.where(row == 6, h1, jnp.where(row == 7, h2, jnp.where(row == 8, h3, 0.0)))
                dorhs_ref[i, p, 0:128, :] = block_diagonal(do_t)
                dorhs_ref[i, p, 128:256, :] = dfeat.astype(jnp.bfloat16)
                qbd_ref[i, p] = stacked_heads(qp)
                dobd_ref[i, p] = stacked_heads(dop)
            return carry

        lax.fori_loop(0, own, prepare, 0)
        acc_ref[...] = jnp.zeros_like(acc_ref)
        for copy in copies_x:
            copy.wait()


    def unit(x):
        x = x.astype(jnp.float32)
        return x * lax.rsqrt(jnp.mean(x * x, axis=1, keepdims=True) + EPS)

    dkacc_ref[...] = jnp.zeros_like(dkacc_ref)
    dvacc_ref[...] = jnp.zeros_like(dvacc_ref)

    def span_body(i, span, near):
        feat = key_features(t, span, b1, b2, b3)
        for p in range(PAIRS):
            cols = slice(p * 128, p * 128 + 128)
            kf = jnp.concatenate([k_ref[:, cols], feat], axis=1)
            s = dot(kf, rhs_ref[i, p])
            if near:
                n0, n1 = near_index(2 * t - span), near_index(2 * t + 1 - span)
                s = s + jnp.concatenate([near_ref[n0, p], near_ref[n1, p]], axis=0)
            prob = jnp.exp(s)
            ds = prob * dot(jnp.concatenate([v_ref[:, cols], feat], axis=1), dorhs_ref[i, p])
            if near:
                nacc_ref[n0, p] += ds[0:128]
                nacc_ref[n1, p] += ds[128:256]
            dsb = ds.astype(jnp.bfloat16)
            dvacc_ref[:, cols] += dot(prob.astype(jnp.bfloat16), dobd_ref[i, p])
            dkacc_ref[:, cols] += dot(dsb, qbd_ref[i, p])
            dq = dot(kf, dsb, 0, 0)
            acc_ref[i, p, 0:64, :] += dq[0:64, 0:128]
            acc_ref[i, p, 64:128, :] += dq[64:128, 128:256]
            far_ref[p] += dq[128:136, :]

    def one_span(i, used):
        span = order_ref[0, ids_ref[0] * own + i]
        low, high = key_range(span, b1, b2, b3, spans * SPAN)
        needed = (t >= low) & (t < high)
        near = (2 * t + 2 >= span) & (2 * t <= span + 1)
        pl.when(needed & near)(lambda: span_body(i, span, True))
        pl.when(needed & jnp.logical_not(near))(lambda: span_body(i, span, False))
        return used + needed.astype(jnp.int32)

    used = lax.fori_loop(0, own, one_span, jnp.int32(0))
    places = []
    for half in range(2):
        slot = inv_ref[2 * t + half]
        piece = lax.bitwise_xor(slot // own, ids_ref[1])
        places.append(pl.ds(pl.multiple_of(piece * own_rows + (slot % own) * SPAN, SPAN), SPAN))

    def fill():
        dkb, dvb = dkacc_ref[...].astype(jnp.bfloat16), dvacc_ref[...].astype(jnp.bfloat16)
        dk_ref[...] = dkb
        dv_ref[...] = dvb
        part = dot(dkb, w_ref[:, D : 2 * D], 1, 1) + dot(dvb, w_ref[:, 2 * D : 3 * D], 1, 1)
        x = jnp.concatenate([x_ref[places[0], :], x_ref[places[1], :]], axis=0)
        dgain_ref[0:1, :] += jnp.sum(part * unit(x), axis=0, keepdims=True)
        part = part.astype(jnp.bfloat16)
        dn_ref[places[0], :] = part[0:128]
        dn_ref[places[1], :] = part[128:256]

    def skip():
        zero = jnp.zeros((256, D), jnp.bfloat16)
        dk_ref[...] = zero
        dv_ref[...] = zero
        dn_ref[places[0], :] = zero[0:128]
        dn_ref[places[1], :] = zero[0:128]

    pl.when(used > 0)(fill)
    pl.when(used == 0)(skip)


    @pl.when(t == spans // 2 - 1)
    def finish():
        for i in range(own):
            for p in range(PAIRS):
                dq_ref[i * SPAN : (i + 1) * SPAN, p * 128 : p * 128 + 128] = acc_ref[i, p].T.astype(jnp.bfloat16)
        mine = pl.multiple_of(lax.bitwise_xor(ids_ref[0], ids_ref[1]) * own_rows, SPAN)
        own_part = dot(dq_ref[...], w_ref[:, 0:D], 1, 1)
        dn_own_ref[...] = own_part
        dgain_ref[0:1, :] += jnp.sum(own_part * unit(x_ref[pl.ds(mine, own_rows), :]), axis=0, keepdims=True)

        row16 = lax.broadcasted_iota(jnp.int32, (16, 128), 0)
        lane16 = lax.broadcasted_iota(jnp.int32, (16, 128), 1)
        grad = jnp.zeros((16, 128), jnp.float32)
        for head in range(H):
            half = slice((head % 2) * 128, (head % 2) * 128 + 128)
            sums = jnp.sum(far_ref[head // 2, 4:6, half], axis=1, keepdims=True)
            grad = grad + jnp.where((row16 == head) & (lane16 == NB // 2 - 1), sums[0:1], 0.0)
            grad = grad + jnp.where((row16 == head) & (lane16 == NB - 1), sums[1:2], 0.0)
        rowd = lax.broadcasted_iota(jnp.int32, (16, 256), 0)
        flip_row = lax.broadcasted_iota(jnp.int32, (128, 128), 0)
        flip_lane = lax.broadcasted_iota(jnp.int32, (128, 128), 1)
        flip = (flip_row + flip_lane == 127).astype(jnp.bfloat16)
        for index in range(3):
            sums = jnp.zeros((16, 256), jnp.float32)
            for p in range(PAIRS):
                both = nacc_ref[index, p]
                high = both.astype(jnp.bfloat16)
                rest = (both - high.astype(jnp.float32)).astype(jnp.bfloat16)
                turned = dot(flip, high) + dot(flip, rest)
                for side in range(2):
                    tile = turned[:, side * 128 : side * 128 + 128]
                    wide = jnp.concatenate([tile, jnp.zeros_like(tile)], axis=1)
                    shifted = pltpu.roll(wide, 0, 1, stride=1, stride_axis=0)
                    sums = sums + jnp.where(rowd == 2 * p + side, jnp.sum(shifted, axis=0, keepdims=True), 0.0)
            hot = diagonal_onehot(index - 1).astype(jnp.float32)
            grad = grad + lax.dot_general(
                sums, hot, (((1,), (1,)), ((), ())), preferred_element_type=jnp.float32, precision=lax.Precision.HIGHEST
            )
        dtab_ref[...] = grad


def backward(ids, order, lengths, table, table_t, gains, dnf, res, cot, o, ot, lse, q, k, v, xs, ws):
    spans, local_rows = order.shape[1], q.shape[0]
    rows, own = spans * SPAN, local_rows // SPAN
    n_x, n_w = sum(x.shape[0] for x in xs), sum(w.shape[0] for w in ws)
    bf, f32 = jnp.bfloat16, jnp.float32
    return pl.pallas_call(
        lambda *refs: backward_kernel((len(xs), len(ws)), *refs),
        name="backward",
        grid=(spans // 2,),
        out_shape=(
            jax.ShapeDtypeStruct((local_rows, D), f32),
            jax.ShapeDtypeStruct((local_rows, D), bf),
            jax.ShapeDtypeStruct((local_rows, D), bf),
            jax.ShapeDtypeStruct((rows, D), bf),
            jax.ShapeDtypeStruct((rows, D), bf),
            jax.ShapeDtypeStruct((rows, D), bf),
            jax.ShapeDtypeStruct((local_rows, D), f32),
            jax.ShapeDtypeStruct((8, D), f32),
            jax.ShapeDtypeStruct((16, 128), f32),
        ),
        in_specs=[smem()] * 4 + [once()] * 9 + [by_chunk()] * 2 + [hbm()] * (len(xs) + len(ws)),
        out_specs=(once(),) * 3 + (by_chunk(),) * 2 + (once(),) * 4,
        scratch_shapes=[
            pltpu.SMEM((spans,), jnp.int32),
            pltpu.VMEM((rows, D), bf),
            pltpu.VMEM((D, 4 * D), bf),
            pltpu.VMEM((local_rows, D), bf),
            pltpu.VMEM((own, PAIRS, 256, 256), bf),
            pltpu.VMEM((own, PAIRS, 256, 256), bf),
            pltpu.VMEM((own, PAIRS, 256, 128), bf),
            pltpu.VMEM((own, PAIRS, 256, 128), bf),
            pltpu.VMEM((4, PAIRS, 128, 256), f32),
            pltpu.VMEM((4, PAIRS, 128, 256), f32),
            pltpu.VMEM((own, PAIRS, 128, 128), f32),
            pltpu.VMEM((PAIRS, 8, 256), f32),
            pltpu.VMEM((256, D), f32),
            pltpu.VMEM((256, D), f32),
            pltpu.SemaphoreType.DMA((n_x,)),
            pltpu.SemaphoreType.DMA((n_w,)),
        ],
        compiler_params=pltpu.CompilerParams(vmem_limit_bytes=VMEM_LIMIT),
    )(ids, order, lengths, table, table_t, gains, dnf, res, cot, o, ot, lse, q, k, v, *xs, *ws)


def swap(x, axis, bit):
    count = lax.axis_size(axis)
    return lax.ppermute(x, axis, [(i, i ^ bit) for i in range(count)])


def block(x, index, count, dim=0):
    size = x.shape[dim] // count
    return lax.dynamic_slice_in_dim(x, index * size, size, dim)


def after(x, *others):
    return lax.optimization_barrier((x,) + others)[0]


def gather_four(x):
    across = swap(x, "fsdp", 2)
    return [x, swap(x, "fsdp", 1), across, swap(across, "fsdp", 1)]


def scatter_four(pieces):
    first, third = swap(pieces[1], "fsdp", 1), swap(pieces[3], "fsdp", 1)
    far = add(pieces[2], third)
    return pieces[0], first, swap(far, "fsdp", 2)


def exchange_four(pieces):
    side, corner = swap(pieces[1], "fsdp", 1), swap(pieces[3], "fsdp", 1)
    return [pieces[0], side, swap(pieces[2], "fsdp", 2), swap(corner, "fsdp", 2)]


def add(*terms):
    total = terms[0].astype(jnp.float32)
    for term in terms[1:]:
        total = total + term.astype(jnp.float32)
    return total.astype(jnp.bfloat16)


def on_device(
    tokens,
    lengths,
    span_order,
    w_query,
    w_key,
    w_value,
    w_out,
    w_in,
    w_ffn_out,
    gain_attn,
    gain_ffn,
    rel_table,
    cotangent,
):
    n_ctx, n_fsdp = lax.axis_size("ctx"), lax.axis_size("fsdp")
    fast = n_ctx == 8 and n_fsdp == 4
    place = lax.axis_index("ctx").astype(jnp.int32)
    shard = lax.axis_index("fsdp").astype(jnp.int32)
    local_rows = tokens.shape[1]
    own_rows = w_query.shape[0]
    bf, f32 = jnp.bfloat16, jnp.float32
    x, cot = tokens[0], cotangent[0]
    table_size = rel_table.size
    small = jnp.concatenate([gain_attn, gain_ffn, rel_table.reshape(-1)])
    small = jnp.pad(small[None], ((0, 15), (0, 4 * D - small.shape[0])))
    weights = jnp.concatenate([jnp.concatenate([w_query, w_key, w_value, w_out], axis=1), small], axis=0)
    width = w_ffn_out.shape[0]

    if fast:
        zero = jnp.int32(0)
        ids = jnp.stack([place, place, shard])
        x1, x2, x4 = swap(x, "ctx", 1), swap(x, "ctx", 2), swap(x, "ctx", 4)
        x3, x6 = swap(x2, "ctx", 1), swap(x4, "ctx", 2)
        x5, x7 = swap(x4, "ctx", 1), swap(x6, "ctx", 1)
        xs = [p[None] for p in (x, x1, x2, x3, x4, x5, x6, x7)]
        w_pieces = gather_four(weights)
        ws = [p[None] for p in w_pieces]
        order = [shard ^ r for r in range(4)]
        smalls = jnp.stack([p[own_rows] for p in w_pieces])
        smalls = jnp.stack([lax.dynamic_index_in_dim(smalls, order[i], 0, False) for i in range(4)])
        columns = after(w_in, w_pieces[2])
        wins = exchange_four([block(columns, order[r], 4, 1) for r in range(4)])
        cots = [p[None] for p in gather_four(after(cot, wins[3]))]
        wins = [p[None] for p in wins]
    else:
        ids = jnp.stack([place, jnp.int32(0), jnp.int32(0)])
        xs = [lax.all_gather(x, "ctx", axis=0)]
        ws = [lax.all_gather(weights, "fsdp", axis=0)]
        smalls = ws[0][:, own_rows]
        parts = jnp.stack([w_in[:, i * width : (i + 1) * width] for i in range(n_fsdp)])
        wins = [lax.all_to_all(parts, "fsdp", 0, 0)]
        cots = [lax.all_gather(cot, "fsdp", axis=0)]

    gains = jnp.stack([smalls[:, :own_rows].reshape(D), smalls[:, own_rows : 2 * own_rows].reshape(D)]).astype(f32)
    table_bf = smalls[:, 2 * own_rows : 2 * own_rows + table_size].reshape(NB, H)
    table = table_bf.astype(f32)
    table_t = jnp.pad(table_bf.T, ((0, 16 - H), (0, 128 - NB)))

    nf, res, o, ot, lse, q, k, v, xn = forward(
        ids, span_order, lengths, table, table_t, gains, xs, ws, local_rows
    )

    if fast:
        nfs = [p[None] for p in gather_four(nf)]
    else:
        nfs = [lax.all_gather(nf, "fsdp", axis=0)]
    act, dup, dn_part = ffn(ids, nfs, cots, wins, w_ffn_out)
    dn_part = dn_part.reshape(n_fsdp, local_rows, D)
    if fast:
        a, b, c = scatter_four([dn_part[r] for r in range(4)])
        dnf = a.astype(f32) + b.astype(f32) + c.astype(f32)
    else:
        dnf = lax.psum_scatter(dn_part, "fsdp", scatter_dimension=0).astype(f32)

    nf_all = jnp.concatenate([p.reshape(-1, D) for p in nfs])
    cot_all = jnp.concatenate([p.reshape(-1, D) for p in cots])
    out_part = dot(act, w_ffn_out).astype(bf).reshape(n_fsdp, local_rows, D)
    grad_ffn_out = dot(act, cot_all, 0, 0).astype(bf)
    grad_in = dot(nf_all, dup, 0, 0).astype(bf).reshape(n_fsdp, own_rows, width)
    if fast:
        a, b, c = scatter_four([out_part[r] for r in range(4)])
        output = (res + a.astype(f32) + b.astype(f32) + c.astype(f32)).astype(bf)
        got = exchange_four([lax.dynamic_index_in_dim(grad_in, order[r], 0, False) for r in range(4)])
        got = jnp.stack(got)
        grad_in = jnp.concatenate([lax.dynamic_index_in_dim(got, shard ^ i, 0, False) for i in range(4)], axis=1)
    else:
        output = (res + lax.psum_scatter(out_part, "fsdp", scatter_dimension=0).astype(f32)).astype(bf)
        got = lax.all_to_all(grad_in, "fsdp", 0, 0)
        grad_in = jnp.transpose(got, (1, 0, 2)).reshape(own_rows, n_fsdp * width)
    grad_ffn_out = lax.psum(grad_ffn_out, "ctx")
    grad_in = lax.psum(grad_in, "ctx")

    dres, dlow, dq, dk, dv, dn, dn_own, dgain, dtab = backward(
        ids, span_order, lengths, table, table_t, gains, dnf, res, cot, o, ot, lse, q, k, v, xs, ws
    )
    dn = dn.reshape(n_ctx, local_rows, D)
    if fast:
        got7, got5, got3, got1 = (swap(dn[r], "ctx", 1) for r in (7, 5, 3, 1))
        s6, s4, s2, s0 = add(dn[6], got7), add(dn[4], got5), add(dn[2], got3), add(dn[0], got1)
        t4 = add(s4, swap(s6, "ctx", 2))
        t2 = swap(s2, "ctx", 2)
        d_normed = dn_own + s0.astype(f32) + t2.astype(f32) + swap(t4, "ctx", 4).astype(f32)
    else:
        d_normed = dn_own + lax.psum_scatter(dn, "ctx", scatter_dimension=0).astype(f32)

    xf = x.astype(f32)
    inv_rms = lax.rsqrt(jnp.mean(xf * xf, axis=1, keepdims=True) + EPS)
    xn_own = (xf * inv_rms * gains[0:1]).astype(bf)
    scaled = d_normed * gains[0:1]
    inner = jnp.mean(scaled * xf, axis=1, keepdims=True)
    grad_tokens = (dres + inv_rms * scaled - xf * (inv_rms * inv_rms * inv_rms * inner)).astype(bf)

    grads = jnp.concatenate(
        [dot(xn_own, dq, 0, 0).astype(bf), dot(xn, dk, 0, 0).astype(bf), dot(xn, dv, 0, 0).astype(bf),
         dot(o, dlow, 0, 0).astype(bf)], axis=1
    )
    tiny = jnp.concatenate(
        [dgain[0].reshape(n_fsdp, own_rows), dgain[1].reshape(n_fsdp, own_rows),
         dtab[:H, :NB].T.reshape(n_fsdp, table_size)], axis=1
    ).astype(bf)
    tiny = jnp.pad(tiny[:, None, :], ((0, 0), (0, 15), (0, 4 * D - tiny.shape[1])))
    payload = jnp.concatenate([grads.reshape(n_fsdp, own_rows, 4 * D), tiny], axis=1)
    if fast:
        a, b, c = scatter_four([lax.dynamic_index_in_dim(payload, order[r], 0, False) for r in range(4)])
        payload = add(a, b, c)
    else:
        payload = lax.psum_scatter(payload, "fsdp", scatter_dimension=0)
    payload = lax.psum(payload, "ctx").astype(f32)
    tiny = payload[own_rows]
    return (
        output[None],
        grad_tokens[None],
        payload[:own_rows, 0:D],
        payload[:own_rows, D : 2 * D],
        payload[:own_rows, 2 * D : 3 * D],
        payload[:own_rows, 3 * D : 4 * D],
        grad_in.astype(f32),
        grad_ffn_out.astype(f32),
        tiny[:own_rows],
        tiny[own_rows : 2 * own_rows],
        tiny[2 * own_rows : 2 * own_rows + table_size].reshape(rel_table.shape),
    )


def solution(mesh):
    rows, vector, whole = P("fsdp", None), P("fsdp"), P("fsdp", "ctx", None)
    return jax.shard_map(
        on_device,
        mesh=mesh,
        in_specs=(whole,) + (rows,) * 8 + (vector, vector, rows, whole),
        out_specs=(whole, whole) + (rows,) * 6 + (vector, vector, rows),
        check_vma=False,
    )
```

time: 867 us -> 509 us (0.59)
  waiting for transfers between devices: 664 us -> 307 us
  starting transfers between devices: 0.91 us -> 51.8 us
  blocking collectives: 42.7 us -> 0 us
  matrix products: 54.4 us -> 18.4 us
  local copies, waits for them, and re-layouts: 8.05 us -> 23.8 us
    reduce_scatter x8 -> x0, waiting for transfers between devices: 340 us -> none  [the longest x1 74.1 us: on_device(): lax.psum_scatter(grad_values.reshape(group_rows, D).astype(jnp.bfloat16),...]
    all_gather x8 -> x0, waiting for transfers between devices: 217 us -> none  [the longest x1 61.7 us: on_device(): lax.all_gather(value_b, 'ctx', axis=0, tiled=True)]
    ppermute x0 -> x40, waiting for transfers between devices: none -> 184 us  [swap(): return lax.ppermute(x, axis, [(i, i ^ bit) for i in range(count)])]
    ppermute x0 -> x40, starting transfers between devices: none -> 51.8 us  [swap(): return lax.ppermute(x, axis, [(i, i ^ bit) for i in range(count)])]
    dot_general x18 -> x7, matrix products: 54.4 us -> 18.4 us  [dot(): lax.dot_general(a, b, (((ca,), (cb,)), ((), ())), preferred_element_type=...]
    psum x1 -> x0, blocking collectives: 23 us -> none  [on_device(): lax.psum(pieces[8].astype(jnp.bfloat16), 'ctx').astype(jnp.float32)]
    psum x1, waiting for transfers between devices: 103 us -> 123 us  [on_device(): payload = lax.psum(payload, 'ctx').astype(f32)]
    unnamed x2 -> x0, blocking collectives: 14.5 us -> none
  transfers between devices with their start and end apart: 17 -> 41, of which waited for: 16 -> 22; matrix products, arithmetic and copies ran while one was open for 7% -> 7% of each run, Pallas kernels for 3% -> 4%
where the time goes in v2:
time: 509 us; the launch traced here: 502 us
  waiting for transfers between devices  307 us (60%)
  Pallas kernels  56.7 us (11%)
  starting transfers between devices  51.8 us (10%)
  other arithmetic  29 us (6%)
  local copies, waits for them, and re-layouts  23.8 us (5%)
  matrix products  18.4 us (4%)
  between operations  15 us (3%)
    ppermute x40, waiting for transfers between devices, swap(): return lax.ppermute(x, axis, [(i, i ^ bit) for i in range(count)])  184 us
    psum x1, waiting for transfers between devices, on_device(): payload = lax.psum(payload, 'ctx').astype(f32)  123 us
    ppermute x40, starting transfers between devices, swap(): return lax.ppermute(x, axis, [(i, i ^ bit) for i in range(count)])  51.8 us
    pallas_call x1, Pallas kernels, backward(): pl.pallas_call(lambda *refs: backward_kernel((len(xs), len(ws)), *refs),...  29.3 us
    dot_general x7, matrix products, dot(): lax.dot_general(a, b, (((ca,), (cb,)), ((), ())), preferred_element_type=...  18.4 us
    pallas_call x1, Pallas kernels, forward(): pl.pallas_call(lambda *refs: forward_kernel((len(xs), len(ws)), *refs), n...  17.6 us
  transfers between devices with their start and end apart: 41, of which 22 were waited for; matrix products, arithmetic and copies ran while one was open for 7% of the time, Pallas kernels for 4%

profile of v2, /device:TPU:0, one launch (start us, length us, event | category | flops | bytes accessed | tf_op | source)
XLA Modules:
  0.0 501.7 jit_solution(10635305618069762850)
XLA Ops:
  8.8 2.4 pad_maximum_fusion.1
  11.2 3.0 collective-permute-start.1
  14.2 28.3 %collective-permute-done.1 = bf16[208,3072]{1,0:T(8,128)(2,1)S(1)} collective-permute-done((bf16[208,3072]{1,0:T(8,128)(2,1)}, bf16[208,3072]{1,0:T(8,128)(2,1)S(1)}, u32[]{:S(2)}, u32[]{:S(2)}) %collective-permute-start.1) | collective-permute-done | bytes 1277984 | tf_op jit(solution)/shard_map/ppermute | solution.py:579
  42.5 2.9 collective-permute-start.6
  47.0 2.4 constant_dynamic-slice_fusion.1
  50.6 13.0 %collective-permute-done.6 = bf16[256,768]{1,0:T(8,128)(2,1)S(1)} collective-permute-done((bf16[256,768]{1,0:T(8,128)(2,1)S(1)}, bf16[256,768]{1,0:T(8,128)(2,1)S(1)}, u32[]{:S(2)}, u32[]{:S(2)}) %collective-permute-start.6) | collective-permute-done | bytes 393248 | tf_op jit(solution)/shard_map/ppermute | solution.py:579
  68.6 5.9 %collective-permute-done.8 = bf16[256,768]{1,0:T(8,128)(2,1)} collective-permute-done((bf16[256,768]{1,0:T(8,128)(2,1)S(1)}, bf16[256,768]{1,0:T(8,128)(2,1)}, u32[]{:S(2)}, u32[]{:S(2)}) %collective-permute-start.8) | collective-permute-done | bytes 393248 | tf_op jit(solution)/shard_map/ppermute | solution.py:579
  81.3 5.7 %collective-permute-done.7 = bf16[256,768]{1,0:T(8,128)(2,1)} collective-permute-done((bf16[256,768]{1,0:T(8,128)(2,1)S(1)}, bf16[256,768]{1,0:T(8,128)(2,1)}, u32[]{:S(2)}, u32[]{:S(2)}) %collective-permute-start.7) | collective-permute-done | bytes 393248 | tf_op jit(solution)/shard_map/ppermute | solution.py:579
  87.1 8.4 %collective-permute-done.5 = bf16[256,768]{1,0:T(8,128)(2,1)} collective-permute-done((bf16[256,768]{1,0:T(8,128)(2,1)}, bf16[256,768]{1,0:T(8,128)(2,1)}, u32[]{:S(2)}, u32[]{:S(2)}) %collective-permute-start.5) | collective-permute-done | bytes 393248 | tf_op jit(solution)/shard_map/ppermute | solution.py:579
  95.5 6.9 %collective-permute-done.9 = bf16[256,768]{1,0:T(8,128)(2,1)} collective-permute-done((bf16[256,768]{1,0:T(8,128)(2,1)}, bf16[256,768]{1,0:T(8,128)(2,1)}, u32[]{:S(2)}, u32[]{:S(2)}) %collective-permute-start.9) | collective-permute-done | bytes 393248 | tf_op jit(solution)/shard_map/ppermute | solution.py:579
  102.4 17.6 %forward.1 = (bf16[256,768]{1,0:T(8,128)(2,1)}, f32[256,768]{1,0:T(8,128)}, bf16[256,768]{1,0:T(8,128)(2,1)}, f32[2,6,128,128]{3,2,1,0:T(8,128)}, f32[2,6,1,256]...) custom-call(s32[3]{0:T(128)} %pad_add_fusion.refs_0_, ...), custom_call_target="tpu_custom_call" | custom-call | tf_op jit(solution)/shard_map/forward/pallas_call | solution.py:275
  120.0 3.0 collective-permute-start.11
  123.1 1.6 collective-permute-start.15
  125.2 7.6 %collective-permute-done.11 = bf16[256,768]{1,0:T(8,128)(2,1)S(1)} collective-permute-done((bf16[256,768]{1,0:T(8,128)(2,1)}, bf16[256,768]{1,0:T(8,128)(2,1)S(1)}, u32[]{:S(2)}, u32[]{:S(2)}) %collective-permute-start.11) | collective-permute-done | bytes 393248 | tf_op jit(solution)/shard_map/ppermute | solution.py:579
  132.8 1.8 collective-permute-start.12
  134.6 4.4 collective-permute-done.19
  141.8 9.8 %ffn.1 = (bf16[1024,768]{1,0:T(8,128)(2,1)}, bf16[1024,768]{1,0:T(8,128)(2,1)}, bf16[1024,768]{1,0:T(8,128)(2,1)}) custom-call(s32[3]{0:T(128)} %pad_add_fusion.refs_0_, bf16[1,256,768]{2,1,0:T(8,128)(2,1)} %bitcast.111, bf16[1,256,768]{2,1,0:T(8,128)(2,1)} %bitcast.113, bf16[1,256,768]{2,1,0:T(8,128)(2,1)} %bitcast.112, bf16[1,256,768]{2,1,0:T(8,128)(2,1)} %bitcast.114, ...), custom_call_target="tpu_custom_call" | custom-call | tf_op jit(solution)/shard_map/ffn/pallas_call | solution.py:338
  155.7 2.5 collective-permute-start.25
  158.3 9.4 %collective-permute-done.25 = bf16[256,768]{1,0:T(8,128)(2,1)S(1)} collective-permute-done((bf16[256,768]{1,0:T(8,128)(2,1)S(1)}, bf16[256,768]{1,0:T(8,128)(2,1)S(1)}, u32[]{:S(2)}, u32[]{:S(2)}) %collective-permute-start.25) | collective-permute-done | bytes 393248 | tf_op jit(solution)/shard_map/ppermute | solution.py:579
  167.7 2.0 convert_add_fusion.2.refs_6_
  169.7 29.3 %backward.1 = (f32[256,768]{1,0:T(8,128)}, bf16[256,768]{1,0:T(8,128)(2,1)}, bf16[256,768]{1,0:T(8,128)(2,1)}, bf16[2048,768]{1,0:T(8,128)(2,1)}, bf16[2048,768]...) custom-call(s32[3]{0:T(128)} %pad_add_fusion.refs_0_, ...), custom_call_target="tpu_custom_call" | custom-call | tf_op jit(solution)/shard_map/backward/pallas_call | solution.py:538
  201.5 7.4 %collective-permute-start.26 = (bf16[256,768]{1,0:T(8,128)(2,1)S(1)}, bf16[256,768]{1,0:T(8,128)(2,1)}, u32[]{:S(2)}, u32[]{:S(2)}) collective-permute-start(bf16[256,768]{1,0:T(8,128)(2,1)S(1)} %get-tuple-element.67), channel_id=1, source_target_pairs={{0,4},{4,0},{8,12},{12,8},{16,20},{20,16},{24,28},{28,24},{1,5},{5... | collective-permute-start | bytes 1179656 | tf_op jit(solution)/shard_map/ppermute | solution.py:579
  208.9 1.9 collective-permute-start.29
  210.9 5.8 %convolution_convert_fusion.3 = bf16[768,768]{0,1:T(8,128)(2,1)} fusion(bf16[2048,768]{1,0:T(8,128)(2,1)S(1)} %copy-done.42, bf16[2048,768]{1,0:T(8,128)(2,1)} %get-tuple-element.51), kind=kOutput, calls=%fused_computation.35 | convolution fusion | flops 2416508928 | bytes 7471104 | tf_op jit(solution)/shard_map/dot_general | solution.py:31
  216.7 3.8 convolution_convert_fusion.2
  221.5 16.9 %collective-permute-done.27 = bf16[256,768]{1,0:T(8,128)(2,1)S(1)} collective-permute-done((bf16[256,768]{1,0:T(8,128)(2,1)S(1)}, bf16[256,768]{1,0:T(8,128)(2,1)S(1)}, u32[]{:S(2)}, u32[]{:S(2)}) %collective-permute-start.27) | collective-permute-done | bytes 393248 | tf_op jit(solution)/shard_map/ppermute | solution.py:579
  238.4 2.0 add_convert_fusion.3
  240.4 5.4 %collective-permute-start.31 = (bf16[256,768]{1,0:T(8,128)(2,1)S(1)}, bf16[256,768]{1,0:T(8,128)(2,1)S(1)}, u32[]{:S(2)}, u32[]{:S(2)}) collective-permute-start(bf16[256,768]{1,0:T(8,128)(2,1)S(1)} %get-tuple-element.72), channel_id=1, source_target_pairs={{0,8},{4,12},{8,0},{12,4},{16,24},{20,28},{24,16},{28,20},{1,9},{5... | collective-permute-start | bytes 1179656 | tf_op jit(solution)/shard_map/ppermute | solution.py:579
  246.5 8.8 %collective-permute-done.31 = bf16[256,768]{1,0:T(8,128)(2,1)S(1)} collective-permute-done((bf16[256,768]{1,0:T(8,128)(2,1)S(1)}, bf16[256,768]{1,0:T(8,128)(2,1)S(1)}, u32[]{:S(2)}, u32[]{:S(2)}) %collective-permute-start.31) | collective-permute-done | bytes 393248 | tf_op jit(solution)/shard_map/ppermute | solution.py:579
  256.5 3.3 collective-permute-start.32
  260.2 7.6 %collective-permute-done.28 = bf16[256,768]{1,0:T(8,128)(2,1)} collective-permute-done((bf16[256,768]{1,0:T(8,128)(2,1)}, bf16[256,768]{1,0:T(8,128)(2,1)}, u32[]{:S(2)}, u32[]{:S(2)}) %collective-permute-start.28) | collective-permute-done | bytes 393248 | tf_op jit(solution)/shard_map/ppermute | solution.py:579
  267.8 9.9 %collective-permute-done.32 = bf16[256,768]{1,0:T(8,128)(2,1)} collective-permute-done((bf16[256,768]{1,0:T(8,128)(2,1)S(1)}, bf16[256,768]{1,0:T(8,128)(2,1)}, u32[]{:S(2)}, u32[]{:S(2)}) %collective-permute-start.32) | collective-permute-done | bytes 393248 | tf_op jit(solution)/shard_map/ppermute | solution.py:579
  277.7 1.9 fusion.33
  281.3 2.5 pad_maximum_fusion
  283.8 6.9 %copy.29 = bf16[768,3072]{1,0:T(8,128)(2,1)} copy(bf16[768,3072]{0,1:T(8,128)(2,1)} %pad_maximum_fusion) | data formatting | bytes 9437184 | tf_op jit(solution)/shard_map/concatenate | solution.py:727
  290.8 1.9 fusion.30
  296.2 2.2 collective-permute-start.35
  298.5 1.9 collective-permute-start.39
  300.5 2.5 fusion.19
  303.0 30.6 %collective-permute-done.37 = bf16[192,768]{1,0:T(8,128)(2,1)S(1)} collective-permute-done((bf16[192,768]{1,0:T(8,128)(2,1)S(1)}, bf16[192,768]{1,0:T(8,128)(2,1)S(1)}, u32[]{:S(2)}, u32[]{:S(2)}) %collective-permute-start.37) | collective-permute-done | bytes 294944 | tf_op jit(solution)/shard_map/ppermute | solution.py:579
  333.6 5.8 %collective-permute-done.39 = bf16[192,768]{1,0:T(8,128)(2,1)S(1)} collective-permute-done((bf16[192,768]{1,0:T(8,128)(2,1)S(1)}, bf16[192,768]{1,0:T(8,128)(2,1)S(1)}, u32[]{:S(2)}, u32[]{:S(2)}) %collective-permute-start.39) | collective-permute-done | bytes 294944 | tf_op jit(solution)/shard_map/ppermute | solution.py:579
  340.9 1.7 fusion.2
  343.9 2.8 convolution_convert_fusion
  348.6 1.8 collective-permute-start.22
  350.4 9.4 %collective-permute-done.22 = bf16[256,768]{1,0:T(8,128)(2,1)S(1)} collective-permute-done((bf16[256,768]{1,0:T(8,128)(2,1)S(1)}, bf16[256,768]{1,0:T(8,128)(2,1)S(1)}, u32[]{:S(2)}, u32[]{:S(2)}) %collective-permute-start.22) | collective-permute-done | bytes 393248 | tf_op jit(solution)/shard_map/ppermute | solution.py:579
  361.8 123.2 %all-reduce.6.cloned.1.call-done = (bf16[208,3072]{1,0:T(8,128)(2,1)}, bf16[192,3072]{1,0:T(8,128)(2,1)}, bf16[768,768]{1,0:T(8,128)(2,1)}) async-done(((bf16[208,3072]{1,0:T(8,128)(2,1)}, bf16[192,3072]{1,0:T(8,128)(2,1)}, bf16[768,768]{1,0:T(8,128)(2,1)}), (bf16[208,3072]{1,0:T(8,128)(2,1)}, bf16[192,3072]{1,0:T(8,128)(2,1)}, bf16[768,768]{1,0:T(8,128)(2,1)})) %all-reduce.6.cloned.1.call-update) | async-done | bytes 3637264 | tf_op jit(solution)/shard_map/psum | solution.py:742
  486.4 2.8 fusion.62
  490.5 1.7 convert_element_type.231
  (202 shorter events, 46.1 us)
Async XLA Ops:
  7.2 35.3 %copy-start.1 = (bf16[1,256,768]{2,1,0:T(8,128)(2,1)S(1)}, bf16[1,256,768]{2,1,0:T(8,128)(2,1)}, u32[]{:S(2)}) copy-start(bf16[1,256,768]{2,1,0:T(8,128)(2,1)} %refs_15_.1) | copy-start | bytes 1179652
  7.2 477.8 %all-reduce.6.cloned.1.call-start = ((), (), s32[]{:S(2)}) async-start(), calls=%async_computation | async-start | bytes 7274496 | tf_op jit(solution)/shard_map/psum | solution.py:742
  11.2 31.2 %collective-permute-start.1 = (bf16[208,3072]{1,0:T(8,128)(2,1)}, bf16[208,3072]{1,0:T(8,128)(2,1)S(1)}, u32[]{:S(2)}, u32[]{:S(2)}) collective-permute-start(bf16[208,3072]{1,0:T(8,128)(2,1)} %pad_maximum_fusion.1), channel_id=1, source_target_pairs={{0,2},{1,3},{2,0},{3,1},{4,6},{5,7},{6,4},{7,5},{8,10},{9,11},{10,... | collective-permute-start | bytes 3833864 | tf_op jit(solution)/shard_map/ppermute | solution.py:579
  14.2 52.2 %collective-permute-start = (bf16[208,3072]{1,0:T(8,128)(2,1)}, bf16[208,3072]{1,0:T(8,128)(2,1)S(1)}, u32[]{:S(2)}, u32[]{:S(2)}) collective-permute-start(bf16[208,3072]{1,0:T(8,128)(2,1)} %pad_maximum_fusion.1), channel_id=1, source_target_pairs={{0,1},{1,0},{2,3},{3,2},{4,5},{5,4},{6,7},{7,6},{8,9},{9,8},{10,11... | collective-permute-start | bytes 3833864 | tf_op jit(solution)/shard_map/ppermute | solution.py:579
  42.5 34.1 %collective-permute-start.2 = (bf16[208,3072]{1,0:T(8,128)(2,1)S(1)}, bf16[208,3072]{1,0:T(8,128)(2,1)}, u32[]{:S(2)}, u32[]{:S(2)}) collective-permute-start(bf16[208,3072]{1,0:T(8,128)(2,1)S(1)} %collective-permute-done.1), channel_id=1, source_target_pairs={{0,1},{1,0},{2,3},{3,2},{4,5},{5,4},{6,7},{7,6},{8,9},{9,8},{10,11... | collective-permute-start | bytes 3833864 | tf_op jit(solution)/shard_map/ppermute | solution.py:579
  42.5 21.1 %collective-permute-start.6 = (bf16[256,768]{1,0:T(8,128)(2,1)S(1)}, bf16[256,768]{1,0:T(8,128)(2,1)S(1)}, u32[]{:S(2)}, u32[]{:S(2)}) collective-permute-start(bf16[256,768]{1,0:T(8,128)(2,1)S(1)} %bitcast.94), channel_id=1, source_target_pairs={{0,16},{4,20},{8,24},{12,28},{16,0},{20,4},{24,8},{28,12},{1,17},{... | collective-permute-start | bytes 1179656 | tf_op jit(solution)/shard_map/ppermute | solution.py:579
  45.4 22.6 %collective-permute-start.4 = (bf16[256,768]{1,0:T(8,128)(2,1)S(1)}, bf16[256,768]{1,0:T(8,128)(2,1)}, u32[]{:S(2)}, u32[]{:S(2)}) collective-permute-start(bf16[256,768]{1,0:T(8,128)(2,1)S(1)} %bitcast.95), channel_id=1, source_target_pairs={{0,8},{4,12},{8,0},{12,4},{16,24},{20,28},{24,16},{28,20},{1,9},{5... | collective-permute-start | bytes 1179656 | tf_op jit(solution)/shard_map/ppermute | solution.py:579
  49.3 15.5 %collective-permute-start.13 = (bf16[192,768]{1,0:T(8,128)(2,1)}, bf16[192,768]{1,0:T(8,128)(2,1)}, u32[]{:S(2)}, u32[]{:S(2)}) collective-permute-start(bf16[192,768]{1,0:T(8,128)(2,1)} %get-tuple-element.94), channel_id=1, source_target_pairs={{0,1},{1,0},{2,3},{3,2},{4,5},{5,4},{6,7},{7,6},{8,9},{9,8},{10,11... | collective-permute-start | bytes 884744 | tf_op jit(solution)/shard_map/ppermute | solution.py:579
  63.6 38.8 %copy-start.6 = (bf16[256,768]{1,0:T(8,128)(2,1)}, bf16[256,768]{1,0:T(8,128)(2,1)S(1)}, u32[]{:S(2)}) copy-start(bf16[256,768]{1,0:T(8,128)(2,1)S(1)} %collective-permute-done.6) | copy-start | bytes 1179652
  63.6 10.9 %collective-permute-start.8 = (bf16[256,768]{1,0:T(8,128)(2,1)S(1)}, bf16[256,768]{1,0:T(8,128)(2,1)}, u32[]{:S(2)}, u32[]{:S(2)}) collective-permute-start(bf16[256,768]{1,0:T(8,128)(2,1)S(1)} %collective-permute-done.6), channel_id=1, source_target_pairs={{0,8},{4,12},{8,0},{12,4},{16,24},{20,28},{24,16},{28,20},{1,9},{5... | collective-permute-start | bytes 1179656 | tf_op jit(solution)/shard_map/ppermute | solution.py:579
  64.9 11.0 %collective-permute-start.14 = (bf16[192,768]{1,0:T(8,128)(2,1)}, bf16[192,768]{1,0:T(8,128)(2,1)S(1)}, u32[]{:S(2)}, u32[]{:S(2)}) collective-permute-start(bf16[192,768]{1,0:T(8,128)(2,1)} %collective-permute-done.13), channel_id=1, source_target_pairs={{0,2},{1,3},{2,0},{3,1},{4,6},{5,7},{6,4},{7,5},{8,10},{9,11},{10,... | collective-permute-start | bytes 884744 | tf_op jit(solution)/shard_map/ppermute | solution.py:579
  66.4 36.0 %copy-start.4 = (bf16[208,3072]{1,0:T(8,128)(2,1)}, bf16[208,3072]{1,0:T(8,128)(2,1)S(1)}, u32[]{:S(2)}) copy-start(bf16[208,3072]{1,0:T(8,128)(2,1)S(1)} %collective-permute-done) | copy-start | bytes 3833860
  66.4 14.9 %collective-permute-start.3 = (bf16[256,768]{1,0:T(8,128)(2,1)S(1)}, bf16[256,768]{1,0:T(8,128)(2,1)}, u32[]{:S(2)}, u32[]{:S(2)}) collective-permute-start(bf16[256,768]{1,0:T(8,128)(2,1)S(1)} %bitcast.96), channel_id=1, source_target_pairs={{0,4},{4,0},{8,12},{12,8},{16,20},{20,16},{24,28},{28,24},{1,5},{5... | collective-permute-start | bytes 1179656 | tf_op jit(solution)/shard_map/ppermute | solution.py:579
  68.0 19.1 %collective-permute-start.7 = (bf16[256,768]{1,0:T(8,128)(2,1)S(1)}, bf16[256,768]{1,0:T(8,128)(2,1)}, u32[]{:S(2)}, u32[]{:S(2)}) collective-permute-start(bf16[256,768]{1,0:T(8,128)(2,1)S(1)} %collective-permute-done.6), channel_id=1, source_target_pairs={{0,4},{4,0},{8,12},{12,8},{16,20},{20,16},{24,28},{28,24},{1,5},{5... | collective-permute-start | bytes 1179656 | tf_op jit(solution)/shard_map/ppermute | solution.py:579
  74.5 21.0 %collective-permute-start.5 = (bf16[256,768]{1,0:T(8,128)(2,1)}, bf16[256,768]{1,0:T(8,128)(2,1)}, u32[]{:S(2)}, u32[]{:S(2)}) collective-permute-start(bf16[256,768]{1,0:T(8,128)(2,1)} %collective-permute-done.4), channel_id=1, source_target_pairs={{0,4},{4,0},{8,12},{12,8},{16,20},{20,16},{24,28},{28,24},{1,5},{5... | collective-permute-start | bytes 1179656 | tf_op jit(solution)/shard_map/ppermute | solution.py:579
  75.9 26.5 %collective-permute-start.9 = (bf16[256,768]{1,0:T(8,128)(2,1)}, bf16[256,768]{1,0:T(8,128)(2,1)}, u32[]{:S(2)}, u32[]{:S(2)}) collective-permute-start(bf16[256,768]{1,0:T(8,128)(2,1)} %collective-permute-done.8), channel_id=1, source_target_pairs={{0,4},{4,0},{8,12},{12,8},{16,20},{20,16},{24,28},{28,24},{1,5},{5... | collective-permute-start | bytes 1179656 | tf_op jit(solution)/shard_map/ppermute | solution.py:579
  76.6 48.1 %collective-permute-start.16 = (bf16[256,768]{1,0:T(8,128)(2,1)}, bf16[256,768]{1,0:T(8,128)(2,1)S(1)}, u32[]{:S(2)}, u32[]{:S(2)}) collective-permute-start(bf16[256,768]{1,0:T(8,128)(2,1)} %bitcast.103), channel_id=1, source_target_pairs={{0,2},{1,3},{2,0},{3,1},{4,6},{5,7},{6,4},{7,5},{8,10},{9,11},{10,... | collective-permute-start | bytes 1179656 | tf_op jit(solution)/shard_map/ppermute | solution.py:579
  102.4 36.6 %copy-start.38 = (bf16[192,768]{1,0:T(8,128)(2,1)S(1)}, bf16[192,768]{1,0:T(8,128)(2,1)}, u32[]{:S(2)}) copy-start(bf16[192,768]{1,0:T(8,128)(2,1)} %get-tuple-element.92) | copy-start | bytes 884740
  120.0 12.8 %collective-permute-start.11 = (bf16[256,768]{1,0:T(8,128)(2,1)}, bf16[256,768]{1,0:T(8,128)(2,1)S(1)}, u32[]{:S(2)}, u32[]{:S(2)}) collective-permute-start(bf16[256,768]{1,0:T(8,128)(2,1)} %get-tuple-element.35), channel_id=1, source_target_pairs={{0,2},{1,3},{2,0},{3,1},{4,6},{5,7},{6,4},{7,5},{8,10},{9,11},{10,... | collective-permute-start | bytes 1179656 | tf_op jit(solution)/shard_map/ppermute | solution.py:579
  123.0 16.0 %collective-permute-start.19 = (bf16[192,768]{1,0:T(8,128)(2,1)S(1)}, bf16[192,768]{1,0:T(8,128)(2,1)S(1)}, u32[]{:S(2)}, u32[]{:S(2)}) collective-permute-start(bf16[192,768]{1,0:T(8,128)(2,1)S(1)} %copy-done.39), channel_id=1, source_target_pairs={{0,2},{1,3},{2,0},{3,1},{4,6},{5,7},{6,4},{7,5},{8,10},{9,11},{10,... | collective-permute-start | bytes 884744 | tf_op jit(solution)/shard_map/ppermute | solution.py:579
  123.1 17.5 %collective-permute-start.15 = (bf16[256,768]{1,0:T(8,128)(2,1)S(1)}, bf16[256,768]{1,0:T(8,128)(2,1)S(1)}, u32[]{:S(2)}, u32[]{:S(2)}) collective-permute-start(bf16[256,768]{1,0:T(8,128)(2,1)S(1)} %bitcast.105), channel_id=1, source_target_pairs={{0,1},{1,0},{2,3},{3,2},{4,5},{5,4},{6,7},{7,6},{8,9},{9,8},{10,11... | collective-permute-start | bytes 1179656 | tf_op jit(solution)/shard_map/ppermute | solution.py:579
  124.7 15.9 %collective-permute-start.17 = (bf16[256,768]{1,0:T(8,128)(2,1)S(1)}, bf16[256,768]{1,0:T(8,128)(2,1)S(1)}, u32[]{:S(2)}, u32[]{:S(2)}) collective-permute-start(bf16[256,768]{1,0:T(8,128)(2,1)S(1)} %collective-permute-done.16), channel_id=1, source_target_pairs={{0,1},{1,0},{2,3},{3,2},{4,5},{5,4},{6,7},{7,6},{8,9},{9,8},{10,11... | collective-permute-start | bytes 1179656 | tf_op jit(solution)/shard_map/ppermute | solution.py:579
  124.8 15.8 %collective-permute-start.10 = (bf16[256,768]{1,0:T(8,128)(2,1)}, bf16[256,768]{1,0:T(8,128)(2,1)S(1)}, u32[]{:S(2)}, u32[]{:S(2)}) collective-permute-start(bf16[256,768]{1,0:T(8,128)(2,1)} %get-tuple-element.35), channel_id=1, source_target_pairs={{0,1},{1,0},{2,3},{3,2},{4,5},{5,4},{6,7},{7,6},{8,9},{9,8},{10,11... | collective-permute-start | bytes 1179656 | tf_op jit(solution)/shard_map/ppermute | solution.py:579
  132.8 7.8 %collective-permute-start.12 = (bf16[256,768]{1,0:T(8,128)(2,1)S(1)}, bf16[256,768]{1,0:T(8,128)(2,1)S(1)}, u32[]{:S(2)}, u32[]{:S(2)}) collective-permute-start(bf16[256,768]{1,0:T(8,128)(2,1)S(1)} %collective-permute-done.11), channel_id=1, source_target_pairs={{0,1},{1,0},{2,3},{3,2},{4,5},{5,4},{6,7},{7,6},{8,9},{9,8},{10,11... | collective-permute-start | bytes 1179656 | tf_op jit(solution)/shard_map/ppermute | solution.py:579
  139.0 1.6 collective-permute-start.18
  152.8 1.8 collective-permute-start.24
  153.2 5.1 %collective-permute-start.23 = (bf16[256,768]{1,0:T(8,128)(2,1)S(1)}, bf16[256,768]{1,0:T(8,128)(2,1)S(1)}, u32[]{:S(2)}, u32[]{:S(2)}) collective-permute-start(bf16[256,768]{1,0:T(8,128)(2,1)S(1)} %get-tuple-element.73), channel_id=1, source_target_pairs={{0,1},{1,0},{2,3},{3,2},{4,5},{5,4},{6,7},{7,6},{8,9},{9,8},{10,11... | collective-permute-start | bytes 1179656 | tf_op jit(solution)/shard_map/ppermute | solution.py:579
  155.7 12.0 %collective-permute-start.25 = (bf16[256,768]{1,0:T(8,128)(2,1)S(1)}, bf16[256,768]{1,0:T(8,128)(2,1)S(1)}, u32[]{:S(2)}, u32[]{:S(2)}) collective-permute-start(bf16[256,768]{1,0:T(8,128)(2,1)S(1)} %add_convert_fusion.5), channel_id=1, source_target_pairs={{0,2},{1,3},{2,0},{3,1},{4,6},{5,7},{6,4},{7,5},{8,10},{9,11},{10,... | collective-permute-start | bytes 1179656 | tf_op jit(solution)/shard_map/ppermute | solution.py:579
  201.5 58.8 %collective-permute-start.26 = (bf16[256,768]{1,0:T(8,128)(2,1)S(1)}, bf16[256,768]{1,0:T(8,128)(2,1)}, u32[]{:S(2)}, u32[]{:S(2)}) collective-permute-start(bf16[256,768]{1,0:T(8,128)(2,1)S(1)} %get-tuple-element.67), channel_id=1, source_target_pairs={{0,4},{4,0},{8,12},{12,8},{16,20},{20,16},{24,28},{28,24},{1,5},{5... | collective-permute-start | bytes 1179656 | tf_op jit(solution)/shard_map/ppermute | solution.py:579
  208.8 12.7 %collective-permute-start.30 = (bf16[256,768]{1,0:T(8,128)(2,1)S(1)}, bf16[256,768]{1,0:T(8,128)(2,1)S(1)}, u32[]{:S(2)}, u32[]{:S(2)}) collective-permute-start(bf16[256,768]{1,0:T(8,128)(2,1)S(1)} %get-tuple-element.68), channel_id=1, source_target_pairs={{0,4},{4,0},{8,12},{12,8},{16,20},{20,16},{24,28},{28,24},{1,5},{5... | collective-permute-start | bytes 1179656 | tf_op jit(solution)/shard_map/ppermute | solution.py:579
  208.9 37.6 %collective-permute-start.29 = (bf16[256,768]{1,0:T(8,128)(2,1)S(1)}, bf16[256,768]{1,0:T(8,128)(2,1)S(1)}, u32[]{:S(2)}, u32[]{:S(2)}) collective-permute-start(bf16[256,768]{1,0:T(8,128)(2,1)S(1)} %get-tuple-element.69), channel_id=1, source_target_pairs={{0,4},{4,0},{8,12},{12,8},{16,20},{20,16},{24,28},{28,24},{1,5},{5... | collective-permute-start | bytes 1179656 | tf_op jit(solution)/shard_map/ppermute | solution.py:579
  210.8 27.5 %collective-permute-start.27 = (bf16[256,768]{1,0:T(8,128)(2,1)S(1)}, bf16[256,768]{1,0:T(8,128)(2,1)S(1)}, u32[]{:S(2)}, u32[]{:S(2)}) collective-permute-start(bf16[256,768]{1,0:T(8,128)(2,1)S(1)} %get-tuple-element.70), channel_id=1, source_target_pairs={{0,4},{4,0},{8,12},{12,8},{16,20},{20,16},{24,28},{28,24},{1,5},{5... | collective-permute-start | bytes 1179656 | tf_op jit(solution)/shard_map/ppermute | solution.py:579
  220.5 25.3 %copy-start.34 = (bf16[256,768]{1,0:T(8,128)(2,1)S(1)}, bf16[256,768]{1,0:T(8,128)(2,1)}, u32[]{:S(2)}) copy-start(bf16[256,768]{1,0:T(8,128)(2,1)} %get-tuple-element.53) | copy-start | bytes 1179652
  240.4 37.3 %copy-start.2 = (bf16[1,256,768]{2,1,0:T(8,128)(2,1)S(1)}, bf16[1,256,768]{2,1,0:T(8,128)(2,1)}, u32[]{:S(2)}) copy-start(bf16[1,256,768]{2,1,0:T(8,128)(2,1)} %refs_15_.1) | copy-start | bytes 1179652
  240.4 37.3 %copy-start.20 = (f32[256,768]{1,0:T(8,128)S(1)}, f32[256,768]{1,0:T(8,128)}, u32[]{:S(2)}) copy-start(f32[256,768]{1,0:T(8,128)} %get-tuple-element.47) | copy-start | bytes 2359300
  240.4 14.9 %collective-permute-start.31 = (bf16[256,768]{1,0:T(8,128)(2,1)S(1)}, bf16[256,768]{1,0:T(8,128)(2,1)S(1)}, u32[]{:S(2)}, u32[]{:S(2)}) collective-permute-start(bf16[256,768]{1,0:T(8,128)(2,1)S(1)} %get-tuple-element.72), channel_id=1, source_target_pairs={{0,8},{4,12},{8,0},{12,4},{16,24},{20,28},{24,16},{28,20},{1,9},{5... | collective-permute-start | bytes 1179656 | tf_op jit(solution)/shard_map/ppermute | solution.py:579
  246.4 21.4 %collective-permute-start.28 = (bf16[256,768]{1,0:T(8,128)(2,1)}, bf16[256,768]{1,0:T(8,128)(2,1)}, u32[]{:S(2)}, u32[]{:S(2)}) collective-permute-start(bf16[256,768]{1,0:T(8,128)(2,1)} %get-tuple-element.71), channel_id=1, source_target_pairs={{0,8},{4,12},{8,0},{12,4},{16,24},{20,28},{24,16},{28,20},{1,9},{5... | collective-permute-start | bytes 1179656 | tf_op jit(solution)/shard_map/ppermute | solution.py:579
  256.5 21.3 %collective-permute-start.32 = (bf16[256,768]{1,0:T(8,128)(2,1)S(1)}, bf16[256,768]{1,0:T(8,128)(2,1)}, u32[]{:S(2)}, u32[]{:S(2)}) collective-permute-start(bf16[256,768]{1,0:T(8,128)(2,1)S(1)} %add_convert_fusion), channel_id=1, source_target_pairs={{0,16},{4,20},{8,24},{12,28},{16,0},{20,4},{24,8},{28,12},{1,17},{... | collective-permute-start | bytes 1179656 | tf_op jit(solution)/shard_map/ppermute | solution.py:579
  292.7 3.1 collective-permute-start.34
  294.9 3.7 collective-permute-start.38
  295.3 45.6 %collective-permute-start.33 = (bf16[208,3072]{1,0:T(8,128)(2,1)S(1)}, bf16[208,3072]{1,0:T(8,128)(2,1)S(1)}, u32[]{:S(2)}, u32[]{:S(2)}) collective-permute-start(bf16[208,3072]{1,0:T(8,128)(2,1)S(1)} %get-tuple-element.65), channel_id=1, source_target_pairs={{0,1},{1,0},{2,3},{3,2},{4,5},{5,4},{6,7},{7,6},{8,9},{9,8},{10,11... | collective-permute-start | bytes 3833864 | tf_op jit(solution)/shard_map/ppermute | solution.py:579
  296.2 44.7 %collective-permute-start.35 = (bf16[208,3072]{1,0:T(8,128)(2,1)S(1)}, bf16[208,3072]{1,0:T(8,128)(2,1)S(1)}, u32[]{:S(2)}, u32[]{:S(2)}) collective-permute-start(bf16[208,3072]{1,0:T(8,128)(2,1)S(1)} %fusion), channel_id=1, source_target_pairs={{0,2},{1,3},{2,0},{3,1},{4,6},{5,7},{6,4},{7,5},{8,10},{9,11},{10,... | collective-permute-start | bytes 3833864 | tf_op jit(solution)/shard_map/ppermute | solution.py:579
  298.5 35.2 %collective-permute-start.37 = (bf16[192,768]{1,0:T(8,128)(2,1)S(1)}, bf16[192,768]{1,0:T(8,128)(2,1)S(1)}, u32[]{:S(2)}, u32[]{:S(2)}) collective-permute-start(bf16[192,768]{1,0:T(8,128)(2,1)S(1)} %get-tuple-element.89), channel_id=1, source_target_pairs={{0,2},{1,3},{2,0},{3,1},{4,6},{5,7},{6,4},{7,5},{8,10},{9,11},{10,... | collective-permute-start | bytes 884744 | tf_op jit(solution)/shard_map/ppermute | solution.py:579
  298.5 35.1 %collective-permute-start.36 = (bf16[192,768]{1,0:T(8,128)(2,1)S(1)}, bf16[192,768]{1,0:T(8,128)(2,1)S(1)}, u32[]{:S(2)}, u32[]{:S(2)}) collective-permute-start(bf16[192,768]{1,0:T(8,128)(2,1)S(1)} %get-tuple-element.90), channel_id=1, source_target_pairs={{0,1},{1,0},{2,3},{3,2},{4,5},{5,4},{6,7},{7,6},{8,9},{9,8},{10,11... | collective-permute-start | bytes 884744 | tf_op jit(solution)/shard_map/ppermute | solution.py:579
  298.5 40.9 %collective-permute-start.39 = (bf16[192,768]{1,0:T(8,128)(2,1)S(1)}, bf16[192,768]{1,0:T(8,128)(2,1)S(1)}, u32[]{:S(2)}, u32[]{:S(2)}) collective-permute-start(bf16[192,768]{1,0:T(8,128)(2,1)S(1)} %collective-permute-done.38), channel_id=1, source_target_pairs={{0,2},{1,3},{2,0},{3,1},{4,6},{5,7},{6,4},{7,5},{8,10},{9,11},{10,... | collective-permute-start | bytes 884744 | tf_op jit(solution)/shard_map/ppermute | solution.py:579
  346.8 1.8 collective-permute-start.21
  346.8 3.6 collective-permute-start.20
  348.6 11.2 %collective-permute-start.22 = (bf16[256,768]{1,0:T(8,128)(2,1)S(1)}, bf16[256,768]{1,0:T(8,128)(2,1)S(1)}, u32[]{:S(2)}, u32[]{:S(2)}) collective-permute-start(bf16[256,768]{1,0:T(8,128)(2,1)S(1)} %add_convert_fusion.7), channel_id=1, source_target_pairs={{0,2},{1,3},{2,0},{3,1},{4,6},{5,7},{6,4},{7,5},{8,10},{9,11},{10,... | collective-permute-start | bytes 1179656 | tf_op jit(solution)/shard_map/ppermute | solution.py:579
  (41 other events, 266.4 us)
Sparse Core Ops, SparseCore 0:
  342.7 142.2 all-reduce.5

commit v3 on v2

--- a/solution.py
+++ b/solution.py
@@ -124,6 +124,10 @@
 
 def hbm():
     return pl.BlockSpec(memory_space=ANY)
+
+
+def cost(us):
+    return pl.CostEstimate(flops=int(us * 1.0e9), bytes_accessed=int(us * 1.0e6), transcendentals=0)
 
 
 def load_pieces(pieces, target_ref, flip, sem):
@@ -275,6 +279,7 @@
     return pl.pallas_call(
         lambda *refs: forward_kernel((len(xs), len(ws)), *refs),
         name="forward",
+        cost_estimate=cost(22),
         out_shape=(
             jax.ShapeDtypeStruct((local_rows, D), bf),
             jax.ShapeDtypeStruct((local_rows, D), f32),
@@ -305,49 +310,169 @@
     )(ids, order, lengths, table, table_t, gains, *xs, *ws)
 
 
-def ffn_kernel(counts, *refs):
-    n_t, n_w = counts
+def join_kernel(counts, flip_at, *refs):
     ids_ref = refs[0]
-    nf_refs, cot_refs = refs[1 : 1 + n_t], refs[1 + n_t : 1 + 2 * n_t]
-    win_refs = refs[1 + 2 * n_t : 1 + 2 * n_t + n_w]
-    wffn_ref, act_ref, dup_ref, dn_ref, w_ref, sem_w = refs[1 + 2 * n_t + n_w :]
-    copies = load_pieces(expand(win_refs), w_ref, ids_ref[2], sem_w)
+    out_ref, sem = refs[1 + counts :]
+    copies = load_pieces(expand(refs[1 : 1 + counts]), out_ref, ids_ref[flip_at], sem)
     for copy in copies:
         copy.wait()
-    start = 0
-    for nf_ref, cot_ref in zip(nf_refs, cot_refs):
-        for piece in range(nf_ref.shape[0]):
-            rows = slice(start, start + nf_ref.shape[1])
-            up = dot(nf_ref[piece], w_ref[...])
-            square = up * up
-            th = jnp.tanh(GELU_C * (up + 0.044715 * square * up))
-            half = 0.5 * (1.0 + th)
-            act_ref[rows, :] = (up * half).astype(jnp.bfloat16)
-            slope = half + 0.5 * up * (1.0 - th * th) * (GELU_C * (1.0 + 3 * 0.044715 * square))
-            d_up = (dot(cot_ref[piece], wffn_ref[...], 1, 1) * slope).astype(jnp.bfloat16)
-            dup_ref[rows, :] = d_up
-            dn_ref[rows, :] = dot(d_up, w_ref[...], 1, 1).astype(jnp.bfloat16)
-            start += nf_ref.shape[1]
-
-
-def ffn(ids, nfs, cots, wins, wffn):
-    rows = sum(x.shape[0] * x.shape[1] for x in nfs)
+
+
+def join(ids, pieces, flip_at):
+    count, width = sum(p.shape[0] for p in pieces), pieces[0].shape[2]
+    rows = pieces[0].shape[1] * count
+    return pl.pallas_call(
+        lambda *refs: join_kernel(len(pieces), flip_at, *refs),
+        name="join",
+        cost_estimate=cost(2),
+        out_shape=jax.ShapeDtypeStruct((rows, width), jnp.bfloat16),
+        in_specs=[smem()] + [hbm()] * len(pieces),
+        out_specs=vmem(),
+        scratch_shapes=[pltpu.SemaphoreType.DMA((count,))],
+    )(ids, *pieces)
+
+
+def ffn_kernel(nf_ref, cot_ref, w_ref, wffn_ref, act_ref, dup_ref, dn_ref):
+    for piece in range(nf_ref.shape[0]):
+        up = dot(nf_ref[piece], w_ref[...])
+        d_act = dot(cot_ref[piece], wffn_ref[...], 1, 1)
+        square = up * up
+        th = jnp.tanh(GELU_C * (up + 0.044715 * square * up))
+        half = 0.5 * (1.0 + th)
+        act_ref[piece] = (up * half).astype(jnp.bfloat16)
+        slope = half + 0.5 * up * (1.0 - th * th) * (GELU_C * (1.0 + 3 * 0.044715 * square))
+        d_up = (d_act * slope).astype(jnp.bfloat16)
+        dup_ref[piece] = d_up
+        dn_ref[piece] = dot(d_up, w_ref[...], 1, 1).astype(jnp.bfloat16)
+
+
+def ffn(nf, cot, win, wffn):
+    count, rows, _ = nf.shape
     width = wffn.shape[0]
-    n_w = sum(w.shape[0] for w in wins)
     bf = jnp.bfloat16
     return pl.pallas_call(
-        lambda *refs: ffn_kernel((len(nfs), len(wins)), *refs),
+        ffn_kernel,
         name="ffn",
+        cost_estimate=cost(3),
         out_shape=(
-            jax.ShapeDtypeStruct((rows, width), bf),
-            jax.ShapeDtypeStruct((rows, width), bf),
-            jax.ShapeDtypeStruct((rows, D), bf),
+            jax.ShapeDtypeStruct((count, rows, width), bf),
+            jax.ShapeDtypeStruct((count, rows, width), bf),
+            jax.ShapeDtypeStruct((count, rows, D), bf),
         ),
-        in_specs=[smem()] + [vmem()] * (2 * len(nfs)) + [hbm()] * len(wins) + [vmem()],
+        in_specs=[vmem()] * 4,
         out_specs=(vmem(),) * 3,
-        scratch_shapes=[pltpu.VMEM((D, width), bf), pltpu.SemaphoreType.DMA((n_w,))],
         compiler_params=pltpu.CompilerParams(vmem_limit_bytes=VMEM_LIMIT),
-    )(ids, *nfs, *cots, *wins, wffn)
+    )(nf, cot, win, wffn)
+
+
+def ffn_grads_kernel(count, *refs):
+    ids_ref = refs[0]
+    nfs, cots, acts, dups = (refs[1 + i * count : 1 + (i + 1) * count] for i in range(4))
+    gout_ref, gin_ref = refs[1 + 4 * count :]
+    rows = nfs[0].shape[0] * nfs[0].shape[1]
+
+    def joined(pieces):
+        parts = [ref[...].reshape(rows, ref.shape[2]) for ref in pieces]
+        return parts[0] if count == 1 else jnp.concatenate(parts, axis=0)
+
+    gout_ref[...] = dot(joined(acts), joined(cots), 0, 0).astype(jnp.bfloat16)
+    whole = dot(joined(nfs), joined(dups), 0, 0).astype(jnp.bfloat16)
+    n, size = gin_ref.shape[0], gin_ref.shape[1]
+    for i in range(n):
+        gin_ref[lax.bitwise_xor(jnp.int32(i), ids_ref[3])] = whole[i * size : (i + 1) * size]
+
+
+def ffn_grads(ids, nfs, cots, acts, dups, n_fsdp):
+    count, width = len(nfs), acts[0].shape[2]
+    bf = jnp.bfloat16
+    return pl.pallas_call(
+        lambda *refs: ffn_grads_kernel(count, *refs),
+        name="ffn_grads",
+        cost_estimate=cost(5),
+        out_shape=(
+            jax.ShapeDtypeStruct((width, D), bf),
+            jax.ShapeDtypeStruct((n_fsdp, D // n_fsdp, width), bf),
+        ),
+        in_specs=[smem()] + [vmem()] * (4 * count),
+        out_specs=(vmem(),) * 2,
+        compiler_params=pltpu.CompilerParams(vmem_limit_bytes=VMEM_LIMIT),
+    )(ids, *nfs, *cots, *acts, *dups)
+
+
+def weight_grads_kernel(ids_ref, x_ref, xn_ref, gain_ref, dq_ref, dk_ref, dv_ref, o_ref, dlow_ref, tiny_ref, out_ref):
+    n, parts, high, wide = out_ref.shape
+    size = D // n
+    x = x_ref[...].astype(jnp.float32)
+    own = (x * lax.rsqrt(jnp.mean(x * x, axis=1, keepdims=True) + EPS) * gain_ref[0:1, :]).astype(jnp.bfloat16)
+    results = (
+        lambda: dot(own, dq_ref[...], 0, 0),
+        lambda: dot(xn_ref[...], dk_ref[...], 0, 0),
+        lambda: dot(xn_ref[...], dv_ref[...], 0, 0),
+        lambda: dot(o_ref[...], dlow_ref[...], 0, 0),
+    )
+    step = min(D, wide)
+    for column, result in enumerate(results):
+        value = result().astype(jnp.bfloat16)
+        for first in range(column * D, column * D + D, step):
+            part = lax.bitwise_xor(jnp.int32(first // wide), ids_ref[1])
+            inside = slice(first % wide, first % wide + step)
+            here = slice(first - column * D, first - column * D + step)
+            for i in range(n):
+                place = lax.bitwise_xor(jnp.int32(i), ids_ref[3])
+                out_ref[place, part, 0:size, inside] = value[i * size : (i + 1) * size, here]
+    for i in range(n):
+        place = lax.bitwise_xor(jnp.int32(i), ids_ref[3])
+        for first in range(0, 4 * D, wide):
+            part = lax.bitwise_xor(jnp.int32(first // wide), ids_ref[1])
+            out_ref[place, part, size : size + 16, :] = tiny_ref[i, :, first : first + wide]
+
+
+def weight_grads(ids, x, xn, gains, dq, dk, dv, o, dlow, tiny, parts):
+    n = tiny.shape[0]
+    return pl.pallas_call(
+        weight_grads_kernel,
+        name="weight_grads",
+        cost_estimate=cost(9),
+        out_shape=jax.ShapeDtypeStruct((n, parts, D // n + 16, 4 * D // parts), jnp.bfloat16),
+        in_specs=[smem()] + [vmem()] * 9,
+        out_specs=vmem(),
+        compiler_params=pltpu.CompilerParams(vmem_limit_bytes=VMEM_LIMIT),
+    )(ids, x, xn, gains, dq, dk, dv, o, dlow, tiny)
+
+
+def finish_kernel(count, *refs):
+    ids_ref = refs[0]
+    parts = refs[1 : 1 + count]
+    outs, tiny_ref, all_ref, sem = refs[1 + count : 5 + count], refs[5 + count], refs[6 + count], refs[7 + count]
+    copies = []
+    for number, ref in enumerate(parts):
+        place = lax.bitwise_xor(jnp.int32(number), ids_ref[1])
+        copies.append(pltpu.make_async_copy(ref, all_ref.at[place], sem.at[number]))
+    for copy in copies:
+        copy.start()
+    for copy in copies:
+        copy.wait()
+    size, wide = outs[0].shape[0], all_ref.shape[2]
+    step = min(D, wide)
+    for first in range(0, 4 * D, step):
+        value = all_ref[first // wide, :, first % wide : first % wide + step].astype(jnp.float32)
+        outs[first // D][:, first % D : first % D + step] = value[0:size]
+        tiny_ref[:, first : first + step] = value[size : size + 8]
+
+
+def finish(ids, parts):
+    high, wide = parts[0].shape
+    f32 = jnp.float32
+    return pl.pallas_call(
+        lambda *refs: finish_kernel(len(parts), *refs),
+        name="finish",
+        cost_estimate=cost(3),
+        out_shape=(jax.ShapeDtypeStruct((high - 16, D), f32),) * 4 + (jax.ShapeDtypeStruct((8, 4 * D), f32),),
+        in_specs=[smem()] + [hbm()] * len(parts),
+        out_specs=(vmem(),) * 5,
+        scratch_shapes=[pltpu.VMEM((len(parts), high, wide), jnp.bfloat16), pltpu.SemaphoreType.DMA((len(parts),))],
+        compiler_params=pltpu.CompilerParams(vmem_limit_bytes=VMEM_LIMIT),
+    )(ids, *parts)
 
 
 def backward_kernel(counts, *refs):
@@ -538,6 +663,7 @@
     return pl.pallas_call(
         lambda *refs: backward_kernel((len(xs), len(ws)), *refs),
         name="backward",
+        cost_estimate=cost(36),
         grid=(spans // 2,),
         out_shape=(
             jax.ShapeDtypeStruct((local_rows, D), f32),
@@ -604,6 +730,21 @@
     return [pieces[0], side, swap(pieces[2], "fsdp", 2), swap(corner, "fsdp", 2)]
 
 
+def ctx_scatter(p):
+    got7, got5 = swap(p[7], "ctx", 1), swap(p[5], "ctx", 1)
+    got3, got1 = swap(after(p[3], got7), "ctx", 1), swap(after(p[1], got5), "ctx", 1)
+    s6, s4, s2 = add(p[6], got7), add(p[4], got5), add(p[2], got3)
+    t4 = add(s4, swap(s6, "ctx", 2))
+    return p[0], got1, swap(s2, "ctx", 2), swap(t4, "ctx", 4)
+
+
+def ctx_gather(x):
+    x1, x2, x4 = swap(x, "ctx", 1), swap(x, "ctx", 2), swap(x, "ctx", 4)
+    x3, x6 = swap(after(x2, x1), "ctx", 1), swap(x4, "ctx", 2)
+    x5 = swap(after(x4, x3), "ctx", 1)
+    return [x, x1, x2, x3, x4, x5, x6, swap(after(x6, x5), "ctx", 1)]
+
+
 def add(*terms):
     total = terms[0].astype(jnp.float32)
     for term in terms[1:]:
@@ -641,35 +782,32 @@
     width = w_ffn_out.shape[0]
 
     if fast:
-        zero = jnp.int32(0)
-        ids = jnp.stack([place, place, shard])
-        x1, x2, x4 = swap(x, "ctx", 1), swap(x, "ctx", 2), swap(x, "ctx", 4)
-        x3, x6 = swap(x2, "ctx", 1), swap(x4, "ctx", 2)
-        x5, x7 = swap(x4, "ctx", 1), swap(x6, "ctx", 1)
-        xs = [p[None] for p in (x, x1, x2, x3, x4, x5, x6, x7)]
-        w_pieces = gather_four(weights)
-        ws = [p[None] for p in w_pieces]
+        ids = jnp.stack([place, place, jnp.int32(0), shard])
         order = [shard ^ r for r in range(4)]
-        smalls = jnp.stack([p[own_rows] for p in w_pieces])
-        smalls = jnp.stack([lax.dynamic_index_in_dim(smalls, order[i], 0, False) for i in range(4)])
-        columns = after(w_in, w_pieces[2])
-        wins = exchange_four([block(columns, order[r], 4, 1) for r in range(4)])
-        cots = [p[None] for p in gather_four(after(cot, wins[3]))]
+        parts = ctx_gather(x)
+        xs = [p[None] for p in parts]
+        columns = after(w_in, parts[6])
+        columns = [block(columns, order[r], 4, 1) for r in range(4)]
+        side, corner = swap(columns[1], "fsdp", 1), swap(columns[3], "fsdp", 1)
+        wins = [columns[0], side, swap(columns[2], "fsdp", 2), swap(corner, "fsdp", 2)]
+        cot2 = swap(after(cot, parts[5]), "fsdp", 2)
+        cots = [p[None] for p in (cot, swap(after(cot, parts[5]), "fsdp", 1), cot2, swap(cot2, "fsdp", 1))]
         wins = [p[None] for p in wins]
     else:
-        ids = jnp.stack([place, jnp.int32(0), jnp.int32(0)])
+        ids = jnp.stack([place, jnp.int32(0), jnp.int32(0), jnp.int32(0)])
         xs = [lax.all_gather(x, "ctx", axis=0)]
-        ws = [lax.all_gather(weights, "fsdp", axis=0)]
-        smalls = ws[0][:, own_rows]
         parts = jnp.stack([w_in[:, i * width : (i + 1) * width] for i in range(n_fsdp)])
         wins = [lax.all_to_all(parts, "fsdp", 0, 0)]
         cots = [lax.all_gather(cot, "fsdp", axis=0)]
 
+    ws = [lax.all_gather(weights, "fsdp", axis=0)]
+    smalls = ws[0][:, own_rows]
     gains = jnp.stack([smalls[:, :own_rows].reshape(D), smalls[:, own_rows : 2 * own_rows].reshape(D)]).astype(f32)
     table_bf = smalls[:, 2 * own_rows : 2 * own_rows + table_size].reshape(NB, H)
     table = table_bf.astype(f32)
     table_t = jnp.pad(table_bf.T, ((0, 16 - H), (0, 128 - NB)))
 
+    win = join(ids, wins, 3)
     nf, res, o, ot, lse, q, k, v, xn = forward(
         ids, span_order, lengths, table, table_t, gains, xs, ws, local_rows
     )
@@ -678,76 +816,69 @@
         nfs = [p[None] for p in gather_four(nf)]
     else:
         nfs = [lax.all_gather(nf, "fsdp", axis=0)]
-    act, dup, dn_part = ffn(ids, nfs, cots, wins, w_ffn_out)
-    dn_part = dn_part.reshape(n_fsdp, local_rows, D)
+    acts, dups, dns = zip(*(ffn(n, c, win, w_ffn_out) for n, c in zip(nfs, cots)))
     if fast:
-        a, b, c = scatter_four([dn_part[r] for r in range(4)])
+        a, b, c = scatter_four([p[0] for p in dns])
         dnf = a.astype(f32) + b.astype(f32) + c.astype(f32)
     else:
-        dnf = lax.psum_scatter(dn_part, "fsdp", scatter_dimension=0).astype(f32)
-
-    nf_all = jnp.concatenate([p.reshape(-1, D) for p in nfs])
-    cot_all = jnp.concatenate([p.reshape(-1, D) for p in cots])
-    out_part = dot(act, w_ffn_out).astype(bf).reshape(n_fsdp, local_rows, D)
-    grad_ffn_out = dot(act, cot_all, 0, 0).astype(bf)
-    grad_in = dot(nf_all, dup, 0, 0).astype(bf).reshape(n_fsdp, own_rows, width)
+        dnf = lax.psum_scatter(dns[0], "fsdp", scatter_dimension=0).astype(f32)
+    grad_ffn_out, grad_in = ffn_grads(ids, nfs, cots, acts, dups, n_fsdp)
     if fast:
-        a, b, c = scatter_four([out_part[r] for r in range(4)])
+        grad_in = jnp.concatenate(exchange_four([grad_in[r] for r in range(4)]))
+    else:
+        grad_in = lax.all_to_all(grad_in, "fsdp", 0, 0).reshape(D, width)
+    dnf = after(dnf, grad_in)
+    grad_ffn_out = lax.psum_scatter(grad_ffn_out, "ctx", scatter_dimension=0, tiled=True)
+    grad_in = lax.psum_scatter(grad_in, "ctx", scatter_dimension=0, tiled=True)
+    out_parts = [dot(p.reshape(-1, width), w_ffn_out).astype(bf) for p in acts]
+    if fast:
+        a, b, c = scatter_four(out_parts)
         output = (res + a.astype(f32) + b.astype(f32) + c.astype(f32)).astype(bf)
-        got = exchange_four([lax.dynamic_index_in_dim(grad_in, order[r], 0, False) for r in range(4)])
-        got = jnp.stack(got)
-        grad_in = jnp.concatenate([lax.dynamic_index_in_dim(got, shard ^ i, 0, False) for i in range(4)], axis=1)
     else:
+        out_part = out_parts[0].reshape(n_fsdp, local_rows, D)
         output = (res + lax.psum_scatter(out_part, "fsdp", scatter_dimension=0).astype(f32)).astype(bf)
-        got = lax.all_to_all(grad_in, "fsdp", 0, 0)
-        grad_in = jnp.transpose(got, (1, 0, 2)).reshape(own_rows, n_fsdp * width)
-    grad_ffn_out = lax.psum(grad_ffn_out, "ctx")
-    grad_in = lax.psum(grad_in, "ctx")
 
     dres, dlow, dq, dk, dv, dn, dn_own, dgain, dtab = backward(
         ids, span_order, lengths, table, table_t, gains, dnf, res, cot, o, ot, lse, q, k, v, xs, ws
     )
     dn = dn.reshape(n_ctx, local_rows, D)
     if fast:
-        got7, got5, got3, got1 = (swap(dn[r], "ctx", 1) for r in (7, 5, 3, 1))
-        s6, s4, s2, s0 = add(dn[6], got7), add(dn[4], got5), add(dn[2], got3), add(dn[0], got1)
-        t4 = add(s4, swap(s6, "ctx", 2))
-        t2 = swap(s2, "ctx", 2)
-        d_normed = dn_own + s0.astype(f32) + t2.astype(f32) + swap(t4, "ctx", 4).astype(f32)
+        a, b, c, d = ctx_scatter([dn[r] for r in range(8)])
+        d_normed = dn_own + a.astype(f32) + b.astype(f32) + c.astype(f32) + d.astype(f32)
     else:
         d_normed = dn_own + lax.psum_scatter(dn, "ctx", scatter_dimension=0).astype(f32)
 
     xf = x.astype(f32)
     inv_rms = lax.rsqrt(jnp.mean(xf * xf, axis=1, keepdims=True) + EPS)
-    xn_own = (xf * inv_rms * gains[0:1]).astype(bf)
     scaled = d_normed * gains[0:1]
     inner = jnp.mean(scaled * xf, axis=1, keepdims=True)
     grad_tokens = (dres + inv_rms * scaled - xf * (inv_rms * inv_rms * inv_rms * inner)).astype(bf)
 
-    grads = jnp.concatenate(
-        [dot(xn_own, dq, 0, 0).astype(bf), dot(xn, dk, 0, 0).astype(bf), dot(xn, dv, 0, 0).astype(bf),
-         dot(o, dlow, 0, 0).astype(bf)], axis=1
-    )
     tiny = jnp.concatenate(
         [dgain[0].reshape(n_fsdp, own_rows), dgain[1].reshape(n_fsdp, own_rows),
          dtab[:H, :NB].T.reshape(n_fsdp, table_size)], axis=1
     ).astype(bf)
     tiny = jnp.pad(tiny[:, None, :], ((0, 0), (0, 15), (0, 4 * D - tiny.shape[1])))
-    payload = jnp.concatenate([grads.reshape(n_fsdp, own_rows, 4 * D), tiny], axis=1)
+    payload = weight_grads(ids, x, xn, gains, dq, dk, dv, o, dlow, tiny, 8 if fast else 1)
     if fast:
-        a, b, c = scatter_four([lax.dynamic_index_in_dim(payload, order[r], 0, False) for r in range(4)])
-        payload = add(a, b, c)
+        payload = after(add(*scatter_four([payload[r] for r in range(4)])), d_normed)
+        grads = ctx_gather(add(*ctx_scatter([payload[r] for r in range(8)])))
     else:
         payload = lax.psum_scatter(payload, "fsdp", scatter_dimension=0)
-    payload = lax.psum(payload, "ctx").astype(f32)
-    tiny = payload[own_rows]
+        grads = [lax.psum(payload, "ctx")[0]]
+    g_query, g_key, g_value, g_out, tiny = finish(ids, grads)
+    tiny = tiny[0]
+    grad_ffn_out = lax.all_gather(grad_ffn_out, "ctx", axis=0, tiled=True)
+    grad_in = lax.all_gather(grad_in, "ctx", axis=0, tiled=True).reshape(n_fsdp, own_rows, width)
+    flip = shard if fast else jnp.int32(0)
+    grad_in = jnp.concatenate([lax.dynamic_index_in_dim(grad_in, flip ^ i, 0, False) for i in range(n_fsdp)], axis=1)
     return (
         output[None],
         grad_tokens[None],
-        payload[:own_rows, 0:D],
-        payload[:own_rows, D : 2 * D],
-        payload[:own_rows, 2 * D : 3 * D],
-        payload[:own_rows, 3 * D : 4 * D],
+        g_query,
+        g_key,
+        g_value,
+        g_out,
         grad_in.astype(f32),
         grad_ffn_out.astype(f32),
         tiny[:own_rows],

time: 509 us -> 357 us (0.70); the launches traced: 502 us -> 357 us
  waiting for transfers between devices: 307 us -> 134 us
  Pallas kernels: 56.7 us -> 100 us
  matrix products: 18.4 us -> 7.42 us
    psum x1 -> x0, waiting for transfers between devices: 123 us -> none  [on_device(): payload = lax.psum(payload, 'ctx').astype(f32)]
    ppermute x40 -> x51, waiting for transfers between devices: 184 us -> 120 us  [swap(): return lax.ppermute(x, axis, [(i, i ^ bit) for i in range(count)])]
    pallas_call x1 -> x8, Pallas kernels: 9.81 us -> 41 us  [the longest x4 15.5 us: ffn(): pl.pallas_call(ffn_kernel, name='ffn', cost_estimate=cost(3), out_shape=(...]
    all_gather x0 -> x3, waiting for transfers between devices: none -> 14.5 us  [the longest x1 14.5 us: on_device(): lax.all_gather(grad_in, 'ctx', axis=0, tiled=True)]
    dot_general x7 -> x4, matrix products: 18.4 us -> 7.42 us  [dot(): lax.dot_general(a, b, (((ca,), (cb,)), ((), ())), preferred_element_type=...]
    pallas_call x1, Pallas kernels: 29.3 us -> 37.2 us  [backward(): pl.pallas_call(lambda *refs: backward_kernel((len(xs), len(ws)), *refs),...]
    concatenate x1 -> x0, local copies, waits for them, and re-layouts: 6.91 us -> none  [on_device(): jnp.concatenate([dot(xn_own, dq, 0, 0).astype(bf), dot(xn, dk, 0, 0).asty...]
    squeeze x1 -> x4, local copies, waits for them, and re-layouts: 0.09 us -> 5.26 us  [the longest x1 3.15 us: on_device(): payload[r]]
  transfers between devices with their start and end apart: 41 -> 56, of which waited for: 22 -> 27; matrix products, arithmetic and copies ran while one was open for 7% -> 11% of each run, Pallas kernels for 4% -> 25%
where the time goes in v3:
time: 357 us
  waiting for transfers between devices  134 us (38%)
  Pallas kernels  100 us (28%)
  starting transfers between devices  56.3 us (16%)
  other arithmetic  25.2 us (7%)
  local copies, waits for them, and re-layouts  19.4 us (5%)
  between operations  14.2 us (4%)
  matrix products  7.42 us (2%)
    ppermute x51, waiting for transfers between devices, swap(): return lax.ppermute(x, axis, [(i, i ^ bit) for i in range(count)])  120 us
    ppermute x51, starting transfers between devices, swap(): return lax.ppermute(x, axis, [(i, i ^ bit) for i in range(count)])  55.6 us
    pallas_call x1, Pallas kernels, backward(): pl.pallas_call(lambda *refs: backward_kernel((len(xs), len(ws)), *refs),...  37.2 us
    pallas_call x1, Pallas kernels, forward(): pl.pallas_call(lambda *refs: forward_kernel((len(xs), len(ws)), *refs), n...  22 us
    pallas_call x4, Pallas kernels, ffn(): pl.pallas_call(ffn_kernel, name='ffn', cost_estimate=cost(3), out_shape=(...  15.5 us
    all_gather x1, waiting for transfers between devices, on_device(): lax.all_gather(grad_in, 'ctx', axis=0, tiled=True)  14.5 us
    pallas_call x1, Pallas kernels, weight_grads(): pl.pallas_call(weight_grads_kernel, name='weight_grads', cost_estimate=co...  12.4 us
    convert_element_type x8, other arithmetic, add(): return total.astype(jnp.bfloat16)  8.22 us
  transfers between devices with their start and end apart: 56, of which 27 were waited for; matrix products, arithmetic and copies ran while one was open for 11% of the time, Pallas kernels for 25%

profile of v3, /device:TPU:0, one launch (start us, length us, event | category | flops | bytes accessed | tf_op | source)
XLA Modules:
  0.0 356.8 jit_solution(6025669507005747842)
XLA Ops:
  8.8 2.5 fusion.4
  11.3 3.0 collective-permute-start
  15.9 2.6 collective-permute-start.3
  18.5 4.9 %collective-permute-done = bf16[256,768]{1,0:T(8,128)(2,1)S(1)} collective-permute-done((bf16[256,768]{1,0:T(8,128)(2,1)S(1)}, bf16[256,768]{1,0:T(8,128)(2,1)S(1)}, u32[]{:S(2)}, u32[]{:S(2)}) %collective-permute-start) | collective-permute-done | bytes 393248 | tf_op jit(solution)/shard_map/ppermute | solution.py:705
  23.4 9.8 %collective-permute-done.1 = bf16[256,768]{1,0:T(8,128)(2,1)S(1)} collective-permute-done((bf16[256,768]{1,0:T(8,128)(2,1)S(1)}, bf16[256,768]{1,0:T(8,128)(2,1)S(1)}, u32[]{:S(2)}, u32[]{:S(2)}) %collective-permute-start.1) | collective-permute-done | bytes 393248 | tf_op jit(solution)/shard_map/ppermute | solution.py:705
  33.6 2.1 collective-permute-done.3
  36.1 6.9 %collective-permute-done.2 = bf16[256,768]{1,0:T(8,128)(2,1)S(1)} collective-permute-done((bf16[256,768]{1,0:T(8,128)(2,1)S(1)}, bf16[256,768]{1,0:T(8,128)(2,1)S(1)}, u32[]{:S(2)}, u32[]{:S(2)}) %collective-permute-start.2) | collective-permute-done | bytes 393248 | tf_op jit(solution)/shard_map/ppermute | solution.py:705
  45.1 7.1 %collective-permute-done.4 = bf16[256,768]{1,0:T(8,128)(2,1)} collective-permute-done((bf16[256,768]{1,0:T(8,128)(2,1)}, bf16[256,768]{1,0:T(8,128)(2,1)}, u32[]{:S(2)}, u32[]{:S(2)}) %collective-permute-start.4) | collective-permute-done | bytes 393248 | tf_op jit(solution)/shard_map/ppermute | solution.py:705
  61.3 22.0 %forward.1 = (bf16[256,768]{1,0:T(8,128)(2,1)}, f32[256,768]{1,0:T(8,128)}, bf16[256,768]{1,0:T(8,128)(2,1)}, f32[2,6,128,128]{3,2,1,0:T(8,128)}, f32[2,6,1,256]...) custom-call(s32[4]{0:T(128)} %pad_add_fusion.refs_0_.ids_ref, ...), custom_call_target="tpu_custom_call" | custom-call | flops 22000001024 | bytes 22000000 | tf_op jit(solution)/shard_map/forward/pallas_call | solution.py:279
  84.1 3.1 join.1.w_ref
  87.9 3.8 %ffn.4 = (bf16[1,256,768]{2,1,0:T(8,128)(2,1)}, bf16[1,256,768]{2,1,0:T(8,128)(2,1)}, bf16[1,256,768]{2,1,0:T(8,128)(2,1)}) custom-call(bf16[1,256,768]{2,1,0:T(8,128)(2,1)} %bitcast.143, bf16[1,256,768]{2,1,0:T(8,128)(2,1)} %refs_5_.1, bf16[768,768]{1,0:T(8,128)(2,1)} %join.1.w_ref, bf16[768,768]{1,0:T(8,128)(2,1)} %wffn_ref.7), custom_call_target="tpu_custom_call" | custom-call | flops 3000000000 | bytes 3000000 | tf_op jit(solution)/shard_map/ffn/pallas_call | solution.py:353
  91.8 2.6 collective-permute-done.14
  95.2 3.9 %ffn.6 = (bf16[1,256,768]{2,1,0:T(8,128)(2,1)}, bf16[1,256,768]{2,1,0:T(8,128)(2,1)}, bf16[1,256,768]{2,1,0:T(8,128)(2,1)}) custom-call(bf16[1,256,768]{2,1,0:T(8,128)(2,1)} %bitcast.145, bf16[1,256,768]{2,1,0:T(8,128)(2,1)} %bitcast.138, bf16[768,768]{1,0:T(8,128)(2,1)} %join.1.w_ref, bf16[768,768]{1,0:T(8,128)(2,1)} %wffn_ref.7), custom_call_target="tpu_custom_call" | custom-call | flops 3000000000 | bytes 3000000 | tf_op jit(solution)/shard_map/ffn/pallas_call | solution.py:353
  100.0 3.9 %ffn.5 = (bf16[1,256,768]{2,1,0:T(8,128)(2,1)}, bf16[1,256,768]{2,1,0:T(8,128)(2,1)}, bf16[1,256,768]{2,1,0:T(8,128)(2,1)}) custom-call(bf16[1,256,768]{2,1,0:T(8,128)(2,1)} %bitcast.150, bf16[1,256,768]{2,1,0:T(8,128)(2,1)} %bitcast.141, bf16[768,768]{1,0:T(8,128)(2,1)} %join.1.w_ref, bf16[768,768]{1,0:T(8,128)(2,1)} %wffn_ref.7), custom_call_target="tpu_custom_call" | custom-call | flops 3000000000 | bytes 3000000 | tf_op jit(solution)/shard_map/ffn/pallas_call | solution.py:353
  104.7 3.9 %ffn.7 = (bf16[1,256,768]{2,1,0:T(8,128)(2,1)}, bf16[1,256,768]{2,1,0:T(8,128)(2,1)}, bf16[1,256,768]{2,1,0:T(8,128)(2,1)}) custom-call(bf16[1,256,768]{2,1,0:T(8,128)(2,1)} %bitcast.152, bf16[1,256,768]{2,1,0:T(8,128)(2,1)} %bitcast.148, bf16[768,768]{1,0:T(8,128)(2,1)} %join.1.w_ref, bf16[768,768]{1,0:T(8,128)(2,1)} %wffn_ref.7), custom_call_target="tpu_custom_call" | custom-call | flops 3000000000 | bytes 3000000 | tf_op jit(solution)/shard_map/ffn/pallas_call | solution.py:353
  108.6 6.5 %ffn_grads.1 = (bf16[768,768]{1,0:T(8,128)(2,1)}, bf16[4,192,768]{2,1,0:T(8,128)(2,1)}) custom-call(s32[4]{0:T(128)} %pad_add_fusion.refs_0_.ids_ref, bf16[1,256,768]{2,1,0:T(8,128)(2,1)} %bitcast.144, bf16[1,256,768]{2,1,0:T(8,128)(2,1)} %bitcast.151, bf16[1,256,768]{2,1,0:T(8,128)(2,1)} %bitcast.146, bf16[1,256,768]{2,1,0:T(8,128)(2,1)} %bitcast.153, ...), custom_call_target="tpu_custom_call" | custom-call | flops 5000000000 | bytes 5000000 | tf_op jit(solution)/shard_map/ffn_grads/pallas_call | solution.py:388
  120.3 6.6 %collective-permute-done.24 = bf16[192,768]{1,0:T(8,128)(2,1)S(1)} collective-permute-done((bf16[192,768]{1,0:T(8,128)(2,1)S(1)}, bf16[192,768]{1,0:T(8,128)(2,1)S(1)}, u32[]{:S(2)}, u32[]{:S(2)}) %collective-permute-start.24) | collective-permute-done | bytes 294944 | tf_op jit(solution)/shard_map/ppermute | solution.py:705
  126.9 6.3 %collective-permute-done.26 = bf16[192,768]{1,0:T(8,128)(2,1)S(1)} collective-permute-done((bf16[192,768]{1,0:T(8,128)(2,1)S(1)}, bf16[192,768]{1,0:T(8,128)(2,1)S(1)}, u32[]{:S(2)}, u32[]{:S(2)}) %collective-permute-start.26) | collective-permute-done | bytes 294944 | tf_op jit(solution)/shard_map/ppermute | solution.py:705
  134.5 6.2 %collective-permute-done.22 = bf16[256,768]{1,0:T(8,128)(2,1)S(1)} collective-permute-done((bf16[256,768]{1,0:T(8,128)(2,1)S(1)}, bf16[256,768]{1,0:T(8,128)(2,1)S(1)}, u32[]{:S(2)}, u32[]{:S(2)}) %collective-permute-start.22) | collective-permute-done | bytes 393248 | tf_op jit(solution)/shard_map/ppermute | solution.py:705
  141.8 37.2 %backward.1 = (f32[256,768]{1,0:T(8,128)}, bf16[256,768]{1,0:T(8,128)(2,1)}, bf16[256,768]{1,0:T(8,128)(2,1)}, bf16[2048,768]{1,0:T(8,128)(2,1)}, bf16[2048,768]...) custom-call(s32[4]{0:T(128)} %pad_add_fusion.refs_0_.ids_ref, ...), custom_call_target="tpu_custom_call" | custom-call | flops 35999997952 | bytes 36000000 | tf_op jit(solution)/shard_map/backward/pallas_call | solution.py:663
  181.6 12.4 %weight_grads.1 = bf16[4,8,208,384]{3,2,1,0:T(8,128)(2,1)} custom-call(s32[4]{0:T(128)} %pad_add_fusion.refs_0_.ids_ref, bf16[256,768]{1,0:T(8,128)(2,1)} %bitcast.114, bf16[2048,768]{1,0:T(8,128)(2,1)} %get-tuple-element.94.xn_ref, f32[2,768]{1,0:T(2,128)} %maximum_convert_fusion.1.refs_5_.gain_ref, bf16[256,768]{1,0:T(8,128)(2,1)} %get-tuple-element.95.dq_ref, ...), custom_call_target="tpu_custom_call" | custom-call | flops 8999999488 | bytes 9000000 | tf_op jit(solution)/shard_map/weight_grads/pallas_call | solution.py:432
  194.1 3.2 slice_bitcast_fusion.2
  199.2 12.4 %collective-permute-done.29 = bf16[256,768]{1,0:T(8,128)(2,1)S(1)} collective-permute-done((bf16[256,768]{1,0:T(8,128)(2,1)S(1)}, bf16[256,768]{1,0:T(8,128)(2,1)S(1)}, u32[]{:S(2)}, u32[]{:S(2)}) %collective-permute-start.29) | collective-permute-done | bytes 393248 | tf_op jit(solution)/shard_map/ppermute | solution.py:705
  213.6 11.9 %collective-permute-done.30 = bf16[256,768]{1,0:T(8,128)(2,1)S(1)} collective-permute-done((bf16[256,768]{1,0:T(8,128)(2,1)S(1)}, bf16[256,768]{1,0:T(8,128)(2,1)S(1)}, u32[]{:S(2)}, u32[]{:S(2)}) %collective-permute-start.30) | collective-permute-done | bytes 393248 | tf_op jit(solution)/shard_map/ppermute | solution.py:705
  226.5 2.7 fusion
  229.2 4.0 %collective-permute-done.27 = bf16[256,768]{1,0:T(8,128)(2,1)S(1)} collective-permute-done((bf16[256,768]{1,0:T(8,128)(2,1)S(1)}, bf16[256,768]{1,0:T(8,128)(2,1)S(1)}, u32[]{:S(2)}, u32[]{:S(2)}) %collective-permute-start.27) | collective-permute-done | bytes 393248 | tf_op jit(solution)/shard_map/ppermute | solution.py:705
  233.5 2.2 collective-permute-done.32
  236.7 10.6 %collective-permute-start.33 = (bf16[256,768]{1,0:T(8,128)(2,1)}, bf16[256,768]{1,0:T(8,128)(2,1)}, u32[]{:S(2)}, u32[]{:S(2)}) collective-permute-start(bf16[256,768]{1,0:T(8,128)(2,1)} %add_convert_fusion), channel_id=1, source_target_pairs={{0,16},{4,20},{8,24},{12,28},{16,0},{20,4},{24,8},{28,12},{1,17},{... | collective-permute-start | bytes 1179656 | tf_op jit(solution)/shard_map/ppermute | solution.py:705
  247.6 9.7 %collective-permute-done.31 = bf16[256,768]{1,0:T(8,128)(2,1)} collective-permute-done((bf16[256,768]{1,0:T(8,128)(2,1)}, bf16[256,768]{1,0:T(8,128)(2,1)}, u32[]{:S(2)}, u32[]{:S(2)}) %collective-permute-start.31) | collective-permute-done | bytes 393248 | tf_op jit(solution)/shard_map/ppermute | solution.py:705
  257.3 2.7 fusion.14
  260.1 2.6 fusion.2
  264.9 5.2 %collective-permute-done.39 = bf16[208,384]{1,0:T(8,128)(2,1)S(1)} collective-permute-done((bf16[208,384]{1,0:T(8,128)(2,1)S(1)}, bf16[208,384]{1,0:T(8,128)(2,1)S(1)}, u32[]{:S(2)}, u32[]{:S(2)}) %collective-permute-start.39) | collective-permute-done | bytes 159776 | tf_op jit(solution)/shard_map/ppermute | solution.py:705
  270.1 2.5 collective-permute-start.40
  273.8 2.0 collective-permute-done.40
  276.6 5.0 %collective-permute-start.42 = (bf16[208,384]{1,0:T(8,128)(2,1)}, bf16[208,384]{1,0:T(8,128)(2,1)S(1)}, u32[]{:S(2)}, u32[]{:S(2)}) collective-permute-start(bf16[208,384]{1,0:T(8,128)(2,1)} %get-tuple-element.131), channel_id=1, source_target_pairs={{0,8},{4,12},{8,0},{12,4},{16,24},{20,28},{24,16},{28,20},{1,9},{5... | collective-permute-start | bytes 479240 | tf_op jit(solution)/shard_map/ppermute | solution.py:705
  283.6 2.0 collective-permute-start.41
  285.6 2.4 collective-permute-start.43
  288.0 2.3 fusion.7
  290.4 2.2 collective-permute-done.38
  292.5 7.6 %collective-permute-done.41 = bf16[208,384]{1,0:T(8,128)(2,1)S(1)} collective-permute-done((bf16[208,384]{1,0:T(8,128)(2,1)}, bf16[208,384]{1,0:T(8,128)(2,1)S(1)}, u32[]{:S(2)}, u32[]{:S(2)}) %collective-permute-start.41) | collective-permute-done | bytes 159776 | tf_op jit(solution)/shard_map/ppermute | solution.py:705
  301.8 2.4 collective-permute-start.45
  305.9 3.2 collective-permute-done.45.refs_3_
  310.3 2.6 fusion.13
  313.3 1.9 collective-permute-start.49
  315.7 4.1 %collective-permute-done.49.refs_7_ = bf16[208,384]{1,0:T(8,128)(2,1)S(1)} collective-permute-done((bf16[208,384]{1,0:T(8,128)(2,1)S(1)}, bf16[208,384]{1,0:T(8,128)(2,1)S(1)}, u32[]{:S(2)}, u32[]{:S(2)}) %collective-permute-start.49) | collective-permute-done | bytes 159776 | tf_op jit(solution)/shard_map/ppermute | solution.py:705
  322.8 2.8 convert_element_type.297
  326.4 3.6 finish.1
  332.8 14.5 %all-gather.5.cloned.1.call-done = bf16[768,768]{1,0:T(8,128)(2,1)} async-done(((bf16[96,768]{1,0:T(8,128)(2,1)}), bf16[768,768]{1,0:T(8,128)(2,1)}) %all-gather.5.cloned.1.call-update) | async-done | bytes 1179664 | tf_op jit(solution)/shard_map/all_gather | solution.py:872
  (206 shorter events, 56.9 us)
Async XLA Ops:
  7.2 49.8 %all-gather.9.cloned.1.call-start = ((), (), s32[]{:S(2)}) async-start(), calls=%async_computation.6 | async-start | bytes 6389760 | tf_op jit(solution)/shard_map/all_gather | solution.py:803
  11.3 236.0 %reduce-scatter.5.cloned.1.call-start = ((), (), s32[]{:S(2)}) async-start(), calls=%async_computation.4 | async-start | bytes 1327104 | tf_op jit(solution)/shard_map/reduce_scatter | solution.py:831
  11.3 12.1 %collective-permute-start = (bf16[256,768]{1,0:T(8,128)(2,1)S(1)}, bf16[256,768]{1,0:T(8,128)(2,1)S(1)}, u32[]{:S(2)}, u32[]{:S(2)}) collective-permute-start(bf16[256,768]{1,0:T(8,128)(2,1)S(1)} %bitcast.115), channel_id=1, source_target_pairs={{0,4},{4,0},{8,12},{12,8},{16,20},{20,16},{24,28},{28,24},{1,5},{5... | collective-permute-start | bytes 1179656 | tf_op jit(solution)/shard_map/ppermute | solution.py:705
  14.3 18.9 %collective-permute-start.1 = (bf16[256,768]{1,0:T(8,128)(2,1)S(1)}, bf16[256,768]{1,0:T(8,128)(2,1)S(1)}, u32[]{:S(2)}, u32[]{:S(2)}) collective-permute-start(bf16[256,768]{1,0:T(8,128)(2,1)S(1)} %bitcast.116), channel_id=1, source_target_pairs={{0,8},{4,12},{8,0},{12,4},{16,24},{20,28},{24,16},{28,20},{1,9},{5... | collective-permute-start | bytes 1179656 | tf_op jit(solution)/shard_map/ppermute | solution.py:705
  15.9 19.8 %collective-permute-start.3 = (bf16[256,768]{1,0:T(8,128)(2,1)S(1)}, bf16[256,768]{1,0:T(8,128)(2,1)}, u32[]{:S(2)}, u32[]{:S(2)}) collective-permute-start(bf16[256,768]{1,0:T(8,128)(2,1)S(1)} %bitcast.117), channel_id=1, source_target_pairs={{0,16},{4,20},{8,24},{12,28},{16,0},{20,4},{24,8},{28,12},{1,17},{... | collective-permute-start | bytes 1179656 | tf_op jit(solution)/shard_map/ppermute | solution.py:705
  33.2 9.8 %collective-permute-start.2 = (bf16[256,768]{1,0:T(8,128)(2,1)S(1)}, bf16[256,768]{1,0:T(8,128)(2,1)S(1)}, u32[]{:S(2)}, u32[]{:S(2)}) collective-permute-start(bf16[256,768]{1,0:T(8,128)(2,1)S(1)} %collective-permute-done.1), channel_id=1, source_target_pairs={{0,4},{4,0},{8,12},{12,8},{16,20},{20,16},{24,28},{28,24},{1,5},{5... | collective-permute-start | bytes 1179656 | tf_op jit(solution)/shard_map/ppermute | solution.py:705
  35.7 8.6 %collective-permute-start.5 = (bf16[256,768]{1,0:T(8,128)(2,1)}, bf16[256,768]{1,0:T(8,128)(2,1)}, u32[]{:S(2)}, u32[]{:S(2)}) collective-permute-start(bf16[256,768]{1,0:T(8,128)(2,1)} %collective-permute-done.3), channel_id=1, source_target_pairs={{0,8},{4,12},{8,0},{12,4},{16,24},{20,28},{24,16},{28,20},{1,9},{5... | collective-permute-start | bytes 1179656 | tf_op jit(solution)/shard_map/ppermute | solution.py:705
  43.0 9.3 %collective-permute-start.4 = (bf16[256,768]{1,0:T(8,128)(2,1)}, bf16[256,768]{1,0:T(8,128)(2,1)}, u32[]{:S(2)}, u32[]{:S(2)}) collective-permute-start(bf16[256,768]{1,0:T(8,128)(2,1)} %collective-permute-done.3), channel_id=1, source_target_pairs={{0,4},{4,0},{8,12},{12,8},{16,20},{20,16},{24,28},{28,24},{1,5},{5... | collective-permute-start | bytes 1179656 | tf_op jit(solution)/shard_map/ppermute | solution.py:705
  45.1 9.8 %collective-permute-start.9 = (bf16[192,768]{1,0:T(8,128)(2,1)S(1)}, bf16[192,768]{1,0:T(8,128)(2,1)S(1)}, u32[]{:S(2)}, u32[]{:S(2)}) collective-permute-start(bf16[192,768]{1,0:T(8,128)(2,1)S(1)} %get-tuple-element.140), channel_id=1, source_target_pairs={{0,1},{1,0},{2,3},{3,2},{4,5},{5,4},{6,7},{7,6},{8,9},{9,8},{10,11... | collective-permute-start | bytes 884744 | tf_op jit(solution)/shard_map/ppermute | solution.py:705
  52.3 8.3 %collective-permute-start.6 = (bf16[256,768]{1,0:T(8,128)(2,1)}, bf16[256,768]{1,0:T(8,128)(2,1)S(1)}, u32[]{:S(2)}, u32[]{:S(2)}) collective-permute-start(bf16[256,768]{1,0:T(8,128)(2,1)} %collective-permute-done.5), channel_id=1, source_target_pairs={{0,4},{4,0},{8,12},{12,8},{16,20},{20,16},{24,28},{28,24},{1,5},{5... | collective-permute-start | bytes 1179656 | tf_op jit(solution)/shard_map/ppermute | solution.py:705
  53.8 29.5 %collective-permute-start.7 = (bf16[192,768]{1,0:T(8,128)(2,1)S(1)}, bf16[192,768]{1,0:T(8,128)(2,1)S(1)}, u32[]{:S(2)}, u32[]{:S(2)}) collective-permute-start(bf16[192,768]{1,0:T(8,128)(2,1)S(1)} %get-tuple-element.142), channel_id=1, source_target_pairs={{0,1},{1,0},{2,3},{3,2},{4,5},{5,4},{6,7},{7,6},{8,9},{9,8},{10,11... | collective-permute-start | bytes 884744 | tf_op jit(solution)/shard_map/ppermute | solution.py:705
  53.9 29.6 %collective-permute-start.8 = (bf16[192,768]{1,0:T(8,128)(2,1)S(1)}, bf16[192,768]{1,0:T(8,128)(2,1)}, u32[]{:S(2)}, u32[]{:S(2)}) collective-permute-start(bf16[192,768]{1,0:T(8,128)(2,1)S(1)} %get-tuple-element.141), channel_id=1, source_target_pairs={{0,2},{1,3},{2,0},{3,1},{4,6},{5,7},{6,4},{7,5},{8,10},{9,11},{10,... | collective-permute-start | bytes 884744 | tf_op jit(solution)/shard_map/ppermute | solution.py:705
  54.9 28.6 %collective-permute-start.10 = (bf16[192,768]{1,0:T(8,128)(2,1)S(1)}, bf16[192,768]{1,0:T(8,128)(2,1)}, u32[]{:S(2)}, u32[]{:S(2)}) collective-permute-start(bf16[192,768]{1,0:T(8,128)(2,1)S(1)} %collective-permute-done.9), channel_id=1, source_target_pairs={{0,2},{1,3},{2,0},{3,1},{4,6},{5,7},{6,4},{7,5},{8,10},{9,11},{10,... | collective-permute-start | bytes 884744 | tf_op jit(solution)/shard_map/ppermute | solution.py:705
  55.9 31.3 %collective-permute-start.15 = (bf16[256,768]{1,0:T(8,128)(2,1)S(1)}, bf16[256,768]{1,0:T(8,128)(2,1)S(1)}, u32[]{:S(2)}, u32[]{:S(2)}) collective-permute-start(bf16[256,768]{1,0:T(8,128)(2,1)S(1)} %bitcast.128), channel_id=1, source_target_pairs={{0,2},{1,3},{2,0},{3,1},{4,6},{5,7},{6,4},{7,5},{8,10},{9,11},{10,... | collective-permute-start | bytes 1179656 | tf_op jit(solution)/shard_map/ppermute | solution.py:705
  60.6 38.5 %collective-permute-start.12 = (bf16[256,768]{1,0:T(8,128)(2,1)S(1)}, bf16[256,768]{1,0:T(8,128)(2,1)S(1)}, u32[]{:S(2)}, u32[]{:S(2)}) collective-permute-start(bf16[256,768]{1,0:T(8,128)(2,1)S(1)} %bitcast.129), channel_id=1, source_target_pairs={{0,1},{1,0},{2,3},{3,2},{4,5},{5,4},{6,7},{7,6},{8,9},{9,8},{10,11... | collective-permute-start | bytes 1179656 | tf_op jit(solution)/shard_map/ppermute | solution.py:705
  83.4 11.1 %collective-permute-start.14 = (bf16[256,768]{1,0:T(8,128)(2,1)}, bf16[256,768]{1,0:T(8,128)(2,1)S(1)}, u32[]{:S(2)}, u32[]{:S(2)}) collective-permute-start(bf16[256,768]{1,0:T(8,128)(2,1)} %get-tuple-element.66), channel_id=1, source_target_pairs={{0,2},{1,3},{2,0},{3,1},{4,6},{5,7},{6,4},{7,5},{8,10},{9,11},{10,... | collective-permute-start | bytes 1179656 | tf_op jit(solution)/shard_map/ppermute | solution.py:705
  87.2 16.6 %collective-permute-start.17 = (bf16[256,768]{1,0:T(8,128)(2,1)S(1)}, bf16[256,768]{1,0:T(8,128)(2,1)S(1)}, u32[]{:S(2)}, u32[]{:S(2)}) collective-permute-start(bf16[256,768]{1,0:T(8,128)(2,1)S(1)} %collective-permute-done.15), channel_id=1, source_target_pairs={{0,1},{1,0},{2,3},{3,2},{4,5},{5,4},{6,7},{7,6},{8,9},{9,8},{10,11... | collective-permute-start | bytes 1179656 | tf_op jit(solution)/shard_map/ppermute | solution.py:705
  87.9 11.2 %collective-permute-start.11 = (bf16[256,768]{1,0:T(8,128)(2,1)S(1)}, bf16[256,768]{1,0:T(8,128)(2,1)S(1)}, u32[]{:S(2)}, u32[]{:S(2)}) collective-permute-start(bf16[256,768]{1,0:T(8,128)(2,1)S(1)} %copy-done.23), channel_id=1, source_target_pairs={{0,1},{1,0},{2,3},{3,2},{4,5},{5,4},{6,7},{7,6},{8,9},{9,8},{10,11... | collective-permute-start | bytes 1179656 | tf_op jit(solution)/shard_map/ppermute | solution.py:705
  94.4 9.4 %collective-permute-start.16 = (bf16[256,768]{1,0:T(8,128)(2,1)S(1)}, bf16[256,768]{1,0:T(8,128)(2,1)S(1)}, u32[]{:S(2)}, u32[]{:S(2)}) collective-permute-start(bf16[256,768]{1,0:T(8,128)(2,1)S(1)} %collective-permute-done.14), channel_id=1, source_target_pairs={{0,1},{1,0},{2,3},{3,2},{4,5},{5,4},{6,7},{7,6},{8,9},{9,8},{10,11... | collective-permute-start | bytes 1179656 | tf_op jit(solution)/shard_map/ppermute | solution.py:705
  115.1 167.8 %reduce-scatter.3.cloned.1.call-start = ((), (), s32[]{:S(2)}) async-start(), calls=%async_computation.2 | async-start | bytes 1327104 | tf_op jit(solution)/shard_map/reduce_scatter | solution.py:832
  116.5 18.0 %collective-permute-start.20 = (bf16[256,768]{1,0:T(8,128)(2,1)S(1)}, bf16[256,768]{1,0:T(8,128)(2,1)S(1)}, u32[]{:S(2)}, u32[]{:S(2)}) collective-permute-start(bf16[256,768]{1,0:T(8,128)(2,1)S(1)} %bitcast.140), channel_id=1, source_target_pairs={{0,1},{1,0},{2,3},{3,2},{4,5},{5,4},{6,7},{7,6},{8,9},{9,8},{10,11... | collective-permute-start | bytes 1179656 | tf_op jit(solution)/shard_map/ppermute | solution.py:705
  117.0 9.9 %collective-permute-start.24 = (bf16[192,768]{1,0:T(8,128)(2,1)S(1)}, bf16[192,768]{1,0:T(8,128)(2,1)S(1)}, u32[]{:S(2)}, u32[]{:S(2)}) collective-permute-start(bf16[192,768]{1,0:T(8,128)(2,1)S(1)} %get-tuple-element.138), channel_id=1, source_target_pairs={{0,2},{1,3},{2,0},{3,1},{4,6},{5,7},{6,4},{7,5},{8,10},{9,11},{10,... | collective-permute-start | bytes 884744 | tf_op jit(solution)/shard_map/ppermute | solution.py:705
  117.8 9.1 %collective-permute-start.23 = (bf16[192,768]{1,0:T(8,128)(2,1)S(1)}, bf16[192,768]{1,0:T(8,128)(2,1)S(1)}, u32[]{:S(2)}, u32[]{:S(2)}) collective-permute-start(bf16[192,768]{1,0:T(8,128)(2,1)S(1)} %get-tuple-element.139), channel_id=1, source_target_pairs={{0,1},{1,0},{2,3},{3,2},{4,5},{5,4},{6,7},{7,6},{8,9},{9,8},{10,11... | collective-permute-start | bytes 884744 | tf_op jit(solution)/shard_map/ppermute | solution.py:705
  118.1 15.1 %collective-permute-start.26 = (bf16[192,768]{1,0:T(8,128)(2,1)S(1)}, bf16[192,768]{1,0:T(8,128)(2,1)S(1)}, u32[]{:S(2)}, u32[]{:S(2)}) collective-permute-start(bf16[192,768]{1,0:T(8,128)(2,1)S(1)} %collective-permute-done.25), channel_id=1, source_target_pairs={{0,2},{1,3},{2,0},{3,1},{4,6},{5,7},{6,4},{7,5},{8,10},{9,11},{10,... | collective-permute-start | bytes 884744 | tf_op jit(solution)/shard_map/ppermute | solution.py:705
  119.1 21.6 %collective-permute-start.22 = (bf16[256,768]{1,0:T(8,128)(2,1)S(1)}, bf16[256,768]{1,0:T(8,128)(2,1)S(1)}, u32[]{:S(2)}, u32[]{:S(2)}) collective-permute-start(bf16[256,768]{1,0:T(8,128)(2,1)S(1)} %fusion.22), channel_id=1, source_target_pairs={{0,2},{1,3},{2,0},{3,1},{4,6},{5,7},{6,4},{7,5},{8,10},{9,11},{10,... | collective-permute-start | bytes 1179656 | tf_op jit(solution)/shard_map/ppermute | solution.py:705
  134.3 188.5 %all-gather.7.cloned.1.call-start = ((), (), s32[]{:S(2)}) async-start(), calls=%async_computation.5 | async-start | bytes 1327104 | tf_op jit(solution)/shard_map/all_gather | solution.py:871
  197.2 29.3 %collective-permute-start.35 = (bf16[8,208,384]{2,1,0:T(8,128)(2,1)S(1)}, bf16[8,208,384]{2,1,0:T(8,128)(2,1)S(1)}, u32[]{:S(2)}, u32[]{:S(2)}) collective-permute-start(bf16[8,208,384]{2,1,0:T(8,128)(2,1)S(1)} %get-tuple-element.119), channel_id=1, source_target_pairs={{0,1},{1,0},{2,3},{3,2},{4,5},{5,4},{6,7},{7,6},{8,9},{9,8},{10,11... | collective-permute-start | bytes 3833864 | tf_op jit(solution)/shard_map/ppermute | solution.py:705
  198.1 13.5 %collective-permute-start.29 = (bf16[256,768]{1,0:T(8,128)(2,1)S(1)}, bf16[256,768]{1,0:T(8,128)(2,1)S(1)}, u32[]{:S(2)}, u32[]{:S(2)}) collective-permute-start(bf16[256,768]{1,0:T(8,128)(2,1)S(1)} %get-tuple-element.121), channel_id=1, source_target_pairs={{0,4},{4,0},{8,12},{12,8},{16,20},{20,16},{24,28},{28,24},{1,5},{5... | collective-permute-start | bytes 1179656 | tf_op jit(solution)/shard_map/ppermute | solution.py:705
  211.6 14.0 %collective-permute-start.30 = (bf16[256,768]{1,0:T(8,128)(2,1)S(1)}, bf16[256,768]{1,0:T(8,128)(2,1)S(1)}, u32[]{:S(2)}, u32[]{:S(2)}) collective-permute-start(bf16[256,768]{1,0:T(8,128)(2,1)S(1)} %get-tuple-element.93), channel_id=1, source_target_pairs={{0,4},{4,0},{8,12},{12,8},{16,20},{20,16},{24,28},{28,24},{1,5},{5... | collective-permute-start | bytes 1179656 | tf_op jit(solution)/shard_map/ppermute | solution.py:705
  212.2 21.1 %collective-permute-start.27 = (bf16[256,768]{1,0:T(8,128)(2,1)S(1)}, bf16[256,768]{1,0:T(8,128)(2,1)S(1)}, u32[]{:S(2)}, u32[]{:S(2)}) collective-permute-start(bf16[256,768]{1,0:T(8,128)(2,1)S(1)} %get-tuple-element.123), channel_id=1, source_target_pairs={{0,4},{4,0},{8,12},{12,8},{16,20},{20,16},{24,28},{28,24},{1,5},{5... | collective-permute-start | bytes 1179656 | tf_op jit(solution)/shard_map/ppermute | solution.py:705
  213.6 46.4 %collective-permute-start.34 = (bf16[8,208,384]{2,1,0:T(8,128)(2,1)}, bf16[8,208,384]{2,1,0:T(8,128)(2,1)}, u32[]{:S(2)}, u32[]{:S(2)}) collective-permute-start(bf16[8,208,384]{2,1,0:T(8,128)(2,1)} %get-tuple-element.118), channel_id=1, source_target_pairs={{0,1},{1,0},{2,3},{3,2},{4,5},{5,4},{6,7},{7,6},{8,9},{9,8},{10,11... | collective-permute-start | bytes 3833864 | tf_op jit(solution)/shard_map/ppermute | solution.py:705
  226.5 9.2 %collective-permute-start.32 = (bf16[256,768]{1,0:T(8,128)(2,1)S(1)}, bf16[256,768]{1,0:T(8,128)(2,1)S(1)}, u32[]{:S(2)}, u32[]{:S(2)}) collective-permute-start(bf16[256,768]{1,0:T(8,128)(2,1)S(1)} %get-tuple-element.125), channel_id=1, source_target_pairs={{0,8},{4,12},{8,0},{12,4},{16,24},{20,28},{24,16},{28,20},{1,9},{5... | collective-permute-start | bytes 1179656 | tf_op jit(solution)/shard_map/ppermute | solution.py:705
  229.2 30.8 %collective-permute-start.36 = (bf16[8,208,384]{2,1,0:T(8,128)(2,1)}, bf16[8,208,384]{2,1,0:T(8,128)(2,1)}, u32[]{:S(2)}, u32[]{:S(2)}) collective-permute-start(bf16[8,208,384]{2,1,0:T(8,128)(2,1)} %fusion), channel_id=1, source_target_pairs={{0,2},{1,3},{2,0},{3,1},{4,6},{5,7},{6,4},{7,5},{8,10},{9,11},{10,... | collective-permute-start | bytes 3833864 | tf_op jit(solution)/shard_map/ppermute | solution.py:705
  233.2 14.4 %collective-permute-start.28 = (bf16[256,768]{1,0:T(8,128)(2,1)}, bf16[256,768]{1,0:T(8,128)(2,1)}, u32[]{:S(2)}, u32[]{:S(2)}) collective-permute-start(bf16[256,768]{1,0:T(8,128)(2,1)} %get-tuple-element.92), channel_id=1, source_target_pairs={{0,4},{4,0},{8,12},{12,8},{16,20},{20,16},{24,28},{28,24},{1,5},{5... | collective-permute-start | bytes 1179656 | tf_op jit(solution)/shard_map/ppermute | solution.py:705
  233.5 23.8 %collective-permute-start.31 = (bf16[256,768]{1,0:T(8,128)(2,1)}, bf16[256,768]{1,0:T(8,128)(2,1)}, u32[]{:S(2)}, u32[]{:S(2)}) collective-permute-start(bf16[256,768]{1,0:T(8,128)(2,1)} %get-tuple-element.124), channel_id=1, source_target_pairs={{0,8},{4,12},{8,0},{12,4},{16,24},{20,28},{24,16},{28,20},{1,9},{5... | collective-permute-start | bytes 1179656 | tf_op jit(solution)/shard_map/ppermute | solution.py:705
  236.7 20.6 %collective-permute-start.33 = (bf16[256,768]{1,0:T(8,128)(2,1)}, bf16[256,768]{1,0:T(8,128)(2,1)}, u32[]{:S(2)}, u32[]{:S(2)}) collective-permute-start(bf16[256,768]{1,0:T(8,128)(2,1)} %add_convert_fusion), channel_id=1, source_target_pairs={{0,16},{4,20},{8,24},{12,28},{16,0},{20,4},{24,8},{28,12},{1,17},{... | collective-permute-start | bytes 1179656 | tf_op jit(solution)/shard_map/ppermute | solution.py:705
  247.3 100.0 %all-gather.5.cloned.1.call-start = ((), (), s32[]{:S(2)}) async-start(), calls=%async_computation.3 | async-start | bytes 1327104 | tf_op jit(solution)/shard_map/all_gather | solution.py:872
  263.4 6.7 %collective-permute-start.39 = (bf16[208,384]{1,0:T(8,128)(2,1)S(1)}, bf16[208,384]{1,0:T(8,128)(2,1)S(1)}, u32[]{:S(2)}, u32[]{:S(2)}) collective-permute-start(bf16[208,384]{1,0:T(8,128)(2,1)S(1)} %get-tuple-element.127), channel_id=1, source_target_pairs={{0,4},{4,0},{8,12},{12,8},{16,20},{20,16},{24,28},{28,24},{1,5},{5... | collective-permute-start | bytes 479240 | tf_op jit(solution)/shard_map/ppermute | solution.py:705
  273.8 14.2 %collective-permute-start.18 = (bf16[256,768]{1,0:T(8,128)(2,1)}, bf16[256,768]{1,0:T(8,128)(2,1)}, u32[]{:S(2)}, u32[]{:S(2)}) collective-permute-start(bf16[256,768]{1,0:T(8,128)(2,1)} %convolution_convert_fusion), channel_id=1, source_target_pairs={{0,1},{1,0},{2,3},{3,2},{4,5},{5,4},{6,7},{7,6},{8,9},{9,8},{10,11... | collective-permute-start | bytes 1179656 | tf_op jit(solution)/shard_map/ppermute | solution.py:705
  273.8 9.1 %collective-permute-start.37 = (bf16[208,384]{1,0:T(8,128)(2,1)}, bf16[208,384]{1,0:T(8,128)(2,1)S(1)}, u32[]{:S(2)}, u32[]{:S(2)}) collective-permute-start(bf16[208,384]{1,0:T(8,128)(2,1)} %get-tuple-element.129), channel_id=1, source_target_pairs={{0,4},{4,0},{8,12},{12,8},{16,20},{20,16},{24,28},{28,24},{1,5},{5... | collective-permute-start | bytes 479240 | tf_op jit(solution)/shard_map/ppermute | solution.py:705
  276.6 8.9 %collective-permute-start.42 = (bf16[208,384]{1,0:T(8,128)(2,1)}, bf16[208,384]{1,0:T(8,128)(2,1)S(1)}, u32[]{:S(2)}, u32[]{:S(2)}) collective-permute-start(bf16[208,384]{1,0:T(8,128)(2,1)} %get-tuple-element.131), channel_id=1, source_target_pairs={{0,8},{4,12},{8,0},{12,4},{16,24},{20,28},{24,16},{28,20},{1,9},{5... | collective-permute-start | bytes 479240 | tf_op jit(solution)/shard_map/ppermute | solution.py:705
  282.9 27.4 %collective-permute-start.13 = (bf16[256,768]{1,0:T(8,128)(2,1)}, bf16[256,768]{1,0:T(8,128)(2,1)}, u32[]{:S(2)}, u32[]{:S(2)}) collective-permute-start(bf16[256,768]{1,0:T(8,128)(2,1)} %convolution_convert_fusion.2), channel_id=1, source_target_pairs={{0,1},{1,0},{2,3},{3,2},{4,5},{5,4},{6,7},{7,6},{8,9},{9,8},{10,11... | collective-permute-start | bytes 1179656 | tf_op jit(solution)/shard_map/ppermute | solution.py:705
  282.9 9.6 %collective-permute-start.38 = (bf16[208,384]{1,0:T(8,128)(2,1)S(1)}, bf16[208,384]{1,0:T(8,128)(2,1)S(1)}, u32[]{:S(2)}, u32[]{:S(2)}) collective-permute-start(bf16[208,384]{1,0:T(8,128)(2,1)S(1)} %get-tuple-element.102), channel_id=1, source_target_pairs={{0,4},{4,0},{8,12},{12,8},{16,20},{20,16},{24,28},{28,24},{1,5},{5... | collective-permute-start | bytes 479240 | tf_op jit(solution)/shard_map/ppermute | solution.py:705
  283.6 16.6 %collective-permute-start.41 = (bf16[208,384]{1,0:T(8,128)(2,1)}, bf16[208,384]{1,0:T(8,128)(2,1)S(1)}, u32[]{:S(2)}, u32[]{:S(2)}) collective-permute-start(bf16[208,384]{1,0:T(8,128)(2,1)} %get-tuple-element.130), channel_id=1, source_target_pairs={{0,8},{4,12},{8,0},{12,4},{16,24},{20,28},{24,16},{28,20},{1,9},{5... | collective-permute-start | bytes 479240 | tf_op jit(solution)/shard_map/ppermute | solution.py:705
  285.6 14.5 %collective-permute-start.43 = (bf16[208,384]{1,0:T(8,128)(2,1)S(1)}, bf16[208,384]{1,0:T(8,128)(2,1)S(1)}, u32[]{:S(2)}, u32[]{:S(2)}) collective-permute-start(bf16[208,384]{1,0:T(8,128)(2,1)S(1)} %add_convert_fusion.4), channel_id=1, source_target_pairs={{0,16},{4,20},{8,24},{12,28},{16,0},{20,4},{24,8},{28,12},{1,17},{... | collective-permute-start | bytes 479240 | tf_op jit(solution)/shard_map/ppermute | solution.py:705
  290.4 19.9 %collective-permute-start.19 = (bf16[256,768]{1,0:T(8,128)(2,1)}, bf16[256,768]{1,0:T(8,128)(2,1)}, u32[]{:S(2)}, u32[]{:S(2)}) collective-permute-start(bf16[256,768]{1,0:T(8,128)(2,1)} %fusion.7), channel_id=1, source_target_pairs={{0,2},{1,3},{2,0},{3,1},{4,6},{5,7},{6,4},{7,5},{8,10},{9,11},{10,... | collective-permute-start | bytes 1179656 | tf_op jit(solution)/shard_map/ppermute | solution.py:705
  301.8 7.3 %collective-permute-start.45 = (bf16[208,384]{1,0:T(8,128)(2,1)S(1)}, bf16[208,384]{1,0:T(8,128)(2,1)S(1)}, u32[]{:S(2)}, u32[]{:S(2)}) collective-permute-start(bf16[208,384]{1,0:T(8,128)(2,1)S(1)} %fusion.39.refs_1_), channel_id=1, source_target_pairs={{0,8},{4,12},{8,0},{12,4},{16,24},{20,28},{24,16},{28,20},{1,9},{5... | collective-permute-start | bytes 479240 | tf_op jit(solution)/shard_map/ppermute | solution.py:705
  304.2 9.1 %collective-permute-start.47 = (bf16[208,384]{1,0:T(8,128)(2,1)S(1)}, bf16[208,384]{1,0:T(8,128)(2,1)S(1)}, u32[]{:S(2)}, u32[]{:S(2)}) collective-permute-start(bf16[208,384]{1,0:T(8,128)(2,1)S(1)} %fusion.39.refs_1_), channel_id=1, source_target_pairs={{0,16},{4,20},{8,24},{12,28},{16,0},{20,4},{24,8},{28,12},{1,17},{... | collective-permute-start | bytes 479240 | tf_op jit(solution)/shard_map/ppermute | solution.py:705
  (45 other events, 416.4 us)
Sparse Core Ops, SparseCore 0:
  11.4 42.3 all-gather.8
  115.2 65.2 reduce-scatter.4
  184.0 71.5 reduce-scatter.2
  257.5 47.1 all-gather.6
  306.8 40.4 all-gather.4

commit v4 on v2

--- a/solution.py
+++ b/solution.py
@@ -126,6 +126,10 @@
     return pl.BlockSpec(memory_space=ANY)
 
 
+def cost(us):
+    return pl.CostEstimate(flops=int(us * 1.0e9), bytes_accessed=int(us * 1.0e6), transcendentals=0)
+
+
 def load_pieces(pieces, target_ref, flip, sem):
     copies = []
     rows = target_ref.shape[0] // len(pieces)
@@ -152,8 +156,8 @@
     ids_ref, order_ref, len_ref, tab_ref, table_t_ref, gain_ref = refs[:6]
     x_refs, w_refs = refs[6 : 6 + n_x], refs[6 + n_x : 6 + n_x + n_w]
     (
-        nf_ref, res_ref, o_ref, ot_ref, lse_ref, q_ref, k_ref, v_ref, xn_ref,
-        inv_ref, x_ref, w_ref, rhs_ref, near_ref, s_ref, m_ref, l_ref, acc_ref, sem_x, sem_w,
+        nf_ref, res_ref, o_ref, ot_ref, lse_ref, q_ref, k_out_ref, v_out_ref,
+        inv_ref, x_ref, w_ref, k_ref, v_ref, rhs_ref, near_ref, m_ref, l_ref, acc_ref, sem_x, sem_w, sem_k, sem_v,
     ) = refs[6 + n_x + n_w :]
     spans, own = order_ref.shape[1], q_ref.shape[0] // SPAN
     b1 = len_ref[0, 0]
@@ -175,13 +179,22 @@
     my_spans = [order_ref[0, ids_ref[0] * own + i] for i in range(own)]
     my_ranges = [key_range(span, b1, b2, b3, spans * SPAN) for span in my_spans]
 
-    def project(t, carry):
+    def chunk_copies(t):
+        rows = pl.ds(pl.multiple_of(t * 256, 256), 256)
+        return (
+            pltpu.make_async_copy(k_ref.at[rows], k_out_ref.at[rows], sem_k.at[t]),
+            pltpu.make_async_copy(v_ref.at[rows], v_out_ref.at[rows], sem_v.at[t]),
+        )
+
+    def if_needed(t, body):
         needed = jnp.bool_(False)
         for low, high in my_ranges:
             needed = needed | ((t >= low) & (t < high))
-        rows = pl.ds(pl.multiple_of(t * 256, 256), 256)
-
+        pl.when(needed)(body)
+
+    def project(t, carry):
         def fill():
+            rows = pl.ds(pl.multiple_of(t * 256, 256), 256)
             parts = []
             for half in range(2):
                 slot = inv_ref[2 * t + half]
@@ -189,15 +202,12 @@
                 start = pl.multiple_of(piece * own_rows + (slot % own) * SPAN, SPAN)
                 parts.append(x_ref[pl.ds(start, SPAN), :])
             xn = normed(jnp.concatenate(parts, axis=0))
-            xn_ref[rows, :] = xn
             k_ref[rows, :] = dot(xn, w_ref[:, D : 2 * D]).astype(jnp.bfloat16)
             v_ref[rows, :] = dot(xn, w_ref[:, 2 * D : 3 * D]).astype(jnp.bfloat16)
-
-        def skip():
-            xn_ref[rows, :] = jnp.zeros((256, D), jnp.bfloat16)
-
-        pl.when(needed)(fill)
-        pl.when(jnp.logical_not(needed))(skip)
+            for copy in chunk_copies(t):
+                copy.start()
+
+        if_needed(t, fill)
         return carry
 
     lax.fori_loop(0, spans // 2, project, 0)
@@ -220,27 +230,40 @@
         def chunk_body(t, near):
             rows = pl.ds(pl.multiple_of(t * 256, 256), 256)
             feat = key_features(t, span, b1, b2, b3)
-            scales, tops = [], []
-            for p in range(PAIRS):
-                kp = k_ref[rows, p * 128 : p * 128 + 128]
-                s = dot(jnp.concatenate([kp, feat], axis=1), rhs_ref[p])
+
+            def scores(p):
+                s = dot(jnp.concatenate([k_ref[rows, p * 128 : p * 128 + 128], feat], axis=1), rhs_ref[p])
                 if near:
                     n0, n1 = near_index(2 * t - span), near_index(2 * t + 1 - span)
                     s = s + jnp.concatenate([near_ref[n0, p], near_ref[n1, p]], axis=0)
-                s_ref[p] = s
+                return s
+
+            def top(p, s):
                 old = m_ref[p]
                 new = jnp.maximum(old, jnp.max(s, axis=0, keepdims=True))
                 m_ref[p] = new
-                scales.append(jnp.exp(old - new))
-                tops.append(new)
-            for p in range(PAIRS):
-                scale = scales[p]
-                e = jnp.exp(s_ref[p] - tops[p])
+                return new, jnp.exp(old - new)
+
+            def weigh(p, s, new, scale):
+                e = jnp.exp(s - new)
                 l_ref[p] = l_ref[p] * scale + jnp.sum(e, axis=0, keepdims=True)
-                vp = v_ref[rows, p * 128 : p * 128 + 128]
-                o = dot(vp, e.astype(jnp.bfloat16), 0, 0)
+                return e.astype(jnp.bfloat16)
+
+            def attend(p, e, scale):
+                o = dot(v_ref[rows, p * 128 : p * 128 + 128], e, 0, 0)
                 acc_ref[p, 0:64, :] = acc_ref[p, 0:64, :] * scale[:, 0:128] + o[0:64, 0:128]
                 acc_ref[p, 64:128, :] = acc_ref[p, 64:128, :] * scale[:, 128:256] + o[64:128, 128:256]
+
+            ss, tops, es = {}, {}, {}
+            for p in range(PAIRS + 3):
+                if p < PAIRS:
+                    ss[p] = scores(p)
+                if 1 <= p <= PAIRS:
+                    tops[p - 1] = top(p - 1, ss[p - 1])
+                if 2 <= p <= PAIRS + 1:
+                    es[p - 2] = weigh(p - 2, ss[p - 2], *tops[p - 2])
+                if p >= 3:
+                    attend(p - 3, es[p - 3], tops[p - 3][1])
 
         def step(t, carry):
             near = (2 * t + 2 >= span) & (2 * t <= span + 1)
@@ -266,6 +289,16 @@
     inv_rms = lax.rsqrt(jnp.mean(res * res, axis=1, keepdims=True) + EPS)
     nf_ref[...] = (res * inv_rms * gain_ref[1:2, :]).astype(jnp.bfloat16)
 
+    def settle(t, carry):
+        def wait():
+            for copy in chunk_copies(t):
+                copy.wait()
+
+        if_needed(t, wait)
+        return carry
+
+    lax.fori_loop(0, spans // 2, settle, 0)
+
 
 def forward(ids, order, lengths, table, table_t, gains, xs, ws, local_rows):
     spans, own = order.shape[1], local_rows // SPAN
@@ -275,6 +308,7 @@
     return pl.pallas_call(
         lambda *refs: forward_kernel((len(xs), len(ws)), *refs),
         name="forward",
+        cost_estimate=cost(22),
         out_shape=(
             jax.ShapeDtypeStruct((local_rows, D), bf),
             jax.ShapeDtypeStruct((local_rows, D), f32),
@@ -284,84 +318,243 @@
             jax.ShapeDtypeStruct((local_rows, D), bf),
             jax.ShapeDtypeStruct((rows, D), bf),
             jax.ShapeDtypeStruct((rows, D), bf),
-            jax.ShapeDtypeStruct((rows, D), bf),
         ),
         in_specs=[smem()] * 4 + [vmem()] * 2 + [hbm()] * (len(xs) + len(ws)),
-        out_specs=(vmem(),) * 9,
+        out_specs=(vmem(),) * 6 + (hbm(),) * 2,
         scratch_shapes=[
             pltpu.SMEM((spans,), jnp.int32),
             pltpu.VMEM((rows, D), bf),
             pltpu.VMEM((D, 4 * D), bf),
+            pltpu.VMEM((rows, D), bf),
+            pltpu.VMEM((rows, D), bf),
             pltpu.VMEM((PAIRS, 256, 256), bf),
             pltpu.VMEM((4, PAIRS, 128, 256), f32),
-            pltpu.VMEM((PAIRS, 256, 256), f32),
             pltpu.VMEM((PAIRS, 1, 256), f32),
             pltpu.VMEM((PAIRS, 1, 256), f32),
             pltpu.VMEM((PAIRS, 128, 128), f32),
             pltpu.SemaphoreType.DMA((n_x,)),
             pltpu.SemaphoreType.DMA((n_w,)),
+            pltpu.SemaphoreType.DMA((spans // 2,)),
+            pltpu.SemaphoreType.DMA((spans // 2,)),
         ],
         compiler_params=pltpu.CompilerParams(vmem_limit_bytes=VMEM_LIMIT),
     )(ids, order, lengths, table, table_t, gains, *xs, *ws)
 
 
 def ffn_kernel(counts, *refs):
-    n_t, n_w = counts
-    ids_ref = refs[0]
-    nf_refs, cot_refs = refs[1 : 1 + n_t], refs[1 + n_t : 1 + 2 * n_t]
-    win_refs = refs[1 + 2 * n_t : 1 + 2 * n_t + n_w]
-    wffn_ref, act_ref, dup_ref, dn_ref, w_ref, sem_w = refs[1 + 2 * n_t + n_w :]
-    copies = load_pieces(expand(win_refs), w_ref, ids_ref[2], sem_w)
-    for copy in copies:
+    count, n_w = counts
+    ids_ref, refs = refs[0], refs[1:]
+    nfs, cots, wins = refs[:count], refs[count : 2 * count], refs[2 * count : 2 * count + n_w]
+    wffn_ref, act_ref, dup_ref = refs[2 * count + n_w : 2 * count + n_w + 3]
+    refs = refs[2 * count + n_w + 3 :]
+    dns, outs, (w_ref, sem) = refs[:count], refs[count : 2 * count], refs[2 * count :]
+    done = 0
+    for copy in load_pieces(expand(wins), w_ref, ids_ref[3], sem):
         copy.wait()
-    start = 0
-    for nf_ref, cot_ref in zip(nf_refs, cot_refs):
+    for nf_ref, cot_ref, dn_ref, out_ref in zip(nfs, cots, dns, outs):
         for piece in range(nf_ref.shape[0]):
-            rows = slice(start, start + nf_ref.shape[1])
             up = dot(nf_ref[piece], w_ref[...])
+            d_act = dot(cot_ref[piece], wffn_ref[...], 1, 1)
             square = up * up
             th = jnp.tanh(GELU_C * (up + 0.044715 * square * up))
             half = 0.5 * (1.0 + th)
-            act_ref[rows, :] = (up * half).astype(jnp.bfloat16)
+            act = (up * half).astype(jnp.bfloat16)
+            act_ref[done] = act
             slope = half + 0.5 * up * (1.0 - th * th) * (GELU_C * (1.0 + 3 * 0.044715 * square))
-            d_up = (dot(cot_ref[piece], wffn_ref[...], 1, 1) * slope).astype(jnp.bfloat16)
-            dup_ref[rows, :] = d_up
-            dn_ref[rows, :] = dot(d_up, w_ref[...], 1, 1).astype(jnp.bfloat16)
-            start += nf_ref.shape[1]
+            d_up = (d_act * slope).astype(jnp.bfloat16)
+            dup_ref[done] = d_up
+            dn_ref[piece] = dot(d_up, w_ref[...], 1, 1).astype(jnp.bfloat16)
+            out_ref[piece] = dot(act, wffn_ref[...]).astype(jnp.bfloat16)
+            done += 1
 
 
 def ffn(ids, nfs, cots, wins, wffn):
-    rows = sum(x.shape[0] * x.shape[1] for x in nfs)
+    total, rows, count = sum(n.shape[0] for n in nfs), nfs[0].shape[1], len(nfs)
     width = wffn.shape[0]
-    n_w = sum(w.shape[0] for w in wins)
     bf = jnp.bfloat16
-    return pl.pallas_call(
-        lambda *refs: ffn_kernel((len(nfs), len(wins)), *refs),
+    act, dup, *rest = pl.pallas_call(
+        lambda *refs: ffn_kernel((count, len(wins)), *refs),
         name="ffn",
-        out_shape=(
-            jax.ShapeDtypeStruct((rows, width), bf),
-            jax.ShapeDtypeStruct((rows, width), bf),
-            jax.ShapeDtypeStruct((rows, D), bf),
-        ),
-        in_specs=[smem()] + [vmem()] * (2 * len(nfs)) + [hbm()] * len(wins) + [vmem()],
-        out_specs=(vmem(),) * 3,
-        scratch_shapes=[pltpu.VMEM((D, width), bf), pltpu.SemaphoreType.DMA((n_w,))],
+        cost_estimate=cost(6),
+        out_shape=(jax.ShapeDtypeStruct((total, rows, width), bf),) * 2
+        + tuple(jax.ShapeDtypeStruct((n.shape[0], rows, D), bf) for n in nfs) * 2,
+        in_specs=[smem()] + [vmem()] * (2 * count) + [hbm()] * len(wins) + [vmem()],
+        out_specs=(vmem(),) * (2 + 2 * count),
+        scratch_shapes=[
+            pltpu.VMEM((D, width), bf),
+            pltpu.SemaphoreType.DMA((sum(w.shape[0] for w in wins),)),
+        ],
         compiler_params=pltpu.CompilerParams(vmem_limit_bytes=VMEM_LIMIT),
     )(ids, *nfs, *cots, *wins, wffn)
+    return act, dup, rest[:count], rest[count:]
+
+
+def by_turn(turn, refs, body):
+    for number, ref in enumerate(refs):
+        pl.when(turn == number)(lambda ref=ref: body(ref))
+
+
+def ffn_grads_kernel(counts, parts, *refs):
+    n, m = counts
+    ids_ref = refs[0]
+    groups, start = [], 1
+    for count in (n, n, m, m):
+        groups.append(refs[start : start + count])
+        start += count
+    nfs, cots, acts, dups = groups
+    outs = refs[start:]
+
+    def joined(pieces):
+        flat = [ref[...].reshape(-1, ref.shape[2]) for ref in pieces]
+        return flat[0] if len(flat) == 1 else jnp.concatenate(flat, axis=0)
+
+    g_out = dot(joined(acts), joined(cots), 0, 0).astype(jnp.bfloat16)
+    g_in = dot(joined(nfs), joined(dups), 0, 0).astype(jnp.bfloat16)
+    if parts == 1:
+        outs[0][...] = g_out
+        size = outs[1].shape[1]
+        for i in range(outs[1].shape[0]):
+            outs[1][i] = g_in[i * size : (i + 1) * size]
+        return
+    out_ref, gin_ref = outs
+    gin_ref[...] = g_in
+    rows = D // parts
+    for part in range(parts):
+        out_ref[part, 0:rows, :] = g_out[part * rows : (part + 1) * rows]
+        side = slice((part % 2) * 384, (part % 2) * 384 + 384)
+        for place in range(4):
+            owner = lax.bitwise_xor(jnp.int32(place), ids_ref[3])
+            down = pl.ds(pl.multiple_of(owner * 192 + (part // 2) * 48, 16), 48)
+            first, left = rows + (place // 2) * 48, (place % 2) * 384
+            out_ref[part, first : first + 48, left : left + 384] = gin_ref[down, side]
+
+
+def ffn_grads(ids, nfs, cots, acts, dups, n_fsdp, parts):
+    width = acts[0].shape[2]
+    bf = jnp.bfloat16
+    if parts == 1:
+        shapes = (jax.ShapeDtypeStruct((width, D), bf), jax.ShapeDtypeStruct((n_fsdp, D // n_fsdp, width), bf))
+    else:
+        shapes = (jax.ShapeDtypeStruct((parts, 2 * D // parts, D), bf),)
+    scratch = [] if parts == 1 else [pltpu.VMEM((D, width), bf)]
+    return pl.pallas_call(
+        lambda *refs: ffn_grads_kernel((len(nfs), len(acts)), parts, *refs),
+        name="ffn_grads",
+        cost_estimate=cost(6),
+        out_shape=shapes,
+        in_specs=[smem()] + [vmem()] * (2 * len(nfs) + 2 * len(acts)),
+        out_specs=(vmem(),) * len(shapes),
+        scratch_shapes=scratch,
+        compiler_params=pltpu.CompilerParams(vmem_limit_bytes=VMEM_LIMIT),
+    )(ids, *nfs, *cots, *acts, *dups)
+
+
+def fetch_turns(pieces, all_ref, flip, sem):
+    copies = []
+    for number, (ref, index, turn) in enumerate(pieces):
+        place = lax.bitwise_xor(jnp.int32(turn), flip)
+        copies.append(pltpu.make_async_copy(ref.at[index], all_ref.at[place], sem.at[number]))
+    for copy in copies:
+        copy.start()
+    for copy in copies:
+        copy.wait()
+
+
+def with_turns(refs, turns):
+    return [(ref, index, turn) for ref, group in zip(refs, turns) for index, turn in enumerate(group)]
+
+
+def finish_ffn_kernel(turns, *refs):
+    count = len(turns)
+    ids_ref = refs[0]
+    gout_ref, gin_ref, all_ref, sem = refs[1 + count :]
+    fetch_turns(with_turns(refs[1 : 1 + count], turns), all_ref, ids_ref[1], sem)
+    rows = all_ref.shape[1] // 2
+    for p in range(all_ref.shape[0]):
+        gout_ref[p * rows : (p + 1) * rows, :] = all_ref[p, 0:rows, :].astype(jnp.float32)
+        for i in range(4):
+            place = lax.bitwise_xor(jnp.int32(i), ids_ref[3])
+            down = pl.ds(pl.multiple_of(rows + (place // 2) * 48, 16), 48)
+            side = pl.ds(pl.multiple_of((place % 2) * 384, 128), 384)
+            first = i * D + (p % 2) * 384
+            gin_ref[(p // 2) * 48 : (p // 2) * 48 + 48, first : first + 384] = all_ref[p, down, side].astype(jnp.float32)
+
+
+def finish_ffn(ids, arrays, turns):
+    f32 = jnp.float32
+    count = sum(a.shape[0] for a in arrays)
+    return pl.pallas_call(
+        lambda *refs: finish_ffn_kernel(turns, *refs),
+        name="finish_ffn",
+        cost_estimate=cost(4),
+        out_shape=(jax.ShapeDtypeStruct((D, D), f32), jax.ShapeDtypeStruct((D // 4, 4 * D), f32)),
+        in_specs=[smem()] + [hbm()] * len(arrays),
+        out_specs=(vmem(),) * 2,
+        scratch_shapes=[pltpu.VMEM((count, *arrays[0].shape[1:]), jnp.bfloat16), pltpu.SemaphoreType.DMA((count,))],
+        compiler_params=pltpu.CompilerParams(vmem_limit_bytes=VMEM_LIMIT),
+    )(ids, *arrays)
+
+
+def put_grads(outs, all_ref, size, part_flip, fsdp_flip):
+    n, parts, wide = sum(ref.shape[0] for ref in outs), outs[0].shape[1], outs[0].shape[3]
+    for turn in range(n):
+        owner = lax.bitwise_xor(jnp.int32(turn), fsdp_flip)
+        rows = pl.ds(pl.multiple_of(owner * size, 16), size)
+        for part in range(parts):
+            source = lax.bitwise_xor(jnp.int32(part), part_flip)
+            columns = pl.ds(pl.multiple_of(source * wide, 128), wide)
+            outs[turn % len(outs)][turn // len(outs), part, 0:size, :] = all_ref[rows, columns].astype(jnp.bfloat16)
+
+
+def grad_shapes(n, parts):
+    high, wide = D // n + 16, 2 * D // parts
+    if parts == 1:
+        return (jax.ShapeDtypeStruct((n, parts, high, wide), jnp.bfloat16),)
+    return (jax.ShapeDtypeStruct((n // 2, parts, high, wide), jnp.bfloat16),) * 2
+
+
+def finish_kernel(turns, *refs):
+    count = len(turns)
+    ids_ref = refs[0]
+    outs, tiny_ref, all_ref, sem = refs[1 + count : 5 + count], refs[5 + count], refs[6 + count], refs[7 + count]
+    fetch_turns(with_turns(refs[1 : 1 + count], turns), all_ref, ids_ref[1], sem)
+    size, wide = outs[0].shape[0], all_ref.shape[2]
+    step = min(D, wide)
+    for first in range(0, 4 * D, step):
+        value = all_ref[first // wide, :, first % wide : first % wide + step].astype(jnp.float32)
+        outs[first // D][:, first % D : first % D + step] = value[0:size]
+        tiny_ref[:, first : first + step] = value[size : size + 16]
+
+
+def finish(ids, arrays, turns):
+    count, high, wide = sum(a.shape[0] for a in arrays), *arrays[0].shape[1:]
+    f32 = jnp.float32
+    return pl.pallas_call(
+        lambda *refs: finish_kernel(turns, *refs),
+        name="finish",
+        cost_estimate=cost(3),
+        out_shape=(jax.ShapeDtypeStruct((high - 16, D), f32),) * 4 + (jax.ShapeDtypeStruct((16, 4 * D), f32),),
+        in_specs=[smem()] + [hbm()] * len(arrays),
+        out_specs=(vmem(),) * 5,
+        scratch_shapes=[pltpu.VMEM((count, high, wide), jnp.bfloat16), pltpu.SemaphoreType.DMA((count,))],
+        compiler_params=pltpu.CompilerParams(vmem_limit_bytes=VMEM_LIMIT),
+    )(ids, *arrays)
 
 
 def backward_kernel(counts, *refs):
-    n_x, n_w = counts
+    n_x, n_w, n_dn, n_grad = counts
     (
         ids_ref, order_ref, len_ref, tab_ref, table_t_ref, gain_ref,
         dnf_ref, res_ref, cot_ref, o_ref, ot_ref, lse_ref, q_ref, k_ref, v_ref,
     ) = refs[:15]
     x_refs, w_refs = refs[15 : 15 + n_x], refs[15 + n_x : 15 + n_x + n_w]
+    refs = refs[15 + n_x + n_w :]
+    dn_refs, mine_refs, shared_refs = refs[:n_dn], refs[n_dn : n_dn + n_grad], refs[n_dn + n_grad : n_dn + 2 * n_grad]
     (
-        dres_ref, dlow_ref, dq_ref, dk_ref, dv_ref, dn_ref, dn_own_ref, dgain_ref, dtab_ref,
-        inv_ref, x_ref, w_ref, do_ref, rhs_ref, dorhs_ref, qbd_ref, dobd_ref, near_ref, nacc_ref, acc_ref, far_ref,
-        dkacc_ref, dvacc_ref, sem_x, sem_w,
-    ) = refs[15 + n_x + n_w :]
+        dres_ref, dn_own_ref,
+        dlow_ref, dq_ref, dgain_ref, own_ref, all_ref, inv_ref, x_ref, w_ref, do_ref, rhs_ref, dorhs_ref, qbd_ref, dobd_ref, near_ref, nacc_ref, acc_ref, far_ref,
+        dkacc_ref, dvacc_ref, kt_ref, sem_x, sem_w,
+    ) = refs[n_dn + 2 * n_grad :]
     spans, own = order_ref.shape[1], q_ref.shape[0] // SPAN
     own_rows = own * SPAN
     b1 = len_ref[0, 0]
@@ -391,6 +584,8 @@
         for copy in copies_w:
             copy.wait()
         do_ref[...] = dot(dlow, w_ref[:, 3 * D : 4 * D], 1, 1).astype(jnp.bfloat16)
+        own_ref[:, D : 2 * D] = dot(o_ref[...], dlow, 0, 0)
+        all_ref[...] = jnp.zeros_like(all_ref)
 
         def prepare(i, carry):
             span = order_ref[0, ids_ref[0] * own + i]
@@ -428,28 +623,47 @@
 
     dkacc_ref[...] = jnp.zeros_like(dkacc_ref)
     dvacc_ref[...] = jnp.zeros_like(dvacc_ref)
+    for p in range(PAIRS):
+        kt_ref[p, 0:128, :] = k_ref[:, p * 128 : p * 128 + 128].T
 
     def span_body(i, span, near):
         feat = key_features(t, span, b1, b2, b3)
         for p in range(PAIRS):
+            kt_ref[p, 128:144, :] = feat.T[0:16]
+
+        def first(p):
             cols = slice(p * 128, p * 128 + 128)
-            kf = jnp.concatenate([k_ref[:, cols], feat], axis=1)
-            s = dot(kf, rhs_ref[i, p])
+            return (
+                dot(jnp.concatenate([k_ref[:, cols], feat], axis=1), rhs_ref[i, p]),
+                dot(jnp.concatenate([v_ref[:, cols], feat], axis=1), dorhs_ref[i, p]),
+            )
+
+        def last(p, prob, ds):
+            cols = slice(p * 128, p * 128 + 128)
+            dvacc_ref[:, cols] += dot(prob, dobd_ref[i, p])
+            dkacc_ref[:, cols] += dot(ds, qbd_ref[i, p])
+            dq = dot(kt_ref[p], ds)
+            acc_ref[i, p, 0:64, :] += dq[0:64, 0:128]
+            acc_ref[i, p, 64:128, :] += dq[64:128, 128:256]
+            far_ref[p] += dq[128:136, :]
+
+        ahead, waiting = first(0), None
+        for p in range(PAIRS):
+            s, dp = ahead
+            if p + 1 < PAIRS:
+                ahead = first(p + 1)
             if near:
                 n0, n1 = near_index(2 * t - span), near_index(2 * t + 1 - span)
                 s = s + jnp.concatenate([near_ref[n0, p], near_ref[n1, p]], axis=0)
             prob = jnp.exp(s)
-            ds = prob * dot(jnp.concatenate([v_ref[:, cols], feat], axis=1), dorhs_ref[i, p])
+            ds = prob * dp
             if near:
                 nacc_ref[n0, p] += ds[0:128]
                 nacc_ref[n1, p] += ds[128:256]
-            dsb = ds.astype(jnp.bfloat16)
-            dvacc_ref[:, cols] += dot(prob.astype(jnp.bfloat16), dobd_ref[i, p])
-            dkacc_ref[:, cols] += dot(dsb, qbd_ref[i, p])
-            dq = dot(kf, dsb, 0, 0)
-            acc_ref[i, p, 0:64, :] += dq[0:64, 0:128]
-            acc_ref[i, p, 64:128, :] += dq[64:128, 128:256]
-            far_ref[p] += dq[128:136, :]
+            if waiting is not None:
+                last(*waiting)
+            waiting = (p, prob.astype(jnp.bfloat16), ds.astype(jnp.bfloat16))
+        last(*waiting)
 
     def one_span(i, used):
         span = order_ref[0, ids_ref[0] * own + i]
@@ -461,29 +675,41 @@
         return used + needed.astype(jnp.int32)
 
     used = lax.fori_loop(0, own, one_span, jnp.int32(0))
-    places = []
+    places, targets = [], []
     for half in range(2):
         slot = inv_ref[2 * t + half]
         piece = lax.bitwise_xor(slot // own, ids_ref[1])
-        places.append(pl.ds(pl.multiple_of(piece * own_rows + (slot % own) * SPAN, SPAN), SPAN))
+        inside = (slot % own) * SPAN
+        places.append(pl.ds(pl.multiple_of(piece * own_rows + inside, SPAN), SPAN))
+        targets.append((piece, inside))
+
+    def store(half, value):
+        piece, inside = targets[half]
+
+        def put(ref, index):
+            ref[pl.ds(pl.multiple_of(index * own_rows + inside, SPAN), SPAN), :] = value
+
+        if n_dn == 1:
+            put(dn_refs[0], piece)
+        else:
+            by_turn(piece, dn_refs, lambda ref: put(ref, 0))
 
     def fill():
         dkb, dvb = dkacc_ref[...].astype(jnp.bfloat16), dvacc_ref[...].astype(jnp.bfloat16)
-        dk_ref[...] = dkb
-        dv_ref[...] = dvb
         part = dot(dkb, w_ref[:, D : 2 * D], 1, 1) + dot(dvb, w_ref[:, 2 * D : 3 * D], 1, 1)
-        x = jnp.concatenate([x_ref[places[0], :], x_ref[places[1], :]], axis=0)
-        dgain_ref[0:1, :] += jnp.sum(part * unit(x), axis=0, keepdims=True)
+        x = unit(jnp.concatenate([x_ref[places[0], :], x_ref[places[1], :]], axis=0))
+        dgain_ref[0:1, :] += jnp.sum(part * x, axis=0, keepdims=True)
+        turned = (x * gain_ref[0:1, :]).astype(jnp.bfloat16).T
+        all_ref[:, 0:D] += dot(turned, dkb)
+        all_ref[:, D : 2 * D] += dot(turned, dvb)
         part = part.astype(jnp.bfloat16)
-        dn_ref[places[0], :] = part[0:128]
-        dn_ref[places[1], :] = part[128:256]
+        store(0, part[0:128])
+        store(1, part[128:256])
 
     def skip():
         zero = jnp.zeros((256, D), jnp.bfloat16)
-        dk_ref[...] = zero
-        dv_ref[...] = zero
-        dn_ref[places[0], :] = zero[0:128]
-        dn_ref[places[1], :] = zero[0:128]
+        store(0, zero[0:128])
+        store(1, zero[0:128])
 
     pl.when(used > 0)(fill)
     pl.when(used == 0)(skip)
@@ -497,7 +723,13 @@
         mine = pl.multiple_of(lax.bitwise_xor(ids_ref[0], ids_ref[1]) * own_rows, SPAN)
         own_part = dot(dq_ref[...], w_ref[:, 0:D], 1, 1)
         dn_own_ref[...] = own_part
-        dgain_ref[0:1, :] += jnp.sum(own_part * unit(x_ref[pl.ds(mine, own_rows), :]), axis=0, keepdims=True)
+        x_own = unit(x_ref[pl.ds(mine, own_rows), :])
+        dgain_ref[0:1, :] += jnp.sum(own_part * x_own, axis=0, keepdims=True)
+        own_ref[:, 0:D] = dot((x_own * gain_ref[0:1, :]).astype(jnp.bfloat16), dq_ref[...], 0, 0)
+        parts, tall = mine_refs[0].shape[1:3]
+        size, part_flip = tall - 16, ids_ref[1] & (parts - 1)
+        put_grads(mine_refs, own_ref, size, part_flip, ids_ref[3])
+        put_grads(shared_refs, all_ref, size, part_flip, ids_ref[3])
 
         row16 = lax.broadcasted_iota(jnp.int32, (16, 128), 0)
         lane16 = lax.broadcasted_iota(jnp.int32, (16, 128), 1)
@@ -527,32 +759,42 @@
             grad = grad + lax.dot_general(
                 sums, hot, (((1,), (1,)), ((), ())), preferred_element_type=jnp.float32, precision=lax.Precision.HIGHEST
             )
-        dtab_ref[...] = grad
-
-
-def backward(ids, order, lengths, table, table_t, gains, dnf, res, cot, o, ot, lse, q, k, v, xs, ws):
+        wide = mine_refs[0].shape[3]
+        own_ref[0:1, 0:D] = dgain_ref[0:1, :]
+        own_ref[0:1, D : 2 * D] = dgain_ref[1:2, :]
+        own_ref[1:16, :] = jnp.zeros((15, 2 * D), jnp.float32)
+        own_ref[16:32, :] = jnp.concatenate([grad, jnp.zeros((16, 2 * D - 128), jnp.float32)], axis=1)
+        for refs, top in ((mine_refs, 0), (shared_refs, 16)):
+            for part in range(parts):
+                columns = pl.ds(pl.multiple_of(lax.bitwise_xor(jnp.int32(part), part_flip) * wide, 128), wide)
+                value = own_ref[top : top + 16, columns].astype(jnp.bfloat16)
+                for ref in refs:
+                    for index in range(ref.shape[0]):
+                        ref[index, part, size:tall, :] = value
+
+
+def backward(ids, order, lengths, table, table_t, gains, dnf, res, cot, o, ot, lse, q, k, v, xs, ws, n_dn, n_fsdp):
     spans, local_rows = order.shape[1], q.shape[0]
     rows, own = spans * SPAN, local_rows // SPAN
     n_x, n_w = sum(x.shape[0] for x in xs), sum(w.shape[0] for w in ws)
     bf, f32 = jnp.bfloat16, jnp.float32
+    shapes = grad_shapes(n_fsdp, 1 if n_dn == 1 else 4)
     return pl.pallas_call(
-        lambda *refs: backward_kernel((len(xs), len(ws)), *refs),
+        lambda *refs: backward_kernel((len(xs), len(ws), n_dn, len(shapes)), *refs),
         name="backward",
+        cost_estimate=cost(36),
         grid=(spans // 2,),
-        out_shape=(
-            jax.ShapeDtypeStruct((local_rows, D), f32),
-            jax.ShapeDtypeStruct((local_rows, D), bf),
-            jax.ShapeDtypeStruct((local_rows, D), bf),
-            jax.ShapeDtypeStruct((rows, D), bf),
-            jax.ShapeDtypeStruct((rows, D), bf),
-            jax.ShapeDtypeStruct((rows, D), bf),
-            jax.ShapeDtypeStruct((local_rows, D), f32),
-            jax.ShapeDtypeStruct((8, D), f32),
-            jax.ShapeDtypeStruct((16, 128), f32),
-        ),
+        out_shape=(jax.ShapeDtypeStruct((rows // n_dn, D), bf),) * n_dn
+        + shapes * 2
+        + (jax.ShapeDtypeStruct((local_rows, D), f32),) * 2,
         in_specs=[smem()] * 4 + [once()] * 9 + [by_chunk()] * 2 + [hbm()] * (len(xs) + len(ws)),
-        out_specs=(once(),) * 3 + (by_chunk(),) * 2 + (once(),) * 4,
+        out_specs=(once(),) * (n_dn + 2 * len(shapes) + 2),
         scratch_shapes=[
+            pltpu.VMEM((local_rows, D), bf),
+            pltpu.VMEM((local_rows, D), bf),
+            pltpu.VMEM((8, D), f32),
+            pltpu.VMEM((D, 2 * D), f32),
+            pltpu.VMEM((D, 2 * D), f32),
             pltpu.SMEM((spans,), jnp.int32),
             pltpu.VMEM((rows, D), bf),
             pltpu.VMEM((D, 4 * D), bf),
@@ -567,6 +809,7 @@
             pltpu.VMEM((PAIRS, 8, 256), f32),
             pltpu.VMEM((256, D), f32),
             pltpu.VMEM((256, D), f32),
+            pltpu.VMEM((PAIRS, 144, 256), bf),
             pltpu.SemaphoreType.DMA((n_x,)),
             pltpu.SemaphoreType.DMA((n_w,)),
         ],
@@ -579,6 +822,10 @@
     return lax.ppermute(x, axis, [(i, i ^ bit) for i in range(count)])
 
 
+def hop(x, pairs):
+    return lax.ppermute(x, "ctx", [(2 * a + i, 2 * b + i) for a, b in pairs for i in range(2)])
+
+
 def block(x, index, count, dim=0):
     size = x.shape[dim] // count
     return lax.dynamic_slice_in_dim(x, index * size, size, dim)
@@ -586,22 +833,6 @@
 
 def after(x, *others):
     return lax.optimization_barrier((x,) + others)[0]
-
-
-def gather_four(x):
-    across = swap(x, "fsdp", 2)
-    return [x, swap(x, "fsdp", 1), across, swap(across, "fsdp", 1)]
-
-
-def scatter_four(pieces):
-    first, third = swap(pieces[1], "fsdp", 1), swap(pieces[3], "fsdp", 1)
-    far = add(pieces[2], third)
-    return pieces[0], first, swap(far, "fsdp", 2)
-
-
-def exchange_four(pieces):
-    side, corner = swap(pieces[1], "fsdp", 1), swap(pieces[3], "fsdp", 1)
-    return [pieces[0], side, swap(pieces[2], "fsdp", 2), swap(corner, "fsdp", 2)]
 
 
 def add(*terms):
@@ -609,6 +840,72 @@
     for term in terms[1:]:
         total = total + term.astype(jnp.float32)
     return total.astype(jnp.bfloat16)
+
+
+def gather_four(x):
+    across = swap(x, "fsdp", 2)
+    return [x, swap(x, "fsdp", 1), across, swap(across, "fsdp", 1)]
+
+
+def scatter_four(pieces):
+    first, third = swap(pieces[1], "fsdp", 1), swap(pieces[3], "fsdp", 1)
+    far = add(pieces[2], third)
+    return pieces[0], first, swap(far, "fsdp", 2), far
+
+
+def scatter_pairs(keep, send):
+    got = swap(send, "fsdp", 1)
+    return keep[0], got[0], swap(add(keep[1], got[1]), "fsdp", 2)
+
+
+TURNS = ((0,), (1,), (2, 6), (3, 7), (4,), (5,))
+
+
+def tail(dn, mine, shared, ffn_own, high):
+    g7, g3 = swap(dn[7], "ctx", 1), swap(dn[3], "ctx", 1)
+    ffn4 = swap(ffn_own, "ctx", 4)
+    mine, shared = (add(*scatter_pairs(*g)) for g in (mine, shared))
+    g5, g1 = swap(after(dn[5], g7), "ctx", 1), swap(after(dn[1], g3), "ctx", 1)
+    n4 = swap(add(dn[6], g7), "ctx", 2)
+    ffn_pair = swap(jnp.concatenate([ffn_own, ffn4]), "ctx", 2)
+    n0 = swap(after(add(dn[2], g3), n4), "ctx", 2)
+    mine, shared = after((mine, shared), g5, n4)
+    low_half, high_half = jnp.where(high, shared, mine), jnp.where(high, mine, shared)
+    p = [jnp.stack([low_half[r], high_half[r]]) for r in range(4)]
+    a = swap(p[3], "ctx", 1)
+    b = swap(after(p[1], g1), "ctx", 1)
+    near = swap(add(p[2], a), "ctx", 2)
+    ffn1 = swap(after(ffn_own, a), "ctx", 1)
+    half = after(add(p[0], b, near), ffn_pair)
+    ffn5 = swap(after(ffn4, b), "ctx", 1)
+    own = add(half[0], swap(half[1], "ctx", 4))[None]
+    ffn_others = swap(after(ffn_pair, near, ffn1), "ctx", 1)
+    own4 = swap(own, "ctx", 4)
+    own1 = swap(after(own, ffn5), "ctx", 1)
+    pair = swap(jnp.concatenate([own, own4]), "ctx", 2)
+    own5 = swap(after(own4, own1), "ctx", 1)
+    others = swap(after(pair, ffn_others, own5), "ctx", 1)
+    far = swap(after(add(dn[4], g5, n4), own4), "ctx", 4)
+    return (
+        (dn[0], g1, n0, far),
+        [ffn_own, ffn1, ffn_pair, ffn_others, ffn4, ffn5],
+        [own, own1, pair, others, own4, own5],
+    )
+
+
+def line_gather(x, x1, early):
+    line = lax.axis_index("ctx") // 2
+    up1, down1 = hop(x, [(0, 1), (1, 2), (2, 3)]), hop(x, [(3, 2), (2, 1), (1, 0)])
+    z1 = jnp.where(line % 2 == 0, down1, up1)
+    z1, up1, down1 = after((z1, up1, down1), x1)
+    x3 = swap(z1, "ctx", 1)
+    up2, down2 = hop(up1, [(1, 2), (2, 3)]), hop(down1, [(2, 1), (1, 0)])
+    z2 = jnp.where(line < 2, down2, up2)
+    z2, up2, down2 = after((z2, up2, down2), x3, early)
+    x5 = swap(z2, "ctx", 1)
+    far = hop(jnp.where(line == 2, up2, down2), [(2, 3), (1, 0)])
+    z3 = jnp.where(line == 1, down1, jnp.where(line == 2, up1, far))
+    return [x, x1, z1, x3, z2, x5, z3, swap(after(z3, x5), "ctx", 1)], x3, x5
 
 
 def on_device(
@@ -634,30 +931,34 @@
     own_rows = w_query.shape[0]
     bf, f32 = jnp.bfloat16, jnp.float32
     x, cot = tokens[0], cotangent[0]
+    width = w_ffn_out.shape[0]
     table_size = rel_table.size
     small = jnp.concatenate([gain_attn, gain_ffn, rel_table.reshape(-1)])
     small = jnp.pad(small[None], ((0, 15), (0, 4 * D - small.shape[0])))
     weights = jnp.concatenate([jnp.concatenate([w_query, w_key, w_value, w_out], axis=1), small], axis=0)
-    width = w_ffn_out.shape[0]
 
     if fast:
-        zero = jnp.int32(0)
-        ids = jnp.stack([place, place, shard])
-        x1, x2, x4 = swap(x, "ctx", 1), swap(x, "ctx", 2), swap(x, "ctx", 4)
-        x3, x6 = swap(x2, "ctx", 1), swap(x4, "ctx", 2)
-        x5, x7 = swap(x4, "ctx", 1), swap(x6, "ctx", 1)
-        xs = [p[None] for p in (x, x1, x2, x3, x4, x5, x6, x7)]
-        w_pieces = gather_four(weights)
-        ws = [p[None] for p in w_pieces]
+        ids = jnp.stack([place, place, shard, shard, jnp.int32(n_ctx)])
         order = [shard ^ r for r in range(4)]
-        smalls = jnp.stack([p[own_rows] for p in w_pieces])
+        tokens_got = swap(x, "ctx", 1)
+        w2 = swap(weights, "fsdp", 2)
+        w1 = swap(after(weights, tokens_got), "fsdp", 1)
+        gathered, third, fifth = line_gather(x, tokens_got, w1)
+        xs = [p[None] for p in gathered]
+        w3 = swap(after(w2, third), "fsdp", 1)
+        ws = [p[None] for p in (weights, w1, w2, w3)]
+        w_in, cot_late = after((w_in, cot), third)
+        columns = [block(w_in, order[r], 4, 1) for r in range(4)]
+        side = swap(jnp.stack([columns[1], columns[3]]), "fsdp", 1)
+        smalls = jnp.stack([p[own_rows] for p in (weights, w1, w2, w3)])
         smalls = jnp.stack([lax.dynamic_index_in_dim(smalls, order[i], 0, False) for i in range(4)])
-        columns = after(w_in, w_pieces[2])
-        wins = exchange_four([block(columns, order[r], 4, 1) for r in range(4)])
-        cots = [p[None] for p in gather_four(after(cot, wins[3]))]
-        wins = [p[None] for p in wins]
+        win2 = swap(after(jnp.stack([columns[2], side[1]]), w2), "fsdp", 2)
+        wins = [columns[0][None], side[:1], win2]
+        cot1 = swap(after(cot, fifth), "fsdp", 1)
+        cot2 = swap(after(cot_late, w2), "fsdp", 2)
+        cots = [p[None] for p in (cot, cot1, cot2, swap(cot2, "fsdp", 1))]
     else:
-        ids = jnp.stack([place, jnp.int32(0), jnp.int32(0)])
+        ids = jnp.stack([place, jnp.int32(0), jnp.int32(0), jnp.int32(0), jnp.int32(n_ctx)])
         xs = [lax.all_gather(x, "ctx", axis=0)]
         ws = [lax.all_gather(weights, "fsdp", axis=0)]
         smalls = ws[0][:, own_rows]
@@ -670,89 +971,85 @@
     table = table_bf.astype(f32)
     table_t = jnp.pad(table_bf.T, ((0, 16 - H), (0, 128 - NB)))
 
-    nf, res, o, ot, lse, q, k, v, xn = forward(
+    nf, res, o, ot, lse, q, k, v = forward(
         ids, span_order, lengths, table, table_t, gains, xs, ws, local_rows
     )
 
     if fast:
-        nfs = [p[None] for p in gather_four(nf)]
+        nfs = [nf[None], swap(nf, "fsdp", 1)[None], swap(nf, "fsdp", 2)[None]]
+        halves = [ffn(ids, nfs[:2], cots[:2], wins, w_ffn_out)]
+        nfs.append(swap(after(nfs[2], halves[0][0]), "fsdp", 1))
+        halves.append(ffn(ids, nfs[2:], cots[2:], wins, w_ffn_out))
     else:
         nfs = [lax.all_gather(nf, "fsdp", axis=0)]
-    act, dup, dn_part = ffn(ids, nfs, cots, wins, w_ffn_out)
-    dn_part = dn_part.reshape(n_fsdp, local_rows, D)
+        halves = [ffn(ids, nfs, cots, wins, w_ffn_out)]
+    acts, dups = [h[0] for h in halves], [h[1] for h in halves]
+    dns, outs = [d for h in halves for d in h[2]], [d for h in halves for d in h[3]]
     if fast:
-        a, b, c = scatter_four([dn_part[r] for r in range(4)])
+        a, b, c, far = scatter_four([p[0] for p in dns])
         dnf = a.astype(f32) + b.astype(f32) + c.astype(f32)
+        ffn_parts = ffn_grads(ids, nfs, cots, after(acts, far), dups, n_fsdp, 8)
+        dnf = after(dnf, *ffn_parts)
+        ffn_got = lax.all_to_all(after(ffn_parts[0], c), "ctx", 0, 0)
     else:
-        dnf = lax.psum_scatter(dn_part, "fsdp", scatter_dimension=0).astype(f32)
-
-    nf_all = jnp.concatenate([p.reshape(-1, D) for p in nfs])
-    cot_all = jnp.concatenate([p.reshape(-1, D) for p in cots])
-    out_part = dot(act, w_ffn_out).astype(bf).reshape(n_fsdp, local_rows, D)
-    grad_ffn_out = dot(act, cot_all, 0, 0).astype(bf)
-    grad_in = dot(nf_all, dup, 0, 0).astype(bf).reshape(n_fsdp, own_rows, width)
+        dnf = lax.psum_scatter(dns[0], "fsdp", scatter_dimension=0).astype(f32)
+        grad_ffn_out, grad_in = ffn_grads(ids, nfs, cots, acts, dups, n_fsdp, 1)
+        grad_in = jnp.transpose(lax.all_to_all(grad_in, "fsdp", 0, 0), (1, 0, 2)).reshape(own_rows, n_fsdp * width)
+        grad_ffn_out, grad_in = (lax.psum(g, "ctx").astype(f32) for g in (grad_ffn_out, grad_in))
     if fast:
-        a, b, c = scatter_four([out_part[r] for r in range(4)])
-        output = (res + a.astype(f32) + b.astype(f32) + c.astype(f32)).astype(bf)
-        got = exchange_four([lax.dynamic_index_in_dim(grad_in, order[r], 0, False) for r in range(4)])
-        got = jnp.stack(got)
-        grad_in = jnp.concatenate([lax.dynamic_index_in_dim(got, shard ^ i, 0, False) for i in range(4)], axis=1)
+        *out_terms, out_far = scatter_four([p[0] for p in outs])
+        dnf = after(dnf, out_terms[1], out_far)
     else:
-        output = (res + lax.psum_scatter(out_part, "fsdp", scatter_dimension=0).astype(f32)).astype(bf)
-        got = lax.all_to_all(grad_in, "fsdp", 0, 0)
-        grad_in = jnp.transpose(got, (1, 0, 2)).reshape(own_rows, n_fsdp * width)
-    grad_ffn_out = lax.psum(grad_ffn_out, "ctx")
-    grad_in = lax.psum(grad_in, "ctx")
-
-    dres, dlow, dq, dk, dv, dn, dn_own, dgain, dtab = backward(
-        ids, span_order, lengths, table, table_t, gains, dnf, res, cot, o, ot, lse, q, k, v, xs, ws
+        out_terms = [lax.psum_scatter(outs[0], "fsdp", scatter_dimension=0)]
+
+    *got, dres, dn_own = backward(
+        ids, span_order, lengths, table, table_t, gains, dnf, res, cot, o, ot, lse, q, k, v, xs, ws,
+        8 if fast else 1, n_fsdp,
     )
-    dn = dn.reshape(n_ctx, local_rows, D)
     if fast:
-        got7, got5, got3, got1 = (swap(dn[r], "ctx", 1) for r in (7, 5, 3, 1))
-        s6, s4, s2, s0 = add(dn[6], got7), add(dn[4], got5), add(dn[2], got3), add(dn[0], got1)
-        t4 = add(s4, swap(s6, "ctx", 2))
-        t2 = swap(s2, "ctx", 2)
-        d_normed = dn_own + s0.astype(f32) + t2.astype(f32) + swap(t4, "ctx", 4).astype(f32)
+        got = after(got, ffn_got, *out_terms)
+        dn, mine, shared = got[:8], got[8:10], got[10:12]
+        ffn_own = jnp.sum(ffn_got.astype(f32), axis=0).astype(bf)
+        blocks = ffn_own[D // 8 :]
+        blocks = [blocks[48 * (r // 2) : 48 * (r // 2) + 48, 384 * (r % 2) : 384 * (r % 2) + 384] for r in range(4)]
+        side = swap(jnp.stack([blocks[1], blocks[3]]), "fsdp", 1)
+        across = swap(jnp.stack([blocks[2], side[1]]), "fsdp", 2)
+        ffn_own = jnp.concatenate(
+            [ffn_own[: D // 8], jnp.concatenate([blocks[0], side[0]], axis=1),
+             jnp.concatenate([across[0], across[1]], axis=1)]
+        )
+        terms, ffn_all, grads = tail(dn, mine, shared, ffn_own[None], place >= 4)
+        d_normed = dn_own
+        for term in terms:
+            d_normed = d_normed + term.astype(f32)
+        grad_ffn_out, grad_in = finish_ffn(ids, ffn_all, TURNS)
     else:
-        d_normed = dn_own + lax.psum_scatter(dn, "ctx", scatter_dimension=0).astype(f32)
-
+        d_normed = dn_own + lax.psum_scatter(got[0].reshape(n_ctx, local_rows, D), "ctx", scatter_dimension=0).astype(f32)
+        grads = [lax.psum(lax.psum_scatter(g, "fsdp", scatter_dimension=0), "ctx") for g in got[1:]]
+    g_query, g_out, g_key, g_value, tiny = finish(ids, grads, TURNS if fast else ((0,), (1,)))
+    table_row = tiny[:H, 2 * D : 2 * D + NB].T
+
+    output = res
+    for term in out_terms:
+        output = output + term.astype(f32)
+    output = output.astype(bf)
     xf = x.astype(f32)
     inv_rms = lax.rsqrt(jnp.mean(xf * xf, axis=1, keepdims=True) + EPS)
-    xn_own = (xf * inv_rms * gains[0:1]).astype(bf)
     scaled = d_normed * gains[0:1]
     inner = jnp.mean(scaled * xf, axis=1, keepdims=True)
     grad_tokens = (dres + inv_rms * scaled - xf * (inv_rms * inv_rms * inv_rms * inner)).astype(bf)
-
-    grads = jnp.concatenate(
-        [dot(xn_own, dq, 0, 0).astype(bf), dot(xn, dk, 0, 0).astype(bf), dot(xn, dv, 0, 0).astype(bf),
-         dot(o, dlow, 0, 0).astype(bf)], axis=1
-    )
-    tiny = jnp.concatenate(
-        [dgain[0].reshape(n_fsdp, own_rows), dgain[1].reshape(n_fsdp, own_rows),
-         dtab[:H, :NB].T.reshape(n_fsdp, table_size)], axis=1
-    ).astype(bf)
-    tiny = jnp.pad(tiny[:, None, :], ((0, 0), (0, 15), (0, 4 * D - tiny.shape[1])))
-    payload = jnp.concatenate([grads.reshape(n_fsdp, own_rows, 4 * D), tiny], axis=1)
-    if fast:
-        a, b, c = scatter_four([lax.dynamic_index_in_dim(payload, order[r], 0, False) for r in range(4)])
-        payload = add(a, b, c)
-    else:
-        payload = lax.psum_scatter(payload, "fsdp", scatter_dimension=0)
-    payload = lax.psum(payload, "ctx").astype(f32)
-    tiny = payload[own_rows]
     return (
         output[None],
         grad_tokens[None],
-        payload[:own_rows, 0:D],
-        payload[:own_rows, D : 2 * D],
-        payload[:own_rows, 2 * D : 3 * D],
-        payload[:own_rows, 3 * D : 4 * D],
-        grad_in.astype(f32),
-        grad_ffn_out.astype(f32),
-        tiny[:own_rows],
-        tiny[own_rows : 2 * own_rows],
-        tiny[2 * own_rows : 2 * own_rows + table_size].reshape(rel_table.shape),
+        g_query,
+        g_key,
+        g_value,
+        g_out,
+        grad_in,
+        grad_ffn_out,
+        block(tiny[0, :D], shard, n_fsdp),
+        block(tiny[0, D : 2 * D], shard, n_fsdp),
+        block(table_row, shard, n_fsdp),
     )
 
 

time: 509 us -> 300 us (0.59); the launches traced: 502 us -> 299 us
  waiting for transfers between devices: 307 us -> 113 us
  Pallas kernels: 56.7 us -> 91.6 us
  matrix products: 18.4 us -> 0 us
  between operations: 15 us -> 1.46 us
  local copies, waits for them, and re-layouts: 23.8 us -> 17 us
  other arithmetic: 29 us -> 23.9 us
    psum x1 -> x0, waiting for transfers between devices: 123 us -> none  [on_device(): payload = lax.psum(payload, 'ctx').astype(f32)]
    ppermute x40 -> x48, waiting for transfers between devices: 184 us -> 100 us  [swap(): return lax.ppermute(x, axis, [(i, i ^ bit) for i in range(count)])]
    pallas_call x2 -> x6, Pallas kernels: 39.1 us -> 69.5 us  [the longest x1 40.1 us: backward(): pl.pallas_call(lambda *refs: backward_kernel((len(xs), len(ws), n_dn, len...]
    dot_general x7 -> x0, matrix products: 18.4 us -> none  [dot(): lax.dot_general(a, b, (((ca,), (cb,)), ((), ())), preferred_element_type=...]
    ppermute x40 -> x48, starting transfers between devices: 51.8 us -> 36.5 us  [swap(): return lax.ppermute(x, axis, [(i, i ^ bit) for i in range(count)])]
    ppermute x0 -> x5, starting transfers between devices: none -> 10.1 us  [hop(): lax.ppermute(x, 'ctx', [(2 * a + i, 2 * b + i) for a, b in pairs for i in...]
    all_to_all x0 -> x1, waiting for transfers between devices: none -> 7.67 us  [on_device(): ffn_got = lax.all_to_all(after(ffn_parts[0], c), 'ctx', 0, 0)]
    concatenate x4 -> x0, local copies, waits for them, and re-layouts: 7.17 us -> none  [the longest x1 6.91 us: on_device(): jnp.concatenate([dot(xn_own, dq, 0, 0).astype(bf), dot(xn, dk, 0, 0).asty...]
  transfers between devices with their start and end apart: 41 -> 54, of which waited for: 22 -> 26; matrix products, arithmetic and copies ran while one was open for 7% -> 11% of each run, Pallas kernels for 4% -> 27%
where the time goes in v4:
time: 300 us; the launch traced here: 299 us
  waiting for transfers between devices  113 us (38%)
  Pallas kernels  91.6 us (31%)
  starting transfers between devices  51.6 us (17%)
  other arithmetic  23.9 us (8%)
  local copies, waits for them, and re-layouts  17 us (6%)
    ppermute x48, waiting for transfers between devices, swap(): return lax.ppermute(x, axis, [(i, i ^ bit) for i in range(count)])  100 us
    pallas_call x1, Pallas kernels, backward(): pl.pallas_call(lambda *refs: backward_kernel((len(xs), len(ws), n_dn, len...  40.1 us
    ppermute x48, starting transfers between devices, swap(): return lax.ppermute(x, axis, [(i, i ^ bit) for i in range(count)])  36.5 us
    pallas_call x1, Pallas kernels, forward(): pl.pallas_call(lambda *refs: forward_kernel((len(xs), len(ws)), *refs), n...  22.2 us
    pallas_call x2, Pallas kernels, ffn(): pl.pallas_call(lambda *refs: ffn_kernel((count, len(wins)), *refs), name=...  14 us
    ppermute x5, starting transfers between devices, hop(): lax.ppermute(x, 'ctx', [(2 * a + i, 2 * b + i) for a, b in pairs for i in...  10.1 us
    convert_element_type x11, other arithmetic, add(): return total.astype(jnp.bfloat16)  8.12 us
    all_to_all x1, waiting for transfers between devices, on_device(): ffn_got = lax.all_to_all(after(ffn_parts[0], c), 'ctx', 0, 0)  7.67 us
  transfers between devices with their start and end apart: 54, of which 26 were waited for; matrix products, arithmetic and copies ran while one was open for 11% of the time, Pallas kernels for 27%

profile of v4, /device:TPU:0, one launch (start us, length us, event | category | flops | bytes accessed | tf_op | source)
XLA Modules:
  0.0 298.9 jit_solution(15074360862644729532)
XLA Ops:
  1.9 5.6 %collective-permute-start.4 = (bf16[256,768]{1,0:T(8,128)(2,1)}, bf16[256,768]{1,0:T(8,128)(2,1)S(1)}, u32[]{:S(2)}, u32[]{:S(2)}) collective-permute-start(bf16[256,768]{1,0:T(8,128)(2,1)} %bitcast.91), channel_id=1, source_target_pairs={{0,8},{4,12},{8,16},{12,20},{16,24},{20,28},{1,9},{5,13},{9,17},{1... | collective-permute-start | bytes 1179656 | tf_op jit(solution)/shard_map/ppermute | solution.py:826
  7.5 2.0 collective-permute-start
  12.5 1.6 collective-permute-start.2
  14.1 4.3 %collective-permute-done = bf16[256,768]{1,0:T(8,128)(2,1)S(1)} collective-permute-done((bf16[256,768]{1,0:T(8,128)(2,1)}, bf16[256,768]{1,0:T(8,128)(2,1)S(1)}, u32[]{:S(2)}, u32[]{:S(2)}) %collective-permute-start) | collective-permute-done | bytes 393248 | tf_op jit(solution)/shard_map/ppermute | solution.py:822
  19.3 1.6 collective-permute-start.5
  22.9 2.2 fusion.21.refs_14_.refs_23_
  25.2 5.9 %collective-permute-done.5 = bf16[256,768]{1,0:T(8,128)(2,1)} collective-permute-done((bf16[256,768]{1,0:T(8,128)(2,1)}, bf16[256,768]{1,0:T(8,128)(2,1)}, u32[]{:S(2)}, u32[]{:S(2)}) %collective-permute-start.5) | collective-permute-done | bytes 393248 | tf_op jit(solution)/shard_map/ppermute | solution.py:822
  31.0 2.0 dynamic-slice_bitcast_fusion
  33.9 7.7 %collective-permute-done.2 = bf16[208,3072]{1,0:T(8,128)(2,1)} collective-permute-done((bf16[208,3072]{1,0:T(8,128)(2,1)S(1)}, bf16[208,3072]{1,0:T(8,128)(2,1)}, u32[]{:S(2)}, u32[]{:S(2)}) %collective-permute-start.2) | collective-permute-done | bytes 1277984 | tf_op jit(solution)/shard_map/ppermute | solution.py:822
  44.5 1.5 collective-permute-start.19
  47.5 1.8 fusion.18
  50.6 5.4 %collective-permute-done.10 = bf16[256,768]{1,0:T(8,128)(2,1)S(1)} collective-permute-done((bf16[256,768]{1,0:T(8,128)(2,1)S(1)}, bf16[256,768]{1,0:T(8,128)(2,1)S(1)}, u32[]{:S(2)}, u32[]{:S(2)}) %collective-permute-start.10) | collective-permute-done | bytes 393248 | tf_op jit(solution)/shard_map/ppermute | solution.py:826
  56.0 2.4 collective-permute-done.9
  62.2 6.7 %collective-permute-done.11 = bf16[256,768]{1,0:T(8,128)(2,1)S(1)} collective-permute-done((bf16[256,768]{1,0:T(8,128)(2,1)S(1)}, bf16[256,768]{1,0:T(8,128)(2,1)S(1)}, u32[]{:S(2)}, u32[]{:S(2)}) %collective-permute-start.11) | collective-permute-done | bytes 393248 | tf_op jit(solution)/shard_map/ppermute | solution.py:822
  69.6 22.2 %forward.1 = (bf16[256,768]{1,0:T(8,128)(2,1)}, f32[256,768]{1,0:T(8,128)}, bf16[256,768]{1,0:T(8,128)(2,1)}, f32[2,6,128,128]{3,2,1,0:T(8,128)}, f32[2,6,1,256]...) custom-call(s32[5]{0:T(128)} %stack.68.refs_0_, ...), custom_call_target="tpu_custom_call" | custom-call | flops 22000001024 | bytes 22000000 | tf_op jit(solution)/shard_map/forward/pallas_call | solution.py:308
  94.5 7.0 %ffn.2 = (bf16[2,256,768]{2,1,0:T(8,128)(2,1)}, bf16[2,256,768]{2,1,0:T(8,128)(2,1)}, bf16[1,256,768]{2,1,0:T(8,128)(2,1)}, bf16[1,256,768]{2,1,0:T(8,128)(2,1)}...) custom-call(s32[5]{0:T(128)} %stack.68.refs_0_, bf16[1,256,768]{2,1,0:T(8,128)(2,1)} %bitcast.109, ...), custom_call_target="tpu_custom_call" | custom-call | flops 6000000000 | bytes 6000000 | tf_op jit(solution)/shard_map/ffn/pallas_call | solution.py:375
  101.5 2.2 collective-permute-done.17
  103.7 1.7 collective-permute-done.18.refs_2_.refs_4_
  106.1 7.0 %ffn.3 = (bf16[2,256,768]{2,1,0:T(8,128)(2,1)}, bf16[2,256,768]{2,1,0:T(8,128)(2,1)}, bf16[1,256,768]{2,1,0:T(8,128)(2,1)}, bf16[1,256,768]{2,1,0:T(8,128)(2,1)}...) custom-call(s32[5]{0:T(128)} %stack.68.refs_0_, bf16[1,256,768]{2,1,0:T(8,128)(2,1)} %bitcast.116, ...), custom_call_target="tpu_custom_call" | custom-call | flops 6000000000 | bytes 6000000 | tf_op jit(solution)/shard_map/ffn/pallas_call | solution.py:375
  116.6 6.9 %ffn_grads.1 = bf16[8,192,768]{2,1,0:T(8,128)(2,1)} custom-call(s32[5]{0:T(128)} %stack.68.refs_0_, bf16[1,256,768]{2,1,0:T(8,128)(2,1)} %bitcast.110, bf16[1,256,768]{2,1,0:T(8,128)(2,1)} %bitcast.112, bf16[1,256,768]{2,1,0:T(8,128)(2,1)} %bitcast.117, bf16[1,256,768]{2,1,0:T(8,128)(2,1)} %copy-done.36, bf16[1,256,768]{2,1,0:T(8,128)(2,1)} %refs_5_.1, ...), custom_call_target="tpu_custom_call" | custom-call | flops 6000000000 | bytes 6000000 | tf_op jit(solution)/shard_map/ffn_grads/pallas_call | solution.py:440
  123.5 4.0 %collective-permute-done.25 = bf16[256,768]{1,0:T(8,128)(2,1)} collective-permute-done((bf16[256,768]{1,0:T(8,128)(2,1)S(1)}, bf16[256,768]{1,0:T(8,128)(2,1)}, u32[]{:S(2)}, u32[]{:S(2)}) %collective-permute-start.25) | collective-permute-done | bytes 393248 | tf_op jit(solution)/shard_map/ppermute | solution.py:822
  127.6 5.0 %all-to-all-start = ((bf16[8,192,768]{2,1,0:T(8,128)(2,1)}), bf16[8,192,768]{2,1,0:T(8,128)(2,1)S(1)}, u32[]{:S(2)}, u32[]{:S(2)}) async-start(bf16[8,192,768]{2,1,0:T(8,128)(2,1)} %ffn_grads.1), calls=%async_computation | async-start | bytes 4718592 | tf_op jit(solution)/shard_map/all_to_all | solution.py:993
  134.3 1.8 collective-permute-start.22
  136.1 2.0 fusion.7.refs_6_
  138.1 40.1 %backward.1 = (bf16[256,768]{1,0:T(8,128)(2,1)}, bf16[256,768]{1,0:T(8,128)(2,1)}, bf16[256,768]{1,0:T(8,128)(2,1)}, bf16[256,768]{1,0:T(8,128)(2,1)}, bf16[256,...) custom-call(s32[5]{0:T(128)} %stack.68.refs_0_, ...), custom_call_target="tpu_custom_call" | custom-call | flops 35999997952 | bytes 36000000 | tf_op jit(solution)/shard_map/backward/pallas_call | solution.py:782
  178.2 7.7 %all-to-all-done = bf16[8,192,768]{2,1,0:T(8,128)(2,1)S(1)} async-done(((bf16[8,192,768]{2,1,0:T(8,128)(2,1)}), bf16[8,192,768]{2,1,0:T(8,128)(2,1)S(1)}, u32[]{:S(2)}, u32[]{:S(2)}) %all-to-all-start) | async-done | bytes 2359328 | tf_op jit(solution)/shard_map/all_to_all | solution.py:993
  187.0 2.1 collective-permute-done.39
  189.2 1.8 collective-permute-start.40
  195.1 1.8 collective-permute-start.35
  198.6 4.5 %collective-permute-done.28 = bf16[256,768]{1,0:T(8,128)(2,1)S(1)} collective-permute-done((bf16[256,768]{1,0:T(8,128)(2,1)}, bf16[256,768]{1,0:T(8,128)(2,1)S(1)}, u32[]{:S(2)}, u32[]{:S(2)}) %collective-permute-start.28) | collective-permute-done | bytes 393248 | tf_op jit(solution)/shard_map/ppermute | solution.py:822
  203.2 1.5 collective-permute-start.31
  204.7 6.9 %collective-permute-done.26 = bf16[256,768]{1,0:T(8,128)(2,1)S(1)} collective-permute-done((bf16[256,768]{1,0:T(8,128)(2,1)}, bf16[256,768]{1,0:T(8,128)(2,1)S(1)}, u32[]{:S(2)}, u32[]{:S(2)}) %collective-permute-start.26) | collective-permute-done | bytes 393248 | tf_op jit(solution)/shard_map/ppermute | solution.py:822
  212.5 1.5 collective-permute-start.27
  215.3 8.8 %collective-permute-done.33 = bf16[4,208,384]{2,1,0:T(8,128)(2,1)S(1)} collective-permute-done((bf16[4,208,384]{2,1,0:T(8,128)(2,1)S(1)}, bf16[4,208,384]{2,1,0:T(8,128)(2,1)S(1)}, u32[]{:S(2)}, u32[]{:S(2)}) %collective-permute-start.33) | collective-permute-done | bytes 639008 | tf_op jit(solution)/shard_map/ppermute | solution.py:822
  226.4 1.5 collective-permute-start.37
  229.8 7.1 %collective-permute-done.37 = bf16[2,208,384]{2,1,0:T(8,128)(2,1)S(1)} collective-permute-done((bf16[2,208,384]{2,1,0:T(8,128)(2,1)S(1)}, bf16[2,208,384]{2,1,0:T(8,128)(2,1)S(1)}, u32[]{:S(2)}, u32[]{:S(2)}) %collective-permute-start.37) | collective-permute-done | bytes 319520 | tf_op jit(solution)/shard_map/ppermute | solution.py:822
  239.5 4.2 %collective-permute-done.36 = bf16[2,208,384]{2,1,0:T(8,128)(2,1)S(1)} collective-permute-done((bf16[2,208,384]{2,1,0:T(8,128)(2,1)S(1)}, bf16[2,208,384]{2,1,0:T(8,128)(2,1)S(1)}, u32[]{:S(2)}, u32[]{:S(2)}) %collective-permute-start.36) | collective-permute-done | bytes 319520 | tf_op jit(solution)/shard_map/ppermute | solution.py:822
  245.2 3.8 %collective-permute-done.38 = bf16[2,208,384]{2,1,0:T(8,128)(2,1)S(1)} collective-permute-done((bf16[2,208,384]{2,1,0:T(8,128)(2,1)S(1)}, bf16[2,208,384]{2,1,0:T(8,128)(2,1)S(1)}, u32[]{:S(2)}, u32[]{:S(2)}) %collective-permute-start.38) | collective-permute-done | bytes 319520 | tf_op jit(solution)/shard_map/ppermute | solution.py:822
  249.7 1.8 collective-permute-start.30
  253.0 4.4 %collective-permute-done.43 = bf16[208,384]{1,0:T(8,128)(2,1)S(1)} collective-permute-done((bf16[208,384]{1,0:T(8,128)(2,1)S(1)}, bf16[208,384]{1,0:T(8,128)(2,1)S(1)}, u32[]{:S(2)}, u32[]{:S(2)}) %collective-permute-start.43) | collective-permute-done | bytes 159776 | tf_op jit(solution)/shard_map/ppermute | solution.py:822
  259.4 10.4 %collective-permute-done.47.refs_2_ = bf16[1,208,384]{2,1,0:T(8,128)(2,1)S(1)} collective-permute-done((bf16[1,208,384]{2,1,0:T(8,128)(2,1)S(1)}, bf16[1,208,384]{2,1,0:T(8,128)(2,1)S(1)}, u32[]{:S(2)}, u32[]{:S(2)}) %collective-permute-start.47) | collective-permute-done | bytes 159776 | tf_op jit(solution)/shard_map/ppermute | solution.py:822
  269.7 1.5 collective-permute-start.51
  271.3 2.1 collective-permute-start.48
  274.3 4.8 %finish_ffn.1 = (f32[768,768]{1,0:T(8,128)}, f32[192,3072]{1,0:T(8,128)}) custom-call(s32[5]{0:T(128)} %stack.68.refs_0_, bf16[1,192,768]{2,1,0:T(8,128)(2,1)} %copy-done.5, bf16[1,192,768]{2,1,0:T(8,128)(2,1)} %copy-done.39, bf16[2,192,768]{2,1,0:T(8,128)(2,1)} %copy-done.26, bf16[2,192,768]{2,1,0:T(8,128)(2,1)} %copy-done.27, ...), custom_call_target="tpu_custom_call" | custom-call | flops 4000000000 | bytes 4000000 | tf_op jit(solution)/shard_map/finish_ffn/pallas_call | solution.py:486
  279.1 4.9 %collective-permute-done.48.refs_3_ = bf16[2,208,384]{2,1,0:T(8,128)(2,1)S(1)} collective-permute-done((bf16[2,208,384]{2,1,0:T(8,128)(2,1)S(1)}, bf16[2,208,384]{2,1,0:T(8,128)(2,1)S(1)}, u32[]{:S(2)}, u32[]{:S(2)}) %collective-permute-start.48) | collective-permute-done | bytes 319520 | tf_op jit(solution)/shard_map/ppermute | solution.py:822
  284.6 2.9 collective-permute-done.45
  287.5 1.5 fusion.2
  291.8 3.6 %finish.1 = (f32[192,768]{1,0:T(8,128)}, f32[192,768]{1,0:T(8,128)}, f32[192,768]{1,0:T(8,128)}, f32[192,768]{1,0:T(8,128)}, f32[16,3072]{1,0:T(8,128)}) custom-call(s32[5]{0:T(128)} %stack.68.refs_0_, bf16[1,208,384]{2,1,0:T(8,128)(2,1)} %copy-done.10, bf16[1,208,384]{2,1,0:T(8,128)(2,1)} %copy-done.41, bf16[2,208,384]{2,1,0:T(8,128)(2,1)} %copy-done.37, ...), custom_call_target="tpu_custom_call" | custom-call | flops 3000000000 | bytes 3000000 | tf_op jit(solution)/shard_map/finish/pallas_call | solution.py:532
  (223 shorter events, 55.5 us)
Async XLA Ops:
  0.6 17.8 %collective-permute-start.3 = (bf16[256,768]{1,0:T(8,128)(2,1)}, bf16[256,768]{1,0:T(8,128)(2,1)S(1)}, u32[]{:S(2)}, u32[]{:S(2)}) collective-permute-start(bf16[256,768]{1,0:T(8,128)(2,1)} %bitcast.90), channel_id=1, source_target_pairs={{24,16},{28,20},{16,8},{20,12},{8,0},{12,4},{25,17},{29,21},{17,9}... | collective-permute-start | bytes 1179656 | tf_op jit(solution)/shard_map/ppermute | solution.py:826
  1.9 16.5 %collective-permute-start.4 = (bf16[256,768]{1,0:T(8,128)(2,1)}, bf16[256,768]{1,0:T(8,128)(2,1)S(1)}, u32[]{:S(2)}, u32[]{:S(2)}) collective-permute-start(bf16[256,768]{1,0:T(8,128)(2,1)} %bitcast.91), channel_id=1, source_target_pairs={{0,8},{4,12},{8,16},{12,20},{16,24},{20,28},{1,9},{5,13},{9,17},{1... | collective-permute-start | bytes 1179656 | tf_op jit(solution)/shard_map/ppermute | solution.py:826
  7.5 10.9 %collective-permute-start = (bf16[256,768]{1,0:T(8,128)(2,1)}, bf16[256,768]{1,0:T(8,128)(2,1)S(1)}, u32[]{:S(2)}, u32[]{:S(2)}) collective-permute-start(bf16[256,768]{1,0:T(8,128)(2,1)} %bitcast.92), channel_id=1, source_target_pairs={{0,4},{4,0},{8,12},{12,8},{16,20},{20,16},{24,28},{28,24},{1,5},{5... | collective-permute-start | bytes 1179656 | tf_op jit(solution)/shard_map/ppermute | solution.py:822
  12.5 29.1 %collective-permute-start.2 = (bf16[208,3072]{1,0:T(8,128)(2,1)S(1)}, bf16[208,3072]{1,0:T(8,128)(2,1)}, u32[]{:S(2)}, u32[]{:S(2)}) collective-permute-start(bf16[208,3072]{1,0:T(8,128)(2,1)S(1)} %pad_maximum_fusion), channel_id=1, source_target_pairs={{0,2},{1,3},{2,0},{3,1},{4,6},{5,7},{6,4},{7,5},{8,10},{9,11},{10,... | collective-permute-start | bytes 3833864 | tf_op jit(solution)/shard_map/ppermute | solution.py:822
  18.4 24.1 %collective-permute-start.1 = (bf16[208,3072]{1,0:T(8,128)(2,1)S(1)}, bf16[208,3072]{1,0:T(8,128)(2,1)}, u32[]{:S(2)}, u32[]{:S(2)}) collective-permute-start(bf16[208,3072]{1,0:T(8,128)(2,1)S(1)} %pad_maximum_fusion), channel_id=1, source_target_pairs={{0,1},{1,0},{2,3},{3,2},{4,5},{5,4},{6,7},{7,6},{8,9},{9,8},{10,11... | collective-permute-start | bytes 3833864 | tf_op jit(solution)/shard_map/ppermute | solution.py:822
  19.3 11.8 %collective-permute-start.5 = (bf16[256,768]{1,0:T(8,128)(2,1)}, bf16[256,768]{1,0:T(8,128)(2,1)}, u32[]{:S(2)}, u32[]{:S(2)}) collective-permute-start(bf16[256,768]{1,0:T(8,128)(2,1)} %broadcast_select_fusion.4), channel_id=1, source_target_pairs={{0,4},{4,0},{8,12},{12,8},{16,20},{20,16},{24,28},{28,24},{1,5},{5... | collective-permute-start | bytes 1179656 | tf_op jit(solution)/shard_map/ppermute | solution.py:822
  20.9 20.8 %collective-permute-start.7 = (bf16[256,768]{1,0:T(8,128)(2,1)S(1)}, bf16[256,768]{1,0:T(8,128)(2,1)S(1)}, u32[]{:S(2)}, u32[]{:S(2)}) collective-permute-start(bf16[256,768]{1,0:T(8,128)(2,1)S(1)} %collective-permute-done.3), channel_id=1, source_target_pairs={{16,8},{20,12},{8,0},{12,4},{17,9},{21,13},{9,1},{13,5},{18,10},{2... | collective-permute-start | bytes 1179656 | tf_op jit(solution)/shard_map/ppermute | solution.py:826
  22.2 19.5 %collective-permute-start.8 = (bf16[256,768]{1,0:T(8,128)(2,1)S(1)}, bf16[256,768]{1,0:T(8,128)(2,1)S(1)}, u32[]{:S(2)}, u32[]{:S(2)}) collective-permute-start(bf16[256,768]{1,0:T(8,128)(2,1)S(1)} %collective-permute-done.4), channel_id=1, source_target_pairs={{8,16},{12,20},{16,24},{20,28},{9,17},{13,21},{17,25},{21,29},{10,... | collective-permute-start | bytes 1179656 | tf_op jit(solution)/shard_map/ppermute | solution.py:826
  33.9 13.5 %collective-permute-start.14 = (bf16[2,192,768]{2,1,0:T(8,128)(2,1)}, bf16[2,192,768]{2,1,0:T(8,128)(2,1)}, u32[]{:S(2)}, u32[]{:S(2)}) collective-permute-start(bf16[2,192,768]{2,1,0:T(8,128)(2,1)} %pad_maximum_fusion.1), channel_id=1, source_target_pairs={{0,1},{1,0},{2,3},{3,2},{4,5},{5,4},{6,7},{7,6},{8,9},{9,8},{10,11... | collective-permute-start | bytes 1769480 | tf_op jit(solution)/shard_map/ppermute | solution.py:822
  41.7 17.3 %collective-permute-start.6 = (bf16[208,3072]{1,0:T(8,128)(2,1)}, bf16[208,3072]{1,0:T(8,128)(2,1)}, u32[]{:S(2)}, u32[]{:S(2)}) collective-permute-start(bf16[208,3072]{1,0:T(8,128)(2,1)} %collective-permute-done.2), channel_id=1, source_target_pairs={{0,1},{1,0},{2,3},{3,2},{4,5},{5,4},{6,7},{7,6},{8,9},{9,8},{10,11... | collective-permute-start | bytes 3833864 | tf_op jit(solution)/shard_map/ppermute | solution.py:822
  42.5 13.4 %collective-permute-start.10 = (bf16[256,768]{1,0:T(8,128)(2,1)S(1)}, bf16[256,768]{1,0:T(8,128)(2,1)S(1)}, u32[]{:S(2)}, u32[]{:S(2)}) collective-permute-start(bf16[256,768]{1,0:T(8,128)(2,1)S(1)} %broadcast_select_fusion.2), channel_id=1, source_target_pairs={{16,24},{20,28},{8,0},{12,4},{17,25},{21,29},{9,1},{13,5},{18,26},... | collective-permute-start | bytes 1179656 | tf_op jit(solution)/shard_map/ppermute | solution.py:826
  44.5 47.3 %collective-permute-start.19 = (bf16[256,768]{1,0:T(8,128)(2,1)}, bf16[256,768]{1,0:T(8,128)(2,1)}, u32[]{:S(2)}, u32[]{:S(2)}) collective-permute-start(bf16[256,768]{1,0:T(8,128)(2,1)} %bitcast.17.refs_8_), channel_id=1, source_target_pairs={{0,2},{1,3},{2,0},{3,1},{4,6},{5,7},{6,4},{7,5},{8,10},{9,11},{10,... | collective-permute-start | bytes 1179656 | tf_op jit(solution)/shard_map/ppermute | solution.py:822
  46.9 11.5 %collective-permute-start.9 = (bf16[256,768]{1,0:T(8,128)(2,1)}, bf16[256,768]{1,0:T(8,128)(2,1)S(1)}, u32[]{:S(2)}, u32[]{:S(2)}) collective-permute-start(bf16[256,768]{1,0:T(8,128)(2,1)} %broadcast_select_fusion.3), channel_id=1, source_target_pairs={{0,4},{4,0},{8,12},{12,8},{16,20},{20,16},{24,28},{28,24},{1,5},{5... | collective-permute-start | bytes 1179656 | tf_op jit(solution)/shard_map/ppermute | solution.py:822
  49.3 43.0 %collective-permute-start.15 = (bf16[2,192,768]{2,1,0:T(8,128)(2,1)S(1)}, bf16[2,192,768]{2,1,0:T(8,128)(2,1)S(1)}, u32[]{:S(2)}, u32[]{:S(2)}) collective-permute-start(bf16[2,192,768]{2,1,0:T(8,128)(2,1)S(1)} %pad_maximum_fusion.2), channel_id=1, source_target_pairs={{0,2},{1,3},{2,0},{3,1},{4,6},{5,7},{6,4},{7,5},{8,10},{9,11},{10,... | collective-permute-start | bytes 1769480 | tf_op jit(solution)/shard_map/ppermute | solution.py:822
  58.4 10.4 %collective-permute-start.11 = (bf16[256,768]{1,0:T(8,128)(2,1)S(1)}, bf16[256,768]{1,0:T(8,128)(2,1)S(1)}, u32[]{:S(2)}, u32[]{:S(2)}) collective-permute-start(bf16[256,768]{1,0:T(8,128)(2,1)S(1)} %select_select_fusion), channel_id=1, source_target_pairs={{0,4},{4,0},{8,12},{12,8},{16,20},{20,16},{24,28},{28,24},{1,5},{5... | collective-permute-start | bytes 1179656 | tf_op jit(solution)/shard_map/ppermute | solution.py:822
  58.9 33.4 %collective-permute-start.13 = (bf16[256,768]{1,0:T(8,128)(2,1)}, bf16[256,768]{1,0:T(8,128)(2,1)S(1)}, u32[]{:S(2)}, u32[]{:S(2)}) collective-permute-start(bf16[256,768]{1,0:T(8,128)(2,1)} %bitcast.17.refs_8_), channel_id=1, source_target_pairs={{0,1},{1,0},{2,3},{3,2},{4,5},{5,4},{6,7},{7,6},{8,9},{9,8},{10,11... | collective-permute-start | bytes 1179656 | tf_op jit(solution)/shard_map/ppermute | solution.py:822
  91.8 11.8 %collective-permute-start.20 = (bf16[256,768]{1,0:T(8,128)(2,1)}, bf16[256,768]{1,0:T(8,128)(2,1)S(1)}, u32[]{:S(2)}, u32[]{:S(2)}) collective-permute-start(bf16[256,768]{1,0:T(8,128)(2,1)} %collective-permute-done.19), channel_id=1, source_target_pairs={{0,1},{1,0},{2,3},{3,2},{4,5},{5,4},{6,7},{7,6},{8,9},{9,8},{10,11... | collective-permute-start | bytes 1179656 | tf_op jit(solution)/shard_map/ppermute | solution.py:822
  92.3 11.3 %collective-permute-start.17 = (bf16[256,768]{1,0:T(8,128)(2,1)}, bf16[256,768]{1,0:T(8,128)(2,1)S(1)}, u32[]{:S(2)}, u32[]{:S(2)}) collective-permute-start(bf16[256,768]{1,0:T(8,128)(2,1)} %get-tuple-element.108), channel_id=1, source_target_pairs={{0,2},{1,3},{2,0},{3,1},{4,6},{5,7},{6,4},{7,5},{8,10},{9,11},{10,... | collective-permute-start | bytes 1179656 | tf_op jit(solution)/shard_map/ppermute | solution.py:822
  113.4 19.8 %collective-permute-start.21 = (bf16[256,768]{1,0:T(8,128)(2,1)}, bf16[256,768]{1,0:T(8,128)(2,1)}, u32[]{:S(2)}, u32[]{:S(2)}) collective-permute-start(bf16[256,768]{1,0:T(8,128)(2,1)} %bitcast.118), channel_id=1, source_target_pairs={{0,1},{1,0},{2,3},{3,2},{4,5},{5,4},{6,7},{7,6},{8,9},{9,8},{10,11... | collective-permute-start | bytes 1179656 | tf_op jit(solution)/shard_map/ppermute | solution.py:822
  116.2 11.3 %collective-permute-start.25 = (bf16[256,768]{1,0:T(8,128)(2,1)S(1)}, bf16[256,768]{1,0:T(8,128)(2,1)}, u32[]{:S(2)}, u32[]{:S(2)}) collective-permute-start(bf16[256,768]{1,0:T(8,128)(2,1)S(1)} %fusion.6), channel_id=1, source_target_pairs={{0,2},{1,3},{2,0},{3,1},{4,6},{5,7},{6,4},{7,5},{8,10},{9,11},{10,... | collective-permute-start | bytes 1179656 | tf_op jit(solution)/shard_map/ppermute | solution.py:822
  127.6 58.3 %all-to-all-start = ((bf16[8,192,768]{2,1,0:T(8,128)(2,1)}), bf16[8,192,768]{2,1,0:T(8,128)(2,1)S(1)}, u32[]{:S(2)}, u32[]{:S(2)}) async-start(bf16[8,192,768]{2,1,0:T(8,128)(2,1)} %ffn_grads.1), calls=%async_computation | async-start | bytes 4718592 | tf_op jit(solution)/shard_map/all_to_all | solution.py:993
  132.7 5.4 %collective-permute-start.16 = (bf16[256,768]{1,0:T(8,128)(2,1)}, bf16[256,768]{1,0:T(8,128)(2,1)S(1)}, u32[]{:S(2)}, u32[]{:S(2)}) collective-permute-start(bf16[256,768]{1,0:T(8,128)(2,1)} %bitcast.108), channel_id=1, source_target_pairs={{0,1},{1,0},{2,3},{3,2},{4,5},{5,4},{6,7},{7,6},{8,9},{9,8},{10,11... | collective-permute-start | bytes 1179656 | tf_op jit(solution)/shard_map/ppermute | solution.py:822
  134.3 44.0 %collective-permute-start.22 = (bf16[256,768]{1,0:T(8,128)(2,1)S(1)}, bf16[256,768]{1,0:T(8,128)(2,1)S(1)}, u32[]{:S(2)}, u32[]{:S(2)}) collective-permute-start(bf16[256,768]{1,0:T(8,128)(2,1)S(1)} %fusion.8), channel_id=1, source_target_pairs={{0,2},{1,3},{2,0},{3,1},{4,6},{5,7},{6,4},{7,5},{8,10},{9,11},{10,... | collective-permute-start | bytes 1179656 | tf_op jit(solution)/shard_map/ppermute | solution.py:822
  185.9 7.7 %collective-permute-start.34 = (bf16[2,4,208,384]{3,2,1,0:T(8,128)(2,1)}, bf16[2,4,208,384]{3,2,1,0:T(8,128)(2,1)}, u32[]{:S(2)}, u32[]{:S(2)}) collective-permute-start(bf16[2,4,208,384]{3,2,1,0:T(8,128)(2,1)} %get-tuple-element.166), channel_id=1, source_target_pairs={{0,1},{1,0},{2,3},{3,2},{4,5},{5,4},{6,7},{7,6},{8,9},{9,8},{10,11... | collective-permute-start | bytes 3833864 | tf_op jit(solution)/shard_map/ppermute | solution.py:822
  185.9 11.0 %collective-permute-start.32 = (bf16[2,4,208,384]{3,2,1,0:T(8,128)(2,1)}, bf16[2,4,208,384]{3,2,1,0:T(8,128)(2,1)}, u32[]{:S(2)}, u32[]{:S(2)}) collective-permute-start(bf16[2,4,208,384]{3,2,1,0:T(8,128)(2,1)} %get-tuple-element.164), channel_id=1, source_target_pairs={{0,1},{1,0},{2,3},{3,2},{4,5},{5,4},{6,7},{7,6},{8,9},{9,8},{10,11... | collective-permute-start | bytes 3833864 | tf_op jit(solution)/shard_map/ppermute | solution.py:822
  191.0 12.2 %collective-permute-start.28 = (bf16[256,768]{1,0:T(8,128)(2,1)}, bf16[256,768]{1,0:T(8,128)(2,1)S(1)}, u32[]{:S(2)}, u32[]{:S(2)}) collective-permute-start(bf16[256,768]{1,0:T(8,128)(2,1)} %get-tuple-element.158), channel_id=1, source_target_pairs={{0,4},{4,0},{8,12},{12,8},{16,20},{20,16},{24,28},{28,24},{1,5},{5... | collective-permute-start | bytes 1179656 | tf_op jit(solution)/shard_map/ppermute | solution.py:822
  192.4 19.2 %collective-permute-start.26 = (bf16[256,768]{1,0:T(8,128)(2,1)}, bf16[256,768]{1,0:T(8,128)(2,1)S(1)}, u32[]{:S(2)}, u32[]{:S(2)}) collective-permute-start(bf16[256,768]{1,0:T(8,128)(2,1)} %get-tuple-element.154), channel_id=1, source_target_pairs={{0,4},{4,0},{8,12},{12,8},{16,20},{20,16},{24,28},{28,24},{1,5},{5... | collective-permute-start | bytes 1179656 | tf_op jit(solution)/shard_map/ppermute | solution.py:822
  195.1 17.4 %collective-permute-start.35 = (bf16[4,208,384]{2,1,0:T(8,128)(2,1)S(1)}, bf16[4,208,384]{2,1,0:T(8,128)(2,1)S(1)}, u32[]{:S(2)}, u32[]{:S(2)}) collective-permute-start(bf16[4,208,384]{2,1,0:T(8,128)(2,1)S(1)} %fusion.10), channel_id=1, source_target_pairs={{0,2},{1,3},{2,0},{3,1},{4,6},{5,7},{6,4},{7,5},{8,10},{9,11},{10,... | collective-permute-start | bytes 1916936 | tf_op jit(solution)/shard_map/ppermute | solution.py:822
  198.2 25.9 %collective-permute-start.33 = (bf16[4,208,384]{2,1,0:T(8,128)(2,1)S(1)}, bf16[4,208,384]{2,1,0:T(8,128)(2,1)S(1)}, u32[]{:S(2)}, u32[]{:S(2)}) collective-permute-start(bf16[4,208,384]{2,1,0:T(8,128)(2,1)S(1)} %fusion.9), channel_id=1, source_target_pairs={{0,2},{1,3},{2,0},{3,1},{4,6},{5,7},{6,4},{7,5},{8,10},{9,11},{10,... | collective-permute-start | bytes 1916936 | tf_op jit(solution)/shard_map/ppermute | solution.py:822
  198.6 29.4 %collective-permute-start.41 = (bf16[1,192,768]{2,1,0:T(8,128)(2,1)S(1)}, bf16[1,192,768]{2,1,0:T(8,128)(2,1)}, u32[]{:S(2)}, u32[]{:S(2)}) collective-permute-start(bf16[1,192,768]{2,1,0:T(8,128)(2,1)S(1)} %maximum_bitcast_fusion.refs_1_), channel_id=1, source_target_pairs={{0,16},{4,20},{8,24},{12,28},{16,0},{20,4},{24,8},{28,12},{1,17},{... | collective-permute-start | bytes 884744 | tf_op jit(solution)/shard_map/ppermute | solution.py:822
  203.2 22.3 %collective-permute-start.31 = (bf16[256,768]{1,0:T(8,128)(2,1)S(1)}, bf16[256,768]{1,0:T(8,128)(2,1)S(1)}, u32[]{:S(2)}, u32[]{:S(2)}) collective-permute-start(bf16[256,768]{1,0:T(8,128)(2,1)S(1)} %copy-done.31), channel_id=1, source_target_pairs={{0,4},{4,0},{8,12},{12,8},{16,20},{20,16},{24,28},{28,24},{1,5},{5... | collective-permute-start | bytes 1179656 | tf_op jit(solution)/shard_map/ppermute | solution.py:822
  211.6 13.8 %collective-permute-start.29 = (bf16[256,768]{1,0:T(8,128)(2,1)S(1)}, bf16[256,768]{1,0:T(8,128)(2,1)S(1)}, u32[]{:S(2)}, u32[]{:S(2)}) collective-permute-start(bf16[256,768]{1,0:T(8,128)(2,1)S(1)} %add_convert_fusion.3), channel_id=1, source_target_pairs={{0,8},{4,12},{8,0},{12,4},{16,24},{20,28},{24,16},{28,20},{1,9},{5... | collective-permute-start | bytes 1179656 | tf_op jit(solution)/shard_map/ppermute | solution.py:822
  212.5 16.7 %collective-permute-start.27 = (bf16[256,768]{1,0:T(8,128)(2,1)}, bf16[256,768]{1,0:T(8,128)(2,1)}, u32[]{:S(2)}, u32[]{:S(2)}) collective-permute-start(bf16[256,768]{1,0:T(8,128)(2,1)} %get-tuple-element.155), channel_id=1, source_target_pairs={{0,4},{4,0},{8,12},{12,8},{16,20},{20,16},{24,28},{28,24},{1,5},{5... | collective-permute-start | bytes 1179656 | tf_op jit(solution)/shard_map/ppermute | solution.py:822
  226.4 10.5 %collective-permute-start.37 = (bf16[2,208,384]{2,1,0:T(8,128)(2,1)S(1)}, bf16[2,208,384]{2,1,0:T(8,128)(2,1)S(1)}, u32[]{:S(2)}, u32[]{:S(2)}) collective-permute-start(bf16[2,208,384]{2,1,0:T(8,128)(2,1)S(1)} %pad_maximum_fusion.5), channel_id=1, source_target_pairs={{0,4},{4,0},{8,12},{12,8},{16,20},{20,16},{24,28},{28,24},{1,5},{5... | collective-permute-start | bytes 958472 | tf_op jit(solution)/shard_map/ppermute | solution.py:822
  229.0 20.2 %collective-permute-start.42 = (bf16[2,192,768]{2,1,0:T(8,128)(2,1)S(1)}, bf16[2,192,768]{2,1,0:T(8,128)(2,1)S(1)}, u32[]{:S(2)}, u32[]{:S(2)}) collective-permute-start(bf16[2,192,768]{2,1,0:T(8,128)(2,1)S(1)} %pad_maximum_fusion.3), channel_id=1, source_target_pairs={{0,8},{4,12},{8,0},{12,4},{16,24},{20,28},{24,16},{28,20},{1,9},{5... | collective-permute-start | bytes 1769480 | tf_op jit(solution)/shard_map/ppermute | solution.py:822
  229.2 14.6 %collective-permute-start.36 = (bf16[2,208,384]{2,1,0:T(8,128)(2,1)S(1)}, bf16[2,208,384]{2,1,0:T(8,128)(2,1)S(1)}, u32[]{:S(2)}, u32[]{:S(2)}) collective-permute-start(bf16[2,208,384]{2,1,0:T(8,128)(2,1)S(1)} %pad_maximum_fusion.4), channel_id=1, source_target_pairs={{0,4},{4,0},{8,12},{12,8},{16,20},{20,16},{24,28},{28,24},{1,5},{5... | collective-permute-start | bytes 958472 | tf_op jit(solution)/shard_map/ppermute | solution.py:822
  237.0 12.1 %collective-permute-start.38 = (bf16[2,208,384]{2,1,0:T(8,128)(2,1)S(1)}, bf16[2,208,384]{2,1,0:T(8,128)(2,1)S(1)}, u32[]{:S(2)}, u32[]{:S(2)}) collective-permute-start(bf16[2,208,384]{2,1,0:T(8,128)(2,1)S(1)} %add_convert_fusion.7), channel_id=1, source_target_pairs={{0,8},{4,12},{8,0},{12,4},{16,24},{20,28},{24,16},{28,20},{1,9},{5... | collective-permute-start | bytes 958472 | tf_op jit(solution)/shard_map/ppermute | solution.py:822
  238.1 13.5 %collective-permute-start.49 = (bf16[1,192,768]{2,1,0:T(8,128)(2,1)S(1)}, bf16[1,192,768]{2,1,0:T(8,128)(2,1)S(1)}, u32[]{:S(2)}, u32[]{:S(2)}) collective-permute-start(bf16[1,192,768]{2,1,0:T(8,128)(2,1)S(1)} %maximum_bitcast_fusion.refs_1_), channel_id=1, source_target_pairs={{0,4},{4,0},{8,12},{12,8},{16,20},{20,16},{24,28},{28,24},{1,5},{5... | collective-permute-start | bytes 884744 | tf_op jit(solution)/shard_map/ppermute | solution.py:822
  243.8 13.9 %collective-permute-start.46 = (bf16[1,192,768]{2,1,0:T(8,128)(2,1)}, bf16[1,192,768]{2,1,0:T(8,128)(2,1)S(1)}, u32[]{:S(2)}, u32[]{:S(2)}) collective-permute-start(bf16[1,192,768]{2,1,0:T(8,128)(2,1)} %collective-permute-done.41.refs_5_), channel_id=1, source_target_pairs={{0,4},{4,0},{8,12},{12,8},{16,20},{20,16},{24,28},{28,24},{1,5},{5... | collective-permute-start | bytes 884744 | tf_op jit(solution)/shard_map/ppermute | solution.py:822
  249.3 8.1 %collective-permute-start.43 = (bf16[208,384]{1,0:T(8,128)(2,1)S(1)}, bf16[208,384]{1,0:T(8,128)(2,1)S(1)}, u32[]{:S(2)}, u32[]{:S(2)}) collective-permute-start(bf16[208,384]{1,0:T(8,128)(2,1)S(1)} %slice_bitcast_fusion), channel_id=1, source_target_pairs={{0,16},{4,20},{8,24},{12,28},{16,0},{20,4},{24,8},{28,12},{1,17},{... | collective-permute-start | bytes 479240 | tf_op jit(solution)/shard_map/ppermute | solution.py:822
  249.7 34.9 %collective-permute-start.30 = (bf16[256,768]{1,0:T(8,128)(2,1)S(1)}, bf16[256,768]{1,0:T(8,128)(2,1)S(1)}, u32[]{:S(2)}, u32[]{:S(2)}) collective-permute-start(bf16[256,768]{1,0:T(8,128)(2,1)S(1)} %add_convert_fusion.4), channel_id=1, source_target_pairs={{0,8},{4,12},{8,0},{12,4},{16,24},{20,28},{24,16},{28,20},{1,9},{5... | collective-permute-start | bytes 1179656 | tf_op jit(solution)/shard_map/ppermute | solution.py:822
  251.6 21.9 %collective-permute-start.50 = (bf16[2,192,768]{2,1,0:T(8,128)(2,1)S(1)}, bf16[2,192,768]{2,1,0:T(8,128)(2,1)S(1)}, u32[]{:S(2)}, u32[]{:S(2)}) collective-permute-start(bf16[2,192,768]{2,1,0:T(8,128)(2,1)S(1)} %collective-permute-done.42.refs_3_), channel_id=1, source_target_pairs={{0,4},{4,0},{8,12},{12,8},{16,20},{20,16},{24,28},{28,24},{1,5},{5... | collective-permute-start | bytes 1769480 | tf_op jit(solution)/shard_map/ppermute | solution.py:822
  257.4 12.3 %collective-permute-start.44 = (bf16[1,208,384]{2,1,0:T(8,128)(2,1)S(1)}, bf16[1,208,384]{2,1,0:T(8,128)(2,1)S(1)}, u32[]{:S(2)}, u32[]{:S(2)}) collective-permute-start(bf16[1,208,384]{2,1,0:T(8,128)(2,1)S(1)} %fusion.14.refs_1_), channel_id=1, source_target_pairs={{0,16},{4,20},{8,24},{12,28},{16,0},{20,4},{24,8},{28,12},{1,17},{... | collective-permute-start | bytes 479240 | tf_op jit(solution)/shard_map/ppermute | solution.py:822
  257.7 12.0 %collective-permute-start.47 = (bf16[1,208,384]{2,1,0:T(8,128)(2,1)S(1)}, bf16[1,208,384]{2,1,0:T(8,128)(2,1)S(1)}, u32[]{:S(2)}, u32[]{:S(2)}) collective-permute-start(bf16[1,208,384]{2,1,0:T(8,128)(2,1)S(1)} %fusion.14.refs_1_), channel_id=1, source_target_pairs={{0,4},{4,0},{8,12},{12,8},{16,20},{20,16},{24,28},{28,24},{1,5},{5... | collective-permute-start | bytes 479240 | tf_op jit(solution)/shard_map/ppermute | solution.py:822
  269.7 9.4 %collective-permute-start.51 = (bf16[1,208,384]{2,1,0:T(8,128)(2,1)S(1)}, bf16[1,208,384]{2,1,0:T(8,128)(2,1)S(1)}, u32[]{:S(2)}, u32[]{:S(2)}) collective-permute-start(bf16[1,208,384]{2,1,0:T(8,128)(2,1)S(1)} %collective-permute-done.44.refs_5_), channel_id=1, source_target_pairs={{0,4},{4,0},{8,12},{12,8},{16,20},{20,16},{24,28},{28,24},{1,5},{5... | collective-permute-start | bytes 479240 | tf_op jit(solution)/shard_map/ppermute | solution.py:822
  271.3 16.2 %collective-permute-start.45 = (bf16[256,768]{1,0:T(8,128)(2,1)S(1)}, bf16[256,768]{1,0:T(8,128)(2,1)S(1)}, u32[]{:S(2)}, u32[]{:S(2)}) collective-permute-start(bf16[256,768]{1,0:T(8,128)(2,1)S(1)} %add_convert_fusion.2), channel_id=1, source_target_pairs={{0,16},{4,20},{8,24},{12,28},{16,0},{20,4},{24,8},{28,12},{1,17},{... | collective-permute-start | bytes 1179656 | tf_op jit(solution)/shard_map/ppermute | solution.py:822
  271.3 12.7 %collective-permute-start.48 = (bf16[2,208,384]{2,1,0:T(8,128)(2,1)S(1)}, bf16[2,208,384]{2,1,0:T(8,128)(2,1)S(1)}, u32[]{:S(2)}, u32[]{:S(2)}) collective-permute-start(bf16[2,208,384]{2,1,0:T(8,128)(2,1)S(1)} %pad_maximum_fusion.6), channel_id=1, source_target_pairs={{0,8},{4,12},{8,0},{12,4},{16,24},{20,28},{24,16},{28,20},{1,9},{5... | collective-permute-start | bytes 958472 | tf_op jit(solution)/shard_map/ppermute | solution.py:822
  284.1 7.0 %collective-permute-start.52 = (bf16[2,208,384]{2,1,0:T(8,128)(2,1)S(1)}, bf16[2,208,384]{2,1,0:T(8,128)(2,1)S(1)}, u32[]{:S(2)}, u32[]{:S(2)}) collective-permute-start(bf16[2,208,384]{2,1,0:T(8,128)(2,1)S(1)} %collective-permute-done.48.refs_3_), channel_id=1, source_target_pairs={{0,4},{4,0},{8,12},{12,8},{16,20},{20,16},{24,28},{28,24},{1,5},{5... | collective-permute-start | bytes 958472 | tf_op jit(solution)/shard_map/ppermute | solution.py:822
  (50 other events, 391.8 us)

commit v5 on v4

--- a/solution.py
+++ b/solution.py
@@ -77,10 +77,16 @@
     pos = (lane % SPAN) + span * SPAN
     seg = (pos >= b1).astype(jnp.int32) + (pos >= b2).astype(jnp.int32) + (pos >= b3).astype(jnp.int32)
     first = lane < 128
-    below = jnp.where(first, tab_ref[NB // 2 - 1, 2 * pair], tab_ref[NB // 2 - 1, 2 * pair + 1])
-    above = jnp.where(first, tab_ref[NB - 1, 2 * pair], tab_ref[NB - 1, 2 * pair + 1])
+    far = [
+        jnp.where(
+            first,
+            jnp.broadcast_to(tab_ref[2 * pair : 2 * pair + 1, b : b + 1], (128, 256)),
+            jnp.broadcast_to(tab_ref[2 * pair + 1 : 2 * pair + 2, b : b + 1], (128, 256)),
+        )
+        for b in (NB // 2 - 1, NB - 1)
+    ]
     feat = jnp.where((row < 4) & (row != seg), -BIG, 0.0)
-    feat = jnp.where(row == 4, below, jnp.where(row == 5, above, feat))
+    feat = jnp.where(row == 4, far[0], jnp.where(row == 5, far[1], feat))
     if extra is not None:
         high = extra.astype(jnp.bfloat16).astype(jnp.float32)
         rest = extra - high
@@ -153,20 +159,34 @@
 
 def forward_kernel(counts, *refs):
     n_x, n_w = counts
-    ids_ref, order_ref, len_ref, tab_ref, table_t_ref, gain_ref = refs[:6]
-    x_refs, w_refs = refs[6 : 6 + n_x], refs[6 + n_x : 6 + n_x + n_w]
+    ids_ref, order_ref, len_ref = refs[:3]
+    refs = refs[3:]
+    x_refs, w_refs = refs[:n_x], refs[n_x : n_x + n_w]
     (
-        nf_ref, res_ref, o_ref, ot_ref, lse_ref, q_ref, k_out_ref, v_out_ref,
-        inv_ref, x_ref, w_ref, k_ref, v_ref, rhs_ref, near_ref, m_ref, l_ref, acc_ref, sem_x, sem_w, sem_k, sem_v,
-    ) = refs[6 + n_x + n_w :]
+        nf_ref, res_ref, o_ref, ot_ref, lse_ref, q_ref, tab_ref, gain_ref, k_out_ref, v_out_ref,
+        small_ref, inv_ref, x_ref, w_ref, k_ref, v_ref, rhs_ref, near_ref, m_ref, l_ref, acc_ref, sem_x, sem_w, sem_k, sem_v, sem_s,
+    ) = refs[n_x + n_w :]
     spans, own = order_ref.shape[1], q_ref.shape[0] // SPAN
     b1 = len_ref[0, 0]
     b2 = b1 + len_ref[0, 1]
     b3 = b2 + len_ref[0, 2]
     copies = load_pieces(expand(x_refs), x_ref, jnp.int32(0), sem_x)
     copies += load_pieces(expand(w_refs), w_ref, ids_ref[2], sem_w)
+    small_copies = []
+    for number, (ref, index, _) in enumerate(expand(w_refs)):
+        source = ref.at[index, pl.ds(ref.shape[1] - 16, 16)]
+        small_copies.append(pltpu.make_async_copy(source, small_ref.at[number], sem_s.at[number]))
+    for copy in small_copies:
+        copy.start()
     fill_inverse(order_ref, inv_ref, spans)
-    fill_near_bias(table_t_ref[...], near_ref)
+    for copy in small_copies:
+        copy.wait()
+    small = small_ref[0, :, 0 : D + 128].astype(jnp.float32)
+    for number in range(1, len(small_copies)):
+        small = small + small_ref[number, :, 0 : D + 128].astype(jnp.float32)
+    gain_ref[...] = small[0:8, 0:D]
+    tab_ref[...] = small[:, D : D + 128]
+    fill_near_bias(tab_ref[...].astype(jnp.bfloat16), near_ref)
     for copy in copies:
         copy.wait()
     own_rows = own * SPAN
@@ -300,7 +320,7 @@
     lax.fori_loop(0, spans // 2, settle, 0)
 
 
-def forward(ids, order, lengths, table, table_t, gains, xs, ws, local_rows):
+def forward(ids, order, lengths, xs, ws, local_rows):
     spans, own = order.shape[1], local_rows // SPAN
     rows = spans * SPAN
     n_x, n_w = sum(x.shape[0] for x in xs), sum(w.shape[0] for w in ws)
@@ -316,12 +336,15 @@
             jax.ShapeDtypeStruct((own, PAIRS, 128, 128), f32),
             jax.ShapeDtypeStruct((own, PAIRS, 1, 256), f32),
             jax.ShapeDtypeStruct((local_rows, D), bf),
+            jax.ShapeDtypeStruct((16, 128), f32),
+            jax.ShapeDtypeStruct((8, D), f32),
             jax.ShapeDtypeStruct((rows, D), bf),
             jax.ShapeDtypeStruct((rows, D), bf),
         ),
-        in_specs=[smem()] * 4 + [vmem()] * 2 + [hbm()] * (len(xs) + len(ws)),
-        out_specs=(vmem(),) * 6 + (hbm(),) * 2,
+        in_specs=[smem()] * 3 + [hbm()] * (len(xs) + len(ws)),
+        out_specs=(vmem(),) * 8 + (hbm(),) * 2,
         scratch_shapes=[
+            pltpu.VMEM((n_w, 16, 4 * D), bf),
             pltpu.SMEM((spans,), jnp.int32),
             pltpu.VMEM((rows, D), bf),
             pltpu.VMEM((D, 4 * D), bf),
@@ -336,9 +359,10 @@
             pltpu.SemaphoreType.DMA((n_w,)),
             pltpu.SemaphoreType.DMA((spans // 2,)),
             pltpu.SemaphoreType.DMA((spans // 2,)),
+            pltpu.SemaphoreType.DMA((n_w,)),
         ],
         compiler_params=pltpu.CompilerParams(vmem_limit_bytes=VMEM_LIMIT),
-    )(ids, order, lengths, table, table_t, gains, *xs, *ws)
+    )(ids, order, lengths, *xs, *ws)
 
 
 def ffn_kernel(counts, *refs):
@@ -516,39 +540,58 @@
 def finish_kernel(turns, *refs):
     count = len(turns)
     ids_ref = refs[0]
-    outs, tiny_ref, all_ref, sem = refs[1 + count : 5 + count], refs[5 + count], refs[6 + count], refs[7 + count]
+    outs, (attn_ref, ffn_ref, table_ref, all_ref, row_ref, sem) = refs[1 + count : 5 + count], refs[5 + count :]
     fetch_turns(with_turns(refs[1 : 1 + count], turns), all_ref, ids_ref[1], sem)
     size, wide = outs[0].shape[0], all_ref.shape[2]
     step = min(D, wide)
     for first in range(0, 4 * D, step):
-        value = all_ref[first // wide, :, first % wide : first % wide + step].astype(jnp.float32)
-        outs[first // D][:, first % D : first % D + step] = value[0:size]
-        tiny_ref[:, first : first + step] = value[size : size + 16]
-
-
-def finish(ids, arrays, turns):
-    count, high, wide = sum(a.shape[0] for a in arrays), *arrays[0].shape[1:]
-    f32 = jnp.float32
+        outs[first // D][:, first % D : first % D + step] = all_ref[
+            first // wide, 0:size, first % wide : first % wide + step
+        ].astype(jnp.float32)
+
+    def row(first):
+        cuts = [all_ref[i // wide, size : size + 16, i % wide : i % wide + step] for i in range(first, first + D, step)]
+        return jnp.concatenate(cuts, axis=1).astype(jnp.float32)[0:8]
+
+    back = D - ids_ref[4] * size
+    attn_ref[...] = pltpu.roll(row(0), back, 1)[0:1, 0:size]
+    ffn_ref[...] = pltpu.roll(row(D), back, 1)[0:1, 0:size]
+    table = all_ref[2 * D // wide, size : size + 16, 2 * D % wide : 2 * D % wide + 128].astype(jnp.float32)
+    row_ref[...] = jnp.concatenate([table, jnp.zeros((112, 128), jnp.float32)], axis=0).T
+    high = table_ref.shape[0]
+    table_ref[...] = row_ref[pl.ds(ids_ref[4] * high, high), 0:H]
+
+
+def finish(ids, arrays, turns, high):
+    count, tall, wide = sum(a.shape[0] for a in arrays), *arrays[0].shape[1:]
+    size, f32 = tall - 16, jnp.float32
     return pl.pallas_call(
         lambda *refs: finish_kernel(turns, *refs),
         name="finish",
         cost_estimate=cost(3),
-        out_shape=(jax.ShapeDtypeStruct((high - 16, D), f32),) * 4 + (jax.ShapeDtypeStruct((16, 4 * D), f32),),
+        out_shape=(jax.ShapeDtypeStruct((size, D), f32),) * 4
+        + (jax.ShapeDtypeStruct((1, size), f32),) * 2
+        + (jax.ShapeDtypeStruct((high, H), f32),),
         in_specs=[smem()] + [hbm()] * len(arrays),
-        out_specs=(vmem(),) * 5,
-        scratch_shapes=[pltpu.VMEM((count, high, wide), jnp.bfloat16), pltpu.SemaphoreType.DMA((count,))],
+        out_specs=(vmem(),) * 7,
+        scratch_shapes=[
+            pltpu.VMEM((count, tall, wide), jnp.bfloat16),
+            pltpu.VMEM((128, 128), f32),
+            pltpu.SemaphoreType.DMA((count,)),
+        ],
         compiler_params=pltpu.CompilerParams(vmem_limit_bytes=VMEM_LIMIT),
     )(ids, *arrays)
 
 
 def backward_kernel(counts, *refs):
-    n_x, n_w, n_dn, n_grad = counts
+    n_x, n_w, n_dnf, n_dn, n_grad = counts
     (
-        ids_ref, order_ref, len_ref, tab_ref, table_t_ref, gain_ref,
-        dnf_ref, res_ref, cot_ref, o_ref, ot_ref, lse_ref, q_ref, k_ref, v_ref,
-    ) = refs[:15]
-    x_refs, w_refs = refs[15 : 15 + n_x], refs[15 + n_x : 15 + n_x + n_w]
-    refs = refs[15 + n_x + n_w :]
+        ids_ref, order_ref, len_ref, tab_ref, gain_ref,
+        res_ref, cot_ref, o_ref, ot_ref, lse_ref, q_ref, k_ref, v_ref,
+    ) = refs[:13]
+    refs = refs[13:]
+    x_refs, w_refs, dnf_refs = refs[:n_x], refs[n_x : n_x + n_w], refs[n_x + n_w : n_x + n_w + n_dnf]
+    refs = refs[n_x + n_w + n_dnf :]
     dn_refs, mine_refs, shared_refs = refs[:n_dn], refs[n_dn : n_dn + n_grad], refs[n_dn + n_grad : n_dn + 2 * n_grad]
     (
         dres_ref, dn_own_ref,
@@ -567,11 +610,13 @@
         copies_x = load_pieces(expand(x_refs), x_ref, jnp.int32(0), sem_x)
         copies_w = load_pieces(expand(w_refs), w_ref, ids_ref[2], sem_w)
         fill_inverse(order_ref, inv_ref, spans)
-        fill_near_bias(table_t_ref[...], near_ref)
+        fill_near_bias(tab_ref[...].astype(jnp.bfloat16), near_ref)
         nacc_ref[...] = jnp.zeros_like(nacc_ref)
         far_ref[...] = jnp.zeros_like(far_ref)
 
-        res, dnf = res_ref[...], dnf_ref[...]
+        res, dnf = res_ref[...], dnf_refs[0][...].astype(jnp.float32)
+        for ref in dnf_refs[1:]:
+            dnf = dnf + ref[...].astype(jnp.float32)
         inv_rms = lax.rsqrt(jnp.mean(res * res, axis=1, keepdims=True) + EPS)
         dgain_ref[...] = jnp.zeros_like(dgain_ref)
         dgain_ref[1:2, :] = jnp.sum(dnf * res * inv_rms, axis=0, keepdims=True)
@@ -621,10 +666,18 @@
         x = x.astype(jnp.float32)
         return x * lax.rsqrt(jnp.mean(x * x, axis=1, keepdims=True) + EPS)
 
-    dkacc_ref[...] = jnp.zeros_like(dkacc_ref)
-    dvacc_ref[...] = jnp.zeros_like(dvacc_ref)
-    for p in range(PAIRS):
-        kt_ref[p, 0:128, :] = k_ref[:, p * 128 : p * 128 + 128].T
+    my_spans = [order_ref[0, ids_ref[0] * own + i] for i in range(own)]
+    used = jnp.bool_(False)
+    for span in my_spans:
+        low, high = key_range(span, b1, b2, b3, spans * SPAN)
+        used = used | ((t >= low) & (t < high))
+
+    @pl.when(used)
+    def ready():
+        dkacc_ref[...] = jnp.zeros_like(dkacc_ref)
+        dvacc_ref[...] = jnp.zeros_like(dvacc_ref)
+        for p in range(PAIRS):
+            kt_ref[p, 0:128, :] = k_ref[:, p * 128 : p * 128 + 128].T
 
     def span_body(i, span, near):
         feat = key_features(t, span, b1, b2, b3)
@@ -665,16 +718,16 @@
             waiting = (p, prob.astype(jnp.bfloat16), ds.astype(jnp.bfloat16))
         last(*waiting)
 
-    def one_span(i, used):
+    def one_span(i, carry):
         span = order_ref[0, ids_ref[0] * own + i]
         low, high = key_range(span, b1, b2, b3, spans * SPAN)
         needed = (t >= low) & (t < high)
         near = (2 * t + 2 >= span) & (2 * t <= span + 1)
         pl.when(needed & near)(lambda: span_body(i, span, True))
         pl.when(needed & jnp.logical_not(near))(lambda: span_body(i, span, False))
-        return used + needed.astype(jnp.int32)
-
-    used = lax.fori_loop(0, own, one_span, jnp.int32(0))
+        return carry
+
+    lax.fori_loop(0, own, one_span, 0)
     places, targets = [], []
     for half in range(2):
         slot = inv_ref[2 * t + half]
@@ -711,8 +764,8 @@
         store(0, zero[0:128])
         store(1, zero[0:128])
 
-    pl.when(used > 0)(fill)
-    pl.when(used == 0)(skip)
+    pl.when(used)(fill)
+    pl.when(jnp.logical_not(used))(skip)
 
 
     @pl.when(t == spans // 2 - 1)
@@ -773,21 +826,21 @@
                         ref[index, part, size:tall, :] = value
 
 
-def backward(ids, order, lengths, table, table_t, gains, dnf, res, cot, o, ot, lse, q, k, v, xs, ws, n_dn, n_fsdp):
+def backward(ids, order, lengths, table, gains, dnf, res, cot, o, ot, lse, q, k, v, xs, ws, n_dn, n_fsdp):
     spans, local_rows = order.shape[1], q.shape[0]
     rows, own = spans * SPAN, local_rows // SPAN
     n_x, n_w = sum(x.shape[0] for x in xs), sum(w.shape[0] for w in ws)
     bf, f32 = jnp.bfloat16, jnp.float32
     shapes = grad_shapes(n_fsdp, 1 if n_dn == 1 else 4)
     return pl.pallas_call(
-        lambda *refs: backward_kernel((len(xs), len(ws), n_dn, len(shapes)), *refs),
+        lambda *refs: backward_kernel((len(xs), len(ws), len(dnf), n_dn, len(shapes)), *refs),
         name="backward",
         cost_estimate=cost(36),
         grid=(spans // 2,),
         out_shape=(jax.ShapeDtypeStruct((rows // n_dn, D), bf),) * n_dn
         + shapes * 2
         + (jax.ShapeDtypeStruct((local_rows, D), f32),) * 2,
-        in_specs=[smem()] * 4 + [once()] * 9 + [by_chunk()] * 2 + [hbm()] * (len(xs) + len(ws)),
+        in_specs=[smem()] * 3 + [once()] * 8 + [by_chunk()] * 2 + [hbm()] * (len(xs) + len(ws)) + [once()] * len(dnf),
         out_specs=(once(),) * (n_dn + 2 * len(shapes) + 2),
         scratch_shapes=[
             pltpu.VMEM((local_rows, D), bf),
@@ -814,7 +867,7 @@
             pltpu.SemaphoreType.DMA((n_w,)),
         ],
         compiler_params=pltpu.CompilerParams(vmem_limit_bytes=VMEM_LIMIT),
-    )(ids, order, lengths, table, table_t, gains, dnf, res, cot, o, ot, lse, q, k, v, *xs, *ws)
+    )(ids, order, lengths, table, gains, res, cot, o, ot, lse, q, k, v, *xs, *ws, *dnf)
 
 
 def swap(x, axis, bit):
@@ -855,7 +908,8 @@
 
 def scatter_pairs(keep, send):
     got = swap(send, "fsdp", 1)
-    return keep[0], got[0], swap(add(keep[1], got[1]), "fsdp", 2)
+    far = add(keep[1], got[1])
+    return (keep[0], got[0], swap(far, "fsdp", 2)), far
 
 
 TURNS = ((0,), (1,), (2, 6), (3, 7), (4,), (5,))
@@ -863,8 +917,16 @@
 
 def tail(dn, mine, shared, ffn_own, high):
     g7, g3 = swap(dn[7], "ctx", 1), swap(dn[3], "ctx", 1)
+    (mine, _), (shared, _) = scatter_pairs(*mine), scatter_pairs(*shared)
+    top, blocks = ffn_own[: D // 8], ffn_own[D // 8 :]
+    blocks = [blocks[48 * (r // 2) : 48 * (r // 2) + 48, 384 * (r % 2) : 384 * (r % 2) + 384] for r in range(4)]
+    side = swap(jnp.stack([blocks[1], blocks[3]]), "fsdp", 1)
+    across = swap(jnp.stack([blocks[2], side[1]]), "fsdp", 2)
+    ffn_own = jnp.concatenate(
+        [top, jnp.concatenate([blocks[0], side[0]], axis=1), jnp.concatenate([across[0], across[1]], axis=1)]
+    )[None]
     ffn4 = swap(ffn_own, "ctx", 4)
-    mine, shared = (add(*scatter_pairs(*g)) for g in (mine, shared))
+    mine, shared = add(*mine), add(*shared)
     g5, g1 = swap(after(dn[5], g7), "ctx", 1), swap(after(dn[1], g3), "ctx", 1)
     n4 = swap(add(dn[6], g7), "ctx", 2)
     ffn_pair = swap(jnp.concatenate([ffn_own, ffn4]), "ctx", 2)
@@ -883,7 +945,7 @@
     own4 = swap(own, "ctx", 4)
     own1 = swap(after(own, ffn5), "ctx", 1)
     pair = swap(jnp.concatenate([own, own4]), "ctx", 2)
-    own5 = swap(after(own4, own1), "ctx", 1)
+    own5 = swap(own4, "ctx", 1)
     others = swap(after(pair, ffn_others, own5), "ctx", 1)
     far = swap(after(add(dn[4], g5, n4), own4), "ctx", 4)
     return (
@@ -893,7 +955,7 @@
     )
 
 
-def line_gather(x, x1, early):
+def line_gather(x, x1, early, late):
     line = lax.axis_index("ctx") // 2
     up1, down1 = hop(x, [(0, 1), (1, 2), (2, 3)]), hop(x, [(3, 2), (2, 1), (1, 0)])
     z1 = jnp.where(line % 2 == 0, down1, up1)
@@ -905,7 +967,7 @@
     x5 = swap(z2, "ctx", 1)
     far = hop(jnp.where(line == 2, up2, down2), [(2, 3), (1, 0)])
     z3 = jnp.where(line == 1, down1, jnp.where(line == 2, up1, far))
-    return [x, x1, z1, x3, z2, x5, z3, swap(after(z3, x5), "ctx", 1)], x3, x5
+    return [x, x1, z1, x3, z2, x5, z3, swap(after(z3, x5, late), "ctx", 1)], (far, x5)
 
 
 def on_device(
@@ -932,48 +994,42 @@
     bf, f32 = jnp.bfloat16, jnp.float32
     x, cot = tokens[0], cotangent[0]
     width = w_ffn_out.shape[0]
-    table_size = rel_table.size
-    small = jnp.concatenate([gain_attn, gain_ffn, rel_table.reshape(-1)])
-    small = jnp.pad(small[None], ((0, 15), (0, 4 * D - small.shape[0])))
-    weights = jnp.concatenate([jnp.concatenate([w_query, w_key, w_value, w_out], axis=1), small], axis=0)
+    high = rel_table.shape[0]
+    spread = jnp.zeros((16, 4 * D), bf)
+    spread = lax.dynamic_update_slice(spread, gain_attn[None], (0, shard * own_rows))
+    spread = lax.dynamic_update_slice(spread, gain_ffn[None], (1, shard * own_rows))
+    spread = lax.dynamic_update_slice(spread, rel_table.T, (0, D + shard * high))
+    weights = jnp.concatenate([jnp.concatenate([w_query, w_key, w_value, w_out], axis=1), spread], axis=0)[None]
+    (weights,) = lax.optimization_barrier((weights,))
 
     if fast:
-        ids = jnp.stack([place, place, shard, shard, jnp.int32(n_ctx)])
+        ids = jnp.stack([place, place, shard, shard, shard])
         order = [shard ^ r for r in range(4)]
         tokens_got = swap(x, "ctx", 1)
         w2 = swap(weights, "fsdp", 2)
         w1 = swap(after(weights, tokens_got), "fsdp", 1)
-        gathered, third, fifth = line_gather(x, tokens_got, w1)
+        columns = [block(w_in, order[r], 4, 1) for r in range(4)]
+        columns = [columns[0], columns[2], jnp.stack([columns[1], columns[3]])]
+        gathered, fifth = line_gather(x, tokens_got, w1, columns)
         xs = [p[None] for p in gathered]
-        w3 = swap(after(w2, third), "fsdp", 1)
-        ws = [p[None] for p in (weights, w1, w2, w3)]
-        w_in, cot_late = after((w_in, cot), third)
-        columns = [block(w_in, order[r], 4, 1) for r in range(4)]
-        side = swap(jnp.stack([columns[1], columns[3]]), "fsdp", 1)
-        smalls = jnp.stack([p[own_rows] for p in (weights, w1, w2, w3)])
-        smalls = jnp.stack([lax.dynamic_index_in_dim(smalls, order[i], 0, False) for i in range(4)])
-        win2 = swap(after(jnp.stack([columns[2], side[1]]), w2), "fsdp", 2)
+        w3 = swap(after(w2, gathered[7]), "fsdp", 1)
+        ws = [weights, w1, w2, w3]
+        cot_late = after(cot, *fifth)
+        side = swap(after(columns[2], *fifth), "fsdp", 1)
+        win2 = swap(after(jnp.stack([columns[1], side[1]]), w2), "fsdp", 2)
         wins = [columns[0][None], side[:1], win2]
-        cot1 = swap(after(cot, fifth), "fsdp", 1)
+        cot1 = swap(after(cot, *fifth), "fsdp", 1)
         cot2 = swap(after(cot_late, w2), "fsdp", 2)
         cots = [p[None] for p in (cot, cot1, cot2, swap(cot2, "fsdp", 1))]
     else:
-        ids = jnp.stack([place, jnp.int32(0), jnp.int32(0), jnp.int32(0), jnp.int32(n_ctx)])
+        ids = jnp.stack([place, jnp.int32(0), jnp.int32(0), jnp.int32(0), shard])
         xs = [lax.all_gather(x, "ctx", axis=0)]
-        ws = [lax.all_gather(weights, "fsdp", axis=0)]
-        smalls = ws[0][:, own_rows]
+        ws = [lax.all_gather(weights[0], "fsdp", axis=0)]
         parts = jnp.stack([w_in[:, i * width : (i + 1) * width] for i in range(n_fsdp)])
         wins = [lax.all_to_all(parts, "fsdp", 0, 0)]
         cots = [lax.all_gather(cot, "fsdp", axis=0)]
 
-    gains = jnp.stack([smalls[:, :own_rows].reshape(D), smalls[:, own_rows : 2 * own_rows].reshape(D)]).astype(f32)
-    table_bf = smalls[:, 2 * own_rows : 2 * own_rows + table_size].reshape(NB, H)
-    table = table_bf.astype(f32)
-    table_t = jnp.pad(table_bf.T, ((0, 16 - H), (0, 128 - NB)))
-
-    nf, res, o, ot, lse, q, k, v = forward(
-        ids, span_order, lengths, table, table_t, gains, xs, ws, local_rows
-    )
+    nf, res, o, ot, lse, q, table, gains, k, v = forward(ids, span_order, lengths, xs, ws, local_rows)
 
     if fast:
         nfs = [nf[None], swap(nf, "fsdp", 1)[None], swap(nf, "fsdp", 2)[None]]
@@ -986,13 +1042,15 @@
     acts, dups = [h[0] for h in halves], [h[1] for h in halves]
     dns, outs = [d for h in halves for d in h[2]], [d for h in halves for d in h[3]]
     if fast:
-        a, b, c, far = scatter_four([p[0] for p in dns])
-        dnf = a.astype(f32) + b.astype(f32) + c.astype(f32)
+        first, third = swap(dns[1][0], "fsdp", 1), swap(dns[3][0], "fsdp", 1)
+        far = add(dns[2][0], third)
+        c = swap(far, "fsdp", 2)
+        dnf = [dns[0][0], first, c]
         ffn_parts = ffn_grads(ids, nfs, cots, after(acts, far), dups, n_fsdp, 8)
         dnf = after(dnf, *ffn_parts)
         ffn_got = lax.all_to_all(after(ffn_parts[0], c), "ctx", 0, 0)
     else:
-        dnf = lax.psum_scatter(dns[0], "fsdp", scatter_dimension=0).astype(f32)
+        dnf = [lax.psum_scatter(dns[0], "fsdp", scatter_dimension=0)]
         grad_ffn_out, grad_in = ffn_grads(ids, nfs, cots, acts, dups, n_fsdp, 1)
         grad_in = jnp.transpose(lax.all_to_all(grad_in, "fsdp", 0, 0), (1, 0, 2)).reshape(own_rows, n_fsdp * width)
         grad_ffn_out, grad_in = (lax.psum(g, "ctx").astype(f32) for g in (grad_ffn_out, grad_in))
@@ -1003,22 +1061,14 @@
         out_terms = [lax.psum_scatter(outs[0], "fsdp", scatter_dimension=0)]
 
     *got, dres, dn_own = backward(
-        ids, span_order, lengths, table, table_t, gains, dnf, res, cot, o, ot, lse, q, k, v, xs, ws,
+        ids, span_order, lengths, table, gains, dnf, res, cot, o, ot, lse, q, k, v, xs, ws,
         8 if fast else 1, n_fsdp,
     )
     if fast:
         got = after(got, ffn_got, *out_terms)
         dn, mine, shared = got[:8], got[8:10], got[10:12]
         ffn_own = jnp.sum(ffn_got.astype(f32), axis=0).astype(bf)
-        blocks = ffn_own[D // 8 :]
-        blocks = [blocks[48 * (r // 2) : 48 * (r // 2) + 48, 384 * (r % 2) : 384 * (r % 2) + 384] for r in range(4)]
-        side = swap(jnp.stack([blocks[1], blocks[3]]), "fsdp", 1)
-        across = swap(jnp.stack([blocks[2], side[1]]), "fsdp", 2)
-        ffn_own = jnp.concatenate(
-            [ffn_own[: D // 8], jnp.concatenate([blocks[0], side[0]], axis=1),
-             jnp.concatenate([across[0], across[1]], axis=1)]
-        )
-        terms, ffn_all, grads = tail(dn, mine, shared, ffn_own[None], place >= 4)
+        terms, ffn_all, grads = tail(dn, mine, shared, ffn_own, place >= 4)
         d_normed = dn_own
         for term in terms:
             d_normed = d_normed + term.astype(f32)
@@ -1026,8 +1076,9 @@
     else:
         d_normed = dn_own + lax.psum_scatter(got[0].reshape(n_ctx, local_rows, D), "ctx", scatter_dimension=0).astype(f32)
         grads = [lax.psum(lax.psum_scatter(g, "fsdp", scatter_dimension=0), "ctx") for g in got[1:]]
-    g_query, g_out, g_key, g_value, tiny = finish(ids, grads, TURNS if fast else ((0,), (1,)))
-    table_row = tiny[:H, 2 * D : 2 * D + NB].T
+    g_query, g_out, g_key, g_value, g_attn, g_ffn, g_table = finish(
+        ids, grads, TURNS if fast else ((0,), (1,)), rel_table.shape[0]
+    )
 
     output = res
     for term in out_terms:
@@ -1047,9 +1098,9 @@
         g_out,
         grad_in,
         grad_ffn_out,
-        block(tiny[0, :D], shard, n_fsdp),
-        block(tiny[0, D : 2 * D], shard, n_fsdp),
-        block(table_row, shard, n_fsdp),
+        g_attn[0],
+        g_ffn[0],
+        g_table,
     )
 
 

time: 300 us -> 284 us (0.947)
  other arithmetic: 23.9 us -> 14.4 us
  Pallas kernels: 91.6 us -> 83.7 us
  local copies, waits for them, and re-layouts: 17 us -> 11.8 us
  starting transfers between devices: 51.6 us -> 55.9 us
  waiting for transfers between devices: 113 us -> 117 us
    ppermute x48, waiting for transfers between devices: 100 us -> 81.9 us  [swap(): return lax.ppermute(x, axis, [(i, i ^ bit) for i in range(count)])]
    ppermute x5, waiting for transfers between devices: 5.38 us -> 19.5 us  [hop(): lax.ppermute(x, 'ctx', [(2 * a + i, 2 * b + i) for a, b in pairs for i in...]
    all_to_all x1, waiting for transfers between devices: 7.67 us -> 15.5 us  [on_device(): ffn_got = lax.all_to_all(after(ffn_parts[0], c), 'ctx', 0, 0)]
    pallas_call x1, Pallas kernels: 40.1 us -> 34.8 us  [backward(): pl.pallas_call(lambda *refs: backward_kernel((len(xs), len(ws), len(dnf),...]
    slice x10 -> x4, local copies, waits for them, and re-layouts: 5.74 us -> 0.81 us  [the longest x1 0.78 us: on_device(): win2 = swap(after(jnp.stack([columns[1], side[1]]), w2), 'fsdp', 2)]
  transfers between devices with their start and end apart: 54 -> 54, of which waited for: 26 -> 33; matrix products, arithmetic and copies ran while one was open for 11% -> 7% of each run, Pallas kernels for 27% -> 26%
where the time goes in v5:
time: 284 us
  waiting for transfers between devices  117 us (41%)
  Pallas kernels  83.7 us (29%)
  starting transfers between devices  55.9 us (20%)
  other arithmetic  14.4 us (5%)
  local copies, waits for them, and re-layouts  11.8 us (4%)
    ppermute x48, waiting for transfers between devices, swap(): return lax.ppermute(x, axis, [(i, i ^ bit) for i in range(count)])  81.9 us
    ppermute x48, starting transfers between devices, swap(): return lax.ppermute(x, axis, [(i, i ^ bit) for i in range(count)])  39.1 us
    pallas_call x1, Pallas kernels, backward(): pl.pallas_call(lambda *refs: backward_kernel((len(xs), len(ws), len(dnf),...  34.8 us
    pallas_call x1, Pallas kernels, forward(): pl.pallas_call(lambda *refs: forward_kernel((len(xs), len(ws)), *refs), n...  19.6 us
    ppermute x5, waiting for transfers between devices, hop(): lax.ppermute(x, 'ctx', [(2 * a + i, 2 * b + i) for a, b in pairs for i in...  19.5 us
    all_to_all x1, waiting for transfers between devices, on_device(): ffn_got = lax.all_to_all(after(ffn_parts[0], c), 'ctx', 0, 0)  15.5 us
    pallas_call x2, Pallas kernels, ffn(): pl.pallas_call(lambda *refs: ffn_kernel((count, len(wins)), *refs), name=...  14 us
    ppermute x5, starting transfers between devices, hop(): lax.ppermute(x, 'ctx', [(2 * a + i, 2 * b + i) for a, b in pairs for i in...  9.11 us
  transfers between devices with their start and end apart: 54, of which 33 were waited for; matrix products, arithmetic and copies ran while one was open for 7% of the time, Pallas kernels for 26%

profile of v5, /device:TPU:0, one launch (start us, length us, event | category | flops | bytes accessed | tf_op | source)
XLA Modules:
  0.0 284.3 jit_solution(8427414624660140620)
XLA Ops:
  0.6 3.0 %collective-permute-start = (bf16[256,768]{1,0:T(8,128)(2,1)}, bf16[256,768]{1,0:T(8,128)(2,1)S(1)}, u32[]{:S(2)}, u32[]{:S(2)}) collective-permute-start(bf16[256,768]{1,0:T(8,128)(2,1)} %bitcast.81), channel_id=1, source_target_pairs={{0,4},{4,0},{8,12},{12,8},{16,20},{20,16},{24,28},{28,24},{1,5},{5... | collective-permute-start | bytes 1179656 | tf_op jit(solution)/shard_map/ppermute | solution.py:875
  4.9 4.6 %collective-permute-start.2 = (bf16[256,768]{1,0:T(8,128)(2,1)}, bf16[256,768]{1,0:T(8,128)(2,1)S(1)}, u32[]{:S(2)}, u32[]{:S(2)}) collective-permute-start(bf16[256,768]{1,0:T(8,128)(2,1)} %bitcast.83), channel_id=1, source_target_pairs={{0,8},{4,12},{8,16},{12,20},{16,24},{20,28},{1,9},{5,13},{9,17},{1... | collective-permute-start | bytes 1179656 | tf_op jit(solution)/shard_map/ppermute | solution.py:879
  12.5 1.4 maximum_bitcast_fusion.refs_11_.refs_21_
  14.0 2.3 collective-permute-done.1
  20.1 1.7 collective-permute-start.10
  21.8 7.8 %collective-permute-done.4 = bf16[256,768]{1,0:T(8,128)(2,1)S(1)} collective-permute-done((bf16[256,768]{1,0:T(8,128)(2,1)S(1)}, bf16[256,768]{1,0:T(8,128)(2,1)S(1)}, u32[]{:S(2)}, u32[]{:S(2)}) %collective-permute-start.4) | collective-permute-done | bytes 393248 | tf_op jit(solution)/shard_map/ppermute | solution.py:879
  33.2 2.0 dynamic-slice_bitcast_fusion.1
  35.3 8.1 %collective-permute-done.8 = bf16[256,768]{1,0:T(8,128)(2,1)} collective-permute-done((bf16[256,768]{1,0:T(8,128)(2,1)}, bf16[256,768]{1,0:T(8,128)(2,1)}, u32[]{:S(2)}, u32[]{:S(2)}) %collective-permute-start.8) | collective-permute-done | bytes 393248 | tf_op jit(solution)/shard_map/ppermute | solution.py:879
  45.6 3.0 %collective-permute-done.10.refs_13_.refs_23_ = bf16[1,208,3072]{2,1,0:T(8,128)(2,1)} collective-permute-done((bf16[1,208,3072]{2,1,0:T(8,128)(2,1)S(1)}, bf16[1,208,3072]{2,1,0:T(8,128)(2,1)}, u32[]{:S(2)}, u32[]{:S(2)}) %collective-permute-start.10) | collective-permute-done | bytes 1277984 | tf_op jit(solution)/shard_map/ppermute | solution.py:875
  48.6 3.8 %collective-permute-done.9 = bf16[256,768]{1,0:T(8,128)(2,1)S(1)} collective-permute-done((bf16[256,768]{1,0:T(8,128)(2,1)S(1)}, bf16[256,768]{1,0:T(8,128)(2,1)S(1)}, u32[]{:S(2)}, u32[]{:S(2)}) %collective-permute-start.9) | collective-permute-done | bytes 393248 | tf_op jit(solution)/shard_map/ppermute | solution.py:875
  53.7 1.5 collective-permute-start.19
  57.2 1.6 collective-permute-start.15
  59.9 19.6 %forward.1 = (bf16[256,768]{1,0:T(8,128)(2,1)}, f32[256,768]{1,0:T(8,128)}, bf16[256,768]{1,0:T(8,128)(2,1)}, f32[2,6,128,128]{3,2,1,0:T(8,128)}, f32[2,6,1,256]...) custom-call(s32[5]{0:T(128)} %stack.56.refs_0_, ...), custom_call_target="tpu_custom_call" | custom-call | flops 22000001024 | bytes 22000000 | tf_op jit(solution)/shard_map/forward/pallas_call | solution.py:328
  79.5 4.6 %collective-permute-start.12 = (bf16[256,768]{1,0:T(8,128)(2,1)}, bf16[256,768]{1,0:T(8,128)(2,1)S(1)}, u32[]{:S(2)}, u32[]{:S(2)}) collective-permute-start(bf16[256,768]{1,0:T(8,128)(2,1)} %get-tuple-element.114), channel_id=1, source_target_pairs={{0,1},{1,0},{2,3},{3,2},{4,5},{5,4},{6,7},{7,6},{8,9},{9,8},{10,11... | collective-permute-start | bytes 1179656 | tf_op jit(solution)/shard_map/ppermute | solution.py:875
  84.2 1.4 collective-permute-done.12
  86.3 7.0 %ffn.2 = (bf16[2,256,768]{2,1,0:T(8,128)(2,1)}, bf16[2,256,768]{2,1,0:T(8,128)(2,1)}, bf16[1,256,768]{2,1,0:T(8,128)(2,1)}, bf16[1,256,768]{2,1,0:T(8,128)(2,1)}...) custom-call(s32[5]{0:T(128)} %stack.56.refs_0_, bf16[1,256,768]{2,1,0:T(8,128)(2,1)} %bitcast.106, ...), custom_call_target="tpu_custom_call" | custom-call | flops 6000000000 | bytes 6000000 | tf_op jit(solution)/shard_map/ffn/pallas_call | solution.py:399
  93.3 2.4 collective-permute-done.17
  95.8 1.7 collective-permute-done.18.refs_2_.refs_4_
  98.3 7.0 %ffn.3 = (bf16[2,256,768]{2,1,0:T(8,128)(2,1)}, bf16[2,256,768]{2,1,0:T(8,128)(2,1)}, bf16[1,256,768]{2,1,0:T(8,128)(2,1)}, bf16[1,256,768]{2,1,0:T(8,128)(2,1)}...) custom-call(s32[5]{0:T(128)} %stack.56.refs_0_, bf16[1,256,768]{2,1,0:T(8,128)(2,1)} %bitcast.113, ...), custom_call_target="tpu_custom_call" | custom-call | flops 6000000000 | bytes 6000000 | tf_op jit(solution)/shard_map/ffn/pallas_call | solution.py:399
  105.5 1.8 collective-permute-done.24
  108.7 6.9 %ffn_grads.1 = bf16[8,192,768]{2,1,0:T(8,128)(2,1)} custom-call(s32[5]{0:T(128)} %stack.56.refs_0_, bf16[1,256,768]{2,1,0:T(8,128)(2,1)} %bitcast.107, bf16[1,256,768]{2,1,0:T(8,128)(2,1)} %bitcast.109, bf16[1,256,768]{2,1,0:T(8,128)(2,1)} %bitcast.114, bf16[1,256,768]{2,1,0:T(8,128)(2,1)} %copy-done.34, bf16[1,256,768]{2,1,0:T(8,128)(2,1)} %refs_5_.1, ...), custom_call_target="tpu_custom_call" | custom-call | flops 6000000000 | bytes 6000000 | tf_op jit(solution)/shard_map/ffn_grads/pallas_call | solution.py:464
  115.7 4.1 %collective-permute-done.25.refs_27_ = bf16[256,768]{1,0:T(8,128)(2,1)} collective-permute-done((bf16[256,768]{1,0:T(8,128)(2,1)S(1)}, bf16[256,768]{1,0:T(8,128)(2,1)}, u32[]{:S(2)}, u32[]{:S(2)}) %collective-permute-start.25) | collective-permute-done | bytes 393248 | tf_op jit(solution)/shard_map/ppermute | solution.py:875
  119.7 7.7 %all-to-all-start = ((bf16[8,192,768]{2,1,0:T(8,128)(2,1)}), bf16[8,192,768]{2,1,0:T(8,128)(2,1)S(1)}, u32[]{:S(2)}, u32[]{:S(2)}) async-start(bf16[8,192,768]{2,1,0:T(8,128)(2,1)} %ffn_grads.1), calls=%async_computation | async-start | bytes 4718592 | tf_op jit(solution)/shard_map/all_to_all | solution.py:1051
  130.7 34.8 %backward.1 = (bf16[256,768]{1,0:T(8,128)(2,1)}, bf16[256,768]{1,0:T(8,128)(2,1)}, bf16[256,768]{1,0:T(8,128)(2,1)}, bf16[256,768]{1,0:T(8,128)(2,1)}, bf16[256,...) custom-call(s32[5]{0:T(128)} %stack.56.refs_0_, ...), custom_call_target="tpu_custom_call" | custom-call | flops 35999997952 | bytes 36000000 | tf_op jit(solution)/shard_map/backward/pallas_call | solution.py:835
  165.5 15.5 %all-to-all-done = bf16[8,192,768]{2,1,0:T(8,128)(2,1)S(1)} async-done(((bf16[8,192,768]{2,1,0:T(8,128)(2,1)}), bf16[8,192,768]{2,1,0:T(8,128)(2,1)S(1)}, u32[]{:S(2)}, u32[]{:S(2)}) %all-to-all-start) | async-done | bytes 2359328 | tf_op jit(solution)/shard_map/all_to_all | solution.py:1051
  182.1 2.1 collective-permute-done.39
  186.6 2.0 collective-permute-done.40
  188.7 1.4 fusion.8
  191.8 1.8 collective-permute-start.35
  193.7 3.1 %collective-permute-done.28 = bf16[256,768]{1,0:T(8,128)(2,1)S(1)} collective-permute-done((bf16[256,768]{1,0:T(8,128)(2,1)}, bf16[256,768]{1,0:T(8,128)(2,1)S(1)}, u32[]{:S(2)}, u32[]{:S(2)}) %collective-permute-start.28) | collective-permute-done | bytes 393248 | tf_op jit(solution)/shard_map/ppermute | solution.py:875
  197.0 7.2 %collective-permute-done.26 = bf16[256,768]{1,0:T(8,128)(2,1)S(1)} collective-permute-done((bf16[256,768]{1,0:T(8,128)(2,1)}, bf16[256,768]{1,0:T(8,128)(2,1)S(1)}, u32[]{:S(2)}, u32[]{:S(2)}) %collective-permute-start.26) | collective-permute-done | bytes 393248 | tf_op jit(solution)/shard_map/ppermute | solution.py:875
  205.4 2.1 collective-permute-done.33
  210.1 9.0 %collective-permute-done.35 = bf16[4,208,384]{2,1,0:T(8,128)(2,1)S(1)} collective-permute-done((bf16[4,208,384]{2,1,0:T(8,128)(2,1)S(1)}, bf16[4,208,384]{2,1,0:T(8,128)(2,1)S(1)}, u32[]{:S(2)}, u32[]{:S(2)}) %collective-permute-start.35) | collective-permute-done | bytes 639008 | tf_op jit(solution)/shard_map/ppermute | solution.py:875
  225.0 6.4 %collective-permute-done.37 = bf16[2,208,384]{2,1,0:T(8,128)(2,1)S(1)} collective-permute-done((bf16[2,208,384]{2,1,0:T(8,128)(2,1)S(1)}, bf16[2,208,384]{2,1,0:T(8,128)(2,1)S(1)}, u32[]{:S(2)}, u32[]{:S(2)}) %collective-permute-start.37) | collective-permute-done | bytes 319520 | tf_op jit(solution)/shard_map/ppermute | solution.py:875
  234.5 3.7 %collective-permute-done.36 = bf16[2,208,384]{2,1,0:T(8,128)(2,1)S(1)} collective-permute-done((bf16[2,208,384]{2,1,0:T(8,128)(2,1)S(1)}, bf16[2,208,384]{2,1,0:T(8,128)(2,1)S(1)}, u32[]{:S(2)}, u32[]{:S(2)}) %collective-permute-start.36) | collective-permute-done | bytes 319520 | tf_op jit(solution)/shard_map/ppermute | solution.py:875
  238.2 3.9 %collective-permute-done.38 = bf16[2,208,384]{2,1,0:T(8,128)(2,1)S(1)} collective-permute-done((bf16[2,208,384]{2,1,0:T(8,128)(2,1)S(1)}, bf16[2,208,384]{2,1,0:T(8,128)(2,1)S(1)}, u32[]{:S(2)}, u32[]{:S(2)}) %collective-permute-start.38) | collective-permute-done | bytes 319520 | tf_op jit(solution)/shard_map/ppermute | solution.py:875
  242.8 1.8 collective-permute-start.30
  244.6 1.4 collective-permute-start.46
  246.6 3.9 %collective-permute-done.43 = bf16[208,384]{1,0:T(8,128)(2,1)S(1)} collective-permute-done((bf16[208,384]{1,0:T(8,128)(2,1)S(1)}, bf16[208,384]{1,0:T(8,128)(2,1)S(1)}, u32[]{:S(2)}, u32[]{:S(2)}) %collective-permute-start.43) | collective-permute-done | bytes 159776 | tf_op jit(solution)/shard_map/ppermute | solution.py:875
  250.9 3.6 %collective-permute-done.46.refs_6_ = bf16[1,192,768]{2,1,0:T(8,128)(2,1)S(1)} collective-permute-done((bf16[1,192,768]{2,1,0:T(8,128)(2,1)S(1)}, bf16[1,192,768]{2,1,0:T(8,128)(2,1)S(1)}, u32[]{:S(2)}, u32[]{:S(2)}) %collective-permute-start.46) | collective-permute-done | bytes 294944 | tf_op jit(solution)/shard_map/ppermute | solution.py:875
  254.6 1.4 collective-permute-start.47
  255.9 7.4 %collective-permute-done.44.refs_5_ = bf16[1,208,384]{2,1,0:T(8,128)(2,1)S(1)} collective-permute-done((bf16[1,208,384]{2,1,0:T(8,128)(2,1)S(1)}, bf16[1,208,384]{2,1,0:T(8,128)(2,1)S(1)}, u32[]{:S(2)}, u32[]{:S(2)}) %collective-permute-start.44) | collective-permute-done | bytes 159776 | tf_op jit(solution)/shard_map/ppermute | solution.py:875
  263.4 2.0 collective-permute-start.48
  265.9 1.4 collective-permute-start.51
  267.3 4.8 %finish_ffn.1 = (f32[768,768]{1,0:T(8,128)}, f32[192,3072]{1,0:T(8,128)}) custom-call(s32[5]{0:T(128)} %stack.56.refs_0_, bf16[1,192,768]{2,1,0:T(8,128)(2,1)} %copy-done.4, bf16[1,192,768]{2,1,0:T(8,128)(2,1)} %copy-done.37, bf16[2,192,768]{2,1,0:T(8,128)(2,1)} %copy-done.21, bf16[2,192,768]{2,1,0:T(8,128)(2,1)} %copy-done.23, ...), custom_call_target="tpu_custom_call" | custom-call | flops 4000000000 | bytes 4000000 | tf_op jit(solution)/shard_map/finish_ffn/pallas_call | solution.py:510
  272.7 1.4 collective-permute-start.52
  277.5 2.3 collective-permute-done.52.refs_4_
  280.5 3.6 %finish.1 = (f32[192,768]{1,0:T(8,128)}, f32[192,768]{1,0:T(8,128)}, f32[192,768]{1,0:T(8,128)}, f32[192,768]{1,0:T(8,128)}, f32[1,192]{1,0:T(1,128)}, /*index=5*/f32[1,192]{1,0:T(1,128)}, f32[8,12]{1,0:T(8,128)}) custom-call(s32[5]{0:T(128)} %stack.56.refs_0_, bf16[1,208,384]{2,1,0:T(8,128)(2,1)} %copy-done.9, bf16[1,208,384]{2,1,0:T(8,128)(2,1)} %copy-done.39, ...), custom_call_target="tpu_custom_call" | custom-call | flops 3000000000 | bytes 3000000 | tf_op jit(solution)/shard_map/finish/pallas_call | solution.py:568
  (199 shorter events, 49.8 us)
Async XLA Ops:
  0.6 13.3 %collective-permute-start = (bf16[256,768]{1,0:T(8,128)(2,1)}, bf16[256,768]{1,0:T(8,128)(2,1)S(1)}, u32[]{:S(2)}, u32[]{:S(2)}) collective-permute-start(bf16[256,768]{1,0:T(8,128)(2,1)} %bitcast.81), channel_id=1, source_target_pairs={{0,4},{4,0},{8,12},{12,8},{16,20},{20,16},{24,28},{28,24},{1,5},{5... | collective-permute-start | bytes 1179656 | tf_op jit(solution)/shard_map/ppermute | solution.py:875
  3.6 12.7 %collective-permute-start.1 = (bf16[256,768]{1,0:T(8,128)(2,1)}, bf16[256,768]{1,0:T(8,128)(2,1)S(1)}, u32[]{:S(2)}, u32[]{:S(2)}) collective-permute-start(bf16[256,768]{1,0:T(8,128)(2,1)} %bitcast.82), channel_id=1, source_target_pairs={{24,16},{28,20},{16,8},{20,12},{8,0},{12,4},{25,17},{29,21},{17,9}... | collective-permute-start | bytes 1179656 | tf_op jit(solution)/shard_map/ppermute | solution.py:879
  4.9 12.7 %collective-permute-start.2 = (bf16[256,768]{1,0:T(8,128)(2,1)}, bf16[256,768]{1,0:T(8,128)(2,1)S(1)}, u32[]{:S(2)}, u32[]{:S(2)}) collective-permute-start(bf16[256,768]{1,0:T(8,128)(2,1)} %bitcast.83), channel_id=1, source_target_pairs={{0,8},{4,12},{8,16},{12,20},{16,24},{20,28},{1,9},{5,13},{9,17},{1... | collective-permute-start | bytes 1179656 | tf_op jit(solution)/shard_map/ppermute | solution.py:879
  13.9 16.4 %collective-permute-start.6 = (bf16[1,208,3072]{2,1,0:T(8,128)(2,1)S(1)}, bf16[1,208,3072]{2,1,0:T(8,128)(2,1)}, u32[]{:S(2)}, u32[]{:S(2)}) collective-permute-start(bf16[1,208,3072]{2,1,0:T(8,128)(2,1)S(1)} %maximum_bitcast_fusion.refs_11_.refs_21_), channel_id=1, source_target_pairs={{0,1},{1,0},{2,3},{3,2},{4,5},{5,4},{6,7},{7,6},{8,9},{9,8},{10,11... | collective-permute-start | bytes 3833864 | tf_op jit(solution)/shard_map/ppermute | solution.py:875
  17.7 11.9 %collective-permute-start.4 = (bf16[256,768]{1,0:T(8,128)(2,1)S(1)}, bf16[256,768]{1,0:T(8,128)(2,1)S(1)}, u32[]{:S(2)}, u32[]{:S(2)}) collective-permute-start(bf16[256,768]{1,0:T(8,128)(2,1)S(1)} %collective-permute-done.1), channel_id=1, source_target_pairs={{16,8},{20,12},{8,0},{12,4},{17,9},{21,13},{9,1},{13,5},{18,10},{2... | collective-permute-start | bytes 1179656 | tf_op jit(solution)/shard_map/ppermute | solution.py:879
  19.0 10.6 %collective-permute-start.5 = (bf16[256,768]{1,0:T(8,128)(2,1)S(1)}, bf16[256,768]{1,0:T(8,128)(2,1)S(1)}, u32[]{:S(2)}, u32[]{:S(2)}) collective-permute-start(bf16[256,768]{1,0:T(8,128)(2,1)S(1)} %collective-permute-done.2), channel_id=1, source_target_pairs={{8,16},{12,20},{16,24},{20,28},{9,17},{13,21},{17,25},{21,29},{10,... | collective-permute-start | bytes 1179656 | tf_op jit(solution)/shard_map/ppermute | solution.py:879
  19.7 10.7 %collective-permute-start.3 = (bf16[256,768]{1,0:T(8,128)(2,1)S(1)}, bf16[256,768]{1,0:T(8,128)(2,1)}, u32[]{:S(2)}, u32[]{:S(2)}) collective-permute-start(bf16[256,768]{1,0:T(8,128)(2,1)S(1)} %broadcast_select_fusion.4), channel_id=1, source_target_pairs={{0,4},{4,0},{8,12},{12,8},{16,20},{20,16},{24,28},{28,24},{1,5},{5... | collective-permute-start | bytes 1179656 | tf_op jit(solution)/shard_map/ppermute | solution.py:875
  20.1 28.5 %collective-permute-start.10 = (bf16[1,208,3072]{2,1,0:T(8,128)(2,1)S(1)}, bf16[1,208,3072]{2,1,0:T(8,128)(2,1)}, u32[]{:S(2)}, u32[]{:S(2)}) collective-permute-start(bf16[1,208,3072]{2,1,0:T(8,128)(2,1)S(1)} %maximum_bitcast_fusion.refs_11_.refs_21_), channel_id=1, source_target_pairs={{0,2},{1,3},{2,0},{3,1},{4,6},{5,7},{6,4},{7,5},{8,10},{9,11},{10,... | collective-permute-start | bytes 3833864 | tf_op jit(solution)/shard_map/ppermute | solution.py:875
  31.2 12.3 %collective-permute-start.8 = (bf16[256,768]{1,0:T(8,128)(2,1)}, bf16[256,768]{1,0:T(8,128)(2,1)}, u32[]{:S(2)}, u32[]{:S(2)}) collective-permute-start(bf16[256,768]{1,0:T(8,128)(2,1)} %broadcast_select_fusion.2), channel_id=1, source_target_pairs={{16,24},{20,28},{8,0},{12,4},{17,25},{21,29},{9,1},{13,5},{18,26},... | collective-permute-start | bytes 1179656 | tf_op jit(solution)/shard_map/ppermute | solution.py:879
  32.5 12.0 %collective-permute-start.7 = (bf16[256,768]{1,0:T(8,128)(2,1)}, bf16[256,768]{1,0:T(8,128)(2,1)}, u32[]{:S(2)}, u32[]{:S(2)}) collective-permute-start(bf16[256,768]{1,0:T(8,128)(2,1)} %broadcast_select_fusion.3), channel_id=1, source_target_pairs={{0,4},{4,0},{8,12},{12,8},{16,20},{20,16},{24,28},{28,24},{1,5},{5... | collective-permute-start | bytes 1179656 | tf_op jit(solution)/shard_map/ppermute | solution.py:875
  44.5 7.8 %collective-permute-start.9 = (bf16[256,768]{1,0:T(8,128)(2,1)S(1)}, bf16[256,768]{1,0:T(8,128)(2,1)S(1)}, u32[]{:S(2)}, u32[]{:S(2)}) collective-permute-start(bf16[256,768]{1,0:T(8,128)(2,1)S(1)} %select_select_fusion), channel_id=1, source_target_pairs={{0,4},{4,0},{8,12},{12,8},{16,20},{20,16},{24,28},{28,24},{1,5},{5... | collective-permute-start | bytes 1179656 | tf_op jit(solution)/shard_map/ppermute | solution.py:875
  52.4 6.5 %collective-permute-start.11 = (bf16[1,208,3072]{2,1,0:T(8,128)(2,1)}, bf16[1,208,3072]{2,1,0:T(8,128)(2,1)S(1)}, u32[]{:S(2)}, u32[]{:S(2)}) collective-permute-start(bf16[1,208,3072]{2,1,0:T(8,128)(2,1)} %collective-permute-done.10.refs_13_.refs_23_), channel_id=1, source_target_pairs={{0,1},{1,0},{2,3},{3,2},{4,5},{5,4},{6,7},{7,6},{8,9},{9,8},{10,11... | collective-permute-start | bytes 3833864 | tf_op jit(solution)/shard_map/ppermute | solution.py:875
  52.4 4.0 %collective-permute-start.14 = (bf16[2,192,768]{2,1,0:T(8,128)(2,1)S(1)}, bf16[2,192,768]{2,1,0:T(8,128)(2,1)S(1)}, u32[]{:S(2)}, u32[]{:S(2)}) collective-permute-start(bf16[2,192,768]{2,1,0:T(8,128)(2,1)S(1)} %pad_maximum_fusion), channel_id=1, source_target_pairs={{0,1},{1,0},{2,3},{3,2},{4,5},{5,4},{6,7},{7,6},{8,9},{9,8},{10,11... | collective-permute-start | bytes 1769480 | tf_op jit(solution)/shard_map/ppermute | solution.py:875
  53.7 30.4 %collective-permute-start.13 = (bf16[256,768]{1,0:T(8,128)(2,1)}, bf16[256,768]{1,0:T(8,128)(2,1)S(1)}, u32[]{:S(2)}, u32[]{:S(2)}) collective-permute-start(bf16[256,768]{1,0:T(8,128)(2,1)} %bitcast.94), channel_id=1, source_target_pairs={{0,1},{1,0},{2,3},{3,2},{4,5},{5,4},{6,7},{7,6},{8,9},{9,8},{10,11... | collective-permute-start | bytes 1179656 | tf_op jit(solution)/shard_map/ppermute | solution.py:875
  53.7 30.3 %collective-permute-start.19 = (bf16[256,768]{1,0:T(8,128)(2,1)}, bf16[256,768]{1,0:T(8,128)(2,1)S(1)}, u32[]{:S(2)}, u32[]{:S(2)}) collective-permute-start(bf16[256,768]{1,0:T(8,128)(2,1)} %bitcast.95), channel_id=1, source_target_pairs={{0,2},{1,3},{2,0},{3,1},{4,6},{5,7},{6,4},{7,5},{8,10},{9,11},{10,... | collective-permute-start | bytes 1179656 | tf_op jit(solution)/shard_map/ppermute | solution.py:875
  57.2 26.9 %collective-permute-start.15 = (bf16[2,192,768]{2,1,0:T(8,128)(2,1)S(1)}, bf16[2,192,768]{2,1,0:T(8,128)(2,1)S(1)}, u32[]{:S(2)}, u32[]{:S(2)}) collective-permute-start(bf16[2,192,768]{2,1,0:T(8,128)(2,1)S(1)} %pad_maximum_fusion.1), channel_id=1, source_target_pairs={{0,2},{1,3},{2,0},{3,1},{4,6},{5,7},{6,4},{7,5},{8,10},{9,11},{10,... | collective-permute-start | bytes 1769480 | tf_op jit(solution)/shard_map/ppermute | solution.py:875
  79.5 6.1 %collective-permute-start.12 = (bf16[256,768]{1,0:T(8,128)(2,1)}, bf16[256,768]{1,0:T(8,128)(2,1)S(1)}, u32[]{:S(2)}, u32[]{:S(2)}) collective-permute-start(bf16[256,768]{1,0:T(8,128)(2,1)} %get-tuple-element.114), channel_id=1, source_target_pairs={{0,1},{1,0},{2,3},{3,2},{4,5},{5,4},{6,7},{7,6},{8,9},{9,8},{10,11... | collective-permute-start | bytes 1179656 | tf_op jit(solution)/shard_map/ppermute | solution.py:875
  84.0 11.8 %collective-permute-start.20 = (bf16[256,768]{1,0:T(8,128)(2,1)S(1)}, bf16[256,768]{1,0:T(8,128)(2,1)S(1)}, u32[]{:S(2)}, u32[]{:S(2)}) collective-permute-start(bf16[256,768]{1,0:T(8,128)(2,1)S(1)} %collective-permute-done.19), channel_id=1, source_target_pairs={{0,1},{1,0},{2,3},{3,2},{4,5},{5,4},{6,7},{7,6},{8,9},{9,8},{10,11... | collective-permute-start | bytes 1179656 | tf_op jit(solution)/shard_map/ppermute | solution.py:875
  84.1 11.7 %collective-permute-start.17 = (bf16[256,768]{1,0:T(8,128)(2,1)}, bf16[256,768]{1,0:T(8,128)(2,1)S(1)}, u32[]{:S(2)}, u32[]{:S(2)}) collective-permute-start(bf16[256,768]{1,0:T(8,128)(2,1)} %get-tuple-element.114), channel_id=1, source_target_pairs={{0,2},{1,3},{2,0},{3,1},{4,6},{5,7},{6,4},{7,5},{8,10},{9,11},{10,... | collective-permute-start | bytes 1179656 | tf_op jit(solution)/shard_map/ppermute | solution.py:875
  108.4 11.3 %collective-permute-start.25 = (bf16[256,768]{1,0:T(8,128)(2,1)S(1)}, bf16[256,768]{1,0:T(8,128)(2,1)}, u32[]{:S(2)}, u32[]{:S(2)}) collective-permute-start(bf16[256,768]{1,0:T(8,128)(2,1)S(1)} %fusion.6), channel_id=1, source_target_pairs={{0,2},{1,3},{2,0},{3,1},{4,6},{5,7},{6,4},{7,5},{8,10},{9,11},{10,... | collective-permute-start | bytes 1179656 | tf_op jit(solution)/shard_map/ppermute | solution.py:875
  119.7 61.3 %all-to-all-start = ((bf16[8,192,768]{2,1,0:T(8,128)(2,1)}), bf16[8,192,768]{2,1,0:T(8,128)(2,1)S(1)}, u32[]{:S(2)}, u32[]{:S(2)}) async-start(bf16[8,192,768]{2,1,0:T(8,128)(2,1)} %ffn_grads.1), calls=%async_computation | async-start | bytes 4718592 | tf_op jit(solution)/shard_map/all_to_all | solution.py:1051
  129.5 36.0 %collective-permute-start.22 = (bf16[256,768]{1,0:T(8,128)(2,1)S(1)}, bf16[256,768]{1,0:T(8,128)(2,1)S(1)}, u32[]{:S(2)}, u32[]{:S(2)}) collective-permute-start(bf16[256,768]{1,0:T(8,128)(2,1)S(1)} %fusion.7), channel_id=1, source_target_pairs={{0,2},{1,3},{2,0},{3,1},{4,6},{5,7},{6,4},{7,5},{8,10},{9,11},{10,... | collective-permute-start | bytes 1179656 | tf_op jit(solution)/shard_map/ppermute | solution.py:875
  181.0 7.7 %collective-permute-start.32 = (bf16[2,4,208,384]{3,2,1,0:T(8,128)(2,1)}, bf16[2,4,208,384]{3,2,1,0:T(8,128)(2,1)}, u32[]{:S(2)}, u32[]{:S(2)}) collective-permute-start(bf16[2,4,208,384]{3,2,1,0:T(8,128)(2,1)} %get-tuple-element.175), channel_id=1, source_target_pairs={{0,1},{1,0},{2,3},{3,2},{4,5},{5,4},{6,7},{7,6},{8,9},{9,8},{10,11... | collective-permute-start | bytes 3833864 | tf_op jit(solution)/shard_map/ppermute | solution.py:875
  181.0 9.5 %collective-permute-start.34 = (bf16[2,4,208,384]{3,2,1,0:T(8,128)(2,1)}, bf16[2,4,208,384]{3,2,1,0:T(8,128)(2,1)}, u32[]{:S(2)}, u32[]{:S(2)}) collective-permute-start(bf16[2,4,208,384]{3,2,1,0:T(8,128)(2,1)} %get-tuple-element.177), channel_id=1, source_target_pairs={{0,1},{1,0},{2,3},{3,2},{4,5},{5,4},{6,7},{7,6},{8,9},{9,8},{10,11... | collective-permute-start | bytes 3833864 | tf_op jit(solution)/shard_map/ppermute | solution.py:875
  184.2 4.4 %collective-permute-start.40 = (bf16[2,48,384]{2,1,0:T(8,128)(2,1)S(1)}, bf16[2,48,384]{2,1,0:T(8,128)(2,1)S(1)}, u32[]{:S(2)}, u32[]{:S(2)}) collective-permute-start(bf16[2,48,384]{2,1,0:T(8,128)(2,1)S(1)} %pad_maximum_fusion.7), channel_id=1, source_target_pairs={{0,2},{1,3},{2,0},{3,1},{4,6},{5,7},{6,4},{7,5},{8,10},{9,11},{10,... | collective-permute-start | bytes 221192 | tf_op jit(solution)/shard_map/ppermute | solution.py:875
  184.6 12.2 %collective-permute-start.28 = (bf16[256,768]{1,0:T(8,128)(2,1)}, bf16[256,768]{1,0:T(8,128)(2,1)S(1)}, u32[]{:S(2)}, u32[]{:S(2)}) collective-permute-start(bf16[256,768]{1,0:T(8,128)(2,1)} %get-tuple-element.169), channel_id=1, source_target_pairs={{0,4},{4,0},{8,12},{12,8},{16,20},{20,16},{24,28},{28,24},{1,5},{5... | collective-permute-start | bytes 1179656 | tf_op jit(solution)/shard_map/ppermute | solution.py:875
  185.8 18.3 %collective-permute-start.26 = (bf16[256,768]{1,0:T(8,128)(2,1)}, bf16[256,768]{1,0:T(8,128)(2,1)S(1)}, u32[]{:S(2)}, u32[]{:S(2)}) collective-permute-start(bf16[256,768]{1,0:T(8,128)(2,1)} %get-tuple-element.165), channel_id=1, source_target_pairs={{0,4},{4,0},{8,12},{12,8},{16,20},{20,16},{24,28},{28,24},{1,5},{5... | collective-permute-start | bytes 1179656 | tf_op jit(solution)/shard_map/ppermute | solution.py:875
  190.1 17.4 %collective-permute-start.33 = (bf16[4,208,384]{2,1,0:T(8,128)(2,1)S(1)}, bf16[4,208,384]{2,1,0:T(8,128)(2,1)S(1)}, u32[]{:S(2)}, u32[]{:S(2)}) collective-permute-start(bf16[4,208,384]{2,1,0:T(8,128)(2,1)S(1)} %fusion.8), channel_id=1, source_target_pairs={{0,2},{1,3},{2,0},{3,1},{4,6},{5,7},{6,4},{7,5},{8,10},{9,11},{10,... | collective-permute-start | bytes 1916936 | tf_op jit(solution)/shard_map/ppermute | solution.py:875
  191.8 27.3 %collective-permute-start.35 = (bf16[4,208,384]{2,1,0:T(8,128)(2,1)S(1)}, bf16[4,208,384]{2,1,0:T(8,128)(2,1)S(1)}, u32[]{:S(2)}, u32[]{:S(2)}) collective-permute-start(bf16[4,208,384]{2,1,0:T(8,128)(2,1)S(1)} %fusion.9), channel_id=1, source_target_pairs={{0,2},{1,3},{2,0},{3,1},{4,6},{5,7},{6,4},{7,5},{8,10},{9,11},{10,... | collective-permute-start | bytes 1916936 | tf_op jit(solution)/shard_map/ppermute | solution.py:875
  193.7 28.5 %collective-permute-start.41 = (bf16[1,192,768]{2,1,0:T(8,128)(2,1)S(1)}, bf16[1,192,768]{2,1,0:T(8,128)(2,1)S(1)}, u32[]{:S(2)}, u32[]{:S(2)}) collective-permute-start(bf16[1,192,768]{2,1,0:T(8,128)(2,1)S(1)} %maximum_bitcast_fusion.1.refs_1_), channel_id=1, source_target_pairs={{0,16},{4,20},{8,24},{12,28},{16,0},{20,4},{24,8},{28,12},{1,17},{... | collective-permute-start | bytes 884744 | tf_op jit(solution)/shard_map/ppermute | solution.py:875
  196.9 23.6 %collective-permute-start.29 = (bf16[256,768]{1,0:T(8,128)(2,1)S(1)}, bf16[256,768]{1,0:T(8,128)(2,1)S(1)}, u32[]{:S(2)}, u32[]{:S(2)}) collective-permute-start(bf16[256,768]{1,0:T(8,128)(2,1)S(1)} %add_convert_fusion.3), channel_id=1, source_target_pairs={{0,8},{4,12},{8,0},{12,4},{16,24},{20,28},{24,16},{28,20},{1,9},{5... | collective-permute-start | bytes 1179656 | tf_op jit(solution)/shard_map/ppermute | solution.py:875
  204.2 16.3 %collective-permute-start.31 = (bf16[256,768]{1,0:T(8,128)(2,1)S(1)}, bf16[256,768]{1,0:T(8,128)(2,1)S(1)}, u32[]{:S(2)}, u32[]{:S(2)}) collective-permute-start(bf16[256,768]{1,0:T(8,128)(2,1)S(1)} %copy-done.27), channel_id=1, source_target_pairs={{0,4},{4,0},{8,12},{12,8},{16,20},{20,16},{24,28},{28,24},{1,5},{5... | collective-permute-start | bytes 1179656 | tf_op jit(solution)/shard_map/ppermute | solution.py:875
  207.5 16.2 %collective-permute-start.27 = (bf16[256,768]{1,0:T(8,128)(2,1)S(1)}, bf16[256,768]{1,0:T(8,128)(2,1)S(1)}, u32[]{:S(2)}, u32[]{:S(2)}) collective-permute-start(bf16[256,768]{1,0:T(8,128)(2,1)S(1)} %copy-done.25), channel_id=1, source_target_pairs={{0,4},{4,0},{8,12},{12,8},{16,20},{20,16},{24,28},{28,24},{1,5},{5... | collective-permute-start | bytes 1179656 | tf_op jit(solution)/shard_map/ppermute | solution.py:875
  220.8 10.5 %collective-permute-start.37 = (bf16[2,208,384]{2,1,0:T(8,128)(2,1)S(1)}, bf16[2,208,384]{2,1,0:T(8,128)(2,1)S(1)}, u32[]{:S(2)}, u32[]{:S(2)}) collective-permute-start(bf16[2,208,384]{2,1,0:T(8,128)(2,1)S(1)} %pad_maximum_fusion.4), channel_id=1, source_target_pairs={{0,4},{4,0},{8,12},{12,8},{16,20},{20,16},{24,28},{28,24},{1,5},{5... | collective-permute-start | bytes 958472 | tf_op jit(solution)/shard_map/ppermute | solution.py:875
  222.2 20.1 %collective-permute-start.42 = (bf16[2,192,768]{2,1,0:T(8,128)(2,1)S(1)}, bf16[2,192,768]{2,1,0:T(8,128)(2,1)S(1)}, u32[]{:S(2)}, u32[]{:S(2)}) collective-permute-start(bf16[2,192,768]{2,1,0:T(8,128)(2,1)S(1)} %pad_maximum_fusion.2), channel_id=1, source_target_pairs={{0,8},{4,12},{8,0},{12,4},{16,24},{20,28},{24,16},{28,20},{1,9},{5... | collective-permute-start | bytes 1769480 | tf_op jit(solution)/shard_map/ppermute | solution.py:875
  223.7 14.5 %collective-permute-start.36 = (bf16[2,208,384]{2,1,0:T(8,128)(2,1)S(1)}, bf16[2,208,384]{2,1,0:T(8,128)(2,1)S(1)}, u32[]{:S(2)}, u32[]{:S(2)}) collective-permute-start(bf16[2,208,384]{2,1,0:T(8,128)(2,1)S(1)} %pad_maximum_fusion.3), channel_id=1, source_target_pairs={{0,4},{4,0},{8,12},{12,8},{16,20},{20,16},{24,28},{28,24},{1,5},{5... | collective-permute-start | bytes 958472 | tf_op jit(solution)/shard_map/ppermute | solution.py:875
  231.5 10.7 %collective-permute-start.38 = (bf16[2,208,384]{2,1,0:T(8,128)(2,1)S(1)}, bf16[2,208,384]{2,1,0:T(8,128)(2,1)S(1)}, u32[]{:S(2)}, u32[]{:S(2)}) collective-permute-start(bf16[2,208,384]{2,1,0:T(8,128)(2,1)S(1)} %add_convert_fusion.7), channel_id=1, source_target_pairs={{0,8},{4,12},{8,0},{12,4},{16,24},{20,28},{24,16},{28,20},{1,9},{5... | collective-permute-start | bytes 958472 | tf_op jit(solution)/shard_map/ppermute | solution.py:875
  233.2 12.8 %collective-permute-start.49 = (bf16[1,192,768]{2,1,0:T(8,128)(2,1)S(1)}, bf16[1,192,768]{2,1,0:T(8,128)(2,1)S(1)}, u32[]{:S(2)}, u32[]{:S(2)}) collective-permute-start(bf16[1,192,768]{2,1,0:T(8,128)(2,1)S(1)} %maximum_bitcast_fusion.1.refs_1_), channel_id=1, source_target_pairs={{0,4},{4,0},{8,12},{12,8},{16,20},{20,16},{24,28},{28,24},{1,5},{5... | collective-permute-start | bytes 884744 | tf_op jit(solution)/shard_map/ppermute | solution.py:875
  242.3 8.2 %collective-permute-start.43 = (bf16[208,384]{1,0:T(8,128)(2,1)S(1)}, bf16[208,384]{1,0:T(8,128)(2,1)S(1)}, u32[]{:S(2)}, u32[]{:S(2)}) collective-permute-start(bf16[208,384]{1,0:T(8,128)(2,1)S(1)} %slice_bitcast_fusion), channel_id=1, source_target_pairs={{0,16},{4,20},{8,24},{12,28},{16,0},{20,4},{24,8},{28,12},{1,17},{... | collective-permute-start | bytes 479240 | tf_op jit(solution)/shard_map/ppermute | solution.py:875
  242.8 31.4 %collective-permute-start.30 = (bf16[256,768]{1,0:T(8,128)(2,1)S(1)}, bf16[256,768]{1,0:T(8,128)(2,1)S(1)}, u32[]{:S(2)}, u32[]{:S(2)}) collective-permute-start(bf16[256,768]{1,0:T(8,128)(2,1)S(1)} %add_convert_fusion.4), channel_id=1, source_target_pairs={{0,8},{4,12},{8,0},{12,4},{16,24},{20,28},{24,16},{28,20},{1,9},{5... | collective-permute-start | bytes 1179656 | tf_op jit(solution)/shard_map/ppermute | solution.py:875
  244.6 9.9 %collective-permute-start.46 = (bf16[1,192,768]{2,1,0:T(8,128)(2,1)S(1)}, bf16[1,192,768]{2,1,0:T(8,128)(2,1)S(1)}, u32[]{:S(2)}, u32[]{:S(2)}) collective-permute-start(bf16[1,192,768]{2,1,0:T(8,128)(2,1)S(1)} %collective-permute-done.41.refs_5_), channel_id=1, source_target_pairs={{0,4},{4,0},{8,12},{12,8},{16,20},{20,16},{24,28},{28,24},{1,5},{5... | collective-permute-start | bytes 884744 | tf_op jit(solution)/shard_map/ppermute | solution.py:875
  246.0 19.9 %collective-permute-start.50 = (bf16[2,192,768]{2,1,0:T(8,128)(2,1)S(1)}, bf16[2,192,768]{2,1,0:T(8,128)(2,1)S(1)}, u32[]{:S(2)}, u32[]{:S(2)}) collective-permute-start(bf16[2,192,768]{2,1,0:T(8,128)(2,1)S(1)} %collective-permute-done.42.refs_3_), channel_id=1, source_target_pairs={{0,4},{4,0},{8,12},{12,8},{16,20},{20,16},{24,28},{28,24},{1,5},{5... | collective-permute-start | bytes 1769480 | tf_op jit(solution)/shard_map/ppermute | solution.py:875
  250.6 12.7 %collective-permute-start.44 = (bf16[1,208,384]{2,1,0:T(8,128)(2,1)S(1)}, bf16[1,208,384]{2,1,0:T(8,128)(2,1)S(1)}, u32[]{:S(2)}, u32[]{:S(2)}) collective-permute-start(bf16[1,208,384]{2,1,0:T(8,128)(2,1)S(1)} %fusion.13.refs_1_), channel_id=1, source_target_pairs={{0,16},{4,20},{8,24},{12,28},{16,0},{20,4},{24,8},{28,12},{1,17},{... | collective-permute-start | bytes 479240 | tf_op jit(solution)/shard_map/ppermute | solution.py:875
  254.6 23.0 %collective-permute-start.47 = (bf16[1,208,384]{2,1,0:T(8,128)(2,1)S(1)}, bf16[1,208,384]{2,1,0:T(8,128)(2,1)S(1)}, u32[]{:S(2)}, u32[]{:S(2)}) collective-permute-start(bf16[1,208,384]{2,1,0:T(8,128)(2,1)S(1)} %fusion.13.refs_1_), channel_id=1, source_target_pairs={{0,4},{4,0},{8,12},{12,8},{16,20},{20,16},{24,28},{28,24},{1,5},{5... | collective-permute-start | bytes 479240 | tf_op jit(solution)/shard_map/ppermute | solution.py:875
  263.3 12.1 %collective-permute-start.45 = (bf16[256,768]{1,0:T(8,128)(2,1)S(1)}, bf16[256,768]{1,0:T(8,128)(2,1)S(1)}, u32[]{:S(2)}, u32[]{:S(2)}) collective-permute-start(bf16[256,768]{1,0:T(8,128)(2,1)S(1)} %add_convert_fusion.2), channel_id=1, source_target_pairs={{0,16},{4,20},{8,24},{12,28},{16,0},{20,4},{24,8},{28,12},{1,17},{... | collective-permute-start | bytes 1179656 | tf_op jit(solution)/shard_map/ppermute | solution.py:875
  263.4 9.4 %collective-permute-start.48 = (bf16[2,208,384]{2,1,0:T(8,128)(2,1)S(1)}, bf16[2,208,384]{2,1,0:T(8,128)(2,1)S(1)}, u32[]{:S(2)}, u32[]{:S(2)}) collective-permute-start(bf16[2,208,384]{2,1,0:T(8,128)(2,1)S(1)} %pad_maximum_fusion.5), channel_id=1, source_target_pairs={{0,8},{4,12},{8,0},{12,4},{16,24},{20,28},{24,16},{28,20},{1,9},{5... | collective-permute-start | bytes 958472 | tf_op jit(solution)/shard_map/ppermute | solution.py:875
  265.9 6.8 %collective-permute-start.51 = (bf16[1,208,384]{2,1,0:T(8,128)(2,1)S(1)}, bf16[1,208,384]{2,1,0:T(8,128)(2,1)S(1)}, u32[]{:S(2)}, u32[]{:S(2)}) collective-permute-start(bf16[1,208,384]{2,1,0:T(8,128)(2,1)S(1)} %collective-permute-done.44.refs_5_), channel_id=1, source_target_pairs={{0,4},{4,0},{8,12},{12,8},{16,20},{20,16},{24,28},{28,24},{1,5},{5... | collective-permute-start | bytes 479240 | tf_op jit(solution)/shard_map/ppermute | solution.py:875
  272.7 7.0 %collective-permute-start.52 = (bf16[2,208,384]{2,1,0:T(8,128)(2,1)S(1)}, bf16[2,208,384]{2,1,0:T(8,128)(2,1)S(1)}, u32[]{:S(2)}, u32[]{:S(2)}) collective-permute-start(bf16[2,208,384]{2,1,0:T(8,128)(2,1)S(1)} %collective-permute-done.48.refs_3_), channel_id=1, source_target_pairs={{0,4},{4,0},{8,12},{12,8},{16,20},{20,16},{24,28},{28,24},{1,5},{5... | collective-permute-start | bytes 958472 | tf_op jit(solution)/shard_map/ppermute | solution.py:875
  (48 other events, 380.5 us)

commit v6 on v5

--- a/solution.py
+++ b/solution.py
@@ -136,13 +136,15 @@
     return pl.CostEstimate(flops=int(us * 1.0e9), bytes_accessed=int(us * 1.0e6), transcendentals=0)
 
 
-def load_pieces(pieces, target_ref, flip, sem):
+def load_pieces(pieces, target_ref, flip, sem, first=0, columns=None):
     copies = []
     rows = target_ref.shape[0] // len(pieces)
     for number, (ref, index, place) in enumerate(pieces):
         start = pl.multiple_of(lax.bitwise_xor(jnp.int32(place), flip) * rows, 16)
-        source = ref.at[index, pl.ds(0, rows)]
-        copies.append(pltpu.make_async_copy(source, target_ref.at[pl.ds(start, rows)], sem.at[number]))
+        source, target = ref.at[index, pl.ds(0, rows)], target_ref.at[pl.ds(start, rows)]
+        if columns is not None:
+            source, target = ref.at[index, pl.ds(0, rows), columns], target_ref.at[pl.ds(start, rows), columns]
+        copies.append(pltpu.make_async_copy(source, target, sem.at[first + number]))
     for copy in copies:
         copy.start()
     return copies
@@ -171,7 +173,10 @@
     b2 = b1 + len_ref[0, 1]
     b3 = b2 + len_ref[0, 2]
     copies = load_pieces(expand(x_refs), x_ref, jnp.int32(0), sem_x)
-    copies += load_pieces(expand(w_refs), w_ref, ids_ref[2], sem_w)
+    pieces = expand(w_refs)
+    copies += load_pieces(pieces, w_ref, ids_ref[2], sem_w, 0, pl.ds(D, 2 * D))
+    late = load_pieces(pieces, w_ref, ids_ref[2], sem_w, len(pieces), pl.ds(0, D))
+    late += load_pieces(pieces, w_ref, ids_ref[2], sem_w, 2 * len(pieces), pl.ds(3 * D, D))
     small_copies = []
     for number, (ref, index, _) in enumerate(expand(w_refs)):
         source = ref.at[index, pl.ds(ref.shape[1] - 16, 16)]
@@ -233,6 +238,8 @@
     lax.fori_loop(0, spans // 2, project, 0)
     mine = pl.multiple_of(lax.bitwise_xor(ids_ref[0], ids_ref[1]) * own_rows, SPAN)
     x_own = x_ref[pl.ds(mine, own_rows), :]
+    for copy in late:
+        copy.wait()
     q_ref[...] = dot(normed(x_own), w_ref[:, 0:D]).astype(jnp.bfloat16)
 
     def one_span(i, carry):
@@ -356,7 +363,7 @@
             pltpu.VMEM((PAIRS, 1, 256), f32),
             pltpu.VMEM((PAIRS, 128, 128), f32),
             pltpu.SemaphoreType.DMA((n_x,)),
-            pltpu.SemaphoreType.DMA((n_w,)),
+            pltpu.SemaphoreType.DMA((3 * n_w,)),
             pltpu.SemaphoreType.DMA((spans // 2,)),
             pltpu.SemaphoreType.DMA((spans // 2,)),
             pltpu.SemaphoreType.DMA((n_w,)),

time: 284 us -> 285 us (level)
  Pallas kernels: 83.7 us -> 80.8 us
  transfers between devices with their start and end apart: 54 -> 54, of which waited for: 33 -> 33; matrix products, arithmetic and copies ran while one was open for 7% -> 7% of each run, Pallas kernels for 26% -> 25%
where the time goes in v6:
time: 285 us; the launch traced here: 286 us
  waiting for transfers between devices  119 us (42%)
  Pallas kernels  80.8 us (28%)
  starting transfers between devices  58.5 us (21%)
  other arithmetic  14.4 us (5%)
  local copies, waits for them, and re-layouts  11.8 us (4%)
    ppermute x48, waiting for transfers between devices, swap(): return lax.ppermute(x, axis, [(i, i ^ bit) for i in range(count)])  81.9 us
    ppermute x48, starting transfers between devices, swap(): return lax.ppermute(x, axis, [(i, i ^ bit) for i in range(count)])  39.9 us
    pallas_call x1, Pallas kernels, backward(): pl.pallas_call(lambda *refs: backward_kernel((len(xs), len(ws), len(dnf),...  33 us
    ppermute x5, waiting for transfers between devices, hop(): lax.ppermute(x, 'ctx', [(2 * a + i, 2 * b + i) for a, b in pairs for i in...  19.5 us
    pallas_call x1, Pallas kernels, forward(): pl.pallas_call(lambda *refs: forward_kernel((len(xs), len(ws)), *refs), n...  18.5 us
    all_to_all x1, waiting for transfers between devices, on_device(): ffn_got = lax.all_to_all(after(ffn_parts[0], c), 'ctx', 0, 0)  17.2 us
    pallas_call x2, Pallas kernels, ffn(): pl.pallas_call(lambda *refs: ffn_kernel((count, len(wins)), *refs), name=...  14 us
    all_to_all x1, starting transfers between devices, on_device(): ffn_got = lax.all_to_all(after(ffn_parts[0], c), 'ctx', 0, 0)  9.5 us
  transfers between devices with their start and end apart: 54, of which 33 were waited for; matrix products, arithmetic and copies ran while one was open for 7% of the time, Pallas kernels for 25%

profile of v6, /device:TPU:0, one launch (start us, length us, event | category | flops | bytes accessed | tf_op | source)
XLA Modules:
  0.0 285.8 jit_solution(18349996480255696835)
XLA Ops:
  0.6 3.0 %collective-permute-start = (bf16[256,768]{1,0:T(8,128)(2,1)}, bf16[256,768]{1,0:T(8,128)(2,1)S(1)}, u32[]{:S(2)}, u32[]{:S(2)}) collective-permute-start(bf16[256,768]{1,0:T(8,128)(2,1)} %bitcast.81), channel_id=1, source_target_pairs={{0,4},{4,0},{8,12},{12,8},{16,20},{20,16},{24,28},{28,24},{1,5},{5... | collective-permute-start | bytes 1179656 | tf_op jit(solution)/shard_map/ppermute | solution.py:882
  4.9 4.6 %collective-permute-start.2 = (bf16[256,768]{1,0:T(8,128)(2,1)}, bf16[256,768]{1,0:T(8,128)(2,1)S(1)}, u32[]{:S(2)}, u32[]{:S(2)}) collective-permute-start(bf16[256,768]{1,0:T(8,128)(2,1)} %bitcast.83), channel_id=1, source_target_pairs={{0,8},{4,12},{8,16},{12,20},{16,24},{20,28},{1,9},{5,13},{9,17},{1... | collective-permute-start | bytes 1179656 | tf_op jit(solution)/shard_map/ppermute | solution.py:886
  14.0 2.3 collective-permute-done.1
  20.1 1.7 collective-permute-start.10
  21.8 7.8 %collective-permute-done.4 = bf16[256,768]{1,0:T(8,128)(2,1)S(1)} collective-permute-done((bf16[256,768]{1,0:T(8,128)(2,1)S(1)}, bf16[256,768]{1,0:T(8,128)(2,1)S(1)}, u32[]{:S(2)}, u32[]{:S(2)}) %collective-permute-start.4) | collective-permute-done | bytes 393248 | tf_op jit(solution)/shard_map/ppermute | solution.py:886
  33.2 2.0 dynamic-slice_bitcast_fusion.1
  35.3 8.1 %collective-permute-done.8 = bf16[256,768]{1,0:T(8,128)(2,1)} collective-permute-done((bf16[256,768]{1,0:T(8,128)(2,1)}, bf16[256,768]{1,0:T(8,128)(2,1)}, u32[]{:S(2)}, u32[]{:S(2)}) %collective-permute-start.8) | collective-permute-done | bytes 393248 | tf_op jit(solution)/shard_map/ppermute | solution.py:886
  45.6 3.0 %collective-permute-done.10.refs_13_.refs_23_ = bf16[1,208,3072]{2,1,0:T(8,128)(2,1)} collective-permute-done((bf16[1,208,3072]{2,1,0:T(8,128)(2,1)S(1)}, bf16[1,208,3072]{2,1,0:T(8,128)(2,1)}, u32[]{:S(2)}, u32[]{:S(2)}) %collective-permute-start.10) | collective-permute-done | bytes 1277984 | tf_op jit(solution)/shard_map/ppermute | solution.py:882
  48.6 3.8 %collective-permute-done.9 = bf16[256,768]{1,0:T(8,128)(2,1)S(1)} collective-permute-done((bf16[256,768]{1,0:T(8,128)(2,1)S(1)}, bf16[256,768]{1,0:T(8,128)(2,1)S(1)}, u32[]{:S(2)}, u32[]{:S(2)}) %collective-permute-start.9) | collective-permute-done | bytes 393248 | tf_op jit(solution)/shard_map/ppermute | solution.py:882
  53.7 1.5 collective-permute-start.19
  57.2 1.6 collective-permute-start.15
  59.9 18.5 %forward.1 = (bf16[256,768]{1,0:T(8,128)(2,1)}, f32[256,768]{1,0:T(8,128)}, bf16[256,768]{1,0:T(8,128)(2,1)}, f32[2,6,128,128]{3,2,1,0:T(8,128)}, f32[2,6,1,256]...) custom-call(s32[5]{0:T(128)} %stack.56.refs_0_, ...), custom_call_target="tpu_custom_call" | custom-call | flops 22000001024 | bytes 22000000 | tf_op jit(solution)/shard_map/forward/pallas_call | solution.py:335
  78.4 5.4 %collective-permute-start.12 = (bf16[256,768]{1,0:T(8,128)(2,1)}, bf16[256,768]{1,0:T(8,128)(2,1)S(1)}, u32[]{:S(2)}, u32[]{:S(2)}) collective-permute-start(bf16[256,768]{1,0:T(8,128)(2,1)} %get-tuple-element.114), channel_id=1, source_target_pairs={{0,1},{1,0},{2,3},{3,2},{4,5},{5,4},{6,7},{7,6},{8,9},{9,8},{10,11... | collective-permute-start | bytes 1179656 | tf_op jit(solution)/shard_map/ppermute | solution.py:882
  83.9 1.4 collective-permute-done.12
  86.1 7.0 %ffn.2 = (bf16[2,256,768]{2,1,0:T(8,128)(2,1)}, bf16[2,256,768]{2,1,0:T(8,128)(2,1)}, bf16[1,256,768]{2,1,0:T(8,128)(2,1)}, bf16[1,256,768]{2,1,0:T(8,128)(2,1)}...) custom-call(s32[5]{0:T(128)} %stack.56.refs_0_, bf16[1,256,768]{2,1,0:T(8,128)(2,1)} %bitcast.106, ...), custom_call_target="tpu_custom_call" | custom-call | flops 6000000000 | bytes 6000000 | tf_op jit(solution)/shard_map/ffn/pallas_call | solution.py:406
  93.1 2.4 collective-permute-done.17
  95.6 1.7 collective-permute-done.18.refs_2_.refs_4_
  98.0 7.0 %ffn.3 = (bf16[2,256,768]{2,1,0:T(8,128)(2,1)}, bf16[2,256,768]{2,1,0:T(8,128)(2,1)}, bf16[1,256,768]{2,1,0:T(8,128)(2,1)}, bf16[1,256,768]{2,1,0:T(8,128)(2,1)}...) custom-call(s32[5]{0:T(128)} %stack.56.refs_0_, bf16[1,256,768]{2,1,0:T(8,128)(2,1)} %bitcast.113, ...), custom_call_target="tpu_custom_call" | custom-call | flops 6000000000 | bytes 6000000 | tf_op jit(solution)/shard_map/ffn/pallas_call | solution.py:406
  105.2 1.8 collective-permute-done.24
  108.5 6.9 %ffn_grads.1 = bf16[8,192,768]{2,1,0:T(8,128)(2,1)} custom-call(s32[5]{0:T(128)} %stack.56.refs_0_, bf16[1,256,768]{2,1,0:T(8,128)(2,1)} %bitcast.107, bf16[1,256,768]{2,1,0:T(8,128)(2,1)} %bitcast.109, bf16[1,256,768]{2,1,0:T(8,128)(2,1)} %bitcast.114, bf16[1,256,768]{2,1,0:T(8,128)(2,1)} %copy-done.34, bf16[1,256,768]{2,1,0:T(8,128)(2,1)} %refs_5_.1, ...), custom_call_target="tpu_custom_call" | custom-call | flops 6000000000 | bytes 6000000 | tf_op jit(solution)/shard_map/ffn_grads/pallas_call | solution.py:471
  115.4 4.1 %collective-permute-done.25.refs_27_ = bf16[256,768]{1,0:T(8,128)(2,1)} collective-permute-done((bf16[256,768]{1,0:T(8,128)(2,1)S(1)}, bf16[256,768]{1,0:T(8,128)(2,1)}, u32[]{:S(2)}, u32[]{:S(2)}) %collective-permute-start.25) | collective-permute-done | bytes 393248 | tf_op jit(solution)/shard_map/ppermute | solution.py:882
  119.5 9.5 %all-to-all-start = ((bf16[8,192,768]{2,1,0:T(8,128)(2,1)}), bf16[8,192,768]{2,1,0:T(8,128)(2,1)S(1)}, u32[]{:S(2)}, u32[]{:S(2)}) async-start(bf16[8,192,768]{2,1,0:T(8,128)(2,1)} %ffn_grads.1), calls=%async_computation | async-start | bytes 4718592 | tf_op jit(solution)/shard_map/all_to_all | solution.py:1058
  132.2 33.0 %backward.1 = (bf16[256,768]{1,0:T(8,128)(2,1)}, bf16[256,768]{1,0:T(8,128)(2,1)}, bf16[256,768]{1,0:T(8,128)(2,1)}, bf16[256,768]{1,0:T(8,128)(2,1)}, bf16[256,...) custom-call(s32[5]{0:T(128)} %stack.56.refs_0_, ...), custom_call_target="tpu_custom_call" | custom-call | flops 35999997952 | bytes 36000000 | tf_op jit(solution)/shard_map/backward/pallas_call | solution.py:842
  165.3 17.2 %all-to-all-done = bf16[8,192,768]{2,1,0:T(8,128)(2,1)S(1)} async-done(((bf16[8,192,768]{2,1,0:T(8,128)(2,1)}), bf16[8,192,768]{2,1,0:T(8,128)(2,1)S(1)}, u32[]{:S(2)}, u32[]{:S(2)}) %all-to-all-start) | async-done | bytes 2359328 | tf_op jit(solution)/shard_map/all_to_all | solution.py:1058
  183.6 2.1 collective-permute-done.39
  188.1 2.0 collective-permute-done.40
  190.2 1.4 fusion.8
  193.3 1.8 collective-permute-start.35
  195.2 3.0 %collective-permute-done.28 = bf16[256,768]{1,0:T(8,128)(2,1)S(1)} collective-permute-done((bf16[256,768]{1,0:T(8,128)(2,1)}, bf16[256,768]{1,0:T(8,128)(2,1)S(1)}, u32[]{:S(2)}, u32[]{:S(2)}) %collective-permute-start.28) | collective-permute-done | bytes 393248 | tf_op jit(solution)/shard_map/ppermute | solution.py:882
  198.5 7.2 %collective-permute-done.26 = bf16[256,768]{1,0:T(8,128)(2,1)S(1)} collective-permute-done((bf16[256,768]{1,0:T(8,128)(2,1)}, bf16[256,768]{1,0:T(8,128)(2,1)S(1)}, u32[]{:S(2)}, u32[]{:S(2)}) %collective-permute-start.26) | collective-permute-done | bytes 393248 | tf_op jit(solution)/shard_map/ppermute | solution.py:882
  206.9 2.1 collective-permute-done.33
  211.6 9.0 %collective-permute-done.35 = bf16[4,208,384]{2,1,0:T(8,128)(2,1)S(1)} collective-permute-done((bf16[4,208,384]{2,1,0:T(8,128)(2,1)S(1)}, bf16[4,208,384]{2,1,0:T(8,128)(2,1)S(1)}, u32[]{:S(2)}, u32[]{:S(2)}) %collective-permute-start.35) | collective-permute-done | bytes 639008 | tf_op jit(solution)/shard_map/ppermute | solution.py:882
  223.9 1.4 collective-permute-done.27
  226.5 6.4 %collective-permute-done.37 = bf16[2,208,384]{2,1,0:T(8,128)(2,1)S(1)} collective-permute-done((bf16[2,208,384]{2,1,0:T(8,128)(2,1)S(1)}, bf16[2,208,384]{2,1,0:T(8,128)(2,1)S(1)}, u32[]{:S(2)}, u32[]{:S(2)}) %collective-permute-start.37) | collective-permute-done | bytes 319520 | tf_op jit(solution)/shard_map/ppermute | solution.py:882
  236.0 3.7 %collective-permute-done.36 = bf16[2,208,384]{2,1,0:T(8,128)(2,1)S(1)} collective-permute-done((bf16[2,208,384]{2,1,0:T(8,128)(2,1)S(1)}, bf16[2,208,384]{2,1,0:T(8,128)(2,1)S(1)}, u32[]{:S(2)}, u32[]{:S(2)}) %collective-permute-start.36) | collective-permute-done | bytes 319520 | tf_op jit(solution)/shard_map/ppermute | solution.py:882
  239.7 3.9 %collective-permute-done.38 = bf16[2,208,384]{2,1,0:T(8,128)(2,1)S(1)} collective-permute-done((bf16[2,208,384]{2,1,0:T(8,128)(2,1)S(1)}, bf16[2,208,384]{2,1,0:T(8,128)(2,1)S(1)}, u32[]{:S(2)}, u32[]{:S(2)}) %collective-permute-start.38) | collective-permute-done | bytes 319520 | tf_op jit(solution)/shard_map/ppermute | solution.py:882
  244.3 1.8 collective-permute-start.30
  246.1 1.4 collective-permute-start.46
  248.2 3.9 %collective-permute-done.43 = bf16[208,384]{1,0:T(8,128)(2,1)S(1)} collective-permute-done((bf16[208,384]{1,0:T(8,128)(2,1)S(1)}, bf16[208,384]{1,0:T(8,128)(2,1)S(1)}, u32[]{:S(2)}, u32[]{:S(2)}) %collective-permute-start.43) | collective-permute-done | bytes 159776 | tf_op jit(solution)/shard_map/ppermute | solution.py:882
  252.4 3.6 %collective-permute-done.46.refs_6_ = bf16[1,192,768]{2,1,0:T(8,128)(2,1)S(1)} collective-permute-done((bf16[1,192,768]{2,1,0:T(8,128)(2,1)S(1)}, bf16[1,192,768]{2,1,0:T(8,128)(2,1)S(1)}, u32[]{:S(2)}, u32[]{:S(2)}) %collective-permute-start.46) | collective-permute-done | bytes 294944 | tf_op jit(solution)/shard_map/ppermute | solution.py:882
  256.1 1.4 collective-permute-start.47
  257.4 7.4 %collective-permute-done.44.refs_5_ = bf16[1,208,384]{2,1,0:T(8,128)(2,1)S(1)} collective-permute-done((bf16[1,208,384]{2,1,0:T(8,128)(2,1)S(1)}, bf16[1,208,384]{2,1,0:T(8,128)(2,1)S(1)}, u32[]{:S(2)}, u32[]{:S(2)}) %collective-permute-start.44) | collective-permute-done | bytes 159776 | tf_op jit(solution)/shard_map/ppermute | solution.py:882
  264.9 2.0 collective-permute-start.48
  267.4 1.4 collective-permute-start.51
  268.8 4.8 %finish_ffn.1 = (f32[768,768]{1,0:T(8,128)}, f32[192,3072]{1,0:T(8,128)}) custom-call(s32[5]{0:T(128)} %stack.56.refs_0_, bf16[1,192,768]{2,1,0:T(8,128)(2,1)} %copy-done.4, bf16[1,192,768]{2,1,0:T(8,128)(2,1)} %copy-done.37, bf16[2,192,768]{2,1,0:T(8,128)(2,1)} %copy-done.21, bf16[2,192,768]{2,1,0:T(8,128)(2,1)} %copy-done.23, ...), custom_call_target="tpu_custom_call" | custom-call | flops 4000000000 | bytes 4000000 | tf_op jit(solution)/shard_map/finish_ffn/pallas_call | solution.py:517
  274.3 1.4 collective-permute-start.52
  279.0 2.3 collective-permute-done.52.refs_4_
  282.0 3.6 %finish.1 = (f32[192,768]{1,0:T(8,128)}, f32[192,768]{1,0:T(8,128)}, f32[192,768]{1,0:T(8,128)}, f32[192,768]{1,0:T(8,128)}, f32[1,192]{1,0:T(1,128)}, /*index=5*/f32[1,192]{1,0:T(1,128)}, f32[8,12]{1,0:T(8,128)}) custom-call(s32[5]{0:T(128)} %stack.56.refs_0_, bf16[1,208,384]{2,1,0:T(8,128)(2,1)} %copy-done.9, bf16[1,208,384]{2,1,0:T(8,128)(2,1)} %copy-done.39, ...), custom_call_target="tpu_custom_call" | custom-call | flops 3000000000 | bytes 3000000 | tf_op jit(solution)/shard_map/finish/pallas_call | solution.py:575
  (199 shorter events, 49.7 us)
Async XLA Ops:
  0.6 13.3 %collective-permute-start = (bf16[256,768]{1,0:T(8,128)(2,1)}, bf16[256,768]{1,0:T(8,128)(2,1)S(1)}, u32[]{:S(2)}, u32[]{:S(2)}) collective-permute-start(bf16[256,768]{1,0:T(8,128)(2,1)} %bitcast.81), channel_id=1, source_target_pairs={{0,4},{4,0},{8,12},{12,8},{16,20},{20,16},{24,28},{28,24},{1,5},{5... | collective-permute-start | bytes 1179656 | tf_op jit(solution)/shard_map/ppermute | solution.py:882
  3.6 12.7 %collective-permute-start.1 = (bf16[256,768]{1,0:T(8,128)(2,1)}, bf16[256,768]{1,0:T(8,128)(2,1)S(1)}, u32[]{:S(2)}, u32[]{:S(2)}) collective-permute-start(bf16[256,768]{1,0:T(8,128)(2,1)} %bitcast.82), channel_id=1, source_target_pairs={{24,16},{28,20},{16,8},{20,12},{8,0},{12,4},{25,17},{29,21},{17,9}... | collective-permute-start | bytes 1179656 | tf_op jit(solution)/shard_map/ppermute | solution.py:886
  4.9 12.7 %collective-permute-start.2 = (bf16[256,768]{1,0:T(8,128)(2,1)}, bf16[256,768]{1,0:T(8,128)(2,1)S(1)}, u32[]{:S(2)}, u32[]{:S(2)}) collective-permute-start(bf16[256,768]{1,0:T(8,128)(2,1)} %bitcast.83), channel_id=1, source_target_pairs={{0,8},{4,12},{8,16},{12,20},{16,24},{20,28},{1,9},{5,13},{9,17},{1... | collective-permute-start | bytes 1179656 | tf_op jit(solution)/shard_map/ppermute | solution.py:886
  13.9 16.4 %collective-permute-start.6 = (bf16[1,208,3072]{2,1,0:T(8,128)(2,1)S(1)}, bf16[1,208,3072]{2,1,0:T(8,128)(2,1)}, u32[]{:S(2)}, u32[]{:S(2)}) collective-permute-start(bf16[1,208,3072]{2,1,0:T(8,128)(2,1)S(1)} %maximum_bitcast_fusion.refs_11_.refs_21_), channel_id=1, source_target_pairs={{0,1},{1,0},{2,3},{3,2},{4,5},{5,4},{6,7},{7,6},{8,9},{9,8},{10,11... | collective-permute-start | bytes 3833864 | tf_op jit(solution)/shard_map/ppermute | solution.py:882
  17.7 11.9 %collective-permute-start.4 = (bf16[256,768]{1,0:T(8,128)(2,1)S(1)}, bf16[256,768]{1,0:T(8,128)(2,1)S(1)}, u32[]{:S(2)}, u32[]{:S(2)}) collective-permute-start(bf16[256,768]{1,0:T(8,128)(2,1)S(1)} %collective-permute-done.1), channel_id=1, source_target_pairs={{16,8},{20,12},{8,0},{12,4},{17,9},{21,13},{9,1},{13,5},{18,10},{2... | collective-permute-start | bytes 1179656 | tf_op jit(solution)/shard_map/ppermute | solution.py:886
  19.0 10.6 %collective-permute-start.5 = (bf16[256,768]{1,0:T(8,128)(2,1)S(1)}, bf16[256,768]{1,0:T(8,128)(2,1)S(1)}, u32[]{:S(2)}, u32[]{:S(2)}) collective-permute-start(bf16[256,768]{1,0:T(8,128)(2,1)S(1)} %collective-permute-done.2), channel_id=1, source_target_pairs={{8,16},{12,20},{16,24},{20,28},{9,17},{13,21},{17,25},{21,29},{10,... | collective-permute-start | bytes 1179656 | tf_op jit(solution)/shard_map/ppermute | solution.py:886
  19.7 10.7 %collective-permute-start.3 = (bf16[256,768]{1,0:T(8,128)(2,1)S(1)}, bf16[256,768]{1,0:T(8,128)(2,1)}, u32[]{:S(2)}, u32[]{:S(2)}) collective-permute-start(bf16[256,768]{1,0:T(8,128)(2,1)S(1)} %broadcast_select_fusion.4), channel_id=1, source_target_pairs={{0,4},{4,0},{8,12},{12,8},{16,20},{20,16},{24,28},{28,24},{1,5},{5... | collective-permute-start | bytes 1179656 | tf_op jit(solution)/shard_map/ppermute | solution.py:882
  20.1 28.5 %collective-permute-start.10 = (bf16[1,208,3072]{2,1,0:T(8,128)(2,1)S(1)}, bf16[1,208,3072]{2,1,0:T(8,128)(2,1)}, u32[]{:S(2)}, u32[]{:S(2)}) collective-permute-start(bf16[1,208,3072]{2,1,0:T(8,128)(2,1)S(1)} %maximum_bitcast_fusion.refs_11_.refs_21_), channel_id=1, source_target_pairs={{0,2},{1,3},{2,0},{3,1},{4,6},{5,7},{6,4},{7,5},{8,10},{9,11},{10,... | collective-permute-start | bytes 3833864 | tf_op jit(solution)/shard_map/ppermute | solution.py:882
  31.2 12.3 %collective-permute-start.8 = (bf16[256,768]{1,0:T(8,128)(2,1)}, bf16[256,768]{1,0:T(8,128)(2,1)}, u32[]{:S(2)}, u32[]{:S(2)}) collective-permute-start(bf16[256,768]{1,0:T(8,128)(2,1)} %broadcast_select_fusion.2), channel_id=1, source_target_pairs={{16,24},{20,28},{8,0},{12,4},{17,25},{21,29},{9,1},{13,5},{18,26},... | collective-permute-start | bytes 1179656 | tf_op jit(solution)/shard_map/ppermute | solution.py:886
  32.5 12.0 %collective-permute-start.7 = (bf16[256,768]{1,0:T(8,128)(2,1)}, bf16[256,768]{1,0:T(8,128)(2,1)}, u32[]{:S(2)}, u32[]{:S(2)}) collective-permute-start(bf16[256,768]{1,0:T(8,128)(2,1)} %broadcast_select_fusion.3), channel_id=1, source_target_pairs={{0,4},{4,0},{8,12},{12,8},{16,20},{20,16},{24,28},{28,24},{1,5},{5... | collective-permute-start | bytes 1179656 | tf_op jit(solution)/shard_map/ppermute | solution.py:882
  44.5 7.8 %collective-permute-start.9 = (bf16[256,768]{1,0:T(8,128)(2,1)S(1)}, bf16[256,768]{1,0:T(8,128)(2,1)S(1)}, u32[]{:S(2)}, u32[]{:S(2)}) collective-permute-start(bf16[256,768]{1,0:T(8,128)(2,1)S(1)} %select_select_fusion), channel_id=1, source_target_pairs={{0,4},{4,0},{8,12},{12,8},{16,20},{20,16},{24,28},{28,24},{1,5},{5... | collective-permute-start | bytes 1179656 | tf_op jit(solution)/shard_map/ppermute | solution.py:882
  52.4 6.5 %collective-permute-start.11 = (bf16[1,208,3072]{2,1,0:T(8,128)(2,1)}, bf16[1,208,3072]{2,1,0:T(8,128)(2,1)S(1)}, u32[]{:S(2)}, u32[]{:S(2)}) collective-permute-start(bf16[1,208,3072]{2,1,0:T(8,128)(2,1)} %collective-permute-done.10.refs_13_.refs_23_), channel_id=1, source_target_pairs={{0,1},{1,0},{2,3},{3,2},{4,5},{5,4},{6,7},{7,6},{8,9},{9,8},{10,11... | collective-permute-start | bytes 3833864 | tf_op jit(solution)/shard_map/ppermute | solution.py:882
  52.4 4.0 %collective-permute-start.14 = (bf16[2,192,768]{2,1,0:T(8,128)(2,1)S(1)}, bf16[2,192,768]{2,1,0:T(8,128)(2,1)S(1)}, u32[]{:S(2)}, u32[]{:S(2)}) collective-permute-start(bf16[2,192,768]{2,1,0:T(8,128)(2,1)S(1)} %pad_maximum_fusion), channel_id=1, source_target_pairs={{0,1},{1,0},{2,3},{3,2},{4,5},{5,4},{6,7},{7,6},{8,9},{9,8},{10,11... | collective-permute-start | bytes 1769480 | tf_op jit(solution)/shard_map/ppermute | solution.py:882
  53.7 30.2 %collective-permute-start.13 = (bf16[256,768]{1,0:T(8,128)(2,1)}, bf16[256,768]{1,0:T(8,128)(2,1)S(1)}, u32[]{:S(2)}, u32[]{:S(2)}) collective-permute-start(bf16[256,768]{1,0:T(8,128)(2,1)} %bitcast.94), channel_id=1, source_target_pairs={{0,1},{1,0},{2,3},{3,2},{4,5},{5,4},{6,7},{7,6},{8,9},{9,8},{10,11... | collective-permute-start | bytes 1179656 | tf_op jit(solution)/shard_map/ppermute | solution.py:882
  53.7 30.1 %collective-permute-start.19 = (bf16[256,768]{1,0:T(8,128)(2,1)}, bf16[256,768]{1,0:T(8,128)(2,1)S(1)}, u32[]{:S(2)}, u32[]{:S(2)}) collective-permute-start(bf16[256,768]{1,0:T(8,128)(2,1)} %bitcast.95), channel_id=1, source_target_pairs={{0,2},{1,3},{2,0},{3,1},{4,6},{5,7},{6,4},{7,5},{8,10},{9,11},{10,... | collective-permute-start | bytes 1179656 | tf_op jit(solution)/shard_map/ppermute | solution.py:882
  57.2 26.7 %collective-permute-start.15 = (bf16[2,192,768]{2,1,0:T(8,128)(2,1)S(1)}, bf16[2,192,768]{2,1,0:T(8,128)(2,1)S(1)}, u32[]{:S(2)}, u32[]{:S(2)}) collective-permute-start(bf16[2,192,768]{2,1,0:T(8,128)(2,1)S(1)} %pad_maximum_fusion.1), channel_id=1, source_target_pairs={{0,2},{1,3},{2,0},{3,1},{4,6},{5,7},{6,4},{7,5},{8,10},{9,11},{10,... | collective-permute-start | bytes 1769480 | tf_op jit(solution)/shard_map/ppermute | solution.py:882
  78.4 7.0 %collective-permute-start.12 = (bf16[256,768]{1,0:T(8,128)(2,1)}, bf16[256,768]{1,0:T(8,128)(2,1)S(1)}, u32[]{:S(2)}, u32[]{:S(2)}) collective-permute-start(bf16[256,768]{1,0:T(8,128)(2,1)} %get-tuple-element.114), channel_id=1, source_target_pairs={{0,1},{1,0},{2,3},{3,2},{4,5},{5,4},{6,7},{7,6},{8,9},{9,8},{10,11... | collective-permute-start | bytes 1179656 | tf_op jit(solution)/shard_map/ppermute | solution.py:882
  83.8 11.8 %collective-permute-start.20 = (bf16[256,768]{1,0:T(8,128)(2,1)S(1)}, bf16[256,768]{1,0:T(8,128)(2,1)S(1)}, u32[]{:S(2)}, u32[]{:S(2)}) collective-permute-start(bf16[256,768]{1,0:T(8,128)(2,1)S(1)} %collective-permute-done.19), channel_id=1, source_target_pairs={{0,1},{1,0},{2,3},{3,2},{4,5},{5,4},{6,7},{7,6},{8,9},{9,8},{10,11... | collective-permute-start | bytes 1179656 | tf_op jit(solution)/shard_map/ppermute | solution.py:882
  83.9 11.7 %collective-permute-start.17 = (bf16[256,768]{1,0:T(8,128)(2,1)}, bf16[256,768]{1,0:T(8,128)(2,1)S(1)}, u32[]{:S(2)}, u32[]{:S(2)}) collective-permute-start(bf16[256,768]{1,0:T(8,128)(2,1)} %get-tuple-element.114), channel_id=1, source_target_pairs={{0,2},{1,3},{2,0},{3,1},{4,6},{5,7},{6,4},{7,5},{8,10},{9,11},{10,... | collective-permute-start | bytes 1179656 | tf_op jit(solution)/shard_map/ppermute | solution.py:882
  108.1 11.3 %collective-permute-start.25 = (bf16[256,768]{1,0:T(8,128)(2,1)S(1)}, bf16[256,768]{1,0:T(8,128)(2,1)}, u32[]{:S(2)}, u32[]{:S(2)}) collective-permute-start(bf16[256,768]{1,0:T(8,128)(2,1)S(1)} %fusion.6), channel_id=1, source_target_pairs={{0,2},{1,3},{2,0},{3,1},{4,6},{5,7},{6,4},{7,5},{8,10},{9,11},{10,... | collective-permute-start | bytes 1179656 | tf_op jit(solution)/shard_map/ppermute | solution.py:882
  119.5 63.0 %all-to-all-start = ((bf16[8,192,768]{2,1,0:T(8,128)(2,1)}), bf16[8,192,768]{2,1,0:T(8,128)(2,1)S(1)}, u32[]{:S(2)}, u32[]{:S(2)}) async-start(bf16[8,192,768]{2,1,0:T(8,128)(2,1)} %ffn_grads.1), calls=%async_computation | async-start | bytes 4718592 | tf_op jit(solution)/shard_map/all_to_all | solution.py:1058
  131.0 34.3 %collective-permute-start.22 = (bf16[256,768]{1,0:T(8,128)(2,1)S(1)}, bf16[256,768]{1,0:T(8,128)(2,1)S(1)}, u32[]{:S(2)}, u32[]{:S(2)}) collective-permute-start(bf16[256,768]{1,0:T(8,128)(2,1)S(1)} %fusion.7), channel_id=1, source_target_pairs={{0,2},{1,3},{2,0},{3,1},{4,6},{5,7},{6,4},{7,5},{8,10},{9,11},{10,... | collective-permute-start | bytes 1179656 | tf_op jit(solution)/shard_map/ppermute | solution.py:882
  182.5 7.7 %collective-permute-start.32 = (bf16[2,4,208,384]{3,2,1,0:T(8,128)(2,1)}, bf16[2,4,208,384]{3,2,1,0:T(8,128)(2,1)}, u32[]{:S(2)}, u32[]{:S(2)}) collective-permute-start(bf16[2,4,208,384]{3,2,1,0:T(8,128)(2,1)} %get-tuple-element.175), channel_id=1, source_target_pairs={{0,1},{1,0},{2,3},{3,2},{4,5},{5,4},{6,7},{7,6},{8,9},{9,8},{10,11... | collective-permute-start | bytes 3833864 | tf_op jit(solution)/shard_map/ppermute | solution.py:882
  182.5 9.5 %collective-permute-start.34 = (bf16[2,4,208,384]{3,2,1,0:T(8,128)(2,1)}, bf16[2,4,208,384]{3,2,1,0:T(8,128)(2,1)}, u32[]{:S(2)}, u32[]{:S(2)}) collective-permute-start(bf16[2,4,208,384]{3,2,1,0:T(8,128)(2,1)} %get-tuple-element.177), channel_id=1, source_target_pairs={{0,1},{1,0},{2,3},{3,2},{4,5},{5,4},{6,7},{7,6},{8,9},{9,8},{10,11... | collective-permute-start | bytes 3833864 | tf_op jit(solution)/shard_map/ppermute | solution.py:882
  185.7 4.4 %collective-permute-start.40 = (bf16[2,48,384]{2,1,0:T(8,128)(2,1)S(1)}, bf16[2,48,384]{2,1,0:T(8,128)(2,1)S(1)}, u32[]{:S(2)}, u32[]{:S(2)}) collective-permute-start(bf16[2,48,384]{2,1,0:T(8,128)(2,1)S(1)} %pad_maximum_fusion.7), channel_id=1, source_target_pairs={{0,2},{1,3},{2,0},{3,1},{4,6},{5,7},{6,4},{7,5},{8,10},{9,11},{10,... | collective-permute-start | bytes 221192 | tf_op jit(solution)/shard_map/ppermute | solution.py:882
  186.1 12.2 %collective-permute-start.28 = (bf16[256,768]{1,0:T(8,128)(2,1)}, bf16[256,768]{1,0:T(8,128)(2,1)S(1)}, u32[]{:S(2)}, u32[]{:S(2)}) collective-permute-start(bf16[256,768]{1,0:T(8,128)(2,1)} %get-tuple-element.169), channel_id=1, source_target_pairs={{0,4},{4,0},{8,12},{12,8},{16,20},{20,16},{24,28},{28,24},{1,5},{5... | collective-permute-start | bytes 1179656 | tf_op jit(solution)/shard_map/ppermute | solution.py:882
  187.3 18.3 %collective-permute-start.26 = (bf16[256,768]{1,0:T(8,128)(2,1)}, bf16[256,768]{1,0:T(8,128)(2,1)S(1)}, u32[]{:S(2)}, u32[]{:S(2)}) collective-permute-start(bf16[256,768]{1,0:T(8,128)(2,1)} %get-tuple-element.165), channel_id=1, source_target_pairs={{0,4},{4,0},{8,12},{12,8},{16,20},{20,16},{24,28},{28,24},{1,5},{5... | collective-permute-start | bytes 1179656 | tf_op jit(solution)/shard_map/ppermute | solution.py:882
  191.6 17.4 %collective-permute-start.33 = (bf16[4,208,384]{2,1,0:T(8,128)(2,1)S(1)}, bf16[4,208,384]{2,1,0:T(8,128)(2,1)S(1)}, u32[]{:S(2)}, u32[]{:S(2)}) collective-permute-start(bf16[4,208,384]{2,1,0:T(8,128)(2,1)S(1)} %fusion.8), channel_id=1, source_target_pairs={{0,2},{1,3},{2,0},{3,1},{4,6},{5,7},{6,4},{7,5},{8,10},{9,11},{10,... | collective-permute-start | bytes 1916936 | tf_op jit(solution)/shard_map/ppermute | solution.py:882
  193.3 27.3 %collective-permute-start.35 = (bf16[4,208,384]{2,1,0:T(8,128)(2,1)S(1)}, bf16[4,208,384]{2,1,0:T(8,128)(2,1)S(1)}, u32[]{:S(2)}, u32[]{:S(2)}) collective-permute-start(bf16[4,208,384]{2,1,0:T(8,128)(2,1)S(1)} %fusion.9), channel_id=1, source_target_pairs={{0,2},{1,3},{2,0},{3,1},{4,6},{5,7},{6,4},{7,5},{8,10},{9,11},{10,... | collective-permute-start | bytes 1916936 | tf_op jit(solution)/shard_map/ppermute | solution.py:882
  195.2 28.5 %collective-permute-start.41 = (bf16[1,192,768]{2,1,0:T(8,128)(2,1)S(1)}, bf16[1,192,768]{2,1,0:T(8,128)(2,1)S(1)}, u32[]{:S(2)}, u32[]{:S(2)}) collective-permute-start(bf16[1,192,768]{2,1,0:T(8,128)(2,1)S(1)} %maximum_bitcast_fusion.1.refs_1_), channel_id=1, source_target_pairs={{0,16},{4,20},{8,24},{12,28},{16,0},{20,4},{24,8},{28,12},{1,17},{... | collective-permute-start | bytes 884744 | tf_op jit(solution)/shard_map/ppermute | solution.py:882
  198.4 23.6 %collective-permute-start.29 = (bf16[256,768]{1,0:T(8,128)(2,1)S(1)}, bf16[256,768]{1,0:T(8,128)(2,1)S(1)}, u32[]{:S(2)}, u32[]{:S(2)}) collective-permute-start(bf16[256,768]{1,0:T(8,128)(2,1)S(1)} %add_convert_fusion.3), channel_id=1, source_target_pairs={{0,8},{4,12},{8,0},{12,4},{16,24},{20,28},{24,16},{28,20},{1,9},{5... | collective-permute-start | bytes 1179656 | tf_op jit(solution)/shard_map/ppermute | solution.py:882
  205.7 16.3 %collective-permute-start.31 = (bf16[256,768]{1,0:T(8,128)(2,1)S(1)}, bf16[256,768]{1,0:T(8,128)(2,1)S(1)}, u32[]{:S(2)}, u32[]{:S(2)}) collective-permute-start(bf16[256,768]{1,0:T(8,128)(2,1)S(1)} %copy-done.27), channel_id=1, source_target_pairs={{0,4},{4,0},{8,12},{12,8},{16,20},{20,16},{24,28},{28,24},{1,5},{5... | collective-permute-start | bytes 1179656 | tf_op jit(solution)/shard_map/ppermute | solution.py:882
  209.0 16.2 %collective-permute-start.27 = (bf16[256,768]{1,0:T(8,128)(2,1)S(1)}, bf16[256,768]{1,0:T(8,128)(2,1)S(1)}, u32[]{:S(2)}, u32[]{:S(2)}) collective-permute-start(bf16[256,768]{1,0:T(8,128)(2,1)S(1)} %copy-done.25), channel_id=1, source_target_pairs={{0,4},{4,0},{8,12},{12,8},{16,20},{20,16},{24,28},{28,24},{1,5},{5... | collective-permute-start | bytes 1179656 | tf_op jit(solution)/shard_map/ppermute | solution.py:882
  222.3 10.5 %collective-permute-start.37 = (bf16[2,208,384]{2,1,0:T(8,128)(2,1)S(1)}, bf16[2,208,384]{2,1,0:T(8,128)(2,1)S(1)}, u32[]{:S(2)}, u32[]{:S(2)}) collective-permute-start(bf16[2,208,384]{2,1,0:T(8,128)(2,1)S(1)} %pad_maximum_fusion.4), channel_id=1, source_target_pairs={{0,4},{4,0},{8,12},{12,8},{16,20},{20,16},{24,28},{28,24},{1,5},{5... | collective-permute-start | bytes 958472 | tf_op jit(solution)/shard_map/ppermute | solution.py:882
  223.7 20.1 %collective-permute-start.42 = (bf16[2,192,768]{2,1,0:T(8,128)(2,1)S(1)}, bf16[2,192,768]{2,1,0:T(8,128)(2,1)S(1)}, u32[]{:S(2)}, u32[]{:S(2)}) collective-permute-start(bf16[2,192,768]{2,1,0:T(8,128)(2,1)S(1)} %pad_maximum_fusion.2), channel_id=1, source_target_pairs={{0,8},{4,12},{8,0},{12,4},{16,24},{20,28},{24,16},{28,20},{1,9},{5... | collective-permute-start | bytes 1769480 | tf_op jit(solution)/shard_map/ppermute | solution.py:882
  225.3 14.5 %collective-permute-start.36 = (bf16[2,208,384]{2,1,0:T(8,128)(2,1)S(1)}, bf16[2,208,384]{2,1,0:T(8,128)(2,1)S(1)}, u32[]{:S(2)}, u32[]{:S(2)}) collective-permute-start(bf16[2,208,384]{2,1,0:T(8,128)(2,1)S(1)} %pad_maximum_fusion.3), channel_id=1, source_target_pairs={{0,4},{4,0},{8,12},{12,8},{16,20},{20,16},{24,28},{28,24},{1,5},{5... | collective-permute-start | bytes 958472 | tf_op jit(solution)/shard_map/ppermute | solution.py:882
  233.0 10.7 %collective-permute-start.38 = (bf16[2,208,384]{2,1,0:T(8,128)(2,1)S(1)}, bf16[2,208,384]{2,1,0:T(8,128)(2,1)S(1)}, u32[]{:S(2)}, u32[]{:S(2)}) collective-permute-start(bf16[2,208,384]{2,1,0:T(8,128)(2,1)S(1)} %add_convert_fusion.7), channel_id=1, source_target_pairs={{0,8},{4,12},{8,0},{12,4},{16,24},{20,28},{24,16},{28,20},{1,9},{5... | collective-permute-start | bytes 958472 | tf_op jit(solution)/shard_map/ppermute | solution.py:882
  234.7 12.8 %collective-permute-start.49 = (bf16[1,192,768]{2,1,0:T(8,128)(2,1)S(1)}, bf16[1,192,768]{2,1,0:T(8,128)(2,1)S(1)}, u32[]{:S(2)}, u32[]{:S(2)}) collective-permute-start(bf16[1,192,768]{2,1,0:T(8,128)(2,1)S(1)} %maximum_bitcast_fusion.1.refs_1_), channel_id=1, source_target_pairs={{0,4},{4,0},{8,12},{12,8},{16,20},{20,16},{24,28},{28,24},{1,5},{5... | collective-permute-start | bytes 884744 | tf_op jit(solution)/shard_map/ppermute | solution.py:882
  243.8 8.2 %collective-permute-start.43 = (bf16[208,384]{1,0:T(8,128)(2,1)S(1)}, bf16[208,384]{1,0:T(8,128)(2,1)S(1)}, u32[]{:S(2)}, u32[]{:S(2)}) collective-permute-start(bf16[208,384]{1,0:T(8,128)(2,1)S(1)} %slice_bitcast_fusion), channel_id=1, source_target_pairs={{0,16},{4,20},{8,24},{12,28},{16,0},{20,4},{24,8},{28,12},{1,17},{... | collective-permute-start | bytes 479240 | tf_op jit(solution)/shard_map/ppermute | solution.py:882
  244.3 31.4 %collective-permute-start.30 = (bf16[256,768]{1,0:T(8,128)(2,1)S(1)}, bf16[256,768]{1,0:T(8,128)(2,1)S(1)}, u32[]{:S(2)}, u32[]{:S(2)}) collective-permute-start(bf16[256,768]{1,0:T(8,128)(2,1)S(1)} %add_convert_fusion.4), channel_id=1, source_target_pairs={{0,8},{4,12},{8,0},{12,4},{16,24},{20,28},{24,16},{28,20},{1,9},{5... | collective-permute-start | bytes 1179656 | tf_op jit(solution)/shard_map/ppermute | solution.py:882
  246.1 9.9 %collective-permute-start.46 = (bf16[1,192,768]{2,1,0:T(8,128)(2,1)S(1)}, bf16[1,192,768]{2,1,0:T(8,128)(2,1)S(1)}, u32[]{:S(2)}, u32[]{:S(2)}) collective-permute-start(bf16[1,192,768]{2,1,0:T(8,128)(2,1)S(1)} %collective-permute-done.41.refs_5_), channel_id=1, source_target_pairs={{0,4},{4,0},{8,12},{12,8},{16,20},{20,16},{24,28},{28,24},{1,5},{5... | collective-permute-start | bytes 884744 | tf_op jit(solution)/shard_map/ppermute | solution.py:882
  247.5 19.9 %collective-permute-start.50 = (bf16[2,192,768]{2,1,0:T(8,128)(2,1)S(1)}, bf16[2,192,768]{2,1,0:T(8,128)(2,1)S(1)}, u32[]{:S(2)}, u32[]{:S(2)}) collective-permute-start(bf16[2,192,768]{2,1,0:T(8,128)(2,1)S(1)} %collective-permute-done.42.refs_3_), channel_id=1, source_target_pairs={{0,4},{4,0},{8,12},{12,8},{16,20},{20,16},{24,28},{28,24},{1,5},{5... | collective-permute-start | bytes 1769480 | tf_op jit(solution)/shard_map/ppermute | solution.py:882
  252.1 12.7 %collective-permute-start.44 = (bf16[1,208,384]{2,1,0:T(8,128)(2,1)S(1)}, bf16[1,208,384]{2,1,0:T(8,128)(2,1)S(1)}, u32[]{:S(2)}, u32[]{:S(2)}) collective-permute-start(bf16[1,208,384]{2,1,0:T(8,128)(2,1)S(1)} %fusion.13.refs_1_), channel_id=1, source_target_pairs={{0,16},{4,20},{8,24},{12,28},{16,0},{20,4},{24,8},{28,12},{1,17},{... | collective-permute-start | bytes 479240 | tf_op jit(solution)/shard_map/ppermute | solution.py:882
  256.1 23.0 %collective-permute-start.47 = (bf16[1,208,384]{2,1,0:T(8,128)(2,1)S(1)}, bf16[1,208,384]{2,1,0:T(8,128)(2,1)S(1)}, u32[]{:S(2)}, u32[]{:S(2)}) collective-permute-start(bf16[1,208,384]{2,1,0:T(8,128)(2,1)S(1)} %fusion.13.refs_1_), channel_id=1, source_target_pairs={{0,4},{4,0},{8,12},{12,8},{16,20},{20,16},{24,28},{28,24},{1,5},{5... | collective-permute-start | bytes 479240 | tf_op jit(solution)/shard_map/ppermute | solution.py:882
  264.8 12.1 %collective-permute-start.45 = (bf16[256,768]{1,0:T(8,128)(2,1)S(1)}, bf16[256,768]{1,0:T(8,128)(2,1)S(1)}, u32[]{:S(2)}, u32[]{:S(2)}) collective-permute-start(bf16[256,768]{1,0:T(8,128)(2,1)S(1)} %add_convert_fusion.2), channel_id=1, source_target_pairs={{0,16},{4,20},{8,24},{12,28},{16,0},{20,4},{24,8},{28,12},{1,17},{... | collective-permute-start | bytes 1179656 | tf_op jit(solution)/shard_map/ppermute | solution.py:882
  264.9 9.4 %collective-permute-start.48 = (bf16[2,208,384]{2,1,0:T(8,128)(2,1)S(1)}, bf16[2,208,384]{2,1,0:T(8,128)(2,1)S(1)}, u32[]{:S(2)}, u32[]{:S(2)}) collective-permute-start(bf16[2,208,384]{2,1,0:T(8,128)(2,1)S(1)} %pad_maximum_fusion.5), channel_id=1, source_target_pairs={{0,8},{4,12},{8,0},{12,4},{16,24},{20,28},{24,16},{28,20},{1,9},{5... | collective-permute-start | bytes 958472 | tf_op jit(solution)/shard_map/ppermute | solution.py:882
  267.4 6.8 %collective-permute-start.51 = (bf16[1,208,384]{2,1,0:T(8,128)(2,1)S(1)}, bf16[1,208,384]{2,1,0:T(8,128)(2,1)S(1)}, u32[]{:S(2)}, u32[]{:S(2)}) collective-permute-start(bf16[1,208,384]{2,1,0:T(8,128)(2,1)S(1)} %collective-permute-done.44.refs_5_), channel_id=1, source_target_pairs={{0,4},{4,0},{8,12},{12,8},{16,20},{20,16},{24,28},{28,24},{1,5},{5... | collective-permute-start | bytes 479240 | tf_op jit(solution)/shard_map/ppermute | solution.py:882
  274.3 7.0 %collective-permute-start.52 = (bf16[2,208,384]{2,1,0:T(8,128)(2,1)S(1)}, bf16[2,208,384]{2,1,0:T(8,128)(2,1)S(1)}, u32[]{:S(2)}, u32[]{:S(2)}) collective-permute-start(bf16[2,208,384]{2,1,0:T(8,128)(2,1)S(1)} %collective-permute-done.48.refs_3_), channel_id=1, source_target_pairs={{0,4},{4,0},{8,12},{12,8},{16,20},{20,16},{24,28},{28,24},{1,5},{5... | collective-permute-start | bytes 958472 | tf_op jit(solution)/shard_map/ppermute | solution.py:882
  (48 other events, 382.3 us)
